TPU v7x, 128 devices: a whole 4x4x4 slice. The times are simulated.
128 devices in a mesh: row: 8 (over y, core), col: 16 (over x, z).
Axes of the slice: x: 4, y: 4, z: 4, core: 2. Of those that a mesh axis runs over, the one named last changes fastest.
Arguments:
- x_feat: bfloat16 [65536, 256], P(('row', 'col')), may hold values from -6 to 6
- block_values: bfloat16 [8, 16, 128, 128, 128], P('row', 'col')
- block_rows: int32 [8, 16, 128], P('row', 'col'), may hold values from 0 to 63, as said below
- block_cols: int32 [8, 16, 128], P('row', 'col'), may hold values from 0 to 31
- weight: bfloat16 [256, 256], replicated, may hold values from -0.375 to 0.375
- bias: float32 [256], replicated, may hold values from -3 to 3
- cotangent: bfloat16 [65536, 256], P(('row', 'col')), may hold values from -6 to 6
Outputs:
- out_act: bfloat16 [65536, 256], P(('row', 'col'))
- x_grad: bfloat16 [65536, 256], P(('row', 'col'))
- weight_grad: float32 [256, 256], replicated
- bias_grad: float32 [256], replicated
Inputs may be any that keep to these rules, and one draw needn't show every extreme that they name: `block_rows`: in tile (i, j), slots g * 8 to (g + 1) * 8 - 1 hold blocks of block rows g * 4 to (g + 1) * 4 - 1 of the tile; within a tile no pair of block row and block column repeats.
All inputs are finite; a program needn't handle non-finite values.
Results may differ from a plain program's by a relative error of at most 0.025.
Values may be sent and summed in bfloat16 or wider, within the bound.
No kernel may reach another device: no remote copies, remote signals or barrier semaphores. Data moves between devices by JAX's collectives and lax.ppermute only.
A program may use at most 64 MiB of HBM per device.

v0:
```python
import math

import jax
import jax.numpy as jnp
from jax import lax
from jax.sharding import PartitionSpec as P


def shards(x_feat, block_values, block_rows, block_cols, weight, bias, cotangent):
    block_size = block_values.shape[-1]
    block_count = block_values.shape[2]
    shard_rows = x_feat.shape[0]
    feature_width = x_feat.shape[1]
    per_shard = shard_rows // block_size
    cols_count = lax.axis_size("col")
    rows_count = lax.axis_size("row")
    per_group = block_count // cols_count
    values = block_values.reshape(cols_count, per_group, block_size, block_size)
    row_ids = block_rows.reshape(cols_count, per_group)
    col_ids = block_cols.reshape(cols_count, per_group)
    select = jnp.arange(per_shard, dtype=jnp.int32)
    gathered = lax.all_gather(x_feat, "row", axis=0, tiled=True)
    panel_blocks = gathered.reshape(rows_count * per_shard, block_size, feature_width)

    def forward_group(group):
        group_values = lax.dynamic_index_in_dim(values, group, 0, keepdims=False)
        local_rows = lax.dynamic_index_in_dim(row_ids, group, 0, keepdims=False) - group * per_shard
        group_cols = lax.dynamic_index_in_dim(col_ids, group, 0, keepdims=False)
        picked = jnp.take(panel_blocks, group_cols, axis=0)
        products = jnp.einsum(
            "bij,bjf->bif", group_values, picked, preferred_element_type=jnp.float32
        )
        onehot = (local_rows[None, :] == select[:, None]).astype(jnp.float32)
        summed = jnp.einsum("pb,bif->pif", onehot, products, precision=lax.Precision.HIGHEST)
        return summed.reshape(shard_rows, feature_width)

    count = cols_count * shard_rows
    first_group = 0 // shard_rows
    group_total = count // shard_rows

    def one_group(offset):
        return forward_group(first_group + offset)

    terms = lax.map(one_group, jnp.arange(group_total, dtype=jnp.int32))
    aggregated_sum = lax.psum_scatter(
        terms.reshape(count, feature_width).astype(jnp.bfloat16),
        "col",
        scatter_dimension=0,
        tiled=True,
    )
    pre = jnp.dot(aggregated_sum, weight, preferred_element_type=jnp.float32) + bias
    sigmoid_pre = jax.nn.sigmoid(pre)
    out_act = (pre * sigmoid_pre).astype(jnp.bfloat16)
    grad_pre = (
        cotangent.astype(jnp.float32) * sigmoid_pre * (1.0 + pre * (1.0 - sigmoid_pre))
    ).astype(jnp.bfloat16)
    local_weight = lax.dot_general(
        aggregated_sum, grad_pre, (((0,), (0,)), ((), ())), preferred_element_type=jnp.float32
    )
    local_bias = jnp.sum(grad_pre.astype(jnp.float32), axis=0)
    total_weight, total_bias = lax.psum((local_weight, local_bias), ("row", "col"))
    scale = 1.0 / math.sqrt(shard_rows * rows_count * cols_count)
    grad_agg = lax.dot_general(
        grad_pre, weight, (((1,), (1,)), ((), ())), preferred_element_type=jnp.float32
    ).astype(jnp.bfloat16)

    def backward_group(carry, group, shard_grad):
        grad_blocks = shard_grad.reshape(per_shard, block_size, feature_width)
        group_values = lax.dynamic_index_in_dim(values, group, 0, keepdims=False)
        local_rows = lax.dynamic_index_in_dim(row_ids, group, 0, keepdims=False) - group * per_shard
        group_cols = lax.dynamic_index_in_dim(col_ids, group, 0, keepdims=False)
        picked = jnp.take(grad_blocks, local_rows, axis=0)
        products = jnp.einsum(
            "bij,bif->bjf", group_values, picked, preferred_element_type=jnp.float32
        )
        return carry.at[group_cols].add(products)

    zeros_panel = jnp.zeros((rows_count * per_shard, block_size, feature_width), jnp.float32)
    gathered_grad = lax.all_gather(grad_agg, "col", axis=0, tiled=True)

    def advance_whole(group, inner):
        shard_grad = lax.dynamic_slice_in_dim(gathered_grad, group * shard_rows, shard_rows, 0)
        return backward_group(inner, group, shard_grad)

    collected = lax.fori_loop(0, cols_count, advance_whole, zeros_panel)
    feature_sum = lax.psum_scatter(
        collected.reshape(rows_count * shard_rows, feature_width).astype(jnp.bfloat16),
        "row",
        scatter_dimension=0,
        tiled=True,
    )
    return (out_act, feature_sum, total_weight * scale, total_bias * scale)


def solution(mesh):
    placed = (
        P(("row", "col"), None),
        P("row", "col", None, None, None),
        P("row", "col", None),
        P("row", "col", None),
        P(),
        P(),
        P(("row", "col"), None),
    )
    return jax.shard_map(
        shards,
        mesh=mesh,
        in_specs=placed,
        out_specs=(P(("row", "col"), None), P(("row", "col"), None), P(), P()),
        check_vma=False,
    )
```

profile of v0, /device:TPU:1, one launch (start us, length us, event | category | flops | bytes accessed | tf_op | source)
XLA Modules:
  0.0 494.9 jit_solution(14785330268408700120)
XLA Ops:
  8.5 1.3 reduce.6
  9.9 1.3 reduce.7
  11.3 27.3 %all-gather.3.cloned.1.call-done = bf16[4096,256]{1,0:T(8,128)(2,1)} async-done(((bf16[512,256]{1,0:T(8,128)(2,1)}), bf16[4096,256]{1,0:T(8,128)(2,1)}) %all-gather.3.cloned.1.call-update) | async-done | bytes 2097168 | tf_op jit(solution)/shard_map/all_gather | solution.py:22
  38.6 139.2 %while.25 = (s32[]{:T(128)}, bf16[16,512,256]{2,1,0:T(8,128)(2,1)}, s32[16]{0:T(128)S(1)}, s32[16,8]{1,0:T(8,128)S(1)}, bf16[16,8,128,128]{3,2,1,0:T(8,128)(2,1)...) while((s32[]{:T(128)}, bf16[16,512,256]{2,1,0:T(8,128)(2,1)}, ...), condition=%wide.region_1.2_spmd.clone, body=%wide.region_0.1_spmd.clone.sunk | while | flops 79955064 | bytes 5247947 | solution.py:44
  41.1 2.2 gather_fusion.1
  43.3 1.3 fusion.58
  49.8 2.2 gather_fusion.1
  52.0 1.3 fusion.58
  58.5 2.2 gather_fusion.1
  60.7 1.3 fusion.58
  67.2 2.2 gather_fusion.1
  69.4 1.3 fusion.58
  75.9 2.2 gather_fusion.1
  78.1 1.3 fusion.58
  84.6 2.2 gather_fusion.1
  86.8 1.3 fusion.58
  93.3 2.2 gather_fusion.1
  95.5 1.3 fusion.58
  102.0 2.2 gather_fusion.1
  104.2 1.3 fusion.58
  110.7 2.2 gather_fusion.1
  112.9 1.3 fusion.58
  119.4 2.2 gather_fusion.1
  121.7 1.3 fusion.58
  128.1 2.2 gather_fusion.1
  130.3 1.3 fusion.58
  136.8 2.2 gather_fusion.1
  139.0 1.3 fusion.58
  145.5 2.2 gather_fusion.1
  147.8 1.3 fusion.58
  154.3 2.2 gather_fusion.1
  156.5 1.3 fusion.58
  163.0 2.2 gather_fusion.1
  171.7 2.2 gather_fusion.1
  173.9 1.3 fusion.58
  177.9 76.2 %reduce-scatter.3.cloned.1.call-done = bf16[512,256]{1,0:T(8,128)(2,1)} async-done(((bf16[8192,256]{1,0:T(8,128)(2,1)}), bf16[512,256]{1,0:T(8,128)(2,1)}) %reduce-scatter.3.cloned.1.call-update) | async-done | bytes 262160 | tf_op jit(solution)/shard_map/reduce_scatter | solution.py:45
  254.1 2.1 convert_reduce_fusion
  258.3 51.6 %all-gather.5.cloned.1.call-done = bf16[8192,256]{1,0:T(8,128)(2,1)} async-done(((bf16[512,256]{1,0:T(8,128)(2,1)}), bf16[8192,256]{1,0:T(8,128)(2,1)}) %all-gather.5.cloned.1.call-update) | async-done | bytes 4194320 | tf_op jit(solution)/shard_map/all_gather | solution.py:79
  310.0 2.5 broadcast_in_dim.47
  312.4 100.0 %while.24 = (s32[]{:T(128)}, f32[32,128,256]{2,1,0:T(8,128)}, s32[16,8]{1,0:T(8,128)S(1)}, bf16[16,8,128,128]{3,2,1,0:T(8,128)(2,1)}, s32[16,8]{1,0:T(8,128)S(1)...) while((s32[]{:T(128)}, f32[32,128,256]{2,1,0:T(8,128)}, ...), condition=%wide.region_5.6_spmd, body=%wide.region_3.5_spmd.sunk | while | flops 67634296 | bytes 6558667 | solution.py:85
  315.4 3.3 scatter_fusion
  321.7 3.3 scatter_fusion
  326.5 1.3 fusion.52
  327.9 3.2 scatter_fusion
  332.7 1.3 fusion.52
  334.1 3.3 scatter_fusion
  339.0 1.3 fusion.52
  340.3 3.3 scatter_fusion
  345.3 1.3 fusion.52
  346.6 3.3 scatter_fusion
  352.8 3.3 scatter_fusion
  359.1 3.4 scatter_fusion
  365.4 3.3 scatter_fusion
  371.7 3.3 scatter_fusion
  377.9 3.3 scatter_fusion
  384.2 3.3 scatter_fusion
  390.4 3.3 scatter_fusion
  396.6 3.3 scatter_fusion
  402.8 3.4 scatter_fusion
  409.1 3.3 scatter_fusion
  412.4 3.9 convert_element_type.34
  416.3 65.2 %psum.15 = f32[256]{0:T(256)S(1)} all-reduce(f32[256]{0:T(256)S(1)} %get-tuple-element.211), channel_id=1, replica_groups=mesh['row'=8,'col'=16] {'row','col'}, use_global_device_ids=true, to_apply=%region_9.10 | all-reduce | flops 256 | bytes 2048 | tf_op jit(solution)/shard_map/psum | solution.py:61
  482.1 1.7 broadcast_multiply_fusion
  483.8 4.6 reduce-scatter.5.cloned.1.call-done
  (248 shorter events, 87.6 us)
Async XLA Ops:
  7.2 246.9 %copy-start = (bf16[256,256]{1,0:T(8,128)(2,1)S(1)}, bf16[256,256]{1,0:T(8,128)(2,1)}, u32[]{:S(2)}) copy-start(bf16[256,256]{1,0:T(8,128)(2,1)} %param.15) | copy-start | bytes 393220
  7.2 31.4 %all-gather.3.cloned.1.call-start = ((), (), s32[]{:S(2)}) async-start(), calls=%async_computation.2 | async-start | bytes 2359296 | tf_op jit(solution)/shard_map/all_gather | solution.py:22
  7.9 246.2 %reduce-scatter.3.cloned.1.call-start = ((), (), s32[]{:S(2)}) async-start(), calls=%async_computation.3 | async-start | bytes 4456448 | tf_op jit(solution)/shard_map/reduce_scatter | solution.py:45
  177.8 76.3 %copy-start.2 = (bf16[512,256]{1,0:T(8,128)(2,1)S(1)}, bf16[512,256]{1,0:T(8,128)(2,1)}, u32[]{:S(2)}) copy-start(bf16[512,256]{1,0:T(8,128)(2,1)} %param.17) | copy-start | bytes 786436
  177.8 76.3 %copy-start.3 = (f32[256]{0:T(256)S(1)}, f32[256]{0:T(256)}, u32[]{:S(2)}) copy-start(f32[256]{0:T(256)} %param.16) | copy-start | bytes 3076
  177.8 132.2 %all-gather.5.cloned.1.call-start = ((), (), s32[]{:S(2)}) async-start(), calls=%async_computation.4 | async-start | bytes 4456448 | tf_op jit(solution)/shard_map/all_gather | solution.py:79
  254.1 3.2 copy-start.1
  257.2 224.9 %all-reduce.2.cloned.1.call-start = ((), (), s32[]{:S(2)}) async-start(), calls=%async_computation.6 | async-start | bytes 524288 | tf_op jit(solution)/shard_map/psum | solution.py:61
  258.3 230.1 %reduce-scatter.5.cloned.1.call-start = ((), (), s32[]{:S(2)}) async-start(), calls=%async_computation.5 | async-start | bytes 2359296 | tf_op jit(solution)/shard_map/reduce_scatter | solution.py:86
Sparse Core Ops, SparseCore 0:
  9.7 28.7 all-gather.2
  177.9 76.1 reduce-scatter.2
  257.4 52.5 all-gather.4
  315.9 141.1 all-reduce.1
  460.0 28.3 reduce-scatter.4
where the time goes:
time: 500 us; the launch traced here: 495 us
  waiting for transfers between devices  160 us (32%)
  local copies, waits for them, and re-layouts  84.1 us (17%)
  blocking collectives  65.2 us (13%)
  matrix products  64.9 us (13%)
  other arithmetic  63.1 us (13%)
  loops' own time  43 us (9%)
  between operations  13.8 us (3%)
    reduce_scatter x1, waiting for transfers between devices, shards(): lax.psum_scatter(terms.reshape(count, feature_width).astype(jnp.bfloat16)...  76.2 us
    psum x1, blocking collectives, shards(): lax.psum((local_weight, local_bias), ('row', 'col'))  65.2 us
    scatter-add x16, other arithmetic, backward_group(): return carry.at[group_cols].add(products)  52.9 us
    all_gather x1, waiting for transfers between devices, shards(): gathered_grad = lax.all_gather(grad_agg, 'col', axis=0, tiled=True)  51.6 us
    another operation x1, loops' own time, shards(): terms = lax.map(one_group, jnp.arange(group_total, dtype=jnp.int32))  42.4 us
    gather x16, local copies, waits for them, and re-layouts, forward_group(): picked = jnp.take(panel_blocks, group_cols, axis=0)  34.7 us
    all_gather x1, waiting for transfers between devices, shards(): gathered = lax.all_gather(x_feat, 'row', axis=0, tiled=True)  27.3 us
    dot_general x16, matrix products, forward_group(): jnp.einsum('bij,bjf->bif', group_values, picked, preferred_element_type=j...  21.1 us
  transfers between devices with their start and end apart: 5, of which 4 were waited for; matrix products, arithmetic and copies ran while one was open for 23% of the time, Pallas kernels for 0%

commit v1 on v0

v1 whole, which is shorter than its diff:
```python
import math

import jax
import jax.numpy as jnp
from jax import lax
from jax.experimental import pallas as pl
from jax.experimental.pallas import tpu as pltpu
from jax.sharding import PartitionSpec as P

BF = jnp.bfloat16
F32 = jnp.float32
BLK = 128
PB = 4
ROWS = 512
HALF = 128
F = 256
GRP = 8
MIB = 1 << 20


def vmem():
    return pl.BlockSpec(memory_space=pltpu.VMEM)


def smem():
    return pl.BlockSpec(memory_space=pltpu.SMEM)


def hbm():
    return pl.BlockSpec(memory_space=pl.ANY)


def coords():
    row = lax.axis_index("row")
    col = lax.axis_index("col")
    return col // 4, col % 4, row // 2, row % 2


def fetch_values(values, held, sems, group, step):
    copy = pltpu.make_async_copy(
        values.at[pl.ds(group * GRP, GRP)], held.at[step], sems.at[step]
    )
    return copy


def forward_kernel(rows, cols, values, *refs):
    pieces = refs[:8]
    outs_a = refs[8:12]
    outs_b = refs[12:16]
    panel, held, acc, piece_sems, value_sems = refs[16:]
    x, z, y, c = coords()

    def piece_copy(n):
        dy, dc = n % 4, n // 4
        shard = ((y + 4 - dy) % 4) * 2 + (c + dc) % 2
        return pltpu.make_async_copy(
            pieces[n], panel.at[pl.ds(shard * ROWS, ROWS)], piece_sems.at[n]
        )

    def group_of(step):
        p, r = step // 4, step % 4
        return ((x + p) % 4) * 4 + (z + r) % 4

    for n in range(8):
        piece_copy(n).start()
    for step in range(16):
        fetch_values(values, held, value_sems, group_of(step), step).start()
    for n in range(8):
        piece_copy(n).wait()
    for step in range(16):
        p, r = step // 4, step % 4
        group = group_of(step)
        fetch_values(values, held, value_sems, group, step).wait()
        acc[...] = jnp.zeros_like(acc)
        for k in range(GRP):
            local = rows[0, group * GRP + k] - group * PB
            block = cols[0, group * GRP + k]
            here = pl.ds(pl.multiple_of(local * BLK, BLK), BLK)
            there = pl.ds(pl.multiple_of(block * BLK, BLK), BLK)
            acc[here, :] += jnp.dot(
                held[step, k], panel[there, :], preferred_element_type=F32
            )
        outs_a[p][r * ROWS:(r + 1) * ROWS, :] = acc[:, :HALF].astype(BF)
        outs_b[r][p * ROWS:(p + 1) * ROWS, :] = acc[:, HALF:].astype(BF)


def forward_call(rows, cols, values, pieces):
    part = jax.ShapeDtypeStruct((4 * ROWS, HALF), BF)
    return pl.pallas_call(
        forward_kernel,
        out_shape=[part] * 8,
        in_specs=[smem(), smem(), hbm()] + [hbm()] * 8,
        out_specs=[vmem()] * 8,
        scratch_shapes=[
            pltpu.VMEM((8 * ROWS, F), BF),
            pltpu.VMEM((16, GRP, BLK, BLK), BF),
            pltpu.VMEM((ROWS, F), F32),
            pltpu.SemaphoreType.DMA((8,)),
            pltpu.SemaphoreType.DMA((16,)),
        ],
        compiler_params=pltpu.CompilerParams(vmem_limit_bytes=40 * MIB),
        cost_estimate=pl.CostEstimate(
            flops=2 * 128 * BLK * BLK * F, bytes_accessed=10 * MIB, transcendentals=0
        ),
        name="forward_tile",
    )(rows, cols, values, *pieces)


def add_kernel(*refs):
    total = (refs[0][...].astype(F32) + refs[2][...].astype(F32)) + (
        refs[1][...].astype(F32) + refs[3][...].astype(F32)
    )
    total = total.astype(BF)
    for n, out in enumerate(refs[4:]):
        out[...] = total[n * ROWS:(n + 1) * ROWS, :]


def add_call(parts, width, count, name):
    out = jax.ShapeDtypeStruct((ROWS, width), BF)
    return pl.pallas_call(
        add_kernel,
        out_shape=[out] * count,
        in_specs=[vmem()] * 4,
        out_specs=[vmem()] * count,
        compiler_params=pltpu.CompilerParams(vmem_limit_bytes=24 * MIB),
        cost_estimate=pl.CostEstimate(
            flops=4 * count * ROWS * width, bytes_accessed=10 * count * ROWS * width,
            transcendentals=0,
        ),
        name=name,
    )(*parts)


def point_kernel(scale, *refs):
    parts_a = refs[:4]
    parts_b = refs[4:8]
    weight, bias, cotangent = refs[8:11]
    out_act, grad_a, grad_b, gradients = refs[11:]

    def join(parts):
        return (
            (parts[0][...].astype(F32) + parts[2][...].astype(F32))
            + (parts[1][...].astype(F32) + parts[3][...].astype(F32))
        ).astype(BF)

    aggregated = jnp.concatenate([join(parts_a), join(parts_b)], axis=1)
    pre = jnp.dot(aggregated, weight[...], preferred_element_type=F32) + bias[...]
    gate = jax.nn.sigmoid(pre)
    out_act[...] = (pre * gate).astype(BF)
    grad_pre = (
        cotangent[...].astype(F32) * gate * (1.0 + pre * (1.0 - gate))
    ).astype(BF)
    grad_agg = lax.dot_general(
        grad_pre, weight[...], (((1,), (1,)), ((), ())), preferred_element_type=F32
    ).astype(BF)
    grad_a[...] = grad_agg[:, :HALF]
    grad_b[...] = grad_agg[:, HALF:]
    weight_grad = lax.dot_general(
        aggregated, grad_pre, (((0,), (0,)), ((), ())), preferred_element_type=F32
    ) * scale
    bias_grad = jnp.sum(grad_pre.astype(F32), axis=0, keepdims=True) * scale
    for n in range(8):
        gradients[n, :32, :] = weight_grad[n * 32:(n + 1) * 32, :]
        gradients[n, 32:, :] = jnp.broadcast_to(bias_grad, (8, F))


def point_call(parts_a, parts_b, weight, bias, cotangent, scale):
    half = jax.ShapeDtypeStruct((ROWS, HALF), BF)
    return pl.pallas_call(
        lambda *refs: point_kernel(scale, *refs),
        out_shape=[
            jax.ShapeDtypeStruct((ROWS, F), BF),
            half,
            half,
            jax.ShapeDtypeStruct((8, 40, F), F32),
        ],
        in_specs=[vmem()] * 11,
        out_specs=[vmem()] * 4,
        compiler_params=pltpu.CompilerParams(vmem_limit_bytes=24 * MIB),
        cost_estimate=pl.CostEstimate(
            flops=3 * 2 * ROWS * F * F, bytes_accessed=2 * MIB, transcendentals=ROWS * F
        ),
        name="pointwise",
    )(*parts_a, *parts_b, weight, bias, cotangent)


def backward_kernel(rows, cols, values, *refs):
    parts_a = refs[:4]
    parts_b = refs[4:8]
    mine, other = refs[8:10]
    acc, held, value_sems = refs[10:]
    x, z, y, c = coords()

    def group_of(step):
        p, r = step // 4, step % 4
        return ((x + 4 - p) % 4) * 4 + (z + 4 - r) % 4

    for step in range(16):
        fetch_values(values, held, value_sems, group_of(step), step).start()
    acc[...] = jnp.zeros_like(acc)
    for step in range(16):
        p, r = step // 4, step % 4
        group = group_of(step)
        fetch_values(values, held, value_sems, group, step).wait()
        for k in range(GRP):
            local = rows[0, group * GRP + k] - group * PB
            block = cols[0, group * GRP + k]
            in_a = pl.ds(pl.multiple_of(r * ROWS + local * BLK, BLK), BLK)
            in_b = pl.ds(pl.multiple_of(p * ROWS + local * BLK, BLK), BLK)
            grads = jnp.concatenate([parts_a[p][in_a, :], parts_b[r][in_b, :]], axis=1)
            there = pl.ds(pl.multiple_of(block * BLK, BLK), BLK)
            acc[there, :] += lax.dot_general(
                held[step, k], grads, (((0,), (0,)), ((), ())), preferred_element_type=F32
            )
    for dy in range(4):
        base = ((y + dy) % 4) * 2
        own = pl.ds(pl.multiple_of((base + c) * ROWS, ROWS), ROWS)
        peer = pl.ds(pl.multiple_of((base + 1 - c) * ROWS, ROWS), ROWS)
        mine[dy * ROWS:(dy + 1) * ROWS, :] = acc[own, :].astype(BF)
        other[dy * ROWS:(dy + 1) * ROWS, :] = acc[peer, :].astype(BF)


def backward_call(rows, cols, values, parts_a, parts_b):
    part = jax.ShapeDtypeStruct((4 * ROWS, F), BF)
    return pl.pallas_call(
        backward_kernel,
        out_shape=[part] * 2,
        in_specs=[smem(), smem(), hbm()] + [vmem()] * 8,
        out_specs=[vmem()] * 2,
        scratch_shapes=[
            pltpu.VMEM((8 * ROWS, F), F32),
            pltpu.VMEM((16, GRP, BLK, BLK), BF),
            pltpu.SemaphoreType.DMA((16,)),
        ],
        compiler_params=pltpu.CompilerParams(vmem_limit_bytes=40 * MIB),
        cost_estimate=pl.CostEstimate(
            flops=2 * 128 * BLK * BLK * F, bytes_accessed=10 * MIB, transcendentals=0
        ),
        name="backward_tile",
    )(rows, cols, values, *parts_a, *parts_b)


def pair_kernel(mine, other, *outs):
    for n, out in enumerate(outs):
        here = pl.ds(n * ROWS, ROWS)
        out[...] = (mine[here, :].astype(F32) + other[here, :].astype(F32)).astype(BF)


def pair_call(mine, other):
    out = jax.ShapeDtypeStruct((ROWS, F), BF)
    return pl.pallas_call(
        pair_kernel,
        out_shape=[out] * 4,
        in_specs=[vmem()] * 2,
        out_specs=[vmem()] * 4,
        compiler_params=pltpu.CompilerParams(vmem_limit_bytes=24 * MIB),
        cost_estimate=pl.CostEstimate(
            flops=4 * ROWS * F, bytes_accessed=24 * ROWS * F, transcendentals=0
        ),
        name="pair_sum",
    )(mine, other)


def along_col(value, dx, dz):
    pairs = [
        (a * 4 + b, ((a + dx) % 4) * 4 + (b + dz) % 4) for a in range(4) for b in range(4)
    ]
    return lax.ppermute(value, "col", pairs)


def along_row(value, dy, dc):
    pairs = [
        (a * 2 + b, ((a + dy) % 4) * 2 + (b + dc) % 2) for a in range(4) for b in range(2)
    ]
    return lax.ppermute(value, "row", pairs)


def shards(x_feat, block_values, block_rows, block_cols, weight, bias, cotangent):
    values = block_values.reshape(128, BLK, BLK)
    rows = block_rows.reshape(1, 128)
    cols = block_cols.reshape(1, 128)
    scale = 1.0 / math.sqrt(65536)

    near = {d: along_row(x_feat, d, 0) for d in (2, 1, 3)}
    swap = [along_row(x_feat, 0, 1)] + [None] * 3
    for d in (1, 3, 2):
        swap[d] = along_row(near[d], 0, 1)
    pieces = [x_feat, near[1], near[2], near[3]] + swap

    outs = forward_call(rows, cols, values, pieces)
    outs_a, outs_b = outs[:4], outs[4:]
    got_a, got_b = [outs_a[0]] + [None] * 3, [outs_b[0]] + [None] * 3
    for d in (2, 1, 3):
        got_a[d] = along_col(outs_a[d], d, 0)
        got_b[d] = along_col(outs_b[d], 0, d)
    sum_a = add_call(got_a, HALF, 4, "sum_a")
    sum_b = add_call(got_b, HALF, 4, "sum_b")
    part_a, part_b = [sum_a[0]] + [None] * 3, [sum_b[0]] + [None] * 3
    for d in (2, 1, 3):
        part_a[d] = along_col(sum_a[d], 0, d)
        part_b[d] = along_col(sum_b[d], d, 0)
    out_act, grad_a, grad_b, gradients = point_call(
        part_a, part_b, weight, bias.reshape(1, F), cotangent, scale
    )

    first_a, first_b = [grad_a] + [None] * 3, [grad_b] + [None] * 3
    for d in (2, 1, 3):
        first_a[d] = along_col(grad_a, 0, d)
        first_b[d] = along_col(grad_b, d, 0)
    join_a = jnp.concatenate(first_a, axis=0)
    join_b = jnp.concatenate(first_b, axis=0)
    full_a, full_b = [join_a] + [None] * 3, [join_b] + [None] * 3
    for d in (2, 1, 3):
        full_a[d] = along_col(join_a, d, 0)
        full_b[d] = along_col(join_b, 0, d)

    spread = lax.all_to_all(gradients, "row", 0, 0)
    piece = jnp.sum(spread, axis=0)
    for dx, dz in ((1, 0), (0, 1)):
        r1, r2, r3 = (along_col(piece, d * dx, d * dz) for d in (1, 2, 3))
        piece = (piece + r2) + (r1 + r3)
    complete = lax.all_gather(piece, "row", axis=0, tiled=False)
    weight_grad = complete[:, :32, :].reshape(F, F)
    bias_grad = complete[0, 32, :]

    mine, other = backward_call(rows, cols, values, full_a, full_b)
    other = along_row(other, 0, 1)
    sums = pair_call(mine, other)
    last = [sums[0]] + [None] * 3
    for d in (2, 1, 3):
        last[d] = along_row(sums[d], d, 0)
    x_grad = add_call(last, F, 1, "sum_x")[0]
    return (out_act, x_grad, weight_grad, bias_grad)


def solution(mesh):
    placed = (
        P(("row", "col"), None),
        P("row", "col", None, None, None),
        P("row", "col", None),
        P("row", "col", None),
        P(),
        P(),
        P(("row", "col"), None),
    )
    return jax.shard_map(
        shards,
        mesh=mesh,
        in_specs=placed,
        out_specs=(P(("row", "col"), None), P(("row", "col"), None), P(), P()),
        check_vma=False,
    )
```

time: 500 us -> 187 us (0.37); the launches traced: 495 us -> 187 us
  waiting for transfers between devices: 160 us -> 64.2 us
  local copies, waits for them, and re-layouts: 84.1 us -> 5.87 us
  starting transfers between devices: 0.2 us -> 68.8 us
  matrix products: 64.9 us -> 0 us
  other arithmetic: 63.1 us -> 0.05 us
  loops' own time: 43 us -> 0 us
  blocking collectives: 65.2 us -> 31 us
  Pallas kernels: 0 us -> 16.4 us
  between operations: 13.8 us -> 0.77 us
    reduce_scatter x2 -> x0, waiting for transfers between devices: 80.8 us -> none  [the longest x1 76.2 us: shards(): lax.psum_scatter(terms.reshape(count, feature_width).astype(jnp.bfloat16)...]
    all_gather x2 -> x0, waiting for transfers between devices: 78.9 us -> none  [the longest x1 51.6 us: shards(): gathered_grad = lax.all_gather(grad_agg, 'col', axis=0, tiled=True)]
    ppermute x0 -> x41, starting transfers between devices: none -> 68.8 us  [the longest x30 43.9 us: along_col(): return lax.ppermute(value, 'col', pairs)]
    psum x1 -> x0, blocking collectives: 65.2 us -> none  [shards(): lax.psum((local_weight, local_bias), ('row', 'col'))]
    dot_general x51 -> x0, matrix products: 64.9 us -> none  [the longest x16 21.1 us: forward_group(): jnp.einsum('bij,bjf->bif', group_values, picked, preferred_element_type=j...]
    ppermute x0 -> x41, waiting for transfers between devices: none -> 64.2 us  [the longest x30 51.7 us: along_col(): return lax.ppermute(value, 'col', pairs)]
    scatter-add x16 -> x0, other arithmetic: 52.9 us -> none  [backward_group(): return carry.at[group_cols].add(products)]
    gather x32 -> x0, local copies, waits for them, and re-layouts: 44 us -> none  [the longest x16 34.7 us: forward_group(): picked = jnp.take(panel_blocks, group_cols, axis=0)]
  transfers between devices with their start and end apart: 5 -> 41, of which waited for: 4 -> 18; matrix products, arithmetic and copies ran while one was open for 23% -> 1% of each run, Pallas kernels for 0% -> 0%
where the time goes in v1:
time: 187 us
  starting transfers between devices  68.8 us (37%)
  waiting for transfers between devices  64.2 us (34%)
  blocking collectives  31 us (17%)
  Pallas kernels  16.4 us (9%)
  local copies, waits for them, and re-layouts  5.87 us (3%)
    ppermute x30, waiting for transfers between devices, along_col(): return lax.ppermute(value, 'col', pairs)  51.7 us
    ppermute x30, starting transfers between devices, along_col(): return lax.ppermute(value, 'col', pairs)  43.9 us
    ppermute x11, starting transfers between devices, along_row(): return lax.ppermute(value, 'row', pairs)  24.9 us
    all_gather x1, blocking collectives, shards(): complete = lax.all_gather(piece, 'row', axis=0, tiled=False)  21.1 us
    ppermute x11, waiting for transfers between devices, along_row(): return lax.ppermute(value, 'row', pairs)  12.5 us
    all_to_all x1, blocking collectives, shards(): spread = lax.all_to_all(gradients, 'row', 0, 0)  9.88 us
    pallas_call x1, Pallas kernels, backward_call(): pl.pallas_call(backward_kernel, out_shape=[part] * 2, in_specs=[smem(), s...  6.95 us
    pallas_call x1, Pallas kernels, forward_call(): pl.pallas_call(forward_kernel, out_shape=[part] * 8, in_specs=[smem(), sm...  6.73 us
  transfers between devices with their start and end apart: 41, of which 18 were waited for; matrix products, arithmetic and copies ran while one was open for 1% of the time, Pallas kernels for 0%

profile of v1, /device:TPU:1, one launch (start us, length us, event | category | flops | bytes accessed | tf_op | source)
XLA Modules:
  0.0 187.1 jit_solution(2958518030292888626)
XLA Ops:
  0.6 3.6 %collective-permute-start.2 = (bf16[512,256]{1,0:T(8,128)(2,1)}, bf16[512,256]{1,0:T(8,128)(2,1)S(1)}, u32[]{:S(2)}, u32[]{:S(2)}) collective-permute-start(bf16[512,256]{1,0:T(8,128)(2,1)} %refs_0_.1), channel_id=1, source_target_pairs={{0,96},{16,112},{32,0},{48,16},{64,32},{80,48},{96,64},{112,80},{1... | collective-permute-start | bytes 786440 | tf_op jit(solution)/shard_map/ppermute | solution.py:275
  4.3 0.3 collective-permute-start.1
  4.6 0.7 collective-permute-start
  5.3 1.5 collective-permute-start.3
  6.8 8.2 %collective-permute-done.2.refs_3_ = bf16[512,256]{1,0:T(8,128)(2,1)S(1)} collective-permute-done((bf16[512,256]{1,0:T(8,128)(2,1)}, bf16[512,256]{1,0:T(8,128)(2,1)S(1)}, u32[]{:S(2)}, u32[]{:S(2)}) %collective-permute-start.2) | collective-permute-done | bytes 262176 | tf_op jit(solution)/shard_map/ppermute | solution.py:275
  15.0 1.7 collective-permute-start.6
  16.7 3.1 %collective-permute-done.refs_1_ = bf16[512,256]{1,0:T(8,128)(2,1)S(1)} collective-permute-done((bf16[512,256]{1,0:T(8,128)(2,1)}, bf16[512,256]{1,0:T(8,128)(2,1)S(1)}, u32[]{:S(2)}, u32[]{:S(2)}) %collective-permute-start) | collective-permute-done | bytes 262176 | tf_op jit(solution)/shard_map/ppermute | solution.py:275
  19.8 0.5 collective-permute-start.4
  20.3 1.1 collective-permute-done.4.refs_5_
  21.5 2.2 %copy-done = bf16[1,1,128,128,128]{4,3,2,1,0:T(8,128)(2,1)S(1)} copy-done((bf16[1,1,128,128,128]{4,3,2,1,0:T(8,128)(2,1)S(1)}, bf16[1,1,128,128,128]{4,3,2,1,0:T(8,128)(2,1)}, u32[]{:S(2)}) %copy-start) | copy-done | bytes 4194328
  23.7 0.9 copy-done.2
  24.6 0.7 copy-done.4
  25.3 0.7 copy-done.5
  25.9 6.7 %forward_tile.1 = (bf16[2048,128]{1,0:T(8,128)(2,1)S(1)}, bf16[2048,128]{1,0:T(8,128)(2,1)S(1)}, bf16[2048,128]{1,0:T(8,128)(2,1)S(1)}, bf16[2048,128]{1,0:T(8,1...) custom-call(s32[1,128]{1,0:T(1,128)S(1)} %bitcast.9, ...), custom_call_target="tpu_custom_call" | custom-call | flops 1073741824 | bytes 10485760 | tf_op jit(solution)/shard_map/forward_tile/pallas_call | solution.py:89
  32.7 1.3 collective-permute-start.7
  34.0 2.4 %collective-permute-start.8 = (bf16[2048,128]{1,0:T(8,128)(2,1)S(1)}, bf16[2048,128]{1,0:T(8,128)(2,1)S(1)}, u32[]{:S(2)}, u32[]{:S(2)}) collective-permute-start(bf16[2048,128]{1,0:T(8,128)(2,1)S(1)} %get-tuple-element.32), channel_id=1, source_target_pairs={{0,8},{1,9},{2,10},{3,11},{4,12},{5,13},{6,14},{7,15},{8,0},{9,1},... | collective-permute-start | bytes 1572872 | tf_op jit(solution)/shard_map/ppermute | solution.py:268
  36.4 1.2 collective-permute-start.9
  37.6 1.6 collective-permute-start.13
  39.2 3.3 %collective-permute-start.14 = (bf16[2048,128]{1,0:T(8,128)(2,1)S(1)}, bf16[2048,128]{1,0:T(8,128)(2,1)S(1)}, u32[]{:S(2)}, u32[]{:S(2)}) collective-permute-start(bf16[2048,128]{1,0:T(8,128)(2,1)S(1)} %get-tuple-element.40), channel_id=1, source_target_pairs={{0,2},{1,3},{2,0},{3,1},{4,6},{5,7},{6,4},{7,5},{8,10},{9,11},{10,... | collective-permute-start | bytes 1572872 | tf_op jit(solution)/shard_map/ppermute | solution.py:268
  42.5 4.6 %collective-permute-done.7.refs_1_ = bf16[2048,128]{1,0:T(8,128)(2,1)S(1)} collective-permute-done((bf16[2048,128]{1,0:T(8,128)(2,1)S(1)}, bf16[2048,128]{1,0:T(8,128)(2,1)S(1)}, u32[]{:S(2)}, u32[]{:S(2)}) %collective-permute-start.7) | collective-permute-done | bytes 524320 | tf_op jit(solution)/shard_map/ppermute | solution.py:268
  47.1 3.7 %collective-permute-start.15 = (bf16[2048,128]{1,0:T(8,128)(2,1)S(1)}, bf16[2048,128]{1,0:T(8,128)(2,1)S(1)}, u32[]{:S(2)}, u32[]{:S(2)}) collective-permute-start(bf16[2048,128]{1,0:T(8,128)(2,1)S(1)} %get-tuple-element.41), channel_id=1, source_target_pairs={{0,3},{1,0},{2,1},{3,2},{4,7},{5,4},{6,5},{7,6},{8,11},{9,8},{10,9... | collective-permute-start | bytes 1572872 | tf_op jit(solution)/shard_map/ppermute | solution.py:268
  50.8 8.5 %collective-permute-done.8.refs_2_ = bf16[2048,128]{1,0:T(8,128)(2,1)S(1)} collective-permute-done((bf16[2048,128]{1,0:T(8,128)(2,1)S(1)}, bf16[2048,128]{1,0:T(8,128)(2,1)S(1)}, u32[]{:S(2)}, u32[]{:S(2)}) %collective-permute-start.8) | collective-permute-done | bytes 524320 | tf_op jit(solution)/shard_map/ppermute | solution.py:268
  59.6 1.7 collective-permute-start.10
  61.3 3.3 %collective-permute-start.11 = (bf16[512,128]{1,0:T(8,128)(2,1)S(1)}, bf16[512,128]{1,0:T(8,128)(2,1)S(1)}, u32[]{:S(2)}, u32[]{:S(2)}) collective-permute-start(bf16[512,128]{1,0:T(8,128)(2,1)S(1)} %get-tuple-element.36), channel_id=1, source_target_pairs={{0,2},{1,3},{2,0},{3,1},{4,6},{5,7},{6,4},{7,5},{8,10},{9,11},{10,... | collective-permute-start | bytes 393224 | tf_op jit(solution)/shard_map/ppermute | solution.py:268
  64.6 0.8 collective-permute-start.12
  65.6 1.1 collective-permute-start.16
  66.7 2.8 %collective-permute-start.17 = (bf16[512,128]{1,0:T(8,128)(2,1)S(1)}, bf16[512,128]{1,0:T(8,128)(2,1)S(1)}, u32[]{:S(2)}, u32[]{:S(2)}) collective-permute-start(bf16[512,128]{1,0:T(8,128)(2,1)S(1)} %get-tuple-element.44), channel_id=1, source_target_pairs={{0,8},{1,9},{2,10},{3,11},{4,12},{5,13},{6,14},{7,15},{8,0},{9,1},... | collective-permute-start | bytes 393224 | tf_op jit(solution)/shard_map/ppermute | solution.py:268
  69.5 0.6 collective-permute-done.10.refs_1_
  70.2 0.3 collective-permute-done.11.refs_2_
  70.5 0.5 collective-permute-done.16.refs_5_
  71.0 3.2 %collective-permute-done.17.refs_6_ = bf16[512,128]{1,0:T(8,128)(2,1)S(1)} collective-permute-done((bf16[512,128]{1,0:T(8,128)(2,1)S(1)}, bf16[512,128]{1,0:T(8,128)(2,1)S(1)}, u32[]{:S(2)}, u32[]{:S(2)}) %collective-permute-start.17) | collective-permute-done | bytes 131104 | tf_op jit(solution)/shard_map/ppermute | solution.py:268
  74.2 1.4 collective-permute-done.18.refs_7_
  75.6 1.1 pointwise.1
  76.7 2.7 %collective-permute-start.27 = (bf16[512,128]{1,0:T(8,128)(2,1)S(1)}, bf16[512,128]{1,0:T(8,128)(2,1)S(1)}, u32[]{:S(2)}, u32[]{:S(2)}) collective-permute-start(bf16[512,128]{1,0:T(8,128)(2,1)S(1)} %get-tuple-element.48), channel_id=1, source_target_pairs={{0,12},{1,13},{2,14},{3,15},{4,0},{5,1},{6,2},{7,3},{8,4},{9,5},{1... | collective-permute-start | bytes 393224 | tf_op jit(solution)/shard_map/ppermute | solution.py:268
  79.4 2.3 %collective-permute-done.25 = bf16[512,128]{1,0:T(8,128)(2,1)S(1)} collective-permute-done((bf16[512,128]{1,0:T(8,128)(2,1)S(1)}, bf16[512,128]{1,0:T(8,128)(2,1)S(1)}, u32[]{:S(2)}, u32[]{:S(2)}) %collective-permute-start.25) | collective-permute-done | bytes 131104 | tf_op jit(solution)/shard_map/ppermute | solution.py:268
  81.8 4.2 %collective-permute-done.26 = bf16[512,128]{1,0:T(8,128)(2,1)S(1)} collective-permute-done((bf16[512,128]{1,0:T(8,128)(2,1)S(1)}, bf16[512,128]{1,0:T(8,128)(2,1)S(1)}, u32[]{:S(2)}, u32[]{:S(2)}) %collective-permute-start.26) | collective-permute-done | bytes 131104 | tf_op jit(solution)/shard_map/ppermute | solution.py:268
  86.0 0.6 collective-permute-start.30
  86.6 1.0 collective-permute-start.19
  87.5 1.7 collective-permute-start.21
  89.2 1.2 collective-permute-start.20
  90.5 1.8 collective-permute-start.29
  92.3 3.3 %collective-permute-done.20 = bf16[512,128]{1,0:T(8,128)(2,1)S(1)} collective-permute-done((bf16[512,128]{1,0:T(8,128)(2,1)S(1)}, bf16[512,128]{1,0:T(8,128)(2,1)S(1)}, u32[]{:S(2)}, u32[]{:S(2)}) %collective-permute-start.20) | collective-permute-done | bytes 131104 | tf_op jit(solution)/shard_map/ppermute | solution.py:268
  95.6 4.3 %collective-permute-done.21 = bf16[512,128]{1,0:T(8,128)(2,1)S(1)} collective-permute-done((bf16[512,128]{1,0:T(8,128)(2,1)S(1)}, bf16[512,128]{1,0:T(8,128)(2,1)S(1)}, u32[]{:S(2)}, u32[]{:S(2)}) %collective-permute-start.21) | collective-permute-done | bytes 131104 | tf_op jit(solution)/shard_map/ppermute | solution.py:268
  100.2 1.3 collective-permute-start.22
  101.5 4.1 %collective-permute-done.29.refs_6_ = bf16[2048,128]{1,0:T(8,128)(2,1)S(1)} collective-permute-done((bf16[2048,128]{1,0:T(8,128)(2,1)S(1)}, bf16[2048,128]{1,0:T(8,128)(2,1)S(1)}, u32[]{:S(2)}, u32[]{:S(2)}) %collective-permute-start.29) | collective-permute-done | bytes 524320 | tf_op jit(solution)/shard_map/ppermute | solution.py:268
  105.6 11.3 %collective-permute-done.28.refs_5_ = bf16[2048,128]{1,0:T(8,128)(2,1)S(1)} collective-permute-done((bf16[2048,128]{1,0:T(8,128)(2,1)S(1)}, bf16[2048,128]{1,0:T(8,128)(2,1)S(1)}, u32[]{:S(2)}, u32[]{:S(2)}) %collective-permute-start.28) | collective-permute-done | bytes 524320 | tf_op jit(solution)/shard_map/ppermute | solution.py:268
  116.9 7.0 %backward_tile.1 = (bf16[2048,256]{1,0:T(8,128)(2,1)S(1)}, bf16[2048,256]{1,0:T(8,128)(2,1)S(1)}) custom-call(s32[1,128]{1,0:T(1,128)S(1)} %bitcast.10, s32[1,128]{1,0:T(1,128)S(1)} %bitcast.12, bf16[128,128,128]{2,1,0:T(8,128)(2,1)S(1)} %bitcast.8, bf16[2048,128]{1,0:T(8,128)(2,1)S(1)} %constant_dynamic-update-slice_fusion.refs_0_, ...), custom_call_target="tpu_custom_call" | custom-call | flops 1073741824 | bytes 10485760 | tf_op jit(solution)/shard_map/backward_tile/pallas_call | solution.py:225
  123.9 13.7 %collective-permute-start.31 = (bf16[2048,256]{1,0:T(8,128)(2,1)S(1)}, bf16[2048,256]{1,0:T(8,128)(2,1)S(1)}, u32[]{:S(2)}, u32[]{:S(2)}) collective-permute-start(bf16[2048,256]{1,0:T(8,128)(2,1)S(1)} %get-tuple-element.50), channel_id=1, source_target_pairs={{0,16},{16,0},{32,48},{48,32},{64,80},{80,64},{96,112},{112,96},{1... | collective-permute-start | bytes 3145736 | tf_op jit(solution)/shard_map/ppermute | solution.py:275
  137.6 9.9 %all_to_all.5 = f32[8,40,256]{2,1,0:T(8,128)S(1)} all-to-all(f32[8,40,256]{2,1,0:T(8,128)S(1)} %get-tuple-element.55), channel_id=1, replica_groups=mesh['row'=8,'col'=16] {'row'}, dimensions={0} | all-to-all | bytes 655360 | tf_op jit(solution)/shard_map/all_to_all | solution.py:317
  147.5 0.4 collective-permute-start.37
  147.9 1.5 collective-permute-start.36
  149.5 1.7 collective-permute-start.35
  151.2 0.8 collective-permute-done.36
  152.0 2.2 %collective-permute-done.35 = f32[40,256]{1,0:T(8,128)S(1)} collective-permute-done((f32[40,256]{1,0:T(8,128)S(1)}, f32[40,256]{1,0:T(8,128)S(1)}, u32[]{:S(2)}, u32[]{:S(2)}) %collective-permute-start.35) | collective-permute-done | bytes 40992 | tf_op jit(solution)/shard_map/ppermute | solution.py:268
  154.2 3.4 %collective-permute-start.40 = (f32[40,256]{1,0:T(8,128)S(1)}, f32[40,256]{1,0:T(8,128)S(1)}, u32[]{:S(2)}, u32[]{:S(2)}) collective-permute-start(f32[40,256]{1,0:T(8,128)S(1)} %add_add_fusion.1), channel_id=1, source_target_pairs={{0,3},{1,0},{2,1},{3,2},{4,7},{5,4},{6,5},{7,6},{8,11},{9,8},{10,9... | collective-permute-start | bytes 122888 | tf_op jit(solution)/shard_map/ppermute | solution.py:268
  157.7 1.3 collective-permute-start.39
  159.0 1.7 collective-permute-start.38
  161.0 0.4 collective-permute-start.32
  161.3 1.8 collective-permute-start.33
  163.1 0.7 collective-permute-start.34
  163.8 21.1 %all-gather = f32[320,256]{1,0:T(8,128)S(1)} all-gather(f32[40,256]{1,0:T(8,128)S(1)} %add_add_fusion), channel_id=2, replica_groups=mesh['row'=8,'col'=16] {'row'}, dimensions={0}, use_global_device_ids=true | all-gather | bytes 368640 | tf_op jit(solution)/shard_map/all_gather | solution.py:322
  184.9 0.6 slice.9
  185.5 0.7 slice.8
  186.2 0.8 sum_x.1
  (54 shorter events, 1.2 us)
Async XLA Ops:
  0.6 14.4 %collective-permute-start.2 = (bf16[512,256]{1,0:T(8,128)(2,1)}, bf16[512,256]{1,0:T(8,128)(2,1)S(1)}, u32[]{:S(2)}, u32[]{:S(2)}) collective-permute-start(bf16[512,256]{1,0:T(8,128)(2,1)} %refs_0_.1), channel_id=1, source_target_pairs={{0,96},{16,112},{32,0},{48,16},{64,32},{80,48},{96,64},{112,80},{1... | collective-permute-start | bytes 786440 | tf_op jit(solution)/shard_map/ppermute | solution.py:275
  4.3 12.5 %collective-permute-start.1 = (bf16[512,256]{1,0:T(8,128)(2,1)}, bf16[512,256]{1,0:T(8,128)(2,1)S(1)}, u32[]{:S(2)}, u32[]{:S(2)}) collective-permute-start(bf16[512,256]{1,0:T(8,128)(2,1)} %refs_0_.1), channel_id=1, source_target_pairs={{0,64},{16,80},{32,96},{48,112},{64,0},{80,16},{96,32},{112,48},{1... | collective-permute-start | bytes 786440 | tf_op jit(solution)/shard_map/ppermute | solution.py:275
  4.6 15.2 %collective-permute-start = (bf16[512,256]{1,0:T(8,128)(2,1)}, bf16[512,256]{1,0:T(8,128)(2,1)S(1)}, u32[]{:S(2)}, u32[]{:S(2)}) collective-permute-start(bf16[512,256]{1,0:T(8,128)(2,1)} %refs_0_.1), channel_id=1, source_target_pairs={{0,32},{16,48},{32,64},{48,80},{64,96},{80,112},{96,0},{112,16},{1... | collective-permute-start | bytes 786440 | tf_op jit(solution)/shard_map/ppermute | solution.py:275
  5.3 15.0 %collective-permute-start.3 = (bf16[512,256]{1,0:T(8,128)(2,1)}, bf16[512,256]{1,0:T(8,128)(2,1)S(1)}, u32[]{:S(2)}, u32[]{:S(2)}) collective-permute-start(bf16[512,256]{1,0:T(8,128)(2,1)} %refs_0_.1), channel_id=1, source_target_pairs={{0,16},{16,0},{32,48},{48,32},{64,80},{80,64},{96,112},{112,96},{1... | collective-permute-start | bytes 786440 | tf_op jit(solution)/shard_map/ppermute | solution.py:275
  15.0 5.3 %collective-permute-start.6 = (bf16[512,256]{1,0:T(8,128)(2,1)S(1)}, bf16[512,256]{1,0:T(8,128)(2,1)S(1)}, u32[]{:S(2)}, u32[]{:S(2)}) collective-permute-start(bf16[512,256]{1,0:T(8,128)(2,1)S(1)} %collective-permute-done.2.refs_3_), channel_id=1, source_target_pairs={{0,16},{16,0},{32,48},{48,32},{64,80},{80,64},{96,112},{112,96},{1... | collective-permute-start | bytes 786440 | tf_op jit(solution)/shard_map/ppermute | solution.py:275
  16.7 3.6 %collective-permute-start.5 = (bf16[512,256]{1,0:T(8,128)(2,1)S(1)}, bf16[512,256]{1,0:T(8,128)(2,1)S(1)}, u32[]{:S(2)}, u32[]{:S(2)}) collective-permute-start(bf16[512,256]{1,0:T(8,128)(2,1)S(1)} %collective-permute-done.1.refs_2_), channel_id=1, source_target_pairs={{0,16},{16,0},{32,48},{48,32},{64,80},{80,64},{96,112},{112,96},{1... | collective-permute-start | bytes 786440 | tf_op jit(solution)/shard_map/ppermute | solution.py:275
  19.8 1.7 collective-permute-start.4
  21.5 2.2 %copy-start = (bf16[1,1,128,128,128]{4,3,2,1,0:T(8,128)(2,1)S(1)}, bf16[1,1,128,128,128]{4,3,2,1,0:T(8,128)(2,1)}, u32[]{:S(2)}) copy-start(bf16[1,1,128,128,128]{4,3,2,1,0:T(8,128)(2,1)} %param.8) | copy-start | bytes 12582916
  23.7 0.9 copy-start.2
  24.6 0.7 copy-start.4
  25.3 0.7 copy-start.5
  25.9 49.7 %copy-start.1 = (bf16[512,256]{1,0:T(8,128)(2,1)S(1)}, bf16[512,256]{1,0:T(8,128)(2,1)}, u32[]{:S(2)}) copy-start(bf16[512,256]{1,0:T(8,128)(2,1)} %refs_10_.1) | copy-start | bytes 786436
  25.9 49.7 %copy-start.3 = (bf16[256,256]{1,0:T(8,128)(2,1)S(1)}, bf16[256,256]{1,0:T(8,128)(2,1)}, u32[]{:S(2)}) copy-start(bf16[256,256]{1,0:T(8,128)(2,1)} %refs_8_.1) | copy-start | bytes 393220
  25.9 49.7 %copy-start.6 = (f32[256]{0:T(256)S(1)}, f32[256]{0:T(256)}, u32[]{:S(2)}) copy-start(f32[256]{0:T(256)} %param.12) | copy-start | bytes 3076
  32.7 14.4 %collective-permute-start.7 = (bf16[2048,128]{1,0:T(8,128)(2,1)S(1)}, bf16[2048,128]{1,0:T(8,128)(2,1)S(1)}, u32[]{:S(2)}, u32[]{:S(2)}) collective-permute-start(bf16[2048,128]{1,0:T(8,128)(2,1)S(1)} %get-tuple-element.31), channel_id=1, source_target_pairs={{0,4},{1,5},{2,6},{3,7},{4,8},{5,9},{6,10},{7,11},{8,12},{9,13},{1... | collective-permute-start | bytes 1572872 | tf_op jit(solution)/shard_map/ppermute | solution.py:268
  34.0 25.3 %collective-permute-start.8 = (bf16[2048,128]{1,0:T(8,128)(2,1)S(1)}, bf16[2048,128]{1,0:T(8,128)(2,1)S(1)}, u32[]{:S(2)}, u32[]{:S(2)}) collective-permute-start(bf16[2048,128]{1,0:T(8,128)(2,1)S(1)} %get-tuple-element.32), channel_id=1, source_target_pairs={{0,8},{1,9},{2,10},{3,11},{4,12},{5,13},{6,14},{7,15},{8,0},{9,1},... | collective-permute-start | bytes 1572872 | tf_op jit(solution)/shard_map/ppermute | solution.py:268
  36.4 22.9 %collective-permute-start.9 = (bf16[2048,128]{1,0:T(8,128)(2,1)S(1)}, bf16[2048,128]{1,0:T(8,128)(2,1)S(1)}, u32[]{:S(2)}, u32[]{:S(2)}) collective-permute-start(bf16[2048,128]{1,0:T(8,128)(2,1)S(1)} %get-tuple-element.33), channel_id=1, source_target_pairs={{0,12},{1,13},{2,14},{3,15},{4,0},{5,1},{6,2},{7,3},{8,4},{9,5},{1... | collective-permute-start | bytes 1572872 | tf_op jit(solution)/shard_map/ppermute | solution.py:268
  37.6 27.0 %collective-permute-start.13 = (bf16[2048,128]{1,0:T(8,128)(2,1)S(1)}, bf16[2048,128]{1,0:T(8,128)(2,1)S(1)}, u32[]{:S(2)}, u32[]{:S(2)}) collective-permute-start(bf16[2048,128]{1,0:T(8,128)(2,1)S(1)} %get-tuple-element.39), channel_id=1, source_target_pairs={{0,1},{1,2},{2,3},{3,0},{4,5},{5,6},{6,7},{7,4},{8,9},{9,10},{10,1... | collective-permute-start | bytes 1572872 | tf_op jit(solution)/shard_map/ppermute | solution.py:268
  39.2 26.1 %collective-permute-start.14 = (bf16[2048,128]{1,0:T(8,128)(2,1)S(1)}, bf16[2048,128]{1,0:T(8,128)(2,1)S(1)}, u32[]{:S(2)}, u32[]{:S(2)}) collective-permute-start(bf16[2048,128]{1,0:T(8,128)(2,1)S(1)} %get-tuple-element.40), channel_id=1, source_target_pairs={{0,2},{1,3},{2,0},{3,1},{4,6},{5,7},{6,4},{7,5},{8,10},{9,11},{10,... | collective-permute-start | bytes 1572872 | tf_op jit(solution)/shard_map/ppermute | solution.py:268
  47.1 18.2 %collective-permute-start.15 = (bf16[2048,128]{1,0:T(8,128)(2,1)S(1)}, bf16[2048,128]{1,0:T(8,128)(2,1)S(1)}, u32[]{:S(2)}, u32[]{:S(2)}) collective-permute-start(bf16[2048,128]{1,0:T(8,128)(2,1)S(1)} %get-tuple-element.41), channel_id=1, source_target_pairs={{0,3},{1,0},{2,1},{3,2},{4,7},{5,4},{6,5},{7,6},{8,11},{9,8},{10,9... | collective-permute-start | bytes 1572872 | tf_op jit(solution)/shard_map/ppermute | solution.py:268
  59.6 10.6 %collective-permute-start.10 = (bf16[512,128]{1,0:T(8,128)(2,1)S(1)}, bf16[512,128]{1,0:T(8,128)(2,1)S(1)}, u32[]{:S(2)}, u32[]{:S(2)}) collective-permute-start(bf16[512,128]{1,0:T(8,128)(2,1)S(1)} %get-tuple-element.35), channel_id=1, source_target_pairs={{0,1},{1,2},{2,3},{3,0},{4,5},{5,6},{6,7},{7,4},{8,9},{9,10},{10,1... | collective-permute-start | bytes 393224 | tf_op jit(solution)/shard_map/ppermute | solution.py:268
  61.3 9.2 %collective-permute-start.11 = (bf16[512,128]{1,0:T(8,128)(2,1)S(1)}, bf16[512,128]{1,0:T(8,128)(2,1)S(1)}, u32[]{:S(2)}, u32[]{:S(2)}) collective-permute-start(bf16[512,128]{1,0:T(8,128)(2,1)S(1)} %get-tuple-element.36), channel_id=1, source_target_pairs={{0,2},{1,3},{2,0},{3,1},{4,6},{5,7},{6,4},{7,5},{8,10},{9,11},{10,... | collective-permute-start | bytes 393224 | tf_op jit(solution)/shard_map/ppermute | solution.py:268
  64.6 5.9 %collective-permute-start.12 = (bf16[512,128]{1,0:T(8,128)(2,1)S(1)}, bf16[512,128]{1,0:T(8,128)(2,1)S(1)}, u32[]{:S(2)}, u32[]{:S(2)}) collective-permute-start(bf16[512,128]{1,0:T(8,128)(2,1)S(1)} %get-tuple-element.37), channel_id=1, source_target_pairs={{0,3},{1,0},{2,1},{3,2},{4,7},{5,4},{6,5},{7,6},{8,11},{9,8},{10,9... | collective-permute-start | bytes 393224 | tf_op jit(solution)/shard_map/ppermute | solution.py:268
  65.6 5.4 %collective-permute-start.16 = (bf16[512,128]{1,0:T(8,128)(2,1)S(1)}, bf16[512,128]{1,0:T(8,128)(2,1)S(1)}, u32[]{:S(2)}, u32[]{:S(2)}) collective-permute-start(bf16[512,128]{1,0:T(8,128)(2,1)S(1)} %get-tuple-element.43), channel_id=1, source_target_pairs={{0,4},{1,5},{2,6},{3,7},{4,8},{5,9},{6,10},{7,11},{8,12},{9,13},{1... | collective-permute-start | bytes 393224 | tf_op jit(solution)/shard_map/ppermute | solution.py:268
  66.7 7.5 %collective-permute-start.17 = (bf16[512,128]{1,0:T(8,128)(2,1)S(1)}, bf16[512,128]{1,0:T(8,128)(2,1)S(1)}, u32[]{:S(2)}, u32[]{:S(2)}) collective-permute-start(bf16[512,128]{1,0:T(8,128)(2,1)S(1)} %get-tuple-element.44), channel_id=1, source_target_pairs={{0,8},{1,9},{2,10},{3,11},{4,12},{5,13},{6,14},{7,15},{8,0},{9,1},... | collective-permute-start | bytes 393224 | tf_op jit(solution)/shard_map/ppermute | solution.py:268
  70.2 5.4 %collective-permute-start.18 = (bf16[512,128]{1,0:T(8,128)(2,1)S(1)}, bf16[512,128]{1,0:T(8,128)(2,1)S(1)}, u32[]{:S(2)}, u32[]{:S(2)}) collective-permute-start(bf16[512,128]{1,0:T(8,128)(2,1)S(1)} %get-tuple-element.45), channel_id=1, source_target_pairs={{0,12},{1,13},{2,14},{3,15},{4,0},{5,1},{6,2},{7,3},{8,4},{9,5},{1... | collective-permute-start | bytes 393224 | tf_op jit(solution)/shard_map/ppermute | solution.py:268
  76.7 5.0 %collective-permute-start.25 = (bf16[512,128]{1,0:T(8,128)(2,1)S(1)}, bf16[512,128]{1,0:T(8,128)(2,1)S(1)}, u32[]{:S(2)}, u32[]{:S(2)}) collective-permute-start(bf16[512,128]{1,0:T(8,128)(2,1)S(1)} %get-tuple-element.48), channel_id=1, source_target_pairs={{0,4},{1,5},{2,6},{3,7},{4,8},{5,9},{6,10},{7,11},{8,12},{9,13},{1... | collective-permute-start | bytes 393224 | tf_op jit(solution)/shard_map/ppermute | solution.py:268
  76.7 9.2 %collective-permute-start.27 = (bf16[512,128]{1,0:T(8,128)(2,1)S(1)}, bf16[512,128]{1,0:T(8,128)(2,1)S(1)}, u32[]{:S(2)}, u32[]{:S(2)}) collective-permute-start(bf16[512,128]{1,0:T(8,128)(2,1)S(1)} %get-tuple-element.48), channel_id=1, source_target_pairs={{0,12},{1,13},{2,14},{3,15},{4,0},{5,1},{6,2},{7,3},{8,4},{9,5},{1... | collective-permute-start | bytes 393224 | tf_op jit(solution)/shard_map/ppermute | solution.py:268
  79.4 6.5 %collective-permute-start.26 = (bf16[512,128]{1,0:T(8,128)(2,1)S(1)}, bf16[512,128]{1,0:T(8,128)(2,1)S(1)}, u32[]{:S(2)}, u32[]{:S(2)}) collective-permute-start(bf16[512,128]{1,0:T(8,128)(2,1)S(1)} %get-tuple-element.48), channel_id=1, source_target_pairs={{0,8},{1,9},{2,10},{3,11},{4,12},{5,13},{6,14},{7,15},{8,0},{9,1},... | collective-permute-start | bytes 393224 | tf_op jit(solution)/shard_map/ppermute | solution.py:268
  86.0 14.2 %collective-permute-start.30 = (bf16[2048,128]{1,0:T(8,128)(2,1)S(1)}, bf16[2048,128]{1,0:T(8,128)(2,1)S(1)}, u32[]{:S(2)}, u32[]{:S(2)}) collective-permute-start(bf16[2048,128]{1,0:T(8,128)(2,1)S(1)} %constant_dynamic-update-slice_fusion.4.refs_4_), channel_id=1, source_target_pairs={{0,3},{1,0},{2,1},{3,2},{4,7},{5,4},{6,5},{7,6},{8,11},{9,8},{10,9... | collective-permute-start | bytes 1572872 | tf_op jit(solution)/shard_map/ppermute | solution.py:268
  86.6 5.7 %collective-permute-start.19 = (bf16[512,128]{1,0:T(8,128)(2,1)S(1)}, bf16[512,128]{1,0:T(8,128)(2,1)S(1)}, u32[]{:S(2)}, u32[]{:S(2)}) collective-permute-start(bf16[512,128]{1,0:T(8,128)(2,1)S(1)} %get-tuple-element.47), channel_id=1, source_target_pairs={{0,1},{1,2},{2,3},{3,0},{4,5},{5,6},{6,7},{7,4},{8,9},{9,10},{10,1... | collective-permute-start | bytes 393224 | tf_op jit(solution)/shard_map/ppermute | solution.py:268
  87.5 12.4 %collective-permute-start.21 = (bf16[512,128]{1,0:T(8,128)(2,1)S(1)}, bf16[512,128]{1,0:T(8,128)(2,1)S(1)}, u32[]{:S(2)}, u32[]{:S(2)}) collective-permute-start(bf16[512,128]{1,0:T(8,128)(2,1)S(1)} %get-tuple-element.47), channel_id=1, source_target_pairs={{0,3},{1,0},{2,1},{3,2},{4,7},{5,4},{6,5},{7,6},{8,11},{9,8},{10,9... | collective-permute-start | bytes 393224 | tf_op jit(solution)/shard_map/ppermute | solution.py:268
  89.2 6.3 %collective-permute-start.20 = (bf16[512,128]{1,0:T(8,128)(2,1)S(1)}, bf16[512,128]{1,0:T(8,128)(2,1)S(1)}, u32[]{:S(2)}, u32[]{:S(2)}) collective-permute-start(bf16[512,128]{1,0:T(8,128)(2,1)S(1)} %get-tuple-element.47), channel_id=1, source_target_pairs={{0,2},{1,3},{2,0},{3,1},{4,6},{5,7},{6,4},{7,5},{8,10},{9,11},{10,... | collective-permute-start | bytes 393224 | tf_op jit(solution)/shard_map/ppermute | solution.py:268
  90.5 15.1 %collective-permute-start.29 = (bf16[2048,128]{1,0:T(8,128)(2,1)S(1)}, bf16[2048,128]{1,0:T(8,128)(2,1)S(1)}, u32[]{:S(2)}, u32[]{:S(2)}) collective-permute-start(bf16[2048,128]{1,0:T(8,128)(2,1)S(1)} %constant_dynamic-update-slice_fusion.4.refs_4_), channel_id=1, source_target_pairs={{0,2},{1,3},{2,0},{3,1},{4,6},{5,7},{6,4},{7,5},{8,10},{9,11},{10,... | collective-permute-start | bytes 1572872 | tf_op jit(solution)/shard_map/ppermute | solution.py:268
  92.3 24.6 %collective-permute-start.28 = (bf16[2048,128]{1,0:T(8,128)(2,1)S(1)}, bf16[2048,128]{1,0:T(8,128)(2,1)S(1)}, u32[]{:S(2)}, u32[]{:S(2)}) collective-permute-start(bf16[2048,128]{1,0:T(8,128)(2,1)S(1)} %constant_dynamic-update-slice_fusion.4.refs_4_), channel_id=1, source_target_pairs={{0,1},{1,2},{2,3},{3,0},{4,5},{5,6},{6,7},{7,4},{8,9},{9,10},{10,1... | collective-permute-start | bytes 1572872 | tf_op jit(solution)/shard_map/ppermute | solution.py:268
  99.9 17.0 %collective-permute-start.24 = (bf16[2048,128]{1,0:T(8,128)(2,1)S(1)}, bf16[2048,128]{1,0:T(8,128)(2,1)S(1)}, u32[]{:S(2)}, u32[]{:S(2)}) collective-permute-start(bf16[2048,128]{1,0:T(8,128)(2,1)S(1)} %constant_dynamic-update-slice_fusion.refs_0_), channel_id=1, source_target_pairs={{0,12},{1,13},{2,14},{3,15},{4,0},{5,1},{6,2},{7,3},{8,4},{9,5},{1... | collective-permute-start | bytes 1572872 | tf_op jit(solution)/shard_map/ppermute | solution.py:268
  100.2 16.8 %collective-permute-start.23 = (bf16[2048,128]{1,0:T(8,128)(2,1)S(1)}, bf16[2048,128]{1,0:T(8,128)(2,1)S(1)}, u32[]{:S(2)}, u32[]{:S(2)}) collective-permute-start(bf16[2048,128]{1,0:T(8,128)(2,1)S(1)} %constant_dynamic-update-slice_fusion.refs_0_), channel_id=1, source_target_pairs={{0,8},{1,9},{2,10},{3,11},{4,12},{5,13},{6,14},{7,15},{8,0},{9,1},... | collective-permute-start | bytes 1572872 | tf_op jit(solution)/shard_map/ppermute | solution.py:268
  100.2 16.8 %collective-permute-start.22 = (bf16[2048,128]{1,0:T(8,128)(2,1)S(1)}, bf16[2048,128]{1,0:T(8,128)(2,1)S(1)}, u32[]{:S(2)}, u32[]{:S(2)}) collective-permute-start(bf16[2048,128]{1,0:T(8,128)(2,1)S(1)} %constant_dynamic-update-slice_fusion.refs_0_), channel_id=1, source_target_pairs={{0,4},{1,5},{2,6},{3,7},{4,8},{5,9},{6,10},{7,11},{8,12},{9,13},{1... | collective-permute-start | bytes 1572872 | tf_op jit(solution)/shard_map/ppermute | solution.py:268
  123.9 36.8 %collective-permute-start.31 = (bf16[2048,256]{1,0:T(8,128)(2,1)S(1)}, bf16[2048,256]{1,0:T(8,128)(2,1)S(1)}, u32[]{:S(2)}, u32[]{:S(2)}) collective-permute-start(bf16[2048,256]{1,0:T(8,128)(2,1)S(1)} %get-tuple-element.50), channel_id=1, source_target_pairs={{0,16},{16,0},{32,48},{48,32},{64,80},{80,64},{96,112},{112,96},{1... | collective-permute-start | bytes 3145736 | tf_op jit(solution)/shard_map/ppermute | solution.py:275
  147.5 3.7 %collective-permute-start.37 = (f32[40,256]{1,0:T(8,128)S(1)}, f32[40,256]{1,0:T(8,128)S(1)}, u32[]{:S(2)}, u32[]{:S(2)}) collective-permute-start(f32[40,256]{1,0:T(8,128)S(1)} %reduce_sum.9), channel_id=1, source_target_pairs={{0,12},{1,13},{2,14},{3,15},{4,0},{5,1},{6,2},{7,3},{8,4},{9,5},{1... | collective-permute-start | bytes 122888 | tf_op jit(solution)/shard_map/ppermute | solution.py:268
  147.9 4.1 %collective-permute-start.36 = (f32[40,256]{1,0:T(8,128)S(1)}, f32[40,256]{1,0:T(8,128)S(1)}, u32[]{:S(2)}, u32[]{:S(2)}) collective-permute-start(f32[40,256]{1,0:T(8,128)S(1)} %reduce_sum.9), channel_id=1, source_target_pairs={{0,4},{1,5},{2,6},{3,7},{4,8},{5,9},{6,10},{7,11},{8,12},{9,13},{1... | collective-permute-start | bytes 122888 | tf_op jit(solution)/shard_map/ppermute | solution.py:268
  149.5 4.7 %collective-permute-start.35 = (f32[40,256]{1,0:T(8,128)S(1)}, f32[40,256]{1,0:T(8,128)S(1)}, u32[]{:S(2)}, u32[]{:S(2)}) collective-permute-start(f32[40,256]{1,0:T(8,128)S(1)} %reduce_sum.9), channel_id=1, source_target_pairs={{0,8},{1,9},{2,10},{3,11},{4,12},{5,13},{6,14},{7,15},{8,0},{9,1},... | collective-permute-start | bytes 122888 | tf_op jit(solution)/shard_map/ppermute | solution.py:268
  154.2 8.9 %collective-permute-start.40 = (f32[40,256]{1,0:T(8,128)S(1)}, f32[40,256]{1,0:T(8,128)S(1)}, u32[]{:S(2)}, u32[]{:S(2)}) collective-permute-start(f32[40,256]{1,0:T(8,128)S(1)} %add_add_fusion.1), channel_id=1, source_target_pairs={{0,3},{1,0},{2,1},{3,2},{4,7},{5,4},{6,5},{7,6},{8,11},{9,8},{10,9... | collective-permute-start | bytes 122888 | tf_op jit(solution)/shard_map/ppermute | solution.py:268
  157.7 6.1 %collective-permute-start.39 = (f32[40,256]{1,0:T(8,128)S(1)}, f32[40,256]{1,0:T(8,128)S(1)}, u32[]{:S(2)}, u32[]{:S(2)}) collective-permute-start(f32[40,256]{1,0:T(8,128)S(1)} %add_add_fusion.1), channel_id=1, source_target_pairs={{0,1},{1,2},{2,3},{3,0},{4,5},{5,6},{6,7},{7,4},{8,9},{9,10},{10,1... | collective-permute-start | bytes 122888 | tf_op jit(solution)/shard_map/ppermute | solution.py:268
  159.0 4.8 %collective-permute-start.38 = (f32[40,256]{1,0:T(8,128)S(1)}, f32[40,256]{1,0:T(8,128)S(1)}, u32[]{:S(2)}, u32[]{:S(2)}) collective-permute-start(f32[40,256]{1,0:T(8,128)S(1)} %add_add_fusion.1), channel_id=1, source_target_pairs={{0,2},{1,3},{2,0},{3,1},{4,6},{5,7},{6,4},{7,5},{8,10},{9,11},{10,... | collective-permute-start | bytes 122888 | tf_op jit(solution)/shard_map/ppermute | solution.py:268
  161.0 25.3 %collective-permute-start.32 = (bf16[512,256]{1,0:T(8,128)(2,1)S(1)}, bf16[512,256]{1,0:T(8,128)(2,1)S(1)}, u32[]{:S(2)}, u32[]{:S(2)}) collective-permute-start(bf16[512,256]{1,0:T(8,128)(2,1)S(1)} %get-tuple-element.52), channel_id=1, source_target_pairs={{0,32},{16,48},{32,64},{48,80},{64,96},{80,112},{96,0},{112,16},{1... | collective-permute-start | bytes 786440 | tf_op jit(solution)/shard_map/ppermute | solution.py:275
  161.3 24.9 %collective-permute-start.33 = (bf16[512,256]{1,0:T(8,128)(2,1)S(1)}, bf16[512,256]{1,0:T(8,128)(2,1)S(1)}, u32[]{:S(2)}, u32[]{:S(2)}) collective-permute-start(bf16[512,256]{1,0:T(8,128)(2,1)S(1)} %get-tuple-element.53), channel_id=1, source_target_pairs={{0,64},{16,80},{32,96},{48,112},{64,0},{80,16},{96,32},{112,48},{1... | collective-permute-start | bytes 786440 | tf_op jit(solution)/shard_map/ppermute | solution.py:275
  163.1 23.2 %collective-permute-start.34 = (bf16[512,256]{1,0:T(8,128)(2,1)S(1)}, bf16[512,256]{1,0:T(8,128)(2,1)S(1)}, u32[]{:S(2)}, u32[]{:S(2)}) collective-permute-start(bf16[512,256]{1,0:T(8,128)(2,1)S(1)} %get-tuple-element.54), channel_id=1, source_target_pairs={{0,96},{16,112},{32,0},{48,16},{64,32},{80,48},{96,64},{112,80},{1... | collective-permute-start | bytes 786440 | tf_op jit(solution)/shard_map/ppermute | solution.py:275

commit v2 on v1

v2 whole, which is shorter than its diff:
```python
import math

import jax
import jax.numpy as jnp
from jax import lax
from jax.experimental import pallas as pl
from jax.experimental.pallas import tpu as pltpu
from jax.sharding import PartitionSpec as P

BF = jnp.bfloat16
F32 = jnp.float32
BLK = 128
PB = 4
ROWS = 512
HALF = 128
F = 256
GRP = 8
MIB = 1 << 20


def vmem():
    return pl.BlockSpec(memory_space=pltpu.VMEM)


def smem():
    return pl.BlockSpec(memory_space=pltpu.SMEM)


def hbm():
    return pl.BlockSpec(memory_space=pl.ANY)


def coords():
    row = lax.axis_index("row")
    col = lax.axis_index("col")
    return col // 4, col % 4, row // 2, row % 2


def prologue_kernel(*refs):
    count = (len(refs) - 1) // 2
    sems = refs[-1]
    copies = [
        pltpu.make_async_copy(refs[n], refs[count + n], sems.at[n]) for n in range(count)
    ]
    for copy in copies:
        copy.start()
    for copy in copies:
        copy.wait()


def prologue_call(arrays):
    return pl.pallas_call(
        prologue_kernel,
        out_shape=[jax.ShapeDtypeStruct(a.shape, a.dtype) for a in arrays],
        in_specs=[pl.BlockSpec(memory_space=pltpu.HBM)] * len(arrays),
        out_specs=[vmem()] * len(arrays),
        scratch_shapes=[pltpu.SemaphoreType.DMA((len(arrays),))],
        compiler_params=pltpu.CompilerParams(vmem_limit_bytes=8 * MIB),
        cost_estimate=pl.CostEstimate(
            flops=0, bytes_accessed=10 * MIB, transcendentals=0
        ),
        name="prologue",
    )(*arrays)


def forward_group(rows, cols, values, panel, acc, group, lanes):
    acc[:, lanes] = jnp.zeros_like(acc[:, lanes])
    for k in range(GRP):
        local = rows[0, group * GRP + k] - group * PB
        block = cols[0, group * GRP + k]
        here = pl.ds(pl.multiple_of(local * BLK, BLK), BLK)
        there = pl.ds(pl.multiple_of(block * BLK, BLK), BLK)
        acc[here, lanes] += jnp.dot(
            values[group * GRP + k], panel[there, lanes], preferred_element_type=F32
        )


def target_group(x, z, p, r):
    return ((x + p) % 4) * 4 + (z + r) % 4


LOW, HIGH, ALL = slice(0, HALF), slice(HALF, F), slice(0, F)


def far_kernel(rows, cols, values, *refs):
    pieces = refs[:8]
    panel = refs[8]
    outs_a = refs[9:11]
    outs_b = refs[11:13]
    acc, sems = refs[13:]
    x, z, y, c = coords()
    copies = []
    for n in range(8):
        dy, dc = n % 4, n // 4
        shard = ((y + 4 - dy) % 4) * 2 + (c + dc) % 2
        copies.append(
            pltpu.make_async_copy(
                pieces[n], panel.at[pl.ds(shard * ROWS, ROWS)], sems.at[n]
            )
        )
    for copy in copies:
        copy.start()
    for copy in copies:
        copy.wait()
    for n in range(4):
        lanes = ALL if n == 2 else LOW
        forward_group(rows, cols, values, panel, acc, target_group(x, z, 2, n), lanes)
        here = pl.ds((n % 2) * ROWS, ROWS)
        outs_a[n // 2][here, :] = acc[:, LOW].astype(BF)
        if n == 2:
            outs_b[n // 2][here, :] = acc[:, HIGH].astype(BF)
    for n in (0, 1, 3):
        forward_group(rows, cols, values, panel, acc, target_group(x, z, n, 2), HIGH)
        here = pl.ds((n % 2) * ROWS, ROWS)
        outs_b[n // 2][here, :] = acc[:, HIGH].astype(BF)


def far_call(rows, cols, values, pieces):
    part = jax.ShapeDtypeStruct((2 * ROWS, HALF), BF)
    return pl.pallas_call(
        far_kernel,
        out_shape=[jax.ShapeDtypeStruct((8 * ROWS, F), BF)] + [part] * 4,
        in_specs=[smem(), smem(), vmem()] + [hbm()] * 8,
        out_specs=[vmem()] * 5,
        scratch_shapes=[pltpu.VMEM((ROWS, F), F32), pltpu.SemaphoreType.DMA((8,))],
        compiler_params=pltpu.CompilerParams(vmem_limit_bytes=24 * MIB),
        cost_estimate=pl.CostEstimate(
            flops=32 * 2 * BLK * BLK * F, bytes_accessed=7 * MIB, transcendentals=0
        ),
        name="forward_far",
    )(rows, cols, values, *pieces)


def near_kernel(rows, cols, values, panel, *refs):
    outs_a = (refs[0], refs[1], None, refs[2])
    outs_b = (refs[3], refs[4], None, refs[5])
    acc = refs[6]
    x, z, y, c = coords()
    for p in (1, 3, 0, 2):
        for r in (1, 3, 0, 2):
            if p == 2 and r == 2:
                continue
            lanes = HIGH if p == 2 else LOW if r == 2 else ALL
            forward_group(rows, cols, values, panel, acc, target_group(x, z, p, r), lanes)
            if p != 2:
                outs_a[p][r * ROWS:(r + 1) * ROWS, :] = acc[:, LOW].astype(BF)
            if r != 2:
                outs_b[r][p * ROWS:(p + 1) * ROWS, :] = acc[:, HIGH].astype(BF)


def near_call(rows, cols, values, panel):
    part = jax.ShapeDtypeStruct((4 * ROWS, HALF), BF)
    return pl.pallas_call(
        near_kernel,
        out_shape=[part] * 6,
        in_specs=[smem(), smem(), vmem(), vmem()],
        out_specs=[vmem()] * 6,
        scratch_shapes=[pltpu.VMEM((ROWS, F), F32)],
        compiler_params=pltpu.CompilerParams(vmem_limit_bytes=24 * MIB),
        cost_estimate=pl.CostEstimate(
            flops=96 * 2 * BLK * BLK * F, bytes_accessed=9 * MIB, transcendentals=0
        ),
        name="forward_near",
    )(rows, cols, values, panel)


def relay_kernel(*refs):
    for n in range(4):
        own, extra, out = refs[n], refs[4 + n], refs[8 + n]
        mixed = pl.ds((n % 2) * 2 * ROWS, 2 * ROWS)
        plain = pl.ds((1 - n % 2) * 2 * ROWS, 2 * ROWS)
        out[mixed, :] = (own[mixed, :].astype(F32) + extra[...].astype(F32)).astype(BF)
        out[plain, :] = own[plain, :]


def relay_call(own, extra):
    return pl.pallas_call(
        relay_kernel,
        out_shape=[jax.ShapeDtypeStruct((4 * ROWS, HALF), BF)] * 4,
        in_specs=[vmem()] * 8,
        out_specs=[vmem()] * 4,
        compiler_params=pltpu.CompilerParams(vmem_limit_bytes=24 * MIB),
        cost_estimate=pl.CostEstimate(
            flops=8 * ROWS * HALF, bytes_accessed=5 * MIB, transcendentals=0
        ),
        name="relay_sum",
    )(*own, *extra)


def quad(parts, here=slice(None)):
    p0, p1, p2, p3 = (part[here].astype(F32) for part in parts)
    return (p0 + p2) + (p1 + p3)


def stage_kernel(*refs):
    for half in range(2):
        parts = refs[3 * half:3 * half + 3]
        outs = refs[6 + 4 * half:10 + 4 * half]
        for n, out in enumerate(outs):
            here = pl.ds(n * ROWS, ROWS)
            p0, p1, p3 = (part[here, :].astype(F32) for part in parts)
            out[...] = (p0 + (p1 + p3)).astype(BF)


def stage_call(parts_a, parts_b):
    return pl.pallas_call(
        stage_kernel,
        out_shape=[jax.ShapeDtypeStruct((ROWS, HALF), BF)] * 8,
        in_specs=[vmem()] * 6,
        out_specs=[vmem()] * 8,
        compiler_params=pltpu.CompilerParams(vmem_limit_bytes=24 * MIB),
        cost_estimate=pl.CostEstimate(
            flops=24 * ROWS * HALF, bytes_accessed=4 * MIB, transcendentals=0
        ),
        name="stage_sum",
    )(*parts_a, *parts_b)


def point_kernel(scale, *refs):
    parts_a = refs[:4]
    parts_b = refs[4:8]
    weight, bias, cotangent = refs[8:11]
    out_act, grad_a, grad_b, gradients = refs[11:]

    aggregated = jnp.concatenate(
        [quad(parts_a).astype(BF), quad(parts_b).astype(BF)], axis=1
    )
    pre = jnp.dot(aggregated, weight[...], preferred_element_type=F32) + bias[...]
    gate = jax.nn.sigmoid(pre)
    out_act[...] = (pre * gate).astype(BF)
    grad_pre = (
        cotangent[...].astype(F32) * gate * (1.0 + pre * (1.0 - gate))
    ).astype(BF)
    grad_agg = lax.dot_general(
        grad_pre, weight[...], (((1,), (1,)), ((), ())), preferred_element_type=F32
    ).astype(BF)
    grad_a[...] = grad_agg[:, :HALF]
    grad_b[...] = grad_agg[:, HALF:]
    weight_grad = lax.dot_general(
        aggregated, grad_pre, (((0,), (0,)), ((), ())), preferred_element_type=F32
    ) * scale
    bias_grad = jnp.sum(grad_pre.astype(F32), axis=0, keepdims=True) * scale
    for n in range(8):
        gradients[n, :32, :] = weight_grad[n * 32:(n + 1) * 32, :]
        gradients[n, 32:, :] = jnp.broadcast_to(bias_grad, (8, F))


def point_call(parts_a, parts_b, weight, bias, cotangent, scale):
    half = jax.ShapeDtypeStruct((ROWS, HALF), BF)
    return pl.pallas_call(
        lambda *refs: point_kernel(scale, *refs),
        out_shape=[
            jax.ShapeDtypeStruct((ROWS, F), BF),
            half,
            half,
            jax.ShapeDtypeStruct((8, 40, F), F32),
        ],
        in_specs=[vmem()] * 11,
        out_specs=[vmem()] * 4,
        compiler_params=pltpu.CompilerParams(vmem_limit_bytes=24 * MIB),
        cost_estimate=pl.CostEstimate(
            flops=3 * 2 * ROWS * F * F, bytes_accessed=2 * MIB, transcendentals=ROWS * F
        ),
        name="pointwise",
    )(*parts_a, *parts_b, weight, bias, cotangent)


def join_kernel(*refs):
    spread = refs[8]
    outs = refs[9:11]
    for half in range(2):
        for n in range(4):
            outs[half][n * ROWS:(n + 1) * ROWS, :] = refs[4 * half + n][...]
    refs[11][...] = jnp.sum(spread[...], axis=0)


def join_call(parts_a, parts_b, spread):
    return pl.pallas_call(
        join_kernel,
        out_shape=[jax.ShapeDtypeStruct((4 * ROWS, HALF), BF)] * 2
        + [jax.ShapeDtypeStruct((40, F), F32)],
        in_specs=[vmem()] * 9,
        out_specs=[vmem()] * 3,
        compiler_params=pltpu.CompilerParams(vmem_limit_bytes=24 * MIB),
        cost_estimate=pl.CostEstimate(
            flops=320 * F, bytes_accessed=3 * MIB, transcendentals=0
        ),
        name="join",
    )(*parts_a, *parts_b, spread)


def cut_kernel(*refs):
    for n in range(4):
        refs[4 + n][...] = refs[n][pl.ds((n % 2) * 2 * ROWS, 2 * ROWS), :]


def cut_call(parts):
    return pl.pallas_call(
        cut_kernel,
        out_shape=[jax.ShapeDtypeStruct((2 * ROWS, HALF), BF)] * 4,
        in_specs=[vmem()] * 4,
        out_specs=[vmem()] * 4,
        compiler_params=pltpu.CompilerParams(vmem_limit_bytes=16 * MIB),
        cost_estimate=pl.CostEstimate(
            flops=0, bytes_accessed=2 * MIB, transcendentals=0
        ),
        name="cut",
    )(*parts)


def last_kernel(*refs):
    mine, theirs, x_grad, weight_grad, bias_grad = refs[4:]
    x, z, y, c = coords()
    x_grad[...] = quad(refs[:4]).astype(BF)
    for dy in range(4):
        base = ((y + 4 - dy) % 4) * 2
        for source, core in ((mine, c), (theirs, 1 - c)):
            shard = base + core
            here = pl.ds(pl.multiple_of(shard * 32, 32), 32)
            weight_grad[here, :] = source[dy, :32, :]

            @pl.when(shard == 0)
            def _():
                bias_grad[...] = source[dy, 32:33, :]


def last_call(parts, mine, theirs):
    return pl.pallas_call(
        last_kernel,
        out_shape=[
            jax.ShapeDtypeStruct((ROWS, F), BF),
            jax.ShapeDtypeStruct((F, F), F32),
            jax.ShapeDtypeStruct((1, F), F32),
        ],
        in_specs=[vmem()] * 6,
        out_specs=[vmem()] * 3,
        compiler_params=pltpu.CompilerParams(vmem_limit_bytes=24 * MIB),
        cost_estimate=pl.CostEstimate(
            flops=4 * ROWS * F, bytes_accessed=10 * ROWS * F, transcendentals=0
        ),
        name="last_sum",
    )(*parts, mine, theirs)


def backward_slots(rows, cols, values, acc, group, lanes, read):
    for k in range(GRP):
        local = rows[0, group * GRP + k] - group * PB
        there = pl.ds(pl.multiple_of(cols[0, group * GRP + k] * BLK, BLK), BLK)
        acc[there, lanes] += lax.dot_general(
            values[group * GRP + k],
            read(local),
            (((0,), (0,)), ((), ())),
            preferred_element_type=F32,
        )


def source_group(x, z, p, r):
    return ((x + 4 - p) % 4) * 4 + (z + 4 - r) % 4


def block_at(base, local):
    return pl.ds(pl.multiple_of(base + local * BLK, BLK), BLK)


def early_kernel(rows, cols, values, *refs):
    parts_a = (refs[0], refs[1], None, refs[2])
    parts_b = (refs[3], refs[4], None, refs[5])
    acc = refs[6]
    x, z, y, c = coords()
    acc[...] = jnp.zeros_like(acc)
    for p in range(4):
        for r in range(4):
            if p == 2 and r == 2:
                continue

            def from_a(local, p=p, r=r):
                return parts_a[p][block_at(r * ROWS, local), :]

            def from_b(local, p=p, r=r):
                return parts_b[r][block_at(p * ROWS, local), :]

            def both(local, from_a=from_a, from_b=from_b):
                return jnp.concatenate([from_a(local), from_b(local)], axis=1)

            lanes, read = (HIGH, from_b) if p == 2 else (LOW, from_a) if r == 2 else (ALL, both)
            backward_slots(rows, cols, values, acc, source_group(x, z, p, r), lanes, read)


def early_call(rows, cols, values, parts_a, parts_b):
    return pl.pallas_call(
        early_kernel,
        out_shape=jax.ShapeDtypeStruct((8 * ROWS, F), F32),
        in_specs=[smem(), smem()] + [vmem()] * 7,
        out_specs=vmem(),
        compiler_params=pltpu.CompilerParams(vmem_limit_bytes=24 * MIB),
        cost_estimate=pl.CostEstimate(
            flops=96 * 2 * BLK * BLK * F, bytes_accessed=10 * MIB, transcendentals=0
        ),
        name="backward_early",
    )(rows, cols, values, *parts_a, *parts_b)


def late_kernel(rows, cols, values, start, *refs):
    parts_a = refs[:2]
    parts_b = refs[2:4]
    mine, other, acc = refs[4:]
    x, z, y, c = coords()
    acc[...] = start[...]
    for n in range(4):

        def from_a(local, n=n):
            return parts_a[n // 2][block_at((n % 2) * ROWS, local), :]

        def from_b(local, n=n):
            return parts_b[n // 2][block_at((n % 2) * ROWS, local), :]

        backward_slots(rows, cols, values, acc, source_group(x, z, 2, n), LOW, from_a)
        backward_slots(rows, cols, values, acc, source_group(x, z, n, 2), HIGH, from_b)
    for dy in range(4):
        base = ((y + dy) % 4) * 2
        own = pl.ds(pl.multiple_of((base + c) * ROWS, ROWS), ROWS)
        peer = pl.ds(pl.multiple_of((base + 1 - c) * ROWS, ROWS), ROWS)
        mine[dy * ROWS:(dy + 1) * ROWS, :] = acc[own, :].astype(BF)
        other[dy * ROWS:(dy + 1) * ROWS, :] = acc[peer, :].astype(BF)


def late_call(rows, cols, values, start, parts_a, parts_b):
    part = jax.ShapeDtypeStruct((4 * ROWS, F), BF)
    return pl.pallas_call(
        late_kernel,
        out_shape=[part] * 2,
        in_specs=[smem(), smem()] + [vmem()] * 6,
        out_specs=[vmem()] * 2,
        scratch_shapes=[pltpu.VMEM((8 * ROWS, F), F32)],
        compiler_params=pltpu.CompilerParams(vmem_limit_bytes=32 * MIB),
        cost_estimate=pl.CostEstimate(
            flops=32 * 2 * BLK * BLK * F, bytes_accessed=8 * MIB, transcendentals=0
        ),
        name="backward_late",
    )(rows, cols, values, start, *parts_a, *parts_b)


def pair_kernel(mine, other, *outs):
    for n, out in enumerate(outs):
        here = pl.ds(n * ROWS, ROWS)
        out[...] = (mine[here, :].astype(F32) + other[here, :].astype(F32)).astype(BF)


def pair_call(mine, other):
    out = jax.ShapeDtypeStruct((ROWS, F), BF)
    return pl.pallas_call(
        pair_kernel,
        out_shape=[out] * 4,
        in_specs=[vmem()] * 2,
        out_specs=[vmem()] * 4,
        compiler_params=pltpu.CompilerParams(vmem_limit_bytes=24 * MIB),
        cost_estimate=pl.CostEstimate(
            flops=4 * ROWS * F, bytes_accessed=24 * ROWS * F, transcendentals=0
        ),
        name="pair_sum",
    )(mine, other)


def along_col(value, dx, dz):
    pairs = [
        (a * 4 + b, ((a + dx) % 4) * 4 + (b + dz) % 4) for a in range(4) for b in range(4)
    ]
    return lax.ppermute(value, "col", pairs)


def along_row(value, dy, dc):
    pairs = [
        (a * 2 + b, ((a + dy) % 4) * 2 + (b + dc) % 2) for a in range(4) for b in range(2)
    ]
    return lax.ppermute(value, "row", pairs)


def partner_sum(value, dx, dz):
    pairs = [(a * 4 + b, (a ^ dx) * 4 + (b ^ dz)) for a in range(4) for b in range(4)]
    return value + lax.ppermute(value, "col", pairs)


def shards(x_feat, block_values, block_rows, block_cols, weight, bias, cotangent):
    scale = 1.0 / math.sqrt(65536)

    near = {d: along_row(x_feat, d, 0) for d in (2, 1, 3)}
    swap = [along_row(x_feat, 0, 1)] + [None] * 3
    own, values, rows, cols, weight, bias, cotangent = prologue_call(
        [
            x_feat,
            block_values.reshape(128, BLK, BLK),
            block_rows.reshape(1, 128),
            block_cols.reshape(1, 128),
            weight,
            bias.reshape(1, F),
            cotangent,
        ]
    )
    near[1], own = lax.optimization_barrier((near[1], own))
    for d in (1, 3, 2):
        swap[d] = along_row(near[d], 0, 1)
    pieces = [own, near[1], near[2], near[3]] + swap

    panel, far_a1, far_a2, far_b1, far_b2 = far_call(rows, cols, values, pieces)
    extra = [
        along_col(far_a1, 1, 0),
        along_col(far_a2, 3, 0),
        along_col(far_b1, 0, 1),
        along_col(far_b2, 0, 3),
    ]
    a0, a1, a3, b0, b1, b3 = near_call(rows, cols, values, panel)
    a1, a3, b1, b3 = relay_call([a1, a3, b1, b3], extra)
    sums = stage_call(
        [a0, along_col(a1, 1, 0), along_col(a3, 3, 0)],
        [b0, along_col(b1, 0, 1), along_col(b3, 0, 3)],
    )
    sum_a, sum_b = sums[:4], sums[4:]
    part_a, part_b = [sum_a[0]] + [None] * 3, [sum_b[0]] + [None] * 3
    for d in (2, 1, 3):
        part_a[d] = along_col(sum_a[d], 0, d)
        part_b[d] = along_col(sum_b[d], d, 0)
    out_act, grad_a, grad_b, gradients = point_call(
        part_a, part_b, weight, bias, cotangent, scale
    )

    first_a, first_b = [grad_a] + [None] * 3, [grad_b] + [None] * 3
    for d in (2, 1, 3):
        first_a[d] = along_col(grad_a, 0, d)
        first_b[d] = along_col(grad_b, d, 0)
    spread = lax.all_to_all(gradients, "row", 0, 0)
    join_a, join_b, piece = join_call(first_a, first_b, spread)
    a1, a3 = along_col(join_a, 1, 0), along_col(join_a, 3, 0)
    b1, b3 = along_col(join_b, 0, 1), along_col(join_b, 0, 3)
    piece = partner_sum(partner_sum(piece, 1, 0), 2, 0)
    a1, a3, b1, b3, piece = lax.optimization_barrier((a1, a3, b1, b3, piece))
    cut_a1, cut_a3, cut_b1, cut_b3 = cut_call([a1, a3, b1, b3])
    far = [
        along_col(cut_a1, 1, 0),
        along_col(cut_a3, 3, 0),
        along_col(cut_b1, 0, 1),
        along_col(cut_b3, 0, 3),
    ]
    start = early_call(rows, cols, values, [join_a, a1, a3], [join_b, b1, b3])
    piece = partner_sum(partner_sum(piece, 0, 1), 0, 2)
    *far, piece = lax.optimization_barrier((*far, piece))
    mine, other = late_call(rows, cols, values, start, far[:2], far[2:])
    held = jnp.stack([piece] + [along_row(piece, d, 0) for d in (1, 2, 3)])
    other = along_row(other, 0, 1)
    sums = pair_call(mine, other)
    theirs = along_row(held, 0, 1)
    last = [sums[0]] + [None] * 3
    for d in (2, 1, 3):
        last[d] = along_row(sums[d], d, 0)
    x_grad, weight_grad, bias_grad = last_call(last, held, theirs)
    return (out_act, x_grad, weight_grad, bias_grad.reshape(F))


def solution(mesh):
    placed = (
        P(("row", "col"), None),
        P("row", "col", None, None, None),
        P("row", "col", None),
        P("row", "col", None),
        P(),
        P(),
        P(("row", "col"), None),
    )
    return jax.shard_map(
        shards,
        mesh=mesh,
        in_specs=placed,
        out_specs=(P(("row", "col"), None), P(("row", "col"), None), P(), P()),
        check_vma=False,
    )
```

time: 187 us -> 148 us (0.79)
  blocking collectives: 31 us -> 0 us
  waiting for transfers between devices: 64.2 us -> 43.9 us
  starting transfers between devices: 68.8 us -> 79 us
  local copies, waits for them, and re-layouts: 5.87 us -> 9.17 us
  Pallas kernels: 16.4 us -> 14.3 us
    ppermute x30 -> x28, waiting for transfers between devices: 51.7 us -> 21.5 us  [along_col(): return lax.ppermute(value, 'col', pairs)]
    all_gather x1 -> x0, blocking collectives: 21.1 us -> none  [shards(): complete = lax.all_gather(piece, 'row', axis=0, tiled=False)]
    ppermute x0 -> x4, waiting for transfers between devices: none -> 10.9 us  [partner_sum(): return value + lax.ppermute(value, 'col', pairs)]
    all_to_all x1 -> x0, blocking collectives: 9.88 us -> none  [shards(): spread = lax.all_to_all(gradients, 'row', 0, 0)]
    all_to_all x0 -> x1, starting transfers between devices: none -> 9.07 us  [shards(): spread = lax.all_to_all(gradients, 'row', 0, 0)]
    ppermute x0 -> x4, starting transfers between devices: none -> 6.83 us  [partner_sum(): return value + lax.ppermute(value, 'col', pairs)]
    ppermute x30 -> x28, starting transfers between devices: 43.9 us -> 38.6 us  [along_col(): return lax.ppermute(value, 'col', pairs)]
    unnamed x20, local copies, waits for them, and re-layouts: 4.55 us -> 9.17 us
  transfers between devices with their start and end apart: 41 -> 48, of which waited for: 18 -> 20; matrix products, arithmetic and copies ran while one was open for 1% -> 0% of each run, Pallas kernels for 0% -> 5%
where the time goes in v2:
time: 148 us; the launch traced here: 147 us
  starting transfers between devices  79 us (53%)
  waiting for transfers between devices  43.9 us (30%)
  Pallas kernels  14.3 us (10%)
  local copies, waits for them, and re-layouts  9.17 us (6%)
    ppermute x28, starting transfers between devices, along_col(): return lax.ppermute(value, 'col', pairs)  38.6 us
    ppermute x15, starting transfers between devices, along_row(): return lax.ppermute(value, 'row', pairs)  24.6 us
    ppermute x28, waiting for transfers between devices, along_col(): return lax.ppermute(value, 'col', pairs)  21.5 us
    ppermute x15, waiting for transfers between devices, along_row(): return lax.ppermute(value, 'row', pairs)  11.4 us
    ppermute x4, waiting for transfers between devices, partner_sum(): return value + lax.ppermute(value, 'col', pairs)  10.9 us
    unnamed x20, local copies, waits for them, and re-layouts  9.17 us
    all_to_all x1, starting transfers between devices, shards(): spread = lax.all_to_all(gradients, 'row', 0, 0)  9.07 us
    ppermute x4, starting transfers between devices, partner_sum(): return value + lax.ppermute(value, 'col', pairs)  6.83 us
  transfers between devices with their start and end apart: 48, of which 20 were waited for; matrix products, arithmetic and copies ran while one was open for 0% of the time, Pallas kernels for 5%

profile of v2, /device:TPU:1, one launch (start us, length us, event | category | flops | bytes accessed | tf_op | source)
XLA Modules:
  0.0 147.3 jit_solution(10207996401537111714)
XLA Ops:
  0.6 2.2 %collective-permute-start = (bf16[512,256]{1,0:T(8,128)(2,1)}, bf16[512,256]{1,0:T(8,128)(2,1)S(1)}, u32[]{:S(2)}, u32[]{:S(2)}) collective-permute-start(bf16[512,256]{1,0:T(8,128)(2,1)} %refs_0_.1), channel_id=1, source_target_pairs={{0,32},{16,48},{32,64},{48,80},{64,96},{80,112},{96,0},{112,16},{1... | collective-permute-start | bytes 786440 | tf_op jit(solution)/shard_map/ppermute | solution.py:475
  2.8 2.6 %collective-permute-start.1 = (bf16[512,256]{1,0:T(8,128)(2,1)}, bf16[512,256]{1,0:T(8,128)(2,1)S(1)}, u32[]{:S(2)}, u32[]{:S(2)}) collective-permute-start(bf16[512,256]{1,0:T(8,128)(2,1)} %refs_0_.1), channel_id=1, source_target_pairs={{0,64},{16,80},{32,96},{48,112},{64,0},{80,16},{96,32},{112,48},{1... | collective-permute-start | bytes 786440 | tf_op jit(solution)/shard_map/ppermute | solution.py:475
  5.4 1.1 collective-permute-start.2
  6.5 1.5 %collective-permute-start.3 = (bf16[512,256]{1,0:T(8,128)(2,1)}, bf16[512,256]{1,0:T(8,128)(2,1)S(1)}, u32[]{:S(2)}, u32[]{:S(2)}) collective-permute-start(bf16[512,256]{1,0:T(8,128)(2,1)} %refs_0_.1), channel_id=1, source_target_pairs={{0,16},{16,0},{32,48},{48,32},{64,80},{80,64},{96,112},{112,96},{1... | collective-permute-start | bytes 786440 | tf_op jit(solution)/shard_map/ppermute | solution.py:475
  8.0 2.2 %copy-done.3 = bf16[1,1,128,128,128]{4,3,2,1,0:T(8,128)(2,1)S(1)} copy-done((bf16[1,1,128,128,128]{4,3,2,1,0:T(8,128)(2,1)S(1)}, bf16[1,1,128,128,128]{4,3,2,1,0:T(8,128)(2,1)}, u32[]{:S(2)}) %copy-start.3) | copy-done | bytes 4194328
  10.2 0.9 copy-done.4
  11.2 0.9 copy-done.5
  12.1 0.9 copy-done.6
  13.0 0.7 copy-done.7
  13.7 0.7 copy-done.8
  14.4 0.7 copy-done.9
  15.7 1.3 collective-permute-done.1.refs_2_
  17.0 1.5 %collective-permute-start.5 = (bf16[512,256]{1,0:T(8,128)(2,1)S(1)}, bf16[512,256]{1,0:T(8,128)(2,1)S(1)}, u32[]{:S(2)}, u32[]{:S(2)}) collective-permute-start(bf16[512,256]{1,0:T(8,128)(2,1)S(1)} %collective-permute-done.1.refs_2_), channel_id=1, source_target_pairs={{0,16},{16,0},{32,48},{48,32},{64,80},{80,64},{96,112},{112,96},{1... | collective-permute-start | bytes 786440 | tf_op jit(solution)/shard_map/ppermute | solution.py:475
  18.6 1.1 collective-permute-done.5.refs_6_
  20.1 1.9 %forward_far.1 = (bf16[4096,256]{1,0:T(8,128)(2,1)S(1)}, bf16[1024,128]{1,0:T(8,128)(2,1)S(1)}, bf16[1024,128]{1,0:T(8,128)(2,1)S(1)}, bf16[1024,128]{1,0:T(8,128)(2,1)S(1)}, bf16[1024,128]{1,0:T(8,128)(2,1)S(1)}) custom-call(s32[1,128]{1,0:T(1,128)S(1)} %get-tuple-element.66.rows, s32[1,128]{1,0:T(1,128)S(1)} %get-tuple-element.67.cols, ...), custom_call_target="tpu_custom_call" | custom-call | flops 268435456 | bytes 7340032 | tf_op jit(solution)/shard_map/forward_far/pallas_call | solution.py:120
  22.0 1.3 collective-permute-start.7
  23.3 1.5 collective-permute-start.8
  24.8 1.6 %collective-permute-start.9 = (bf16[1024,128]{1,0:T(8,128)(2,1)S(1)}, bf16[1024,128]{1,0:T(8,128)(2,1)S(1)}, u32[]{:S(2)}, u32[]{:S(2)}) collective-permute-start(bf16[1024,128]{1,0:T(8,128)(2,1)S(1)} %get-tuple-element.80), channel_id=1, source_target_pairs={{0,1},{1,2},{2,3},{3,0},{4,5},{5,6},{6,7},{7,4},{8,9},{9,10},{10,1... | collective-permute-start | bytes 786440 | tf_op jit(solution)/shard_map/ppermute | solution.py:468
  26.4 2.1 %collective-permute-start.10 = (bf16[1024,128]{1,0:T(8,128)(2,1)S(1)}, bf16[1024,128]{1,0:T(8,128)(2,1)S(1)}, u32[]{:S(2)}, u32[]{:S(2)}) collective-permute-start(bf16[1024,128]{1,0:T(8,128)(2,1)S(1)} %get-tuple-element.81), channel_id=1, source_target_pairs={{0,3},{1,0},{2,1},{3,2},{4,7},{5,4},{6,5},{7,6},{8,11},{9,8},{10,9... | collective-permute-start | bytes 786440 | tf_op jit(solution)/shard_map/ppermute | solution.py:468
  28.5 3.4 %forward_near.1 = (bf16[2048,128]{1,0:T(8,128)(2,1)S(1)}, bf16[2048,128]{1,0:T(8,128)(2,1)S(1)}, bf16[2048,128]{1,0:T(8,128)(2,1)S(1)}, bf16[2048,128]{1,0:T(8,1...) custom-call(s32[1,128]{1,0:T(1,128)S(1)} %get-tuple-element.66.rows, ...), custom_call_target="tpu_custom_call" | custom-call | flops 805306368 | bytes 9437184 | tf_op jit(solution)/shard_map/forward_near/pallas_call | solution.py:153
  32.0 2.3 %collective-permute-done.9.refs_6_ = bf16[1024,128]{1,0:T(8,128)(2,1)S(1)} collective-permute-done((bf16[1024,128]{1,0:T(8,128)(2,1)S(1)}, bf16[1024,128]{1,0:T(8,128)(2,1)S(1)}, u32[]{:S(2)}, u32[]{:S(2)}) %collective-permute-start.9) | collective-permute-done | bytes 262176 | tf_op jit(solution)/shard_map/ppermute | solution.py:468
  34.6 2.7 %collective-permute-start.12 = (bf16[2048,128]{1,0:T(8,128)(2,1)S(1)}, bf16[2048,128]{1,0:T(8,128)(2,1)S(1)}, u32[]{:S(2)}, u32[]{:S(2)}) collective-permute-start(bf16[2048,128]{1,0:T(8,128)(2,1)S(1)} %get-tuple-element.83), channel_id=1, source_target_pairs={{0,12},{1,13},{2,14},{3,15},{4,0},{5,1},{6,2},{7,3},{8,4},{9,5},{1... | collective-permute-start | bytes 1572872 | tf_op jit(solution)/shard_map/ppermute | solution.py:468
  37.6 2.3 %collective-permute-start.14 = (bf16[2048,128]{1,0:T(8,128)(2,1)S(1)}, bf16[2048,128]{1,0:T(8,128)(2,1)S(1)}, u32[]{:S(2)}, u32[]{:S(2)}) collective-permute-start(bf16[2048,128]{1,0:T(8,128)(2,1)S(1)} %get-tuple-element.86), channel_id=1, source_target_pairs={{0,3},{1,0},{2,1},{3,2},{4,7},{5,4},{6,5},{7,6},{8,11},{9,8},{10,9... | collective-permute-start | bytes 1572872 | tf_op jit(solution)/shard_map/ppermute | solution.py:468
  40.0 7.8 %collective-permute-done.11.refs_1_ = bf16[2048,128]{1,0:T(8,128)(2,1)S(1)} collective-permute-done((bf16[2048,128]{1,0:T(8,128)(2,1)S(1)}, bf16[2048,128]{1,0:T(8,128)(2,1)S(1)}, u32[]{:S(2)}, u32[]{:S(2)}) %collective-permute-start.11) | collective-permute-done | bytes 524320 | tf_op jit(solution)/shard_map/ppermute | solution.py:468
  47.7 2.1 %collective-permute-done.13.refs_4_ = bf16[2048,128]{1,0:T(8,128)(2,1)S(1)} collective-permute-done((bf16[2048,128]{1,0:T(8,128)(2,1)S(1)}, bf16[2048,128]{1,0:T(8,128)(2,1)S(1)}, u32[]{:S(2)}, u32[]{:S(2)}) %collective-permute-start.13) | collective-permute-done | bytes 524320 | tf_op jit(solution)/shard_map/ppermute | solution.py:468
  50.3 3.6 %collective-permute-start.16 = (bf16[512,128]{1,0:T(8,128)(2,1)S(1)}, bf16[512,128]{1,0:T(8,128)(2,1)S(1)}, u32[]{:S(2)}, u32[]{:S(2)}) collective-permute-start(bf16[512,128]{1,0:T(8,128)(2,1)S(1)} %get-tuple-element.89), channel_id=1, source_target_pairs={{0,2},{1,3},{2,0},{3,1},{4,6},{5,7},{6,4},{7,5},{8,10},{9,11},{10,... | collective-permute-start | bytes 393224 | tf_op jit(solution)/shard_map/ppermute | solution.py:468
  54.1 1.2 collective-permute-start.19
  55.3 1.4 collective-permute-start.20
  56.8 0.9 collective-permute-done.16.refs_2_
  58.0 2.8 %collective-permute-done.18.refs_5_ = bf16[512,128]{1,0:T(8,128)(2,1)S(1)} collective-permute-done((bf16[512,128]{1,0:T(8,128)(2,1)S(1)}, bf16[512,128]{1,0:T(8,128)(2,1)S(1)}, u32[]{:S(2)}, u32[]{:S(2)}) %collective-permute-start.18) | collective-permute-done | bytes 131104 | tf_op jit(solution)/shard_map/ppermute | solution.py:468
  60.8 0.6 collective-permute-done.20.refs_7_
  61.4 1.3 pointwise.1
  62.7 9.1 %all-to-all-start = ((f32[8,40,256]{2,1,0:T(8,128)}), f32[8,40,256]{2,1,0:T(8,128)S(1)}, u32[]{:S(2)}, u32[]{:S(2)}) async-start(f32[8,40,256]{2,1,0:T(8,128)} %get-tuple-element.101), calls=%async_computation | async-start | bytes 655360 | tf_op jit(solution)/shard_map/all_to_all | solution.py:530
  71.8 0.9 collective-permute-start.21
  72.7 2.4 %collective-permute-start.23 = (bf16[512,128]{1,0:T(8,128)(2,1)S(1)}, bf16[512,128]{1,0:T(8,128)(2,1)S(1)}, u32[]{:S(2)}, u32[]{:S(2)}) collective-permute-start(bf16[512,128]{1,0:T(8,128)(2,1)S(1)} %get-tuple-element.99.refs_0_), channel_id=1, source_target_pairs={{0,3},{1,0},{2,1},{3,2},{4,7},{5,4},{6,5},{7,6},{8,11},{9,8},{10,9... | collective-permute-start | bytes 393224 | tf_op jit(solution)/shard_map/ppermute | solution.py:468
  75.4 2.9 %collective-permute-start.25 = (bf16[512,128]{1,0:T(8,128)(2,1)S(1)}, bf16[512,128]{1,0:T(8,128)(2,1)S(1)}, u32[]{:S(2)}, u32[]{:S(2)}) collective-permute-start(bf16[512,128]{1,0:T(8,128)(2,1)S(1)} %get-tuple-element.100.refs_4_), channel_id=1, source_target_pairs={{0,8},{1,9},{2,10},{3,11},{4,12},{5,13},{6,14},{7,15},{8,0},{9,1},... | collective-permute-start | bytes 393224 | tf_op jit(solution)/shard_map/ppermute | solution.py:468
  78.4 2.5 %collective-permute-done.21.refs_1_ = bf16[512,128]{1,0:T(8,128)(2,1)S(1)} collective-permute-done((bf16[512,128]{1,0:T(8,128)(2,1)S(1)}, bf16[512,128]{1,0:T(8,128)(2,1)S(1)}, u32[]{:S(2)}, u32[]{:S(2)}) %collective-permute-start.21) | collective-permute-done | bytes 131104 | tf_op jit(solution)/shard_map/ppermute | solution.py:468
  80.9 2.1 %collective-permute-start.26 = (bf16[512,128]{1,0:T(8,128)(2,1)S(1)}, bf16[512,128]{1,0:T(8,128)(2,1)S(1)}, u32[]{:S(2)}, u32[]{:S(2)}) collective-permute-start(bf16[512,128]{1,0:T(8,128)(2,1)S(1)} %get-tuple-element.100.refs_4_), channel_id=1, source_target_pairs={{0,12},{1,13},{2,14},{3,15},{4,0},{5,1},{6,2},{7,3},{8,4},{9,5},{1... | collective-permute-start | bytes 393224 | tf_op jit(solution)/shard_map/ppermute | solution.py:468
  83.0 1.1 collective-permute-done.25.refs_6_
  84.0 1.1 collective-permute-done.26.refs_7_
  85.6 3.0 %collective-permute-start.28 = (bf16[2048,128]{1,0:T(8,128)(2,1)S(1)}, bf16[2048,128]{1,0:T(8,128)(2,1)S(1)}, u32[]{:S(2)}, u32[]{:S(2)}) collective-permute-start(bf16[2048,128]{1,0:T(8,128)(2,1)S(1)} %get-tuple-element.102.refs_0_), channel_id=1, source_target_pairs={{0,12},{1,13},{2,14},{3,15},{4,0},{5,1},{6,2},{7,3},{8,4},{9,5},{1... | collective-permute-start | bytes 1572872 | tf_op jit(solution)/shard_map/ppermute | solution.py:468
  88.6 2.7 %collective-permute-start.30 = (bf16[2048,128]{1,0:T(8,128)(2,1)S(1)}, bf16[2048,128]{1,0:T(8,128)(2,1)S(1)}, u32[]{:S(2)}, u32[]{:S(2)}) collective-permute-start(bf16[2048,128]{1,0:T(8,128)(2,1)S(1)} %get-tuple-element.103.refs_3_), channel_id=1, source_target_pairs={{0,3},{1,0},{2,1},{3,2},{4,7},{5,4},{6,5},{7,6},{8,11},{9,8},{10,9... | collective-permute-start | bytes 1572872 | tf_op jit(solution)/shard_map/ppermute | solution.py:468
  91.3 6.6 %collective-permute-done.31 = f32[40,256]{1,0:T(8,128)S(1)} collective-permute-done((f32[40,256]{1,0:T(8,128)S(1)}, f32[40,256]{1,0:T(8,128)S(1)}, u32[]{:S(2)}, u32[]{:S(2)}) %collective-permute-start.31) | collective-permute-done | bytes 40992 | tf_op jit(solution)/shard_map/ppermute | solution.py:480
  97.9 4.1 %collective-permute-start.32 = (f32[40,256]{1,0:T(8,128)S(1)}, f32[40,256]{1,0:T(8,128)S(1)}, u32[]{:S(2)}, u32[]{:S(2)}) collective-permute-start(f32[40,256]{1,0:T(8,128)S(1)} %add.12), channel_id=1, source_target_pairs={{0,8},{1,9},{2,10},{3,11},{4,12},{5,13},{6,14},{7,15},{8,0},{9,1},... | collective-permute-start | bytes 122888 | tf_op jit(solution)/shard_map/ppermute | solution.py:480
  102.0 1.4 collective-permute-done.32
  103.8 2.5 %collective-permute-start.34 = (bf16[1024,128]{1,0:T(8,128)(2,1)S(1)}, bf16[1024,128]{1,0:T(8,128)(2,1)S(1)}, u32[]{:S(2)}, u32[]{:S(2)}) collective-permute-start(bf16[1024,128]{1,0:T(8,128)(2,1)S(1)} %get-tuple-element.110), channel_id=1, source_target_pairs={{0,12},{1,13},{2,14},{3,15},{4,0},{5,1},{6,2},{7,3},{8,4},{9,5},{1... | collective-permute-start | bytes 786440 | tf_op jit(solution)/shard_map/ppermute | solution.py:468
  106.3 2.7 %collective-permute-start.36 = (bf16[1024,128]{1,0:T(8,128)(2,1)S(1)}, bf16[1024,128]{1,0:T(8,128)(2,1)S(1)}, u32[]{:S(2)}, u32[]{:S(2)}) collective-permute-start(bf16[1024,128]{1,0:T(8,128)(2,1)S(1)} %get-tuple-element.112), channel_id=1, source_target_pairs={{0,3},{1,0},{2,1},{3,2},{4,7},{5,4},{6,5},{7,6},{8,11},{9,8},{10,9... | collective-permute-start | bytes 786440 | tf_op jit(solution)/shard_map/ppermute | solution.py:468
  109.0 3.0 %collective-permute-done.37 = f32[40,256]{1,0:T(8,128)S(1)} collective-permute-done((f32[40,256]{1,0:T(8,128)S(1)}, f32[40,256]{1,0:T(8,128)S(1)}, u32[]{:S(2)}, u32[]{:S(2)}) %collective-permute-start.37) | collective-permute-done | bytes 40992 | tf_op jit(solution)/shard_map/ppermute | solution.py:480
  111.9 2.7 %collective-permute-start.38 = (f32[40,256]{1,0:T(8,128)S(1)}, f32[40,256]{1,0:T(8,128)S(1)}, u32[]{:S(2)}, u32[]{:S(2)}) collective-permute-start(f32[40,256]{1,0:T(8,128)S(1)} %add.14), channel_id=1, source_target_pairs={{0,2},{1,3},{2,0},{3,1},{4,6},{5,7},{6,4},{7,5},{8,10},{9,11},{10,... | collective-permute-start | bytes 122888 | tf_op jit(solution)/shard_map/ppermute | solution.py:480
  114.6 2.2 %copy-done.1 = bf16[128,128,128]{2,1,0:T(8,128)(2,1)S(1)} copy-done((bf16[128,128,128]{2,1,0:T(8,128)(2,1)S(1)}, bf16[128,128,128]{2,1,0:T(8,128)(2,1)}, u32[]{:S(2)}) %copy-start.1) | copy-done | bytes 4194328
  116.8 3.0 %backward_early.1.start = f32[4096,256]{1,0:T(8,128)S(1)} custom-call(s32[1,128]{1,0:T(1,128)S(1)} %get-tuple-element.66.rows, s32[1,128]{1,0:T(1,128)S(1)} %get-tuple-element.67.cols, bf16[128,128,128]{2,1,0:T(8,128)(2,1)S(1)} %copy-done.1, bf16[2048,128]{1,0:T(8,128)(2,1)S(1)} %get-tuple-element.102.refs_0_, ...), custom_call_target="tpu_custom_call" | custom-call | flops 805306368 | bytes 10485760 | tf_op jit(solution)/shard_map/backward_early/pallas_call | solution.py:390
  119.9 2.0 %backward_late.1 = (bf16[2048,256]{1,0:T(8,128)(2,1)S(1)}, bf16[2048,256]{1,0:T(8,128)(2,1)S(1)}) custom-call(s32[1,128]{1,0:T(1,128)S(1)} %get-tuple-element.66.rows, s32[1,128]{1,0:T(1,128)S(1)} %get-tuple-element.67.cols, bf16[128,128,128]{2,1,0:T(8,128)(2,1)S(1)} %copy-done.2, f32[4096,256]{1,0:T(8,128)S(1)} %backward_early.1.start, ...), custom_call_target="tpu_custom_call" | custom-call | flops 268435456 | bytes 8388608 | tf_op jit(solution)/shard_map/backward_late/pallas_call | solution.py:429
  121.9 6.5 %collective-permute-start.39 = (bf16[2048,256]{1,0:T(8,128)(2,1)S(1)}, bf16[2048,256]{1,0:T(8,128)(2,1)S(1)}, u32[]{:S(2)}, u32[]{:S(2)}) collective-permute-start(bf16[2048,256]{1,0:T(8,128)(2,1)S(1)} %get-tuple-element.119), channel_id=1, source_target_pairs={{0,16},{16,0},{32,48},{48,32},{64,80},{80,64},{96,112},{112,96},{1... | collective-permute-start | bytes 3145736 | tf_op jit(solution)/shard_map/ppermute | solution.py:475
  128.4 1.8 %collective-permute-start.45 = (f32[40,256]{1,0:T(8,128)S(1)}, f32[40,256]{1,0:T(8,128)S(1)}, u32[]{:S(2)}, u32[]{:S(2)}) collective-permute-start(f32[40,256]{1,0:T(8,128)S(1)} %add.15), channel_id=1, source_target_pairs={{0,96},{16,112},{32,0},{48,16},{64,32},{80,48},{96,64},{112,80},{1... | collective-permute-start | bytes 122888 | tf_op jit(solution)/shard_map/ppermute | solution.py:475
  130.3 0.6 collective-permute-start.44
  130.9 0.6 collective-permute-start.43
  131.7 1.6 %collective-permute-start.40 = (bf16[512,256]{1,0:T(8,128)(2,1)S(1)}, bf16[512,256]{1,0:T(8,128)(2,1)S(1)}, u32[]{:S(2)}, u32[]{:S(2)}) collective-permute-start(bf16[512,256]{1,0:T(8,128)(2,1)S(1)} %get-tuple-element.121), channel_id=1, source_target_pairs={{0,32},{16,48},{32,64},{48,80},{64,96},{80,112},{96,0},{112,16},{1... | collective-permute-start | bytes 786440 | tf_op jit(solution)/shard_map/ppermute | solution.py:475
  133.2 1.8 %collective-permute-start.41 = (bf16[512,256]{1,0:T(8,128)(2,1)S(1)}, bf16[512,256]{1,0:T(8,128)(2,1)S(1)}, u32[]{:S(2)}, u32[]{:S(2)}) collective-permute-start(bf16[512,256]{1,0:T(8,128)(2,1)S(1)} %get-tuple-element.122), channel_id=1, source_target_pairs={{0,64},{16,80},{32,96},{48,112},{64,0},{80,16},{96,32},{112,48},{1... | collective-permute-start | bytes 786440 | tf_op jit(solution)/shard_map/ppermute | solution.py:475
  135.0 0.8 collective-permute-start.42
  135.9 1.8 %collective-permute-start.46 = (f32[4,40,256]{2,1,0:T(8,128)S(1)}, f32[4,40,256]{2,1,0:T(8,128)S(1)}, u32[]{:S(2)}, u32[]{:S(2)}) collective-permute-start(f32[4,40,256]{2,1,0:T(8,128)S(1)} %pad_maximum_fusion.refs_4_), channel_id=1, source_target_pairs={{0,16},{16,0},{32,48},{48,32},{64,80},{80,64},{96,112},{112,96},{1... | collective-permute-start | bytes 491528 | tf_op jit(solution)/shard_map/ppermute | solution.py:475
  137.7 1.0 collective-permute-done.46.refs_5_
  138.8 2.8 %collective-permute-done.40.refs_1_ = bf16[512,256]{1,0:T(8,128)(2,1)S(1)} collective-permute-done((bf16[512,256]{1,0:T(8,128)(2,1)S(1)}, bf16[512,256]{1,0:T(8,128)(2,1)S(1)}, u32[]{:S(2)}, u32[]{:S(2)}) %collective-permute-start.40) | collective-permute-done | bytes 262176 | tf_op jit(solution)/shard_map/ppermute | solution.py:475
  141.6 4.5 %collective-permute-done.41.refs_2_ = bf16[512,256]{1,0:T(8,128)(2,1)S(1)} collective-permute-done((bf16[512,256]{1,0:T(8,128)(2,1)S(1)}, bf16[512,256]{1,0:T(8,128)(2,1)S(1)}, u32[]{:S(2)}, u32[]{:S(2)}) %collective-permute-start.41) | collective-permute-done | bytes 262176 | tf_op jit(solution)/shard_map/ppermute | solution.py:475
  146.4 1.0 last_sum.1
  (69 shorter events, 4.5 us)
Async XLA Ops:
  0.6 15.0 %collective-permute-start = (bf16[512,256]{1,0:T(8,128)(2,1)}, bf16[512,256]{1,0:T(8,128)(2,1)S(1)}, u32[]{:S(2)}, u32[]{:S(2)}) collective-permute-start(bf16[512,256]{1,0:T(8,128)(2,1)} %refs_0_.1), channel_id=1, source_target_pairs={{0,32},{16,48},{32,64},{48,80},{64,96},{80,112},{96,0},{112,16},{1... | collective-permute-start | bytes 786440 | tf_op jit(solution)/shard_map/ppermute | solution.py:475
  2.8 14.2 %collective-permute-start.1 = (bf16[512,256]{1,0:T(8,128)(2,1)}, bf16[512,256]{1,0:T(8,128)(2,1)S(1)}, u32[]{:S(2)}, u32[]{:S(2)}) collective-permute-start(bf16[512,256]{1,0:T(8,128)(2,1)} %refs_0_.1), channel_id=1, source_target_pairs={{0,64},{16,80},{32,96},{48,112},{64,0},{80,16},{96,32},{112,48},{1... | collective-permute-start | bytes 786440 | tf_op jit(solution)/shard_map/ppermute | solution.py:475
  5.4 13.1 %collective-permute-start.2 = (bf16[512,256]{1,0:T(8,128)(2,1)}, bf16[512,256]{1,0:T(8,128)(2,1)S(1)}, u32[]{:S(2)}, u32[]{:S(2)}) collective-permute-start(bf16[512,256]{1,0:T(8,128)(2,1)} %refs_0_.1), channel_id=1, source_target_pairs={{0,96},{16,112},{32,0},{48,16},{64,32},{80,48},{96,64},{112,80},{1... | collective-permute-start | bytes 786440 | tf_op jit(solution)/shard_map/ppermute | solution.py:475
  6.5 12.0 %collective-permute-start.3 = (bf16[512,256]{1,0:T(8,128)(2,1)}, bf16[512,256]{1,0:T(8,128)(2,1)S(1)}, u32[]{:S(2)}, u32[]{:S(2)}) collective-permute-start(bf16[512,256]{1,0:T(8,128)(2,1)} %refs_0_.1), channel_id=1, source_target_pairs={{0,16},{16,0},{32,48},{48,32},{64,80},{80,64},{96,112},{112,96},{1... | collective-permute-start | bytes 786440 | tf_op jit(solution)/shard_map/ppermute | solution.py:475
  8.0 2.2 %copy-start.3 = (bf16[1,1,128,128,128]{4,3,2,1,0:T(8,128)(2,1)S(1)}, bf16[1,1,128,128,128]{4,3,2,1,0:T(8,128)(2,1)}, u32[]{:S(2)}) copy-start(bf16[1,1,128,128,128]{4,3,2,1,0:T(8,128)(2,1)} %param.8) | copy-start | bytes 12582916
  10.2 0.9 copy-start.4
  11.2 0.9 copy-start.5
  12.1 0.9 copy-start.6
  13.0 0.7 copy-start.7
  13.7 0.7 copy-start.8
  14.4 0.7 copy-start.9
  15.6 16.4 %copy-start = (bf16[128,128,128]{2,1,0:T(8,128)(2,1)}, bf16[128,128,128]{2,1,0:T(8,128)(2,1)S(1)}, u32[]{:S(2)}) copy-start(bf16[128,128,128]{2,1,0:T(8,128)(2,1)S(1)} %get-tuple-element.68.values) | copy-start | bytes 12582916
  15.6 2.9 %collective-permute-start.4 = (bf16[512,256]{1,0:T(8,128)(2,1)S(1)}, bf16[512,256]{1,0:T(8,128)(2,1)S(1)}, u32[]{:S(2)}, u32[]{:S(2)}) collective-permute-start(bf16[512,256]{1,0:T(8,128)(2,1)S(1)} %collective-permute-done.refs_1_), channel_id=1, source_target_pairs={{0,16},{16,0},{32,48},{48,32},{64,80},{80,64},{96,112},{112,96},{1... | collective-permute-start | bytes 786440 | tf_op jit(solution)/shard_map/ppermute | solution.py:475
  17.0 2.7 %collective-permute-start.5 = (bf16[512,256]{1,0:T(8,128)(2,1)S(1)}, bf16[512,256]{1,0:T(8,128)(2,1)S(1)}, u32[]{:S(2)}, u32[]{:S(2)}) collective-permute-start(bf16[512,256]{1,0:T(8,128)(2,1)S(1)} %collective-permute-done.1.refs_2_), channel_id=1, source_target_pairs={{0,16},{16,0},{32,48},{48,32},{64,80},{80,64},{96,112},{112,96},{1... | collective-permute-start | bytes 786440 | tf_op jit(solution)/shard_map/ppermute | solution.py:475
  18.5 1.5 %collective-permute-start.6 = (bf16[512,256]{1,0:T(8,128)(2,1)S(1)}, bf16[512,256]{1,0:T(8,128)(2,1)S(1)}, u32[]{:S(2)}, u32[]{:S(2)}) collective-permute-start(bf16[512,256]{1,0:T(8,128)(2,1)S(1)} %collective-permute-done.2.refs_3_), channel_id=1, source_target_pairs={{0,16},{16,0},{32,48},{48,32},{64,80},{80,64},{96,112},{112,96},{1... | collective-permute-start | bytes 786440 | tf_op jit(solution)/shard_map/ppermute | solution.py:475
  22.0 9.9 %collective-permute-start.7 = (bf16[1024,128]{1,0:T(8,128)(2,1)S(1)}, bf16[1024,128]{1,0:T(8,128)(2,1)S(1)}, u32[]{:S(2)}, u32[]{:S(2)}) collective-permute-start(bf16[1024,128]{1,0:T(8,128)(2,1)S(1)} %get-tuple-element.78), channel_id=1, source_target_pairs={{0,4},{1,5},{2,6},{3,7},{4,8},{5,9},{6,10},{7,11},{8,12},{9,13},{1... | collective-permute-start | bytes 786440 | tf_op jit(solution)/shard_map/ppermute | solution.py:468
  23.3 8.7 %collective-permute-start.8 = (bf16[1024,128]{1,0:T(8,128)(2,1)S(1)}, bf16[1024,128]{1,0:T(8,128)(2,1)S(1)}, u32[]{:S(2)}, u32[]{:S(2)}) collective-permute-start(bf16[1024,128]{1,0:T(8,128)(2,1)S(1)} %get-tuple-element.79), channel_id=1, source_target_pairs={{0,12},{1,13},{2,14},{3,15},{4,0},{5,1},{6,2},{7,3},{8,4},{9,5},{1... | collective-permute-start | bytes 786440 | tf_op jit(solution)/shard_map/ppermute | solution.py:468
  24.8 9.5 %collective-permute-start.9 = (bf16[1024,128]{1,0:T(8,128)(2,1)S(1)}, bf16[1024,128]{1,0:T(8,128)(2,1)S(1)}, u32[]{:S(2)}, u32[]{:S(2)}) collective-permute-start(bf16[1024,128]{1,0:T(8,128)(2,1)S(1)} %get-tuple-element.80), channel_id=1, source_target_pairs={{0,1},{1,2},{2,3},{3,0},{4,5},{5,6},{6,7},{7,4},{8,9},{9,10},{10,1... | collective-permute-start | bytes 786440 | tf_op jit(solution)/shard_map/ppermute | solution.py:468
  26.4 7.9 %collective-permute-start.10 = (bf16[1024,128]{1,0:T(8,128)(2,1)S(1)}, bf16[1024,128]{1,0:T(8,128)(2,1)S(1)}, u32[]{:S(2)}, u32[]{:S(2)}) collective-permute-start(bf16[1024,128]{1,0:T(8,128)(2,1)S(1)} %get-tuple-element.81), channel_id=1, source_target_pairs={{0,3},{1,0},{2,1},{3,2},{4,7},{5,4},{6,5},{7,6},{8,11},{9,8},{10,9... | collective-permute-start | bytes 786440 | tf_op jit(solution)/shard_map/ppermute | solution.py:468
  34.5 13.2 %collective-permute-start.11 = (bf16[2048,128]{1,0:T(8,128)(2,1)S(1)}, bf16[2048,128]{1,0:T(8,128)(2,1)S(1)}, u32[]{:S(2)}, u32[]{:S(2)}) collective-permute-start(bf16[2048,128]{1,0:T(8,128)(2,1)S(1)} %get-tuple-element.82), channel_id=1, source_target_pairs={{0,4},{1,5},{2,6},{3,7},{4,8},{5,9},{6,10},{7,11},{8,12},{9,13},{1... | collective-permute-start | bytes 1572872 | tf_op jit(solution)/shard_map/ppermute | solution.py:468
  34.6 13.1 %collective-permute-start.12 = (bf16[2048,128]{1,0:T(8,128)(2,1)S(1)}, bf16[2048,128]{1,0:T(8,128)(2,1)S(1)}, u32[]{:S(2)}, u32[]{:S(2)}) collective-permute-start(bf16[2048,128]{1,0:T(8,128)(2,1)S(1)} %get-tuple-element.83), channel_id=1, source_target_pairs={{0,12},{1,13},{2,14},{3,15},{4,0},{5,1},{6,2},{7,3},{8,4},{9,5},{1... | collective-permute-start | bytes 1572872 | tf_op jit(solution)/shard_map/ppermute | solution.py:468
  37.3 12.5 %collective-permute-start.13 = (bf16[2048,128]{1,0:T(8,128)(2,1)S(1)}, bf16[2048,128]{1,0:T(8,128)(2,1)S(1)}, u32[]{:S(2)}, u32[]{:S(2)}) collective-permute-start(bf16[2048,128]{1,0:T(8,128)(2,1)S(1)} %get-tuple-element.85), channel_id=1, source_target_pairs={{0,1},{1,2},{2,3},{3,0},{4,5},{5,6},{6,7},{7,4},{8,9},{9,10},{10,1... | collective-permute-start | bytes 1572872 | tf_op jit(solution)/shard_map/ppermute | solution.py:468
  37.6 12.2 %collective-permute-start.14 = (bf16[2048,128]{1,0:T(8,128)(2,1)S(1)}, bf16[2048,128]{1,0:T(8,128)(2,1)S(1)}, u32[]{:S(2)}, u32[]{:S(2)}) collective-permute-start(bf16[2048,128]{1,0:T(8,128)(2,1)S(1)} %get-tuple-element.86), channel_id=1, source_target_pairs={{0,3},{1,0},{2,1},{3,2},{4,7},{5,4},{6,5},{7,6},{8,11},{9,8},{10,9... | collective-permute-start | bytes 1572872 | tf_op jit(solution)/shard_map/ppermute | solution.py:468
  50.2 5.1 %collective-permute-start.15 = (bf16[512,128]{1,0:T(8,128)(2,1)S(1)}, bf16[512,128]{1,0:T(8,128)(2,1)S(1)}, u32[]{:S(2)}, u32[]{:S(2)}) collective-permute-start(bf16[512,128]{1,0:T(8,128)(2,1)S(1)} %get-tuple-element.88), channel_id=1, source_target_pairs={{0,1},{1,2},{2,3},{3,0},{4,5},{5,6},{6,7},{7,4},{8,9},{9,10},{10,1... | collective-permute-start | bytes 393224 | tf_op jit(solution)/shard_map/ppermute | solution.py:468
  50.3 7.3 %collective-permute-start.16 = (bf16[512,128]{1,0:T(8,128)(2,1)S(1)}, bf16[512,128]{1,0:T(8,128)(2,1)S(1)}, u32[]{:S(2)}, u32[]{:S(2)}) collective-permute-start(bf16[512,128]{1,0:T(8,128)(2,1)S(1)} %get-tuple-element.89), channel_id=1, source_target_pairs={{0,2},{1,3},{2,0},{3,1},{4,6},{5,7},{6,4},{7,5},{8,10},{9,11},{10,... | collective-permute-start | bytes 393224 | tf_op jit(solution)/shard_map/ppermute | solution.py:468
  53.9 4.1 %collective-permute-start.17 = (bf16[512,128]{1,0:T(8,128)(2,1)S(1)}, bf16[512,128]{1,0:T(8,128)(2,1)S(1)}, u32[]{:S(2)}, u32[]{:S(2)}) collective-permute-start(bf16[512,128]{1,0:T(8,128)(2,1)S(1)} %get-tuple-element.90), channel_id=1, source_target_pairs={{0,3},{1,0},{2,1},{3,2},{4,7},{5,4},{6,5},{7,6},{8,11},{9,8},{10,9... | collective-permute-start | bytes 393224 | tf_op jit(solution)/shard_map/ppermute | solution.py:468
  54.1 6.7 %collective-permute-start.18 = (bf16[512,128]{1,0:T(8,128)(2,1)S(1)}, bf16[512,128]{1,0:T(8,128)(2,1)S(1)}, u32[]{:S(2)}, u32[]{:S(2)}) collective-permute-start(bf16[512,128]{1,0:T(8,128)(2,1)S(1)} %get-tuple-element.92), channel_id=1, source_target_pairs={{0,4},{1,5},{2,6},{3,7},{4,8},{5,9},{6,10},{7,11},{8,12},{9,13},{1... | collective-permute-start | bytes 393224 | tf_op jit(solution)/shard_map/ppermute | solution.py:468
  54.1 6.7 %collective-permute-start.19 = (bf16[512,128]{1,0:T(8,128)(2,1)S(1)}, bf16[512,128]{1,0:T(8,128)(2,1)S(1)}, u32[]{:S(2)}, u32[]{:S(2)}) collective-permute-start(bf16[512,128]{1,0:T(8,128)(2,1)S(1)} %get-tuple-element.93), channel_id=1, source_target_pairs={{0,8},{1,9},{2,10},{3,11},{4,12},{5,13},{6,14},{7,15},{8,0},{9,1},... | collective-permute-start | bytes 393224 | tf_op jit(solution)/shard_map/ppermute | solution.py:468
  55.3 6.1 %collective-permute-start.20 = (bf16[512,128]{1,0:T(8,128)(2,1)S(1)}, bf16[512,128]{1,0:T(8,128)(2,1)S(1)}, u32[]{:S(2)}, u32[]{:S(2)}) collective-permute-start(bf16[512,128]{1,0:T(8,128)(2,1)S(1)} %get-tuple-element.94), channel_id=1, source_target_pairs={{0,12},{1,13},{2,14},{3,15},{4,0},{5,1},{6,2},{7,3},{8,4},{9,5},{1... | collective-permute-start | bytes 393224 | tf_op jit(solution)/shard_map/ppermute | solution.py:468
  62.7 22.4 %all-to-all-start = ((f32[8,40,256]{2,1,0:T(8,128)}), f32[8,40,256]{2,1,0:T(8,128)S(1)}, u32[]{:S(2)}, u32[]{:S(2)}) async-start(f32[8,40,256]{2,1,0:T(8,128)} %get-tuple-element.101), calls=%async_computation | async-start | bytes 655360 | tf_op jit(solution)/shard_map/all_to_all | solution.py:530
  71.8 9.1 %collective-permute-start.21 = (bf16[512,128]{1,0:T(8,128)(2,1)S(1)}, bf16[512,128]{1,0:T(8,128)(2,1)S(1)}, u32[]{:S(2)}, u32[]{:S(2)}) collective-permute-start(bf16[512,128]{1,0:T(8,128)(2,1)S(1)} %get-tuple-element.99.refs_0_), channel_id=1, source_target_pairs={{0,1},{1,2},{2,3},{3,0},{4,5},{5,6},{6,7},{7,4},{8,9},{9,10},{10,1... | collective-permute-start | bytes 393224 | tf_op jit(solution)/shard_map/ppermute | solution.py:468
  72.7 10.2 %collective-permute-start.22 = (bf16[512,128]{1,0:T(8,128)(2,1)S(1)}, bf16[512,128]{1,0:T(8,128)(2,1)S(1)}, u32[]{:S(2)}, u32[]{:S(2)}) collective-permute-start(bf16[512,128]{1,0:T(8,128)(2,1)S(1)} %get-tuple-element.99.refs_0_), channel_id=1, source_target_pairs={{0,2},{1,3},{2,0},{3,1},{4,6},{5,7},{6,4},{7,5},{8,10},{9,11},{10,... | collective-permute-start | bytes 393224 | tf_op jit(solution)/shard_map/ppermute | solution.py:468
  72.7 10.2 %collective-permute-start.23 = (bf16[512,128]{1,0:T(8,128)(2,1)S(1)}, bf16[512,128]{1,0:T(8,128)(2,1)S(1)}, u32[]{:S(2)}, u32[]{:S(2)}) collective-permute-start(bf16[512,128]{1,0:T(8,128)(2,1)S(1)} %get-tuple-element.99.refs_0_), channel_id=1, source_target_pairs={{0,3},{1,0},{2,1},{3,2},{4,7},{5,4},{6,5},{7,6},{8,11},{9,8},{10,9... | collective-permute-start | bytes 393224 | tf_op jit(solution)/shard_map/ppermute | solution.py:468
  75.1 7.8 %collective-permute-start.24 = (bf16[512,128]{1,0:T(8,128)(2,1)S(1)}, bf16[512,128]{1,0:T(8,128)(2,1)S(1)}, u32[]{:S(2)}, u32[]{:S(2)}) collective-permute-start(bf16[512,128]{1,0:T(8,128)(2,1)S(1)} %get-tuple-element.100.refs_4_), channel_id=1, source_target_pairs={{0,4},{1,5},{2,6},{3,7},{4,8},{5,9},{6,10},{7,11},{8,12},{9,13},{1... | collective-permute-start | bytes 393224 | tf_op jit(solution)/shard_map/ppermute | solution.py:468
  75.4 8.6 %collective-permute-start.25 = (bf16[512,128]{1,0:T(8,128)(2,1)S(1)}, bf16[512,128]{1,0:T(8,128)(2,1)S(1)}, u32[]{:S(2)}, u32[]{:S(2)}) collective-permute-start(bf16[512,128]{1,0:T(8,128)(2,1)S(1)} %get-tuple-element.100.refs_4_), channel_id=1, source_target_pairs={{0,8},{1,9},{2,10},{3,11},{4,12},{5,13},{6,14},{7,15},{8,0},{9,1},... | collective-permute-start | bytes 393224 | tf_op jit(solution)/shard_map/ppermute | solution.py:468
  80.9 4.2 %collective-permute-start.26 = (bf16[512,128]{1,0:T(8,128)(2,1)S(1)}, bf16[512,128]{1,0:T(8,128)(2,1)S(1)}, u32[]{:S(2)}, u32[]{:S(2)}) collective-permute-start(bf16[512,128]{1,0:T(8,128)(2,1)S(1)} %get-tuple-element.100.refs_4_), channel_id=1, source_target_pairs={{0,12},{1,13},{2,14},{3,15},{4,0},{5,1},{6,2},{7,3},{8,4},{9,5},{1... | collective-permute-start | bytes 393224 | tf_op jit(solution)/shard_map/ppermute | solution.py:468
  85.2 18.2 %collective-permute-start.27 = (bf16[2048,128]{1,0:T(8,128)(2,1)S(1)}, bf16[2048,128]{1,0:T(8,128)(2,1)S(1)}, u32[]{:S(2)}, u32[]{:S(2)}) collective-permute-start(bf16[2048,128]{1,0:T(8,128)(2,1)S(1)} %get-tuple-element.102.refs_0_), channel_id=1, source_target_pairs={{0,4},{1,5},{2,6},{3,7},{4,8},{5,9},{6,10},{7,11},{8,12},{9,13},{1... | collective-permute-start | bytes 1572872 | tf_op jit(solution)/shard_map/ppermute | solution.py:468
  85.6 17.8 %collective-permute-start.28 = (bf16[2048,128]{1,0:T(8,128)(2,1)S(1)}, bf16[2048,128]{1,0:T(8,128)(2,1)S(1)}, u32[]{:S(2)}, u32[]{:S(2)}) collective-permute-start(bf16[2048,128]{1,0:T(8,128)(2,1)S(1)} %get-tuple-element.102.refs_0_), channel_id=1, source_target_pairs={{0,12},{1,13},{2,14},{3,15},{4,0},{5,1},{6,2},{7,3},{8,4},{9,5},{1... | collective-permute-start | bytes 1572872 | tf_op jit(solution)/shard_map/ppermute | solution.py:468
  88.6 14.8 %collective-permute-start.29 = (bf16[2048,128]{1,0:T(8,128)(2,1)S(1)}, bf16[2048,128]{1,0:T(8,128)(2,1)S(1)}, u32[]{:S(2)}, u32[]{:S(2)}) collective-permute-start(bf16[2048,128]{1,0:T(8,128)(2,1)S(1)} %get-tuple-element.103.refs_3_), channel_id=1, source_target_pairs={{0,1},{1,2},{2,3},{3,0},{4,5},{5,6},{6,7},{7,4},{8,9},{9,10},{10,1... | collective-permute-start | bytes 1572872 | tf_op jit(solution)/shard_map/ppermute | solution.py:468
  88.6 14.8 %collective-permute-start.30 = (bf16[2048,128]{1,0:T(8,128)(2,1)S(1)}, bf16[2048,128]{1,0:T(8,128)(2,1)S(1)}, u32[]{:S(2)}, u32[]{:S(2)}) collective-permute-start(bf16[2048,128]{1,0:T(8,128)(2,1)S(1)} %get-tuple-element.103.refs_3_), channel_id=1, source_target_pairs={{0,3},{1,0},{2,1},{3,2},{4,7},{5,4},{6,5},{7,6},{8,11},{9,8},{10,9... | collective-permute-start | bytes 1572872 | tf_op jit(solution)/shard_map/ppermute | solution.py:468
  91.3 6.6 %collective-permute-start.31 = (f32[40,256]{1,0:T(8,128)S(1)}, f32[40,256]{1,0:T(8,128)S(1)}, u32[]{:S(2)}, u32[]{:S(2)}) collective-permute-start(f32[40,256]{1,0:T(8,128)S(1)} %get-tuple-element.104), channel_id=1, source_target_pairs={{0,4},{1,5},{2,6},{3,7},{4,0},{5,1},{6,2},{7,3},{8,12},{9,13},{10,... | collective-permute-start | bytes 122888 | tf_op jit(solution)/shard_map/ppermute | solution.py:480
  97.9 5.5 %collective-permute-start.32 = (f32[40,256]{1,0:T(8,128)S(1)}, f32[40,256]{1,0:T(8,128)S(1)}, u32[]{:S(2)}, u32[]{:S(2)}) collective-permute-start(f32[40,256]{1,0:T(8,128)S(1)} %add.12), channel_id=1, source_target_pairs={{0,8},{1,9},{2,10},{3,11},{4,12},{5,13},{6,14},{7,15},{8,0},{9,1},... | collective-permute-start | bytes 122888 | tf_op jit(solution)/shard_map/ppermute | solution.py:480
  103.5 16.4 %collective-permute-start.33 = (bf16[1024,128]{1,0:T(8,128)(2,1)S(1)}, bf16[1024,128]{1,0:T(8,128)(2,1)S(1)}, u32[]{:S(2)}, u32[]{:S(2)}) collective-permute-start(bf16[1024,128]{1,0:T(8,128)(2,1)S(1)} %get-tuple-element.109), channel_id=1, source_target_pairs={{0,4},{1,5},{2,6},{3,7},{4,8},{5,9},{6,10},{7,11},{8,12},{9,13},{1... | collective-permute-start | bytes 786440 | tf_op jit(solution)/shard_map/ppermute | solution.py:468
  103.8 16.1 %collective-permute-start.34 = (bf16[1024,128]{1,0:T(8,128)(2,1)S(1)}, bf16[1024,128]{1,0:T(8,128)(2,1)S(1)}, u32[]{:S(2)}, u32[]{:S(2)}) collective-permute-start(bf16[1024,128]{1,0:T(8,128)(2,1)S(1)} %get-tuple-element.110), channel_id=1, source_target_pairs={{0,12},{1,13},{2,14},{3,15},{4,0},{5,1},{6,2},{7,3},{8,4},{9,5},{1... | collective-permute-start | bytes 786440 | tf_op jit(solution)/shard_map/ppermute | solution.py:468
  106.3 13.6 %collective-permute-start.35 = (bf16[1024,128]{1,0:T(8,128)(2,1)S(1)}, bf16[1024,128]{1,0:T(8,128)(2,1)S(1)}, u32[]{:S(2)}, u32[]{:S(2)}) collective-permute-start(bf16[1024,128]{1,0:T(8,128)(2,1)S(1)} %get-tuple-element.111), channel_id=1, source_target_pairs={{0,1},{1,2},{2,3},{3,0},{4,5},{5,6},{6,7},{7,4},{8,9},{9,10},{10,1... | collective-permute-start | bytes 786440 | tf_op jit(solution)/shard_map/ppermute | solution.py:468
  106.3 13.7 %collective-permute-start.36 = (bf16[1024,128]{1,0:T(8,128)(2,1)S(1)}, bf16[1024,128]{1,0:T(8,128)(2,1)S(1)}, u32[]{:S(2)}, u32[]{:S(2)}) collective-permute-start(bf16[1024,128]{1,0:T(8,128)(2,1)S(1)} %get-tuple-element.112), channel_id=1, source_target_pairs={{0,3},{1,0},{2,1},{3,2},{4,7},{5,4},{6,5},{7,6},{8,11},{9,8},{10,9... | collective-permute-start | bytes 786440 | tf_op jit(solution)/shard_map/ppermute | solution.py:468
  108.9 3.0 %collective-permute-start.37 = (f32[40,256]{1,0:T(8,128)S(1)}, f32[40,256]{1,0:T(8,128)S(1)}, u32[]{:S(2)}, u32[]{:S(2)}) collective-permute-start(f32[40,256]{1,0:T(8,128)S(1)} %add.13), channel_id=1, source_target_pairs={{0,1},{1,0},{2,3},{3,2},{4,5},{5,4},{6,7},{7,6},{8,9},{9,8},{10,11... | collective-permute-start | bytes 122888 | tf_op jit(solution)/shard_map/ppermute | solution.py:480
  111.9 7.9 %collective-permute-start.38 = (f32[40,256]{1,0:T(8,128)S(1)}, f32[40,256]{1,0:T(8,128)S(1)}, u32[]{:S(2)}, u32[]{:S(2)}) collective-permute-start(f32[40,256]{1,0:T(8,128)S(1)} %add.14), channel_id=1, source_target_pairs={{0,2},{1,3},{2,0},{3,1},{4,6},{5,7},{6,4},{7,5},{8,10},{9,11},{10,... | collective-permute-start | bytes 122888 | tf_op jit(solution)/shard_map/ppermute | solution.py:480
  114.6 2.2 %copy-start.1 = (bf16[128,128,128]{2,1,0:T(8,128)(2,1)S(1)}, bf16[128,128,128]{2,1,0:T(8,128)(2,1)}, u32[]{:S(2)}) copy-start(bf16[128,128,128]{2,1,0:T(8,128)(2,1)} %copy-done) | copy-start | bytes 12582916
  116.8 3.1 %copy-start.2 = (bf16[128,128,128]{2,1,0:T(8,128)(2,1)S(1)}, bf16[128,128,128]{2,1,0:T(8,128)(2,1)}, u32[]{:S(2)}) copy-start(bf16[128,128,128]{2,1,0:T(8,128)(2,1)} %copy-done) | copy-start | bytes 12582916
  121.9 9.5 %collective-permute-start.39 = (bf16[2048,256]{1,0:T(8,128)(2,1)S(1)}, bf16[2048,256]{1,0:T(8,128)(2,1)S(1)}, u32[]{:S(2)}, u32[]{:S(2)}) collective-permute-start(bf16[2048,256]{1,0:T(8,128)(2,1)S(1)} %get-tuple-element.119), channel_id=1, source_target_pairs={{0,16},{16,0},{32,48},{48,32},{64,80},{80,64},{96,112},{112,96},{1... | collective-permute-start | bytes 3145736 | tf_op jit(solution)/shard_map/ppermute | solution.py:475
  128.4 6.6 %collective-permute-start.45 = (f32[40,256]{1,0:T(8,128)S(1)}, f32[40,256]{1,0:T(8,128)S(1)}, u32[]{:S(2)}, u32[]{:S(2)}) collective-permute-start(f32[40,256]{1,0:T(8,128)S(1)} %add.15), channel_id=1, source_target_pairs={{0,96},{16,112},{32,0},{48,16},{64,32},{80,48},{96,64},{112,80},{1... | collective-permute-start | bytes 122888 | tf_op jit(solution)/shard_map/ppermute | solution.py:475
  130.3 5.6 %collective-permute-start.44 = (f32[40,256]{1,0:T(8,128)S(1)}, f32[40,256]{1,0:T(8,128)S(1)}, u32[]{:S(2)}, u32[]{:S(2)}) collective-permute-start(f32[40,256]{1,0:T(8,128)S(1)} %add.15), channel_id=1, source_target_pairs={{0,64},{16,80},{32,96},{48,112},{64,0},{80,16},{96,32},{112,48},{1... | collective-permute-start | bytes 122888 | tf_op jit(solution)/shard_map/ppermute | solution.py:475
  130.9 5.0 %collective-permute-start.43 = (f32[40,256]{1,0:T(8,128)S(1)}, f32[40,256]{1,0:T(8,128)S(1)}, u32[]{:S(2)}, u32[]{:S(2)}) collective-permute-start(f32[40,256]{1,0:T(8,128)S(1)} %add.15), channel_id=1, source_target_pairs={{0,32},{16,48},{32,64},{48,80},{64,96},{80,112},{96,0},{112,16},{1... | collective-permute-start | bytes 122888 | tf_op jit(solution)/shard_map/ppermute | solution.py:475
  131.7 9.9 %collective-permute-start.40 = (bf16[512,256]{1,0:T(8,128)(2,1)S(1)}, bf16[512,256]{1,0:T(8,128)(2,1)S(1)}, u32[]{:S(2)}, u32[]{:S(2)}) collective-permute-start(bf16[512,256]{1,0:T(8,128)(2,1)S(1)} %get-tuple-element.121), channel_id=1, source_target_pairs={{0,32},{16,48},{32,64},{48,80},{64,96},{80,112},{96,0},{112,16},{1... | collective-permute-start | bytes 786440 | tf_op jit(solution)/shard_map/ppermute | solution.py:475
  133.2 12.9 %collective-permute-start.41 = (bf16[512,256]{1,0:T(8,128)(2,1)S(1)}, bf16[512,256]{1,0:T(8,128)(2,1)S(1)}, u32[]{:S(2)}, u32[]{:S(2)}) collective-permute-start(bf16[512,256]{1,0:T(8,128)(2,1)S(1)} %get-tuple-element.122), channel_id=1, source_target_pairs={{0,64},{16,80},{32,96},{48,112},{64,0},{80,16},{96,32},{112,48},{1... | collective-permute-start | bytes 786440 | tf_op jit(solution)/shard_map/ppermute | solution.py:475
  135.0 11.3 %collective-permute-start.42 = (bf16[512,256]{1,0:T(8,128)(2,1)S(1)}, bf16[512,256]{1,0:T(8,128)(2,1)S(1)}, u32[]{:S(2)}, u32[]{:S(2)}) collective-permute-start(bf16[512,256]{1,0:T(8,128)(2,1)S(1)} %get-tuple-element.123), channel_id=1, source_target_pairs={{0,96},{16,112},{32,0},{48,16},{64,32},{80,48},{96,64},{112,80},{1... | collective-permute-start | bytes 786440 | tf_op jit(solution)/shard_map/ppermute | solution.py:475
  135.9 2.9 %collective-permute-start.46 = (f32[4,40,256]{2,1,0:T(8,128)S(1)}, f32[4,40,256]{2,1,0:T(8,128)S(1)}, u32[]{:S(2)}, u32[]{:S(2)}) collective-permute-start(f32[4,40,256]{2,1,0:T(8,128)S(1)} %pad_maximum_fusion.refs_4_), channel_id=1, source_target_pairs={{0,16},{16,0},{32,48},{48,32},{64,80},{80,64},{96,112},{112,96},{1... | collective-permute-start | bytes 491528 | tf_op jit(solution)/shard_map/ppermute | solution.py:475

commit v3 on v2

--- a/solution.py
+++ b/solution.py
@@ -33,7 +33,17 @@
 def coords():
     row = lax.axis_index("row")
     col = lax.axis_index("col")
-    return col // 4, col % 4, row // 2, row % 2
+    y, c = row // 2, row % 2
+    x, z = col // 4, col % 4
+    return x + c * (z - x), z + c * (x - z), y, c
+
+
+def group_at(u, v, c):
+    return u * (4 - 3 * c) + v * (1 + 3 * c)
+
+
+def shard_ahead(y, c, d):
+    return ((y + 4 + (1 - 2 * c) * d) % 4) * 2 + c
 
 
 def prologue_kernel(*refs):
@@ -75,8 +85,8 @@
         )
 
 
-def target_group(x, z, p, r):
-    return ((x + p) % 4) * 4 + (z + r) % 4
+def target_group(u, v, c, p, r):
+    return group_at((u + p) % 4, (v + r) % 4, c)
 
 
 LOW, HIGH, ALL = slice(0, HALF), slice(HALF, F), slice(0, F)
@@ -88,11 +98,11 @@
     outs_a = refs[9:11]
     outs_b = refs[11:13]
     acc, sems = refs[13:]
-    x, z, y, c = coords()
+    u, v, y, c = coords()
     copies = []
     for n in range(8):
         dy, dc = n % 4, n // 4
-        shard = ((y + 4 - dy) % 4) * 2 + (c + dc) % 2
+        shard = shard_ahead(y, c, -dy) if dc == 0 else shard_ahead(y, 1 - c, -dy)
         copies.append(
             pltpu.make_async_copy(
                 pieces[n], panel.at[pl.ds(shard * ROWS, ROWS)], sems.at[n]
@@ -104,13 +114,13 @@
         copy.wait()
     for n in range(4):
         lanes = ALL if n == 2 else LOW
-        forward_group(rows, cols, values, panel, acc, target_group(x, z, 2, n), lanes)
+        forward_group(rows, cols, values, panel, acc, target_group(u, v, c, 2, n), lanes)
         here = pl.ds((n % 2) * ROWS, ROWS)
         outs_a[n // 2][here, :] = acc[:, LOW].astype(BF)
         if n == 2:
             outs_b[n // 2][here, :] = acc[:, HIGH].astype(BF)
     for n in (0, 1, 3):
-        forward_group(rows, cols, values, panel, acc, target_group(x, z, n, 2), HIGH)
+        forward_group(rows, cols, values, panel, acc, target_group(u, v, c, n, 2), HIGH)
         here = pl.ds((n % 2) * ROWS, ROWS)
         outs_b[n // 2][here, :] = acc[:, HIGH].astype(BF)
 
@@ -135,13 +145,13 @@
     outs_a = (refs[0], refs[1], None, refs[2])
     outs_b = (refs[3], refs[4], None, refs[5])
     acc = refs[6]
-    x, z, y, c = coords()
+    u, v, y, c = coords()
     for p in (1, 3, 0, 2):
         for r in (1, 3, 0, 2):
             if p == 2 and r == 2:
                 continue
             lanes = HIGH if p == 2 else LOW if r == 2 else ALL
-            forward_group(rows, cols, values, panel, acc, target_group(x, z, p, r), lanes)
+            forward_group(rows, cols, values, panel, acc, target_group(u, v, c, p, r), lanes)
             if p != 2:
                 outs_a[p][r * ROWS:(r + 1) * ROWS, :] = acc[:, LOW].astype(BF)
             if r != 2:
@@ -220,7 +230,8 @@
     parts_a = refs[:4]
     parts_b = refs[4:8]
     weight, bias, cotangent = refs[8:11]
-    out_act, grad_a, grad_b, gradients = refs[11:]
+    out_act, grad_a, grad_b, keep, give, full = refs[11:]
+    u, v, y, c = coords()
 
     aggregated = jnp.concatenate(
         [quad(parts_a).astype(BF), quad(parts_b).astype(BF)], axis=1
@@ -236,13 +247,13 @@
     ).astype(BF)
     grad_a[...] = grad_agg[:, :HALF]
     grad_b[...] = grad_agg[:, HALF:]
-    weight_grad = lax.dot_general(
+    full[...] = lax.dot_general(
         aggregated, grad_pre, (((0,), (0,)), ((), ())), preferred_element_type=F32
     ) * scale
     bias_grad = jnp.sum(grad_pre.astype(F32), axis=0, keepdims=True) * scale
-    for n in range(8):
-        gradients[n, :32, :] = weight_grad[n * 32:(n + 1) * 32, :]
-        gradients[n, 32:, :] = jnp.broadcast_to(bias_grad, (8, F))
+    for out, core in ((keep, c), (give, 1 - c)):
+        out[:HALF, :] = full[pl.ds(pl.multiple_of(core * HALF, HALF), HALF), :]
+        out[HALF:, :] = jnp.broadcast_to(bias_grad, (8, F))
 
 
 def point_call(parts_a, parts_b, weight, bias, cotangent, scale):
@@ -253,10 +264,12 @@
             jax.ShapeDtypeStruct((ROWS, F), BF),
             half,
             half,
-            jax.ShapeDtypeStruct((8, 40, F), F32),
+            jax.ShapeDtypeStruct((HALF + 8, F), F32),
+            jax.ShapeDtypeStruct((HALF + 8, F), F32),
         ],
         in_specs=[vmem()] * 11,
-        out_specs=[vmem()] * 4,
+        out_specs=[vmem()] * 5,
+        scratch_shapes=[pltpu.VMEM((F, F), F32)],
         compiler_params=pltpu.CompilerParams(vmem_limit_bytes=24 * MIB),
         cost_estimate=pl.CostEstimate(
             flops=3 * 2 * ROWS * F * F, bytes_accessed=2 * MIB, transcendentals=ROWS * F
@@ -266,27 +279,26 @@
 
 
 def join_kernel(*refs):
-    spread = refs[8]
-    outs = refs[9:11]
+    outs = refs[10:12]
     for half in range(2):
         for n in range(4):
             outs[half][n * ROWS:(n + 1) * ROWS, :] = refs[4 * half + n][...]
-    refs[11][...] = jnp.sum(spread[...], axis=0)
-
-
-def join_call(parts_a, parts_b, spread):
+    refs[12][...] = refs[8][...] + refs[9][...]
+
+
+def join_call(parts_a, parts_b, keep, got):
     return pl.pallas_call(
         join_kernel,
         out_shape=[jax.ShapeDtypeStruct((4 * ROWS, HALF), BF)] * 2
-        + [jax.ShapeDtypeStruct((40, F), F32)],
-        in_specs=[vmem()] * 9,
+        + [jax.ShapeDtypeStruct(keep.shape, F32)],
+        in_specs=[vmem()] * 10,
         out_specs=[vmem()] * 3,
-        compiler_params=pltpu.CompilerParams(vmem_limit_bytes=24 * MIB),
-        cost_estimate=pl.CostEstimate(
-            flops=320 * F, bytes_accessed=3 * MIB, transcendentals=0
+        compiler_params=pltpu.CompilerParams(vmem_limit_bytes=8 * MIB),
+        cost_estimate=pl.CostEstimate(
+            flops=136 * F, bytes_accessed=3 * MIB, transcendentals=0
         ),
         name="join",
-    )(*parts_a, *parts_b, spread)
+    )(*parts_a, *parts_b, keep, got)
 
 
 def cut_kernel(*refs):
@@ -310,18 +322,15 @@
 
 def last_kernel(*refs):
     mine, theirs, x_grad, weight_grad, bias_grad = refs[4:]
-    x, z, y, c = coords()
+    u, v, y, c = coords()
     x_grad[...] = quad(refs[:4]).astype(BF)
-    for dy in range(4):
-        base = ((y + 4 - dy) % 4) * 2
-        for source, core in ((mine, c), (theirs, 1 - c)):
-            shard = base + core
-            here = pl.ds(pl.multiple_of(shard * 32, 32), 32)
-            weight_grad[here, :] = source[dy, :32, :]
-
-            @pl.when(shard == 0)
-            def _():
-                bias_grad[...] = source[dy, 32:33, :]
+    for source, core in ((mine, c), (theirs, 1 - c)):
+        here = pl.ds(pl.multiple_of(core * HALF, HALF), HALF)
+        weight_grad[here, :] = source[:HALF, :]
+
+        @pl.when(core == 0)
+        def _(source=source):
+            bias_grad[...] = source[HALF:HALF + 1, :]
 
 
 def last_call(parts, mine, theirs):
@@ -334,7 +343,7 @@
         ],
         in_specs=[vmem()] * 6,
         out_specs=[vmem()] * 3,
-        compiler_params=pltpu.CompilerParams(vmem_limit_bytes=24 * MIB),
+        compiler_params=pltpu.CompilerParams(vmem_limit_bytes=8 * MIB),
         cost_estimate=pl.CostEstimate(
             flops=4 * ROWS * F, bytes_accessed=10 * ROWS * F, transcendentals=0
         ),
@@ -354,8 +363,8 @@
         )
 
 
-def source_group(x, z, p, r):
-    return ((x + 4 - p) % 4) * 4 + (z + 4 - r) % 4
+def source_group(u, v, c, p, r):
+    return group_at((u + 4 - p) % 4, (v + 4 - r) % 4, c)
 
 
 def block_at(base, local):
@@ -366,7 +375,7 @@
     parts_a = (refs[0], refs[1], None, refs[2])
     parts_b = (refs[3], refs[4], None, refs[5])
     acc = refs[6]
-    x, z, y, c = coords()
+    u, v, y, c = coords()
     acc[...] = jnp.zeros_like(acc)
     for p in range(4):
         for r in range(4):
@@ -383,7 +392,7 @@
                 return jnp.concatenate([from_a(local), from_b(local)], axis=1)
 
             lanes, read = (HIGH, from_b) if p == 2 else (LOW, from_a) if r == 2 else (ALL, both)
-            backward_slots(rows, cols, values, acc, source_group(x, z, p, r), lanes, read)
+            backward_slots(rows, cols, values, acc, source_group(u, v, c, p, r), lanes, read)
 
 
 def early_call(rows, cols, values, parts_a, parts_b):
@@ -404,7 +413,7 @@
     parts_a = refs[:2]
     parts_b = refs[2:4]
     mine, other, acc = refs[4:]
-    x, z, y, c = coords()
+    u, v, y, c = coords()
     acc[...] = start[...]
     for n in range(4):
 
@@ -414,12 +423,11 @@
         def from_b(local, n=n):
             return parts_b[n // 2][block_at((n % 2) * ROWS, local), :]
 
-        backward_slots(rows, cols, values, acc, source_group(x, z, 2, n), LOW, from_a)
-        backward_slots(rows, cols, values, acc, source_group(x, z, n, 2), HIGH, from_b)
+        backward_slots(rows, cols, values, acc, source_group(u, v, c, 2, n), LOW, from_a)
+        backward_slots(rows, cols, values, acc, source_group(u, v, c, n, 2), HIGH, from_b)
     for dy in range(4):
-        base = ((y + dy) % 4) * 2
-        own = pl.ds(pl.multiple_of((base + c) * ROWS, ROWS), ROWS)
-        peer = pl.ds(pl.multiple_of((base + 1 - c) * ROWS, ROWS), ROWS)
+        own = pl.ds(pl.multiple_of(shard_ahead(y, c, dy) * ROWS, ROWS), ROWS)
+        peer = pl.ds(pl.multiple_of(shard_ahead(y, 1 - c, dy) * ROWS, ROWS), ROWS)
         mine[dy * ROWS:(dy + 1) * ROWS, :] = acc[own, :].astype(BF)
         other[dy * ROWS:(dy + 1) * ROWS, :] = acc[peer, :].astype(BF)
 
@@ -461,30 +469,52 @@
     )(mine, other)
 
 
-def along_col(value, dx, dz):
-    pairs = [
-        (a * 4 + b, ((a + dx) % 4) * 4 + (b + dz) % 4) for a in range(4) for b in range(4)
-    ]
-    return lax.ppermute(value, "col", pairs)
-
-
-def along_row(value, dy, dc):
-    pairs = [
-        (a * 2 + b, ((a + dy) % 4) * 2 + (b + dc) % 2) for a in range(4) for b in range(2)
-    ]
-    return lax.ppermute(value, "row", pairs)
-
-
-def partner_sum(value, dx, dz):
-    pairs = [(a * 4 + b, (a ^ dx) * 4 + (b ^ dz)) for a in range(4) for b in range(4)]
-    return value + lax.ppermute(value, "col", pairs)
+def permute(value, target):
+    pairs = []
+    for row in range(8):
+        for col in range(16):
+            y, c = row // 2, row % 2
+            x, z = col // 4, col % 4
+            u, v = (z, x) if c else (x, z)
+            u, v, y, c = target(u, v, y, c)
+            x, z = (v, u) if row % 2 else (u, v)
+            pairs.append((row * 16 + col, (y * 2 + c) * 16 + x * 4 + z))
+    return lax.ppermute(value, ("row", "col"), pairs)
+
+
+def along_u(value, d):
+    return permute(value, lambda u, v, y, c: ((u + d) % 4, v, y, c))
+
+
+def along_v(value, d):
+    return permute(value, lambda u, v, y, c: (u, (v + d) % 4, y, c))
+
+
+def along_y(value, d):
+    return permute(value, lambda u, v, y, c: (u, v, (y + (1 - 2 * c) * d) % 4, c))
+
+
+def to_peer(value):
+    return permute(value, lambda u, v, y, c: (u, v, y, 1 - c))
+
+
+def with_u(value, d):
+    return value + permute(value, lambda u, v, y, c: (u ^ d, v, y, c))
+
+
+def with_v(value, d):
+    return value + permute(value, lambda u, v, y, c: (u, v ^ d, y, c))
+
+
+def with_y(value, d):
+    return value + permute(value, lambda u, v, y, c: (u, v, y ^ d, c))
 
 
 def shards(x_feat, block_values, block_rows, block_cols, weight, bias, cotangent):
     scale = 1.0 / math.sqrt(65536)
 
-    near = {d: along_row(x_feat, d, 0) for d in (2, 1, 3)}
-    swap = [along_row(x_feat, 0, 1)] + [None] * 3
+    near = {d: along_y(x_feat, d) for d in (2, 1, 3)}
+    swap = [to_peer(x_feat)] + [None] * 3
     own, values, rows, cols, weight, bias, cotangent = prologue_call(
         [
             x_feat,
@@ -498,60 +528,62 @@
     )
     near[1], own = lax.optimization_barrier((near[1], own))
     for d in (1, 3, 2):
-        swap[d] = along_row(near[d], 0, 1)
+        swap[d] = to_peer(near[d])
     pieces = [own, near[1], near[2], near[3]] + swap
 
     panel, far_a1, far_a2, far_b1, far_b2 = far_call(rows, cols, values, pieces)
     extra = [
-        along_col(far_a1, 1, 0),
-        along_col(far_a2, 3, 0),
-        along_col(far_b1, 0, 1),
-        along_col(far_b2, 0, 3),
+        along_u(far_a1, 1),
+        along_u(far_a2, 3),
+        along_v(far_b1, 1),
+        along_v(far_b2, 3),
     ]
     a0, a1, a3, b0, b1, b3 = near_call(rows, cols, values, panel)
     a1, a3, b1, b3 = relay_call([a1, a3, b1, b3], extra)
     sums = stage_call(
-        [a0, along_col(a1, 1, 0), along_col(a3, 3, 0)],
-        [b0, along_col(b1, 0, 1), along_col(b3, 0, 3)],
+        [a0, along_u(a1, 1), along_u(a3, 3)],
+        [b0, along_v(b1, 1), along_v(b3, 3)],
     )
     sum_a, sum_b = sums[:4], sums[4:]
     part_a, part_b = [sum_a[0]] + [None] * 3, [sum_b[0]] + [None] * 3
     for d in (2, 1, 3):
-        part_a[d] = along_col(sum_a[d], 0, d)
-        part_b[d] = along_col(sum_b[d], d, 0)
-    out_act, grad_a, grad_b, gradients = point_call(
+        part_a[d] = along_v(sum_a[d], d)
+        part_b[d] = along_u(sum_b[d], d)
+    out_act, grad_a, grad_b, keep, give = point_call(
         part_a, part_b, weight, bias, cotangent, scale
     )
 
     first_a, first_b = [grad_a] + [None] * 3, [grad_b] + [None] * 3
     for d in (2, 1, 3):
-        first_a[d] = along_col(grad_a, 0, d)
-        first_b[d] = along_col(grad_b, d, 0)
-    spread = lax.all_to_all(gradients, "row", 0, 0)
-    join_a, join_b, piece = join_call(first_a, first_b, spread)
-    a1, a3 = along_col(join_a, 1, 0), along_col(join_a, 3, 0)
-    b1, b3 = along_col(join_b, 0, 1), along_col(join_b, 0, 3)
-    piece = partner_sum(partner_sum(piece, 1, 0), 2, 0)
+        first_a[d] = along_v(grad_a, d)
+        first_b[d] = along_u(grad_b, d)
+    join_a, join_b, piece = join_call(first_a, first_b, keep, to_peer(give))
+    a1, a3 = along_u(join_a, 1), along_u(join_a, 3)
+    b1, b3 = along_v(join_b, 1), along_v(join_b, 3)
+    piece = with_y(with_y(piece, 1), 2)
     a1, a3, b1, b3, piece = lax.optimization_barrier((a1, a3, b1, b3, piece))
     cut_a1, cut_a3, cut_b1, cut_b3 = cut_call([a1, a3, b1, b3])
     far = [
-        along_col(cut_a1, 1, 0),
-        along_col(cut_a3, 3, 0),
-        along_col(cut_b1, 0, 1),
-        along_col(cut_b3, 0, 3),
+        along_u(cut_a1, 1),
+        along_u(cut_a3, 3),
+        along_v(cut_b1, 1),
+        along_v(cut_b3, 3),
     ]
+    piece = with_u(piece, 1)
     start = early_call(rows, cols, values, [join_a, a1, a3], [join_b, b1, b3])
-    piece = partner_sum(partner_sum(piece, 0, 1), 0, 2)
-    *far, piece = lax.optimization_barrier((*far, piece))
+    piece, start = lax.optimization_barrier((piece, start))
+    piece = with_u(piece, 2)
     mine, other = late_call(rows, cols, values, start, far[:2], far[2:])
-    held = jnp.stack([piece] + [along_row(piece, d, 0) for d in (1, 2, 3)])
-    other = along_row(other, 0, 1)
+    piece, other = lax.optimization_barrier((piece, other))
+    other = to_peer(other)
+    piece = with_v(piece, 1)
+    other, piece = lax.optimization_barrier((other, piece))
     sums = pair_call(mine, other)
-    theirs = along_row(held, 0, 1)
     last = [sums[0]] + [None] * 3
     for d in (2, 1, 3):
-        last[d] = along_row(sums[d], d, 0)
-    x_grad, weight_grad, bias_grad = last_call(last, held, theirs)
+        last[d] = along_y(sums[d], d)
+    piece = with_v(piece, 2)
+    x_grad, weight_grad, bias_grad = last_call(last, piece, to_peer(piece))
     return (out_act, x_grad, weight_grad, bias_grad.reshape(F))
 
 

time: 148 us -> 142 us (0.959)
  starting transfers between devices: 79 us -> 69.3 us
  waiting for transfers between devices: 43.9 us -> 50.3 us
  local copies, waits for them, and re-layouts: 9.17 us -> 6.98 us
    all_to_all x1 -> x0, starting transfers between devices: 9.07 us -> none  [shards(): spread = lax.all_to_all(gradients, 'row', 0, 0)]
    ppermute x47, waiting for transfers between devices: 43.9 us -> 50.3 us  [permute(): return lax.ppermute(value, ('row', 'col'), pairs)]
    unnamed x20 -> x14, local copies, waits for them, and re-layouts: 9.17 us -> 6.98 us
  transfers between devices with their start and end apart: 48 -> 47, of which waited for: 20 -> 21; matrix products, arithmetic and copies ran while one was open for 0% -> 0% of each run, Pallas kernels for 5% -> 7%
where the time goes in v3:
time: 142 us
  starting transfers between devices  69.3 us (49%)
  waiting for transfers between devices  50.3 us (35%)
  Pallas kernels  14 us (10%)
  local copies, waits for them, and re-layouts  6.98 us (5%)
    ppermute x47, starting transfers between devices, permute(): return lax.ppermute(value, ('row', 'col'), pairs)  69.3 us
    ppermute x47, waiting for transfers between devices, permute(): return lax.ppermute(value, ('row', 'col'), pairs)  50.3 us
    unnamed x14, local copies, waits for them, and re-layouts  6.98 us
    pallas_call x1, Pallas kernels, near_call(): pl.pallas_call(near_kernel, out_shape=[part] * 6, in_specs=[smem(), smem(...  3.43 us
    pallas_call x1, Pallas kernels, early_call(): pl.pallas_call(early_kernel, out_shape=jax.ShapeDtypeStruct((8 * ROWS, F)...  3 us
  transfers between devices with their start and end apart: 47, of which 21 were waited for; matrix products, arithmetic and copies ran while one was open for 0% of the time, Pallas kernels for 7%

profile of v3, /device:TPU:1, one launch (start us, length us, event | category | flops | bytes accessed | tf_op | source)
XLA Modules:
  0.0 141.6 jit_solution(7236230097007857708)
XLA Ops:
  0.6 3.6 %collective-permute-start = (bf16[512,256]{1,0:T(8,128)(2,1)}, bf16[512,256]{1,0:T(8,128)(2,1)S(1)}, u32[]{:S(2)}, u32[]{:S(2)}) collective-permute-start(bf16[512,256]{1,0:T(8,128)(2,1)} %refs_0_.1), channel_id=1, source_target_pairs={{0,32},{1,33},{2,34},{3,35},{4,36},{5,37},{6,38},{7,39},{8,40},{9,... | collective-permute-start | bytes 786440 | tf_op jit(solution)/shard_map/ppermute | solution.py:482
  4.6 0.7 collective-permute-start.2
  5.3 2.7 %collective-permute-start.3 = (bf16[512,256]{1,0:T(8,128)(2,1)}, bf16[512,256]{1,0:T(8,128)(2,1)S(1)}, u32[]{:S(2)}, u32[]{:S(2)}) collective-permute-start(bf16[512,256]{1,0:T(8,128)(2,1)} %refs_0_.1), channel_id=1, source_target_pairs={{0,16},{1,17},{2,18},{3,19},{4,20},{5,21},{6,22},{7,23},{8,24},{9,... | collective-permute-start | bytes 786440 | tf_op jit(solution)/shard_map/ppermute | solution.py:482
  8.0 2.2 %copy-done = bf16[1,1,128,128,128]{4,3,2,1,0:T(8,128)(2,1)S(1)} copy-done((bf16[1,1,128,128,128]{4,3,2,1,0:T(8,128)(2,1)S(1)}, bf16[1,1,128,128,128]{4,3,2,1,0:T(8,128)(2,1)}, u32[]{:S(2)}) %copy-start) | copy-done | bytes 4194328
  10.2 0.9 copy-done.1
  11.2 0.9 copy-done.2
  12.1 0.9 copy-done.3
  13.0 0.7 copy-done.4
  13.7 0.7 copy-done.5
  14.4 0.7 copy-done.6
  15.0 0.6 prologue.1
  15.7 3.4 %collective-permute-start.5 = (bf16[512,256]{1,0:T(8,128)(2,1)S(1)}, bf16[512,256]{1,0:T(8,128)(2,1)S(1)}, u32[]{:S(2)}, u32[]{:S(2)}) collective-permute-start(bf16[512,256]{1,0:T(8,128)(2,1)S(1)} %collective-permute-done.1.refs_2_), channel_id=1, source_target_pairs={{0,16},{1,17},{2,18},{3,19},{4,20},{5,21},{6,22},{7,23},{8,24},{9,... | collective-permute-start | bytes 786440 | tf_op jit(solution)/shard_map/ppermute | solution.py:482
  19.1 1.1 collective-permute-done.5.refs_6_
  20.6 2.0 %forward_far.1 = (bf16[4096,256]{1,0:T(8,128)(2,1)S(1)}, bf16[1024,128]{1,0:T(8,128)(2,1)S(1)}, bf16[1024,128]{1,0:T(8,128)(2,1)S(1)}, bf16[1024,128]{1,0:T(8,128)(2,1)S(1)}, bf16[1024,128]{1,0:T(8,128)(2,1)S(1)}) custom-call(s32[1,128]{1,0:T(1,128)S(1)} %get-tuple-element.68.rows, s32[1,128]{1,0:T(1,128)S(1)} %get-tuple-element.69.cols, ...), custom_call_target="tpu_custom_call" | custom-call | flops 268435456 | bytes 7340032 | tf_op jit(solution)/shard_map/forward_far/pallas_call | solution.py:130
  22.6 1.7 %collective-permute-start.7 = (bf16[1024,128]{1,0:T(8,128)(2,1)S(1)}, bf16[1024,128]{1,0:T(8,128)(2,1)S(1)}, u32[]{:S(2)}, u32[]{:S(2)}) collective-permute-start(bf16[1024,128]{1,0:T(8,128)(2,1)S(1)} %get-tuple-element.80), channel_id=1, source_target_pairs={{0,4},{1,5},{2,6},{3,7},{4,8},{5,9},{6,10},{7,11},{8,12},{9,13},{1... | collective-permute-start | bytes 786440 | tf_op jit(solution)/shard_map/ppermute | solution.py:482
  24.3 2.2 %collective-permute-start.8 = (bf16[1024,128]{1,0:T(8,128)(2,1)S(1)}, bf16[1024,128]{1,0:T(8,128)(2,1)S(1)}, u32[]{:S(2)}, u32[]{:S(2)}) collective-permute-start(bf16[1024,128]{1,0:T(8,128)(2,1)S(1)} %get-tuple-element.81), channel_id=1, source_target_pairs={{0,12},{1,13},{2,14},{3,15},{4,0},{5,1},{6,2},{7,3},{8,4},{9,5},{1... | collective-permute-start | bytes 786440 | tf_op jit(solution)/shard_map/ppermute | solution.py:482
  26.5 1.2 collective-permute-start.9
  27.7 1.5 %collective-permute-start.10 = (bf16[1024,128]{1,0:T(8,128)(2,1)S(1)}, bf16[1024,128]{1,0:T(8,128)(2,1)S(1)}, u32[]{:S(2)}, u32[]{:S(2)}) collective-permute-start(bf16[1024,128]{1,0:T(8,128)(2,1)S(1)} %get-tuple-element.83), channel_id=1, source_target_pairs={{0,3},{1,0},{2,1},{3,2},{4,7},{5,4},{6,5},{7,6},{8,11},{9,8},{10,9... | collective-permute-start | bytes 786440 | tf_op jit(solution)/shard_map/ppermute | solution.py:482
  29.2 3.4 %forward_near.1 = (bf16[2048,128]{1,0:T(8,128)(2,1)S(1)}, bf16[2048,128]{1,0:T(8,128)(2,1)S(1)}, bf16[2048,128]{1,0:T(8,128)(2,1)S(1)}, bf16[2048,128]{1,0:T(8,1...) custom-call(s32[1,128]{1,0:T(1,128)S(1)} %get-tuple-element.68.rows, ...), custom_call_target="tpu_custom_call" | custom-call | flops 805306368 | bytes 9437184 | tf_op jit(solution)/shard_map/forward_near/pallas_call | solution.py:163
  32.6 0.6 collective-permute-done.9.refs_6_
  33.6 1.7 %collective-permute-start.11 = (bf16[2048,128]{1,0:T(8,128)(2,1)S(1)}, bf16[2048,128]{1,0:T(8,128)(2,1)S(1)}, u32[]{:S(2)}, u32[]{:S(2)}) collective-permute-start(bf16[2048,128]{1,0:T(8,128)(2,1)S(1)} %get-tuple-element.84), channel_id=1, source_target_pairs={{0,4},{1,5},{2,6},{3,7},{4,8},{5,9},{6,10},{7,11},{8,12},{9,13},{1... | collective-permute-start | bytes 1572872 | tf_op jit(solution)/shard_map/ppermute | solution.py:482
  35.3 2.2 %collective-permute-start.12 = (bf16[2048,128]{1,0:T(8,128)(2,1)S(1)}, bf16[2048,128]{1,0:T(8,128)(2,1)S(1)}, u32[]{:S(2)}, u32[]{:S(2)}) collective-permute-start(bf16[2048,128]{1,0:T(8,128)(2,1)S(1)} %get-tuple-element.85), channel_id=1, source_target_pairs={{0,12},{1,13},{2,14},{3,15},{4,0},{5,1},{6,2},{7,3},{8,4},{9,5},{1... | collective-permute-start | bytes 1572872 | tf_op jit(solution)/shard_map/ppermute | solution.py:482
  37.5 0.9 collective-permute-start.13
  38.4 1.7 %collective-permute-start.14 = (bf16[2048,128]{1,0:T(8,128)(2,1)S(1)}, bf16[2048,128]{1,0:T(8,128)(2,1)S(1)}, u32[]{:S(2)}, u32[]{:S(2)}) collective-permute-start(bf16[2048,128]{1,0:T(8,128)(2,1)S(1)} %get-tuple-element.88), channel_id=1, source_target_pairs={{0,3},{1,0},{2,1},{3,2},{4,7},{5,4},{6,5},{7,6},{8,11},{9,8},{10,9... | collective-permute-start | bytes 1572872 | tf_op jit(solution)/shard_map/ppermute | solution.py:482
  40.1 5.7 %collective-permute-done.11.refs_1_ = bf16[2048,128]{1,0:T(8,128)(2,1)S(1)} collective-permute-done((bf16[2048,128]{1,0:T(8,128)(2,1)S(1)}, bf16[2048,128]{1,0:T(8,128)(2,1)S(1)}, u32[]{:S(2)}, u32[]{:S(2)}) %collective-permute-start.11) | collective-permute-done | bytes 524320 | tf_op jit(solution)/shard_map/ppermute | solution.py:482
  45.8 4.4 %collective-permute-done.13.refs_4_ = bf16[2048,128]{1,0:T(8,128)(2,1)S(1)} collective-permute-done((bf16[2048,128]{1,0:T(8,128)(2,1)S(1)}, bf16[2048,128]{1,0:T(8,128)(2,1)S(1)}, u32[]{:S(2)}, u32[]{:S(2)}) %collective-permute-start.13) | collective-permute-done | bytes 524320 | tf_op jit(solution)/shard_map/ppermute | solution.py:482
  50.7 0.6 collective-permute-start.15
  51.3 3.6 %collective-permute-start.16 = (bf16[512,128]{1,0:T(8,128)(2,1)S(1)}, bf16[512,128]{1,0:T(8,128)(2,1)S(1)}, u32[]{:S(2)}, u32[]{:S(2)}) collective-permute-start(bf16[512,128]{1,0:T(8,128)(2,1)S(1)} %get-tuple-element.91), channel_id=1, source_target_pairs={{0,2},{1,3},{2,0},{3,1},{4,6},{5,7},{6,4},{7,5},{8,10},{9,11},{10,... | collective-permute-start | bytes 393224 | tf_op jit(solution)/shard_map/ppermute | solution.py:482
  54.9 1.2 collective-permute-start.18
  56.1 3.4 %collective-permute-start.19 = (bf16[512,128]{1,0:T(8,128)(2,1)S(1)}, bf16[512,128]{1,0:T(8,128)(2,1)S(1)}, u32[]{:S(2)}, u32[]{:S(2)}) collective-permute-start(bf16[512,128]{1,0:T(8,128)(2,1)S(1)} %get-tuple-element.95), channel_id=1, source_target_pairs={{0,8},{1,9},{2,10},{3,11},{4,12},{5,13},{6,14},{7,15},{8,0},{9,1},... | collective-permute-start | bytes 393224 | tf_op jit(solution)/shard_map/ppermute | solution.py:482
  59.5 0.7 collective-permute-start.20
  60.2 0.6 collective-permute-done.18.refs_5_
  60.8 2.4 %collective-permute-done.19.refs_6_ = bf16[512,128]{1,0:T(8,128)(2,1)S(1)} collective-permute-done((bf16[512,128]{1,0:T(8,128)(2,1)S(1)}, bf16[512,128]{1,0:T(8,128)(2,1)S(1)}, u32[]{:S(2)}, u32[]{:S(2)}) %collective-permute-start.19) | collective-permute-done | bytes 131104 | tf_op jit(solution)/shard_map/ppermute | solution.py:482
  63.3 1.1 pointwise.1
  64.4 1.4 collective-permute-start.21
  65.8 2.1 %collective-permute-start.22 = (bf16[512,128]{1,0:T(8,128)(2,1)S(1)}, bf16[512,128]{1,0:T(8,128)(2,1)S(1)}, u32[]{:S(2)}, u32[]{:S(2)}) collective-permute-start(bf16[512,128]{1,0:T(8,128)(2,1)S(1)} %get-tuple-element.101.refs_0_), channel_id=1, source_target_pairs={{0,2},{1,3},{2,0},{3,1},{4,6},{5,7},{6,4},{7,5},{8,10},{9,11},{10,... | collective-permute-start | bytes 393224 | tf_op jit(solution)/shard_map/ppermute | solution.py:482
  67.9 1.6 %collective-permute-start.27 = (f32[136,256]{1,0:T(8,128)S(1)}, f32[136,256]{1,0:T(8,128)S(1)}, u32[]{:S(2)}, u32[]{:S(2)}) collective-permute-start(f32[136,256]{1,0:T(8,128)S(1)} %get-tuple-element.104), channel_id=1, source_target_pairs={{0,16},{1,17},{2,18},{3,19},{4,20},{5,21},{6,22},{7,23},{8,24},{9,... | collective-permute-start | bytes 417800 | tf_op jit(solution)/shard_map/ppermute | solution.py:482
  69.6 2.4 %collective-permute-start.23 = (bf16[512,128]{1,0:T(8,128)(2,1)S(1)}, bf16[512,128]{1,0:T(8,128)(2,1)S(1)}, u32[]{:S(2)}, u32[]{:S(2)}) collective-permute-start(bf16[512,128]{1,0:T(8,128)(2,1)S(1)} %get-tuple-element.101.refs_0_), channel_id=1, source_target_pairs={{0,3},{1,0},{2,1},{3,2},{4,7},{5,4},{6,5},{7,6},{8,11},{9,8},{10,9... | collective-permute-start | bytes 393224 | tf_op jit(solution)/shard_map/ppermute | solution.py:482
  71.9 1.3 collective-permute-start.24
  73.3 1.3 collective-permute-start.25
  74.5 1.1 collective-permute-start.26
  75.7 1.5 %collective-permute-done.24.refs_5_ = bf16[512,128]{1,0:T(8,128)(2,1)S(1)} collective-permute-done((bf16[512,128]{1,0:T(8,128)(2,1)S(1)}, bf16[512,128]{1,0:T(8,128)(2,1)S(1)}, u32[]{:S(2)}, u32[]{:S(2)}) %collective-permute-start.24) | collective-permute-done | bytes 131104 | tf_op jit(solution)/shard_map/ppermute | solution.py:482
  77.2 1.4 collective-permute-done.25.refs_6_
  79.0 1.2 collective-permute-start.28
  80.2 1.6 %collective-permute-start.29 = (bf16[2048,128]{1,0:T(8,128)(2,1)S(1)}, bf16[2048,128]{1,0:T(8,128)(2,1)S(1)}, u32[]{:S(2)}, u32[]{:S(2)}) collective-permute-start(bf16[2048,128]{1,0:T(8,128)(2,1)S(1)} %get-tuple-element.105.refs_0_), channel_id=1, source_target_pairs={{0,12},{1,13},{2,14},{3,15},{4,0},{5,1},{6,2},{7,3},{8,4},{9,5},{1... | collective-permute-start | bytes 1572872 | tf_op jit(solution)/shard_map/ppermute | solution.py:482
  81.8 2.7 %collective-permute-start.31 = (bf16[2048,128]{1,0:T(8,128)(2,1)S(1)}, bf16[2048,128]{1,0:T(8,128)(2,1)S(1)}, u32[]{:S(2)}, u32[]{:S(2)}) collective-permute-start(bf16[2048,128]{1,0:T(8,128)(2,1)S(1)} %get-tuple-element.106.refs_3_), channel_id=1, source_target_pairs={{0,3},{1,0},{2,1},{3,2},{4,7},{5,4},{6,5},{7,6},{8,11},{9,8},{10,9... | collective-permute-start | bytes 1572872 | tf_op jit(solution)/shard_map/ppermute | solution.py:482
  84.5 4.2 %collective-permute-done.32 = f32[136,256]{1,0:T(8,128)S(1)} collective-permute-done((f32[136,256]{1,0:T(8,128)S(1)}, f32[136,256]{1,0:T(8,128)S(1)}, u32[]{:S(2)}, u32[]{:S(2)}) %collective-permute-start.32) | collective-permute-done | bytes 139296 | tf_op jit(solution)/shard_map/ppermute | solution.py:482
  89.1 6.1 %collective-permute-done.33 = f32[136,256]{1,0:T(8,128)S(1)} collective-permute-done((f32[136,256]{1,0:T(8,128)S(1)}, f32[136,256]{1,0:T(8,128)S(1)}, u32[]{:S(2)}, u32[]{:S(2)}) %collective-permute-start.33) | collective-permute-done | bytes 139296 | tf_op jit(solution)/shard_map/ppermute | solution.py:482
  96.1 2.4 %collective-permute-start.36 = (bf16[1024,128]{1,0:T(8,128)(2,1)S(1)}, bf16[1024,128]{1,0:T(8,128)(2,1)S(1)}, u32[]{:S(2)}, u32[]{:S(2)}) collective-permute-start(bf16[1024,128]{1,0:T(8,128)(2,1)S(1)} %get-tuple-element.115), channel_id=1, source_target_pairs={{0,12},{1,13},{2,14},{3,15},{4,0},{5,1},{6,2},{7,3},{8,4},{9,5},{1... | collective-permute-start | bytes 786440 | tf_op jit(solution)/shard_map/ppermute | solution.py:482
  98.4 2.7 %collective-permute-start.38 = (bf16[1024,128]{1,0:T(8,128)(2,1)S(1)}, bf16[1024,128]{1,0:T(8,128)(2,1)S(1)}, u32[]{:S(2)}, u32[]{:S(2)}) collective-permute-start(bf16[1024,128]{1,0:T(8,128)(2,1)S(1)} %get-tuple-element.117), channel_id=1, source_target_pairs={{0,3},{1,0},{2,1},{3,2},{4,7},{5,4},{6,5},{7,6},{8,11},{9,8},{10,9... | collective-permute-start | bytes 786440 | tf_op jit(solution)/shard_map/ppermute | solution.py:482
  101.1 3.0 %backward_early.1.start = f32[4096,256]{1,0:T(8,128)S(1)} custom-call(s32[1,128]{1,0:T(1,128)S(1)} %get-tuple-element.68.rows, s32[1,128]{1,0:T(1,128)S(1)} %get-tuple-element.69.cols, bf16[128,128,128]{2,1,0:T(8,128)(2,1)S(1)} %get-tuple-element.70.values, bf16[2048,128]{1,0:T(8,128)(2,1)S(1)} %get-tuple-element.105.refs_0_, ...), custom_call_target="tpu_custom_call" | custom-call | flops 805306368 | bytes 10485760 | tf_op jit(solution)/shard_map/backward_early/pallas_call | solution.py:399
  104.1 1.2 collective-permute-done.34
  105.3 1.1 collective-permute-start.39
  106.5 2.0 %backward_late.1 = (bf16[2048,256]{1,0:T(8,128)(2,1)S(1)}, bf16[2048,256]{1,0:T(8,128)(2,1)S(1)}) custom-call(s32[1,128]{1,0:T(1,128)S(1)} %get-tuple-element.68.rows, s32[1,128]{1,0:T(1,128)S(1)} %get-tuple-element.69.cols, bf16[128,128,128]{2,1,0:T(8,128)(2,1)S(1)} %get-tuple-element.70.values, f32[4096,256]{1,0:T(8,128)S(1)} %backward_early.1.start, ...), custom_call_target="tpu_custom_call" | custom-call | flops 268435456 | bytes 8388608 | tf_op jit(solution)/shard_map/backward_late/pallas_call | solution.py:437
  108.5 3.7 %collective-permute-done.39 = f32[136,256]{1,0:T(8,128)S(1)} collective-permute-done((f32[136,256]{1,0:T(8,128)S(1)}, f32[136,256]{1,0:T(8,128)S(1)}, u32[]{:S(2)}, u32[]{:S(2)}) %collective-permute-start.39) | collective-permute-done | bytes 139296 | tf_op jit(solution)/shard_map/ppermute | solution.py:482
  112.2 7.5 %collective-permute-start.40 = (bf16[2048,256]{1,0:T(8,128)(2,1)S(1)}, bf16[2048,256]{1,0:T(8,128)(2,1)S(1)}, u32[]{:S(2)}, u32[]{:S(2)}) collective-permute-start(bf16[2048,256]{1,0:T(8,128)(2,1)S(1)} %get-tuple-element.121), channel_id=1, source_target_pairs={{0,16},{1,17},{2,18},{3,19},{4,20},{5,21},{6,22},{7,23},{8,24},{9,... | collective-permute-start | bytes 3145736 | tf_op jit(solution)/shard_map/ppermute | solution.py:482
  119.7 4.2 %collective-permute-done.41 = f32[136,256]{1,0:T(8,128)S(1)} collective-permute-done((f32[136,256]{1,0:T(8,128)S(1)}, f32[136,256]{1,0:T(8,128)S(1)}, u32[]{:S(2)}, u32[]{:S(2)}) %collective-permute-start.41) | collective-permute-done | bytes 139296 | tf_op jit(solution)/shard_map/ppermute | solution.py:482
  124.3 1.4 %collective-permute-start.42 = (bf16[512,256]{1,0:T(8,128)(2,1)S(1)}, bf16[512,256]{1,0:T(8,128)(2,1)S(1)}, u32[]{:S(2)}, u32[]{:S(2)}) collective-permute-start(bf16[512,256]{1,0:T(8,128)(2,1)S(1)} %get-tuple-element.125), channel_id=1, source_target_pairs={{0,32},{1,33},{2,34},{3,35},{4,36},{5,37},{6,38},{7,39},{8,40},{9,... | collective-permute-start | bytes 786440 | tf_op jit(solution)/shard_map/ppermute | solution.py:482
  125.7 1.1 collective-permute-start.43
  126.8 2.9 %collective-permute-done.45 = f32[136,256]{1,0:T(8,128)S(1)} collective-permute-done((f32[136,256]{1,0:T(8,128)S(1)}, f32[136,256]{1,0:T(8,128)S(1)}, u32[]{:S(2)}, u32[]{:S(2)}) %collective-permute-start.45) | collective-permute-done | bytes 139296 | tf_op jit(solution)/shard_map/ppermute | solution.py:482
  129.7 1.9 %collective-permute-start.46 = (f32[136,256]{1,0:T(8,128)S(1)}, f32[136,256]{1,0:T(8,128)S(1)}, u32[]{:S(2)}, u32[]{:S(2)}) collective-permute-start(f32[136,256]{1,0:T(8,128)S(1)} %add.23.refs_4_), channel_id=1, source_target_pairs={{0,16},{1,17},{2,18},{3,19},{4,20},{5,21},{6,22},{7,23},{8,24},{9,... | collective-permute-start | bytes 417800 | tf_op jit(solution)/shard_map/ppermute | solution.py:482
  131.6 3.8 %collective-permute-done.43.refs_2_ = bf16[512,256]{1,0:T(8,128)(2,1)S(1)} collective-permute-done((bf16[512,256]{1,0:T(8,128)(2,1)S(1)}, bf16[512,256]{1,0:T(8,128)(2,1)S(1)}, u32[]{:S(2)}, u32[]{:S(2)}) %collective-permute-start.43) | collective-permute-done | bytes 262176 | tf_op jit(solution)/shard_map/ppermute | solution.py:482
  135.5 5.2 %collective-permute-done.44.refs_3_ = bf16[512,256]{1,0:T(8,128)(2,1)S(1)} collective-permute-done((bf16[512,256]{1,0:T(8,128)(2,1)S(1)}, bf16[512,256]{1,0:T(8,128)(2,1)S(1)}, u32[]{:S(2)}, u32[]{:S(2)}) %collective-permute-start.44) | collective-permute-done | bytes 262176 | tf_op jit(solution)/shard_map/ppermute | solution.py:482
  140.6 0.9 last_sum.1
  (62 shorter events, 3.8 us)
Async XLA Ops:
  0.6 15.0 %collective-permute-start = (bf16[512,256]{1,0:T(8,128)(2,1)}, bf16[512,256]{1,0:T(8,128)(2,1)S(1)}, u32[]{:S(2)}, u32[]{:S(2)}) collective-permute-start(bf16[512,256]{1,0:T(8,128)(2,1)} %refs_0_.1), channel_id=1, source_target_pairs={{0,32},{1,33},{2,34},{3,35},{4,36},{5,37},{6,38},{7,39},{8,40},{9,... | collective-permute-start | bytes 786440 | tf_op jit(solution)/shard_map/ppermute | solution.py:482
  4.3 11.4 %collective-permute-start.1 = (bf16[512,256]{1,0:T(8,128)(2,1)}, bf16[512,256]{1,0:T(8,128)(2,1)S(1)}, u32[]{:S(2)}, u32[]{:S(2)}) collective-permute-start(bf16[512,256]{1,0:T(8,128)(2,1)} %refs_0_.1), channel_id=1, source_target_pairs={{0,64},{1,65},{2,66},{3,67},{4,68},{5,69},{6,70},{7,71},{8,72},{9,... | collective-permute-start | bytes 786440 | tf_op jit(solution)/shard_map/ppermute | solution.py:482
  4.6 14.5 %collective-permute-start.2 = (bf16[512,256]{1,0:T(8,128)(2,1)}, bf16[512,256]{1,0:T(8,128)(2,1)S(1)}, u32[]{:S(2)}, u32[]{:S(2)}) collective-permute-start(bf16[512,256]{1,0:T(8,128)(2,1)} %refs_0_.1), channel_id=1, source_target_pairs={{0,96},{1,97},{2,98},{3,99},{4,100},{5,101},{6,102},{7,103},{8,104... | collective-permute-start | bytes 786440 | tf_op jit(solution)/shard_map/ppermute | solution.py:482
  5.3 13.8 %collective-permute-start.3 = (bf16[512,256]{1,0:T(8,128)(2,1)}, bf16[512,256]{1,0:T(8,128)(2,1)S(1)}, u32[]{:S(2)}, u32[]{:S(2)}) collective-permute-start(bf16[512,256]{1,0:T(8,128)(2,1)} %refs_0_.1), channel_id=1, source_target_pairs={{0,16},{1,17},{2,18},{3,19},{4,20},{5,21},{6,22},{7,23},{8,24},{9,... | collective-permute-start | bytes 786440 | tf_op jit(solution)/shard_map/ppermute | solution.py:482
  8.0 2.2 %copy-start = (bf16[1,1,128,128,128]{4,3,2,1,0:T(8,128)(2,1)S(1)}, bf16[1,1,128,128,128]{4,3,2,1,0:T(8,128)(2,1)}, u32[]{:S(2)}) copy-start(bf16[1,1,128,128,128]{4,3,2,1,0:T(8,128)(2,1)} %param.8) | copy-start | bytes 12582916
  10.2 0.9 copy-start.1
  11.2 0.9 copy-start.2
  12.1 0.9 copy-start.3
  13.0 0.7 copy-start.4
  13.7 0.7 copy-start.5
  14.4 0.7 copy-start.6
  15.6 3.5 %collective-permute-start.4 = (bf16[512,256]{1,0:T(8,128)(2,1)S(1)}, bf16[512,256]{1,0:T(8,128)(2,1)S(1)}, u32[]{:S(2)}, u32[]{:S(2)}) collective-permute-start(bf16[512,256]{1,0:T(8,128)(2,1)S(1)} %collective-permute-done.refs_1_), channel_id=1, source_target_pairs={{0,16},{1,17},{2,18},{3,19},{4,20},{5,21},{6,22},{7,23},{8,24},{9,... | collective-permute-start | bytes 786440 | tf_op jit(solution)/shard_map/ppermute | solution.py:482
  15.7 4.5 %collective-permute-start.5 = (bf16[512,256]{1,0:T(8,128)(2,1)S(1)}, bf16[512,256]{1,0:T(8,128)(2,1)S(1)}, u32[]{:S(2)}, u32[]{:S(2)}) collective-permute-start(bf16[512,256]{1,0:T(8,128)(2,1)S(1)} %collective-permute-done.1.refs_2_), channel_id=1, source_target_pairs={{0,16},{1,17},{2,18},{3,19},{4,20},{5,21},{6,22},{7,23},{8,24},{9,... | collective-permute-start | bytes 786440 | tf_op jit(solution)/shard_map/ppermute | solution.py:482
  19.1 1.5 %collective-permute-start.6 = (bf16[512,256]{1,0:T(8,128)(2,1)S(1)}, bf16[512,256]{1,0:T(8,128)(2,1)S(1)}, u32[]{:S(2)}, u32[]{:S(2)}) collective-permute-start(bf16[512,256]{1,0:T(8,128)(2,1)S(1)} %collective-permute-done.2.refs_3_), channel_id=1, source_target_pairs={{0,16},{1,17},{2,18},{3,19},{4,20},{5,21},{6,22},{7,23},{8,24},{9,... | collective-permute-start | bytes 786440 | tf_op jit(solution)/shard_map/ppermute | solution.py:482
  22.6 10.0 %collective-permute-start.7 = (bf16[1024,128]{1,0:T(8,128)(2,1)S(1)}, bf16[1024,128]{1,0:T(8,128)(2,1)S(1)}, u32[]{:S(2)}, u32[]{:S(2)}) collective-permute-start(bf16[1024,128]{1,0:T(8,128)(2,1)S(1)} %get-tuple-element.80), channel_id=1, source_target_pairs={{0,4},{1,5},{2,6},{3,7},{4,8},{5,9},{6,10},{7,11},{8,12},{9,13},{1... | collective-permute-start | bytes 786440 | tf_op jit(solution)/shard_map/ppermute | solution.py:482
  24.3 8.3 %collective-permute-start.8 = (bf16[1024,128]{1,0:T(8,128)(2,1)S(1)}, bf16[1024,128]{1,0:T(8,128)(2,1)S(1)}, u32[]{:S(2)}, u32[]{:S(2)}) collective-permute-start(bf16[1024,128]{1,0:T(8,128)(2,1)S(1)} %get-tuple-element.81), channel_id=1, source_target_pairs={{0,12},{1,13},{2,14},{3,15},{4,0},{5,1},{6,2},{7,3},{8,4},{9,5},{1... | collective-permute-start | bytes 786440 | tf_op jit(solution)/shard_map/ppermute | solution.py:482
  26.5 6.7 %collective-permute-start.9 = (bf16[1024,128]{1,0:T(8,128)(2,1)S(1)}, bf16[1024,128]{1,0:T(8,128)(2,1)S(1)}, u32[]{:S(2)}, u32[]{:S(2)}) collective-permute-start(bf16[1024,128]{1,0:T(8,128)(2,1)S(1)} %get-tuple-element.82), channel_id=1, source_target_pairs={{0,1},{1,2},{2,3},{3,0},{4,5},{5,6},{6,7},{7,4},{8,9},{9,10},{10,1... | collective-permute-start | bytes 786440 | tf_op jit(solution)/shard_map/ppermute | solution.py:482
  27.7 5.6 %collective-permute-start.10 = (bf16[1024,128]{1,0:T(8,128)(2,1)S(1)}, bf16[1024,128]{1,0:T(8,128)(2,1)S(1)}, u32[]{:S(2)}, u32[]{:S(2)}) collective-permute-start(bf16[1024,128]{1,0:T(8,128)(2,1)S(1)} %get-tuple-element.83), channel_id=1, source_target_pairs={{0,3},{1,0},{2,1},{3,2},{4,7},{5,4},{6,5},{7,6},{8,11},{9,8},{10,9... | collective-permute-start | bytes 786440 | tf_op jit(solution)/shard_map/ppermute | solution.py:482
  33.6 12.3 %collective-permute-start.11 = (bf16[2048,128]{1,0:T(8,128)(2,1)S(1)}, bf16[2048,128]{1,0:T(8,128)(2,1)S(1)}, u32[]{:S(2)}, u32[]{:S(2)}) collective-permute-start(bf16[2048,128]{1,0:T(8,128)(2,1)S(1)} %get-tuple-element.84), channel_id=1, source_target_pairs={{0,4},{1,5},{2,6},{3,7},{4,8},{5,9},{6,10},{7,11},{8,12},{9,13},{1... | collective-permute-start | bytes 1572872 | tf_op jit(solution)/shard_map/ppermute | solution.py:482
  35.3 10.6 %collective-permute-start.12 = (bf16[2048,128]{1,0:T(8,128)(2,1)S(1)}, bf16[2048,128]{1,0:T(8,128)(2,1)S(1)}, u32[]{:S(2)}, u32[]{:S(2)}) collective-permute-start(bf16[2048,128]{1,0:T(8,128)(2,1)S(1)} %get-tuple-element.85), channel_id=1, source_target_pairs={{0,12},{1,13},{2,14},{3,15},{4,0},{5,1},{6,2},{7,3},{8,4},{9,5},{1... | collective-permute-start | bytes 1572872 | tf_op jit(solution)/shard_map/ppermute | solution.py:482
  37.5 12.8 %collective-permute-start.13 = (bf16[2048,128]{1,0:T(8,128)(2,1)S(1)}, bf16[2048,128]{1,0:T(8,128)(2,1)S(1)}, u32[]{:S(2)}, u32[]{:S(2)}) collective-permute-start(bf16[2048,128]{1,0:T(8,128)(2,1)S(1)} %get-tuple-element.87), channel_id=1, source_target_pairs={{0,1},{1,2},{2,3},{3,0},{4,5},{5,6},{6,7},{7,4},{8,9},{9,10},{10,1... | collective-permute-start | bytes 1572872 | tf_op jit(solution)/shard_map/ppermute | solution.py:482
  38.4 11.9 %collective-permute-start.14 = (bf16[2048,128]{1,0:T(8,128)(2,1)S(1)}, bf16[2048,128]{1,0:T(8,128)(2,1)S(1)}, u32[]{:S(2)}, u32[]{:S(2)}) collective-permute-start(bf16[2048,128]{1,0:T(8,128)(2,1)S(1)} %get-tuple-element.88), channel_id=1, source_target_pairs={{0,3},{1,0},{2,1},{3,2},{4,7},{5,4},{6,5},{7,6},{8,11},{9,8},{10,9... | collective-permute-start | bytes 1572872 | tf_op jit(solution)/shard_map/ppermute | solution.py:482
  50.7 8.8 %collective-permute-start.15 = (bf16[512,128]{1,0:T(8,128)(2,1)S(1)}, bf16[512,128]{1,0:T(8,128)(2,1)S(1)}, u32[]{:S(2)}, u32[]{:S(2)}) collective-permute-start(bf16[512,128]{1,0:T(8,128)(2,1)S(1)} %get-tuple-element.90), channel_id=1, source_target_pairs={{0,1},{1,2},{2,3},{3,0},{4,5},{5,6},{6,7},{7,4},{8,9},{9,10},{10,1... | collective-permute-start | bytes 393224 | tf_op jit(solution)/shard_map/ppermute | solution.py:482
  51.3 8.9 %collective-permute-start.16 = (bf16[512,128]{1,0:T(8,128)(2,1)S(1)}, bf16[512,128]{1,0:T(8,128)(2,1)S(1)}, u32[]{:S(2)}, u32[]{:S(2)}) collective-permute-start(bf16[512,128]{1,0:T(8,128)(2,1)S(1)} %get-tuple-element.91), channel_id=1, source_target_pairs={{0,2},{1,3},{2,0},{3,1},{4,6},{5,7},{6,4},{7,5},{8,10},{9,11},{10,... | collective-permute-start | bytes 393224 | tf_op jit(solution)/shard_map/ppermute | solution.py:482
  54.9 5.3 %collective-permute-start.17 = (bf16[512,128]{1,0:T(8,128)(2,1)S(1)}, bf16[512,128]{1,0:T(8,128)(2,1)S(1)}, u32[]{:S(2)}, u32[]{:S(2)}) collective-permute-start(bf16[512,128]{1,0:T(8,128)(2,1)S(1)} %get-tuple-element.92), channel_id=1, source_target_pairs={{0,3},{1,0},{2,1},{3,2},{4,7},{5,4},{6,5},{7,6},{8,11},{9,8},{10,9... | collective-permute-start | bytes 393224 | tf_op jit(solution)/shard_map/ppermute | solution.py:482
  54.9 5.9 %collective-permute-start.18 = (bf16[512,128]{1,0:T(8,128)(2,1)S(1)}, bf16[512,128]{1,0:T(8,128)(2,1)S(1)}, u32[]{:S(2)}, u32[]{:S(2)}) collective-permute-start(bf16[512,128]{1,0:T(8,128)(2,1)S(1)} %get-tuple-element.94), channel_id=1, source_target_pairs={{0,4},{1,5},{2,6},{3,7},{4,8},{5,9},{6,10},{7,11},{8,12},{9,13},{1... | collective-permute-start | bytes 393224 | tf_op jit(solution)/shard_map/ppermute | solution.py:482
  56.1 7.1 %collective-permute-start.19 = (bf16[512,128]{1,0:T(8,128)(2,1)S(1)}, bf16[512,128]{1,0:T(8,128)(2,1)S(1)}, u32[]{:S(2)}, u32[]{:S(2)}) collective-permute-start(bf16[512,128]{1,0:T(8,128)(2,1)S(1)} %get-tuple-element.95), channel_id=1, source_target_pairs={{0,8},{1,9},{2,10},{3,11},{4,12},{5,13},{6,14},{7,15},{8,0},{9,1},... | collective-permute-start | bytes 393224 | tf_op jit(solution)/shard_map/ppermute | solution.py:482
  59.5 3.8 %collective-permute-start.20 = (bf16[512,128]{1,0:T(8,128)(2,1)S(1)}, bf16[512,128]{1,0:T(8,128)(2,1)S(1)}, u32[]{:S(2)}, u32[]{:S(2)}) collective-permute-start(bf16[512,128]{1,0:T(8,128)(2,1)S(1)} %get-tuple-element.96), channel_id=1, source_target_pairs={{0,12},{1,13},{2,14},{3,15},{4,0},{5,1},{6,2},{7,3},{8,4},{9,5},{1... | collective-permute-start | bytes 393224 | tf_op jit(solution)/shard_map/ppermute | solution.py:482
  64.4 8.9 %collective-permute-start.21 = (bf16[512,128]{1,0:T(8,128)(2,1)S(1)}, bf16[512,128]{1,0:T(8,128)(2,1)S(1)}, u32[]{:S(2)}, u32[]{:S(2)}) collective-permute-start(bf16[512,128]{1,0:T(8,128)(2,1)S(1)} %get-tuple-element.101.refs_0_), channel_id=1, source_target_pairs={{0,1},{1,2},{2,3},{3,0},{4,5},{5,6},{6,7},{7,4},{8,9},{9,10},{10,1... | collective-permute-start | bytes 393224 | tf_op jit(solution)/shard_map/ppermute | solution.py:482
  65.8 8.7 %collective-permute-start.22 = (bf16[512,128]{1,0:T(8,128)(2,1)S(1)}, bf16[512,128]{1,0:T(8,128)(2,1)S(1)}, u32[]{:S(2)}, u32[]{:S(2)}) collective-permute-start(bf16[512,128]{1,0:T(8,128)(2,1)S(1)} %get-tuple-element.101.refs_0_), channel_id=1, source_target_pairs={{0,2},{1,3},{2,0},{3,1},{4,6},{5,7},{6,4},{7,5},{8,10},{9,11},{10,... | collective-permute-start | bytes 393224 | tf_op jit(solution)/shard_map/ppermute | solution.py:482
  67.9 11.0 %collective-permute-start.27 = (f32[136,256]{1,0:T(8,128)S(1)}, f32[136,256]{1,0:T(8,128)S(1)}, u32[]{:S(2)}, u32[]{:S(2)}) collective-permute-start(f32[136,256]{1,0:T(8,128)S(1)} %get-tuple-element.104), channel_id=1, source_target_pairs={{0,16},{1,17},{2,18},{3,19},{4,20},{5,21},{6,22},{7,23},{8,24},{9,... | collective-permute-start | bytes 417800 | tf_op jit(solution)/shard_map/ppermute | solution.py:482
  69.6 6.1 %collective-permute-start.23 = (bf16[512,128]{1,0:T(8,128)(2,1)S(1)}, bf16[512,128]{1,0:T(8,128)(2,1)S(1)}, u32[]{:S(2)}, u32[]{:S(2)}) collective-permute-start(bf16[512,128]{1,0:T(8,128)(2,1)S(1)} %get-tuple-element.101.refs_0_), channel_id=1, source_target_pairs={{0,3},{1,0},{2,1},{3,2},{4,7},{5,4},{6,5},{7,6},{8,11},{9,8},{10,9... | collective-permute-start | bytes 393224 | tf_op jit(solution)/shard_map/ppermute | solution.py:482
  71.9 5.3 %collective-permute-start.24 = (bf16[512,128]{1,0:T(8,128)(2,1)S(1)}, bf16[512,128]{1,0:T(8,128)(2,1)S(1)}, u32[]{:S(2)}, u32[]{:S(2)}) collective-permute-start(bf16[512,128]{1,0:T(8,128)(2,1)S(1)} %get-tuple-element.102.refs_4_), channel_id=1, source_target_pairs={{0,4},{1,5},{2,6},{3,7},{4,8},{5,9},{6,10},{7,11},{8,12},{9,13},{1... | collective-permute-start | bytes 393224 | tf_op jit(solution)/shard_map/ppermute | solution.py:482
  73.3 5.3 %collective-permute-start.25 = (bf16[512,128]{1,0:T(8,128)(2,1)S(1)}, bf16[512,128]{1,0:T(8,128)(2,1)S(1)}, u32[]{:S(2)}, u32[]{:S(2)}) collective-permute-start(bf16[512,128]{1,0:T(8,128)(2,1)S(1)} %get-tuple-element.102.refs_4_), channel_id=1, source_target_pairs={{0,8},{1,9},{2,10},{3,11},{4,12},{5,13},{6,14},{7,15},{8,0},{9,1},... | collective-permute-start | bytes 393224 | tf_op jit(solution)/shard_map/ppermute | solution.py:482
  74.5 4.4 %collective-permute-start.26 = (bf16[512,128]{1,0:T(8,128)(2,1)S(1)}, bf16[512,128]{1,0:T(8,128)(2,1)S(1)}, u32[]{:S(2)}, u32[]{:S(2)}) collective-permute-start(bf16[512,128]{1,0:T(8,128)(2,1)S(1)} %get-tuple-element.102.refs_4_), channel_id=1, source_target_pairs={{0,12},{1,13},{2,14},{3,15},{4,0},{5,1},{6,2},{7,3},{8,4},{9,5},{1... | collective-permute-start | bytes 393224 | tf_op jit(solution)/shard_map/ppermute | solution.py:482
  79.0 16.2 %collective-permute-start.28 = (bf16[2048,128]{1,0:T(8,128)(2,1)S(1)}, bf16[2048,128]{1,0:T(8,128)(2,1)S(1)}, u32[]{:S(2)}, u32[]{:S(2)}) collective-permute-start(bf16[2048,128]{1,0:T(8,128)(2,1)S(1)} %get-tuple-element.105.refs_0_), channel_id=1, source_target_pairs={{0,4},{1,5},{2,6},{3,7},{4,8},{5,9},{6,10},{7,11},{8,12},{9,13},{1... | collective-permute-start | bytes 1572872 | tf_op jit(solution)/shard_map/ppermute | solution.py:482
  80.2 15.1 %collective-permute-start.29 = (bf16[2048,128]{1,0:T(8,128)(2,1)S(1)}, bf16[2048,128]{1,0:T(8,128)(2,1)S(1)}, u32[]{:S(2)}, u32[]{:S(2)}) collective-permute-start(bf16[2048,128]{1,0:T(8,128)(2,1)S(1)} %get-tuple-element.105.refs_0_), channel_id=1, source_target_pairs={{0,12},{1,13},{2,14},{3,15},{4,0},{5,1},{6,2},{7,3},{8,4},{9,5},{1... | collective-permute-start | bytes 1572872 | tf_op jit(solution)/shard_map/ppermute | solution.py:482
  81.8 13.8 %collective-permute-start.30 = (bf16[2048,128]{1,0:T(8,128)(2,1)S(1)}, bf16[2048,128]{1,0:T(8,128)(2,1)S(1)}, u32[]{:S(2)}, u32[]{:S(2)}) collective-permute-start(bf16[2048,128]{1,0:T(8,128)(2,1)S(1)} %get-tuple-element.106.refs_3_), channel_id=1, source_target_pairs={{0,1},{1,2},{2,3},{3,0},{4,5},{5,6},{6,7},{7,4},{8,9},{9,10},{10,1... | collective-permute-start | bytes 1572872 | tf_op jit(solution)/shard_map/ppermute | solution.py:482
  81.8 13.8 %collective-permute-start.31 = (bf16[2048,128]{1,0:T(8,128)(2,1)S(1)}, bf16[2048,128]{1,0:T(8,128)(2,1)S(1)}, u32[]{:S(2)}, u32[]{:S(2)}) collective-permute-start(bf16[2048,128]{1,0:T(8,128)(2,1)S(1)} %get-tuple-element.106.refs_3_), channel_id=1, source_target_pairs={{0,3},{1,0},{2,1},{3,2},{4,7},{5,4},{6,5},{7,6},{8,11},{9,8},{10,9... | collective-permute-start | bytes 1572872 | tf_op jit(solution)/shard_map/ppermute | solution.py:482
  84.5 4.2 %collective-permute-start.32 = (f32[136,256]{1,0:T(8,128)S(1)}, f32[136,256]{1,0:T(8,128)S(1)}, u32[]{:S(2)}, u32[]{:S(2)}) collective-permute-start(f32[136,256]{1,0:T(8,128)S(1)} %get-tuple-element.107), channel_id=1, source_target_pairs={{0,32},{1,33},{2,34},{3,35},{4,36},{5,37},{6,38},{7,39},{8,40},{9,... | collective-permute-start | bytes 417800 | tf_op jit(solution)/shard_map/ppermute | solution.py:482
  88.7 6.6 %collective-permute-start.33 = (f32[136,256]{1,0:T(8,128)S(1)}, f32[136,256]{1,0:T(8,128)S(1)}, u32[]{:S(2)}, u32[]{:S(2)}) collective-permute-start(f32[136,256]{1,0:T(8,128)S(1)} %add.18), channel_id=1, source_target_pairs={{0,64},{1,65},{2,66},{3,67},{4,68},{5,69},{6,70},{7,71},{8,72},{9,... | collective-permute-start | bytes 417800 | tf_op jit(solution)/shard_map/ppermute | solution.py:482
  95.7 10.8 %collective-permute-start.35 = (bf16[1024,128]{1,0:T(8,128)(2,1)S(1)}, bf16[1024,128]{1,0:T(8,128)(2,1)S(1)}, u32[]{:S(2)}, u32[]{:S(2)}) collective-permute-start(bf16[1024,128]{1,0:T(8,128)(2,1)S(1)} %get-tuple-element.114), channel_id=1, source_target_pairs={{0,4},{1,5},{2,6},{3,7},{4,8},{5,9},{6,10},{7,11},{8,12},{9,13},{1... | collective-permute-start | bytes 786440 | tf_op jit(solution)/shard_map/ppermute | solution.py:482
  96.1 10.4 %collective-permute-start.36 = (bf16[1024,128]{1,0:T(8,128)(2,1)S(1)}, bf16[1024,128]{1,0:T(8,128)(2,1)S(1)}, u32[]{:S(2)}, u32[]{:S(2)}) collective-permute-start(bf16[1024,128]{1,0:T(8,128)(2,1)S(1)} %get-tuple-element.115), channel_id=1, source_target_pairs={{0,12},{1,13},{2,14},{3,15},{4,0},{5,1},{6,2},{7,3},{8,4},{9,5},{1... | collective-permute-start | bytes 786440 | tf_op jit(solution)/shard_map/ppermute | solution.py:482
  98.4 8.0 %collective-permute-start.37 = (bf16[1024,128]{1,0:T(8,128)(2,1)S(1)}, bf16[1024,128]{1,0:T(8,128)(2,1)S(1)}, u32[]{:S(2)}, u32[]{:S(2)}) collective-permute-start(bf16[1024,128]{1,0:T(8,128)(2,1)S(1)} %get-tuple-element.116), channel_id=1, source_target_pairs={{0,1},{1,2},{2,3},{3,0},{4,5},{5,6},{6,7},{7,4},{8,9},{9,10},{10,1... | collective-permute-start | bytes 786440 | tf_op jit(solution)/shard_map/ppermute | solution.py:482
  98.4 8.0 %collective-permute-start.38 = (bf16[1024,128]{1,0:T(8,128)(2,1)S(1)}, bf16[1024,128]{1,0:T(8,128)(2,1)S(1)}, u32[]{:S(2)}, u32[]{:S(2)}) collective-permute-start(bf16[1024,128]{1,0:T(8,128)(2,1)S(1)} %get-tuple-element.117), channel_id=1, source_target_pairs={{0,3},{1,0},{2,1},{3,2},{4,7},{5,4},{6,5},{7,6},{8,11},{9,8},{10,9... | collective-permute-start | bytes 786440 | tf_op jit(solution)/shard_map/ppermute | solution.py:482
  101.1 4.2 %collective-permute-start.34 = (f32[136,256]{1,0:T(8,128)S(1)}, f32[136,256]{1,0:T(8,128)S(1)}, u32[]{:S(2)}, u32[]{:S(2)}) collective-permute-start(f32[136,256]{1,0:T(8,128)S(1)} %add.19), channel_id=1, source_target_pairs={{0,4},{1,5},{2,6},{3,7},{4,0},{5,1},{6,2},{7,3},{8,12},{9,13},{10,... | collective-permute-start | bytes 417800 | tf_op jit(solution)/shard_map/ppermute | solution.py:482
  105.3 6.9 %collective-permute-start.39 = (f32[136,256]{1,0:T(8,128)S(1)}, f32[136,256]{1,0:T(8,128)S(1)}, u32[]{:S(2)}, u32[]{:S(2)}) collective-permute-start(f32[136,256]{1,0:T(8,128)S(1)} %add.20), channel_id=1, source_target_pairs={{0,8},{1,9},{2,10},{3,11},{4,12},{5,13},{6,14},{7,15},{8,0},{9,1},... | collective-permute-start | bytes 417800 | tf_op jit(solution)/shard_map/ppermute | solution.py:482
  112.2 11.7 %collective-permute-start.40 = (bf16[2048,256]{1,0:T(8,128)(2,1)S(1)}, bf16[2048,256]{1,0:T(8,128)(2,1)S(1)}, u32[]{:S(2)}, u32[]{:S(2)}) collective-permute-start(bf16[2048,256]{1,0:T(8,128)(2,1)S(1)} %get-tuple-element.121), channel_id=1, source_target_pairs={{0,16},{1,17},{2,18},{3,19},{4,20},{5,21},{6,22},{7,23},{8,24},{9,... | collective-permute-start | bytes 3145736 | tf_op jit(solution)/shard_map/ppermute | solution.py:482
  119.7 4.2 %collective-permute-start.41 = (f32[136,256]{1,0:T(8,128)S(1)}, f32[136,256]{1,0:T(8,128)S(1)}, u32[]{:S(2)}, u32[]{:S(2)}) collective-permute-start(f32[136,256]{1,0:T(8,128)S(1)} %add.21), channel_id=1, source_target_pairs={{0,1},{1,0},{2,3},{3,2},{4,5},{5,4},{6,7},{7,6},{8,9},{9,8},{10,11... | collective-permute-start | bytes 417800 | tf_op jit(solution)/shard_map/ppermute | solution.py:482
  123.9 5.8 %collective-permute-start.45 = (f32[136,256]{1,0:T(8,128)S(1)}, f32[136,256]{1,0:T(8,128)S(1)}, u32[]{:S(2)}, u32[]{:S(2)}) collective-permute-start(f32[136,256]{1,0:T(8,128)S(1)} %add.22), channel_id=1, source_target_pairs={{0,2},{1,3},{2,0},{3,1},{4,6},{5,7},{6,4},{7,5},{8,10},{9,11},{10,... | collective-permute-start | bytes 417800 | tf_op jit(solution)/shard_map/ppermute | solution.py:482
  124.3 7.3 %collective-permute-start.42 = (bf16[512,256]{1,0:T(8,128)(2,1)S(1)}, bf16[512,256]{1,0:T(8,128)(2,1)S(1)}, u32[]{:S(2)}, u32[]{:S(2)}) collective-permute-start(bf16[512,256]{1,0:T(8,128)(2,1)S(1)} %get-tuple-element.125), channel_id=1, source_target_pairs={{0,32},{1,33},{2,34},{3,35},{4,36},{5,37},{6,38},{7,39},{8,40},{9,... | collective-permute-start | bytes 786440 | tf_op jit(solution)/shard_map/ppermute | solution.py:482
  125.7 9.7 %collective-permute-start.43 = (bf16[512,256]{1,0:T(8,128)(2,1)S(1)}, bf16[512,256]{1,0:T(8,128)(2,1)S(1)}, u32[]{:S(2)}, u32[]{:S(2)}) collective-permute-start(bf16[512,256]{1,0:T(8,128)(2,1)S(1)} %get-tuple-element.126), channel_id=1, source_target_pairs={{0,64},{1,65},{2,66},{3,67},{4,68},{5,69},{6,70},{7,71},{8,72},{9,... | collective-permute-start | bytes 786440 | tf_op jit(solution)/shard_map/ppermute | solution.py:482
  126.8 13.8 %collective-permute-start.44 = (bf16[512,256]{1,0:T(8,128)(2,1)S(1)}, bf16[512,256]{1,0:T(8,128)(2,1)S(1)}, u32[]{:S(2)}, u32[]{:S(2)}) collective-permute-start(bf16[512,256]{1,0:T(8,128)(2,1)S(1)} %get-tuple-element.127), channel_id=1, source_target_pairs={{0,96},{1,97},{2,98},{3,99},{4,100},{5,101},{6,102},{7,103},{8,104... | collective-permute-start | bytes 786440 | tf_op jit(solution)/shard_map/ppermute | solution.py:482
  129.7 10.9 %collective-permute-start.46 = (f32[136,256]{1,0:T(8,128)S(1)}, f32[136,256]{1,0:T(8,128)S(1)}, u32[]{:S(2)}, u32[]{:S(2)}) collective-permute-start(f32[136,256]{1,0:T(8,128)S(1)} %add.23.refs_4_), channel_id=1, source_target_pairs={{0,16},{1,17},{2,18},{3,19},{4,20},{5,21},{6,22},{7,23},{8,24},{9,... | collective-permute-start | bytes 417800 | tf_op jit(solution)/shard_map/ppermute | solution.py:482

commit v4 on v0

v4 whole, which is shorter than its diff:
```python
import math

import jax
import jax.numpy as jnp
from jax import lax
from jax.experimental import pallas as pl
from jax.experimental.pallas import tpu as pltpu
from jax.sharding import PartitionSpec as P

BF = jnp.bfloat16
F32 = jnp.float32
BLK = 128
PB = 4
ROWS = 512
HALF = 128
F = 256
GRP = 8
MIB = 1 << 20


def vmem():
    return pl.BlockSpec(memory_space=pltpu.VMEM)


def smem():
    return pl.BlockSpec(memory_space=pltpu.SMEM)


def hbm():
    return pl.BlockSpec(memory_space=pl.ANY)


def coords():
    row = lax.axis_index("row")
    col = lax.axis_index("col")
    y, c = row // 2, row % 2
    x, z = col // 4, col % 4
    return x + c * (z - x), z + c * (x - z), y, c


def group_at(u, v, c):
    return u * (4 - 3 * c) + v * (1 + 3 * c)


def ahead(y, c, d):
    return (y + 4 + (1 - 2 * c) * d) % 4


def target_group(u, v, c, p, r):
    return group_at((u + p) % 4, (v + r) % 4, c)


def source_group(u, v, c, p, r):
    return group_at((u + 4 - p) % 4, (v + 4 - r) % 4, c)


def local_call(kernel, name, ins, outs, args, limit, flops=0, moved=MIB, scratch=()):
    return pl.pallas_call(
        kernel,
        out_shape=outs,
        in_specs=ins,
        out_specs=[vmem()] * len(outs),
        scratch_shapes=list(scratch),
        compiler_params=pltpu.CompilerParams(vmem_limit_bytes=limit * MIB),
        cost_estimate=pl.CostEstimate(
            flops=flops, bytes_accessed=moved, transcendentals=0
        ),
        name=name,
    )(*args)


def shape(rows, width=HALF, dtype=BF):
    return jax.ShapeDtypeStruct((rows, width), dtype)


def lanes_of(core):
    return pl.ds(pl.multiple_of(core * HALF, HALF), HALF)


def rows_at(start, size):
    return pl.ds(pl.multiple_of(start, size), size)


def split_kernel(x_feat, keep, give):
    u, v, y, c = coords()
    keep[...] = x_feat[:, lanes_of(c)]
    give[...] = x_feat[:, lanes_of(1 - c)]


def ids_kernel(rows, cols, ids):
    ids[0:1, :] = rows[...]
    ids[1:2, :] = cols[...]


def stack_kernel(*refs):
    size = refs[0].shape[0]
    for n, ref in enumerate(refs[:-1]):
        refs[-1][n * size:(n + 1) * size, :] = ref[...]


def stack_call(parts, name):
    size, width = parts[0].shape
    return local_call(
        stack_kernel, name, [vmem()] * len(parts), [shape(size * len(parts), width)],
        parts, 8,
    )[0]


def prologue_kernel(*refs):
    count = (len(refs) - 1) // 2
    sems = refs[-1]
    copies = [
        pltpu.make_async_copy(refs[n], refs[count + n], sems.at[n]) for n in range(count)
    ]
    for copy in copies:
        copy.start()
    for copy in copies:
        copy.wait()


def prologue_call(arrays):
    return local_call(
        prologue_kernel, "prologue", [hbm()] * len(arrays),
        [jax.ShapeDtypeStruct(a.shape, a.dtype) for a in arrays], arrays, 8,
        moved=10 * MIB, scratch=[pltpu.SemaphoreType.DMA((len(arrays),))],
    )


def forward_group(ids, values, panel, acc, group):
    acc[...] = jnp.zeros_like(acc)
    for k in range(GRP):
        slot = group * GRP + k
        here = rows_at((ids[0, slot] - group * PB) * BLK, BLK)
        there = rows_at(ids[1, slot] * BLK, BLK)
        acc[here, :] += jnp.dot(
            values[slot], panel[there, :], preferred_element_type=F32
        )


def far_kernel(*refs):
    tiles = (refs[0:2], refs[2:4])
    pieces = refs[4:8]
    panel, low, high, acc, sems = refs[8:]
    u, v, y, c = coords()
    copies = []
    for n in range(8):
        d, t = n // 2, n % 2
        shard = ahead(y, c, -d) * 2 + (c if t == 0 else 1 - c)
        copies.append(
            pltpu.make_async_copy(
                pieces[d].at[pl.ds(t * ROWS, ROWS)],
                panel.at[rows_at(shard * ROWS, ROWS)],
                sems.at[n],
            )
        )
    for copy in copies:
        copy.start()
    for copy in copies:
        copy.wait()
    for r in range(4):
        for t in range(2):
            ids, values = tiles[t]
            forward_group(ids, values, panel, acc.at[t], target_group(u, v, c, 2, r))
            start = ((r % 2) * 2 + t) * ROWS
            (low, high)[r // 2][start:start + ROWS, :] = acc[t].astype(BF)


def near_kernel(*refs):
    tiles = (refs[0:2], refs[2:4])
    panel = refs[4]
    outs = dict(zip((1, 3, 0), refs[5:8]))
    acc = refs[8]
    u, v, y, c = coords()
    for p, out in outs.items():
        for r in range(4):
            for t in range(2):
                ids, values = tiles[t]
                forward_group(ids, values, panel, acc.at[t], target_group(u, v, c, p, r))
                start = (r * 2 + t) * ROWS
                out[start:start + ROWS, :] = acc[t].astype(BF)


def relay_kernel(*refs):
    for n in range(2):
        own, extra, out = refs[n], refs[2 + n], refs[4 + n]
        mixed = pl.ds(n * 4 * ROWS, 4 * ROWS)
        plain = pl.ds((1 - n) * 4 * ROWS, 4 * ROWS)
        out[mixed, :] = (own[mixed, :].astype(F32) + extra[...].astype(F32)).astype(BF)
        out[plain, :] = own[plain, :]


def stage_kernel(*refs):
    for n, out in enumerate(refs[3:]):
        here = pl.ds(n * 2 * ROWS, 2 * ROWS)
        p0, p1, p3 = (part[here, :].astype(F32) for part in refs[:3])
        out[...] = (p0 + (p1 + p3)).astype(BF)


def quad(parts, here):
    p0, p1, p2, p3 = (part[here, :].astype(F32) for part in parts)
    return (p0 + p2) + (p1 + p3)


def finish_kernel(*refs):
    refs[4][...] = quad(refs[:4], pl.ds(0, ROWS)).astype(BF)
    refs[5][...] = quad(refs[:4], pl.ds(ROWS, ROWS)).astype(BF)


def finish_call(parts, name):
    return local_call(
        finish_kernel, name, [vmem()] * 4, [shape(ROWS)] * 2, parts, 8,
        flops=8 * ROWS * HALF,
    )


def point_kernel(scale, *refs):
    own, peer, weight, bias, cotangent = refs[:5]
    out_act, keep_g, give_g, keep_w, give_w, whole, grads, full = refs[5:]
    u, v, y, c = coords()
    whole[:, lanes_of(c)] = own[...]
    whole[:, lanes_of(1 - c)] = peer[...]
    aggregated = whole[...]
    pre = jnp.dot(aggregated, weight[...], preferred_element_type=F32) + bias[...]
    gate = jax.nn.sigmoid(pre)
    out_act[...] = (pre * gate).astype(BF)
    grad_pre = (
        cotangent[...].astype(F32) * gate * (1.0 + pre * (1.0 - gate))
    ).astype(BF)
    grads[...] = lax.dot_general(
        grad_pre, weight[...], (((1,), (1,)), ((), ())), preferred_element_type=F32
    ).astype(BF)
    keep_g[...] = grads[:, lanes_of(c)]
    give_g[...] = grads[:, lanes_of(1 - c)]
    full[...] = lax.dot_general(
        aggregated, grad_pre, (((0,), (0,)), ((), ())), preferred_element_type=F32
    ) * scale
    bias_grad = jnp.sum(grad_pre.astype(F32), axis=0, keepdims=True) * scale
    for out, core in ((keep_w, c), (give_w, 1 - c)):
        out[:HALF, :] = full[rows_at(core * HALF, HALF), :]
        out[HALF:, :] = jnp.broadcast_to(bias_grad, (8, F))


def cut_kernel(left, right, low, high):
    low[...] = left[:4 * ROWS, :]
    high[...] = right[4 * ROWS:, :]


def backward_group(ids, values, acc, part, base, group):
    for k in range(GRP):
        slot = group * GRP + k
        here = rows_at(base + (ids[0, slot] - group * PB) * BLK, BLK)
        there = rows_at(ids[1, slot] * BLK, BLK)
        acc[there, :] += lax.dot_general(
            values[slot], part[here, :], (((0,), (0,)), ((), ())),
            preferred_element_type=F32,
        )


def early_kernel(*refs):
    tiles = (refs[0:2], refs[2:4])
    parts = dict(zip((0, 1, 3), refs[4:7]))
    acc = refs[7]
    u, v, y, c = coords()
    acc[...] = jnp.zeros_like(acc)
    for p, part in parts.items():
        for r in range(4):
            for t in range(2):
                ids, values = tiles[t]
                group = source_group(u, v, c, p, r)
                backward_group(ids, values, acc, part, (r * 2 + t) * ROWS, group)


def late_kernel(*refs):
    tiles = (refs[0:2], refs[2:4])
    start = refs[4]
    parts = refs[5:7]
    outs = refs[7:11]
    acc = refs[11]
    u, v, y, c = coords()
    acc[...] = start[...]
    for r in range(4):
        for t in range(2):
            ids, values = tiles[t]
            group = source_group(u, v, c, 2, r)
            base = ((r % 2) * 2 + t) * ROWS
            backward_group(ids, values, acc, parts[r // 2], base, group)
    for d in range(4):
        first = ahead(y, c, d) * 2
        for t, core in ((0, c), (1, 1 - c)):
            outs[d][t * ROWS:(t + 1) * ROWS, :] = acc[
                rows_at((first + core) * ROWS, ROWS), :
            ].astype(BF)


def sum_kernel(s0, s1, s2, s3, after, out):
    out[...] = (s0[...] + s2[...]) + (s1[...] + s3[...])


def last_kernel(own, peer, mine, theirs, x_grad, weight_grad, bias_grad):
    u, v, y, c = coords()
    x_grad[:, lanes_of(c)] = own[...]
    x_grad[:, lanes_of(1 - c)] = peer[...]
    for source, core in ((mine, c), (theirs, 1 - c)):
        weight_grad[rows_at(core * HALF, HALF), :] = source[:HALF, :]

        @pl.when(core == 0)
        def _(source=source):
            bias_grad[...] = source[HALF:HALF + 1, :]


def permute(value, target):
    pairs = []
    for row in range(8):
        for col in range(16):
            y, c = row // 2, row % 2
            x, z = col // 4, col % 4
            u, v = (z, x) if c else (x, z)
            u, v, y, c = target(u, v, y, c)
            x, z = (v, u) if row % 2 else (u, v)
            pairs.append((row * 16 + col, (y * 2 + c) * 16 + x * 4 + z))
    return lax.ppermute(value, ("row", "col"), pairs)


def along_u(value, d):
    return permute(value, lambda u, v, y, c: ((u + d) % 4, v, y, c))


def along_v(value, d):
    return permute(value, lambda u, v, y, c: (u, (v + d) % 4, y, c))


def along_y(value, d):
    return permute(value, lambda u, v, y, c: (u, v, (y + (1 - 2 * c) * d) % 4, c))


def to_peer(value):
    return permute(value, lambda u, v, y, c: (u, v, y, 1 - c))


def with_u(value, d):
    return value + permute(value, lambda u, v, y, c: (u ^ d, v, y, c))


def with_v(value, d):
    return value + permute(value, lambda u, v, y, c: (u, v ^ d, y, c))


def with_y(value, d):
    return value + permute(value, lambda u, v, y, c: (u, v, y ^ d, c))


def spread(value, along):
    others = {d: along(value, d) for d in (2, 1, 3)}
    return [value, others[1], others[2], others[3]]


def exchange(parts, along):
    others = {d: along(parts[d], d) for d in (2, 1, 3)}
    return [parts[0], others[1], others[2], others[3]]


def shards(x_feat, block_values, block_rows, block_cols, weight, bias, cotangent):
    scale = 1.0 / math.sqrt(65536)
    values = block_values.reshape(128, BLK, BLK)
    slab = 2 * 128 * BLK * BLK * HALF

    keep, give = local_call(
        split_kernel, "split", [vmem()], [shape(ROWS), shape(ROWS)], [x_feat], 4,
    )
    got = to_peer(give)
    got, values, rows, cols = lax.optimization_barrier(
        (got, values, block_rows.reshape(1, 128), block_cols.reshape(1, 128))
    )
    (ids,) = local_call(
        ids_kernel, "ids", [vmem()] * 2, [shape(2, 128, jnp.int32)], [rows, cols], 2,
        moved=2048,
    )
    pair = stack_call([keep, got], "pair")
    pieces = spread(pair, along_y)
    peer_values = to_peer(values)
    peer_ids = to_peer(ids)
    values, weight, bias, cotangent = prologue_call(
        [values, weight, bias.reshape(1, F), cotangent]
    )
    pieces[1], values = lax.optimization_barrier((pieces[1], values))
    tiles = [ids, values, peer_ids, peer_values]
    tile_specs = [smem(), vmem(), smem(), vmem()]

    panel, low, high = local_call(
        far_kernel, "forward_far", tile_specs + [hbm()] * 4,
        [shape(8 * ROWS), shape(4 * ROWS), shape(4 * ROWS)], tiles + pieces, 8,
        flops=slab // 2, moved=6 * MIB,
        scratch=[pltpu.VMEM((2, ROWS, HALF), F32), pltpu.SemaphoreType.DMA((8,))],
    )
    extra = [along_u(low, 1), along_u(high, 3)]
    p1, p3, p0 = local_call(
        near_kernel, "forward_near", tile_specs + [vmem()], [shape(8 * ROWS)] * 3,
        tiles + [panel], 8, flops=3 * slab // 2, moved=10 * MIB,
        scratch=[pltpu.VMEM((2, ROWS, HALF), F32)],
    )
    p1, p3 = local_call(
        relay_kernel, "relay_sum", [vmem()] * 4, [shape(8 * ROWS)] * 2,
        [p1, p3] + extra, 8, flops=8 * ROWS * HALF, moved=5 * MIB,
    )
    sums = local_call(
        stage_kernel, "stage_sum", [vmem()] * 3, [shape(2 * ROWS)] * 4,
        [p0, along_u(p1, 1), along_u(p3, 3)], 8, flops=16 * ROWS * HALF,
        moved=4 * MIB,
    )
    own, other = finish_call(exchange(sums, along_v), "aggregate")
    out_act, keep_g, give_g, keep_w, give_w = local_call(
        lambda *refs: point_kernel(scale, *refs), "pointwise", [vmem()] * 5,
        [shape(ROWS, F), shape(ROWS), shape(ROWS)] + [shape(HALF + 8, F, F32)] * 2,
        [own, to_peer(other), weight, bias, cotangent], 8, flops=6 * ROWS * F * F,
        moved=2 * MIB,
        scratch=[
            pltpu.VMEM((ROWS, F), BF), pltpu.VMEM((ROWS, F), BF), pltpu.VMEM((F, F), F32),
        ],
    )

    got_g = to_peer(give_g)
    piece = to_peer(give_w)
    got_g, piece = lax.optimization_barrier((got_g, piece))
    grads = stack_call([keep_g, got_g], "pair_grads")
    firsts = spread(grads, along_v)
    piece = with_y(keep_w + piece, 1)
    *firsts, piece = lax.optimization_barrier((*firsts, piece))
    join = stack_call(firsts, "join")
    left, right = along_u(join, 1), along_u(join, 3)
    piece = with_y(piece, 2)
    gate = lax.optimization_barrier((left, right, piece))
    left, right = gate[:2]
    s0, s1, s2, s3 = spread(piece, along_u)
    low, high = local_call(
        cut_kernel, "cut", [vmem()] * 2, [shape(4 * ROWS)] * 2, [left, right], 8,
    )
    far = [along_u(low, 1), along_u(high, 3)]
    (start,) = local_call(
        early_kernel, "backward_early", tile_specs + [vmem()] * 3,
        [shape(8 * ROWS, HALF, F32)], tiles + [join, left, right], 8,
        flops=3 * slab // 2, moved=10 * MIB,
    )
    outs = local_call(
        late_kernel, "backward_late", tile_specs + [vmem()] * 3, [shape(2 * ROWS)] * 4,
        tiles + [start] + far, 8, flops=slab // 2, moved=6 * MIB,
        scratch=[pltpu.VMEM((8 * ROWS, HALF), F32)],
    )
    (piece,) = local_call(
        sum_kernel, "sum_u", [vmem()] * 4 + [hbm()], [shape(HALF + 8, F, F32)],
        [s0, s1, s2, s3, outs[0]], 4,
    )
    lasts = exchange(outs, along_y)
    piece = with_v(with_v(piece, 1), 2)
    *lasts, piece = lax.optimization_barrier((*lasts, piece))
    own, other = finish_call(lasts, "sum_x")
    x_grad, weight_grad, bias_grad = local_call(
        last_kernel, "last", [vmem()] * 4,
        [shape(ROWS, F), shape(F, F, F32), shape(1, F, F32)],
        [own, to_peer(other), piece, to_peer(piece)], 8,
    )
    return (out_act, x_grad, weight_grad, bias_grad.reshape(F))


def solution(mesh):
    placed = (
        P(("row", "col"), None),
        P("row", "col", None, None, None),
        P("row", "col", None),
        P("row", "col", None),
        P(),
        P(),
        P(("row", "col"), None),
    )
    return jax.shard_map(
        shards,
        mesh=mesh,
        in_specs=placed,
        out_specs=(P(("row", "col"), None), P(("row", "col"), None), P(), P()),
        check_vma=False,
    )
```

time: 500 us -> 132 us (0.26)
  waiting for transfers between devices: 160 us -> 67.4 us
  local copies, waits for them, and re-layouts: 84.1 us -> 6.97 us
  blocking collectives: 65.2 us -> 0 us
  matrix products: 64.9 us -> 0 us
  other arithmetic: 63.1 us -> 0.1 us
  loops' own time: 43 us -> 0 us
  starting transfers between devices: 0.2 us -> 40.4 us
  Pallas kernels: 0 us -> 15.7 us
  between operations: 13.8 us -> 0.84 us
    reduce_scatter x2 -> x0, waiting for transfers between devices: 80.8 us -> none  [the longest x1 76.2 us: shards(): lax.psum_scatter(terms.reshape(count, feature_width).astype(jnp.bfloat16)...]
    all_gather x2 -> x0, waiting for transfers between devices: 78.9 us -> none  [the longest x1 51.6 us: shards(): gathered_grad = lax.all_gather(grad_agg, 'col', axis=0, tiled=True)]
    ppermute x0 -> x35, waiting for transfers between devices: none -> 67.4 us  [permute(): return lax.ppermute(value, ('row', 'col'), pairs)]
    psum x1 -> x0, blocking collectives: 65.2 us -> none  [shards(): lax.psum((local_weight, local_bias), ('row', 'col'))]
    dot_general x51 -> x0, matrix products: 64.9 us -> none  [the longest x16 21.1 us: forward_group(): jnp.einsum('bij,bjf->bif', group_values, picked, preferred_element_type=j...]
    scatter-add x16 -> x0, other arithmetic: 52.9 us -> none  [backward_group(): return carry.at[group_cols].add(products)]
    gather x32 -> x0, local copies, waits for them, and re-layouts: 44 us -> none  [the longest x16 34.7 us: forward_group(): picked = jnp.take(panel_blocks, group_cols, axis=0)]
    another operation x2 -> x0, loops' own time: 43 us -> none  [the longest x1 42.4 us: shards(): terms = lax.map(one_group, jnp.arange(group_total, dtype=jnp.int32))]
  transfers between devices with their start and end apart: 5 -> 35, of which waited for: 4 -> 21; matrix products, arithmetic and copies ran while one was open for 23% -> 0% of each run, Pallas kernels for 0% -> 7%
where the time goes in v4:
time: 132 us; the launch traced here: 131 us
  waiting for transfers between devices  67.4 us (51%)
  starting transfers between devices  40.4 us (31%)
  Pallas kernels  15.7 us (12%)
  local copies, waits for them, and re-layouts  6.97 us (5%)
    ppermute x35, waiting for transfers between devices, permute(): return lax.ppermute(value, ('row', 'col'), pairs)  67.4 us
    ppermute x35, starting transfers between devices, permute(): return lax.ppermute(value, ('row', 'col'), pairs)  40.4 us
    pallas_call x18, Pallas kernels, local_call(): pl.pallas_call(kernel, out_shape=outs, in_specs=ins, out_specs=[vmem()] *...  15.7 us
    unnamed x14, local copies, waits for them, and re-layouts  6.97 us
  transfers between devices with their start and end apart: 35, of which 21 were waited for; matrix products, arithmetic and copies ran while one was open for 0% of the time, Pallas kernels for 7%

profile of v4, /device:TPU:1, one launch (start us, length us, event | category | flops | bytes accessed | tf_op | source)
XLA Modules:
  0.0 131.5 jit_solution(12047257021243550214)
XLA Ops:
  0.6 0.9 copy-done.2
  1.6 1.5 %collective-permute-start = (bf16[512,128]{1,0:T(8,128)(2,1)S(1)}, bf16[512,128]{1,0:T(8,128)(2,1)S(1)}, u32[]{:S(2)}, u32[]{:S(2)}) collective-permute-start(bf16[512,128]{1,0:T(8,128)(2,1)S(1)} %get-tuple-element.60), channel_id=1, source_target_pairs={{0,16},{1,17},{2,18},{3,19},{4,20},{5,21},{6,22},{7,23},{8,24},{9,... | collective-permute-start | bytes 393224 | tf_op jit(solution)/shard_map/ppermute | solution.py:321
  3.1 1.0 collective-permute-done.refs_1_
  4.1 0.4 collective-permute-start.3
  4.5 2.9 %collective-permute-start.1 = (bf16[1024,128]{1,0:T(8,128)(2,1)S(1)}, bf16[1024,128]{1,0:T(8,128)(2,1)S(1)}, u32[]{:S(2)}, u32[]{:S(2)}) collective-permute-start(bf16[1024,128]{1,0:T(8,128)(2,1)S(1)} %pair.1.refs_4_), channel_id=1, source_target_pairs={{0,32},{1,33},{2,34},{3,35},{4,36},{5,37},{6,38},{7,39},{8,40},{9,... | collective-permute-start | bytes 786440 | tf_op jit(solution)/shard_map/ppermute | solution.py:321
  7.4 1.6 %collective-permute-start.4 = (bf16[1024,128]{1,0:T(8,128)(2,1)S(1)}, bf16[1024,128]{1,0:T(8,128)(2,1)S(1)}, u32[]{:S(2)}, u32[]{:S(2)}) collective-permute-start(bf16[1024,128]{1,0:T(8,128)(2,1)S(1)} %pair.1.refs_4_), channel_id=1, source_target_pairs={{0,64},{1,65},{2,66},{3,67},{4,68},{5,69},{6,70},{7,71},{8,72},{9,... | collective-permute-start | bytes 786440 | tf_op jit(solution)/shard_map/ppermute | solution.py:321
  9.0 0.7 copy-done.5
  9.7 0.7 copy-done.6
  10.3 1.0 collective-permute-start.2
  11.3 2.2 %copy-done = bf16[1,1,128,128,128]{4,3,2,1,0:T(8,128)(2,1)S(1)} copy-done((bf16[1,1,128,128,128]{4,3,2,1,0:T(8,128)(2,1)S(1)}, bf16[1,1,128,128,128]{4,3,2,1,0:T(8,128)(2,1)}, u32[]{:S(2)}) %copy-start) | copy-done | bytes 4194328
  13.5 0.9 copy-done.1
  14.5 0.9 copy-done.3
  15.4 0.7 copy-done.4
  16.1 0.5 prologue.1
  16.6 1.7 %collective-permute-done.1.refs_5_ = bf16[1024,128]{1,0:T(8,128)(2,1)S(1)} collective-permute-done((bf16[1024,128]{1,0:T(8,128)(2,1)S(1)}, bf16[1024,128]{1,0:T(8,128)(2,1)S(1)}, u32[]{:S(2)}, u32[]{:S(2)}) %collective-permute-start.1) | collective-permute-done | bytes 262176 | tf_op jit(solution)/shard_map/ppermute | solution.py:321
  18.3 3.1 %collective-permute-done.4.refs_6_ = bf16[1024,128]{1,0:T(8,128)(2,1)S(1)} collective-permute-done((bf16[1024,128]{1,0:T(8,128)(2,1)S(1)}, bf16[1024,128]{1,0:T(8,128)(2,1)S(1)}, u32[]{:S(2)}, u32[]{:S(2)}) %collective-permute-start.4) | collective-permute-done | bytes 262176 | tf_op jit(solution)/shard_map/ppermute | solution.py:321
  21.4 3.1 %forward_far.1 = (bf16[4096,128]{1,0:T(8,128)(2,1)S(1)}, bf16[2048,128]{1,0:T(8,128)(2,1)S(1)}, bf16[2048,128]{1,0:T(8,128)(2,1)S(1)}) custom-call(s32[2,128]{1,0:T(2,128)S(1)} %ids.1.refs_0_, bf16[128,128,128]{2,1,0:T(8,128)(2,1)S(1)} %get-tuple-element.67.refs_1_, s32[2,128]{1,0:T(2,128)S(1)} %collective-permute-done.2.refs_2_, ...), custom_call_target="tpu_custom_call" | custom-call | flops 268435456 | bytes 6291456 | tf_op jit(solution)/shard_map/forward_far/pallas_call | solution.py:58
  24.5 1.7 %collective-permute-start.6 = (bf16[2048,128]{1,0:T(8,128)(2,1)S(1)}, bf16[2048,128]{1,0:T(8,128)(2,1)S(1)}, u32[]{:S(2)}, u32[]{:S(2)}) collective-permute-start(bf16[2048,128]{1,0:T(8,128)(2,1)S(1)} %get-tuple-element.73), channel_id=1, source_target_pairs={{0,4},{1,5},{2,6},{3,7},{4,8},{5,9},{6,10},{7,11},{8,12},{9,13},{1... | collective-permute-start | bytes 1572872 | tf_op jit(solution)/shard_map/ppermute | solution.py:321
  26.2 2.2 %collective-permute-start.7 = (bf16[2048,128]{1,0:T(8,128)(2,1)S(1)}, bf16[2048,128]{1,0:T(8,128)(2,1)S(1)}, u32[]{:S(2)}, u32[]{:S(2)}) collective-permute-start(bf16[2048,128]{1,0:T(8,128)(2,1)S(1)} %get-tuple-element.74), channel_id=1, source_target_pairs={{0,12},{1,13},{2,14},{3,15},{4,0},{5,1},{6,2},{7,3},{8,4},{9,5},{1... | collective-permute-start | bytes 1572872 | tf_op jit(solution)/shard_map/ppermute | solution.py:321
  28.4 3.8 %forward_near.1 = (bf16[4096,128]{1,0:T(8,128)(2,1)S(1)}, bf16[4096,128]{1,0:T(8,128)(2,1)S(1)}, bf16[4096,128]{1,0:T(8,128)(2,1)S(1)}) custom-call(s32[2,128]{1,0:T(2,128)S(1)} %ids.1.refs_0_, bf16[128,128,128]{2,1,0:T(8,128)(2,1)S(1)} %get-tuple-element.67.refs_1_, s32[2,128]{1,0:T(2,128)S(1)} %collective-permute-done.2.refs_2_, ...), custom_call_target="tpu_custom_call" | custom-call | flops 805306368 | bytes 10485760 | tf_op jit(solution)/shard_map/forward_near/pallas_call | solution.py:58
  32.2 2.9 %collective-permute-done.6.refs_2_ = bf16[2048,128]{1,0:T(8,128)(2,1)S(1)} collective-permute-done((bf16[2048,128]{1,0:T(8,128)(2,1)S(1)}, bf16[2048,128]{1,0:T(8,128)(2,1)S(1)}, u32[]{:S(2)}, u32[]{:S(2)}) %collective-permute-start.6) | collective-permute-done | bytes 524320 | tf_op jit(solution)/shard_map/ppermute | solution.py:321
  35.1 0.3 relay_sum.1
  35.4 1.1 collective-permute-start.8
  36.6 1.8 %collective-permute-start.9 = (bf16[4096,128]{1,0:T(8,128)(2,1)S(1)}, bf16[4096,128]{1,0:T(8,128)(2,1)S(1)}, u32[]{:S(2)}, u32[]{:S(2)}) collective-permute-start(bf16[4096,128]{1,0:T(8,128)(2,1)S(1)} %get-tuple-element.76), channel_id=1, source_target_pairs={{0,12},{1,13},{2,14},{3,15},{4,0},{5,1},{6,2},{7,3},{8,4},{9,5},{1... | collective-permute-start | bytes 3145736 | tf_op jit(solution)/shard_map/ppermute | solution.py:321
  38.4 12.4 %collective-permute-done.8.refs_1_ = bf16[4096,128]{1,0:T(8,128)(2,1)S(1)} collective-permute-done((bf16[4096,128]{1,0:T(8,128)(2,1)S(1)}, bf16[4096,128]{1,0:T(8,128)(2,1)S(1)}, u32[]{:S(2)}, u32[]{:S(2)}) %collective-permute-start.8) | collective-permute-done | bytes 1048608 | tf_op jit(solution)/shard_map/ppermute | solution.py:321
  50.8 0.4 stage_sum.1
  51.2 1.0 collective-permute-start.10
  52.2 2.8 %collective-permute-start.11 = (bf16[1024,128]{1,0:T(8,128)(2,1)S(1)}, bf16[1024,128]{1,0:T(8,128)(2,1)S(1)}, u32[]{:S(2)}, u32[]{:S(2)}) collective-permute-start(bf16[1024,128]{1,0:T(8,128)(2,1)S(1)} %get-tuple-element.79), channel_id=1, source_target_pairs={{0,2},{1,3},{2,0},{3,1},{4,6},{5,7},{6,4},{7,5},{8,10},{9,11},{10,... | collective-permute-start | bytes 786440 | tf_op jit(solution)/shard_map/ppermute | solution.py:321
  54.9 0.8 collective-permute-start.12
  55.8 1.9 %collective-permute-done.10.refs_1_ = bf16[1024,128]{1,0:T(8,128)(2,1)S(1)} collective-permute-done((bf16[1024,128]{1,0:T(8,128)(2,1)S(1)}, bf16[1024,128]{1,0:T(8,128)(2,1)S(1)}, u32[]{:S(2)}, u32[]{:S(2)}) %collective-permute-start.10) | collective-permute-done | bytes 262176 | tf_op jit(solution)/shard_map/ppermute | solution.py:321
  57.7 3.8 %collective-permute-done.11.refs_2_ = bf16[1024,128]{1,0:T(8,128)(2,1)S(1)} collective-permute-done((bf16[1024,128]{1,0:T(8,128)(2,1)S(1)}, bf16[1024,128]{1,0:T(8,128)(2,1)S(1)}, u32[]{:S(2)}, u32[]{:S(2)}) %collective-permute-start.11) | collective-permute-done | bytes 262176 | tf_op jit(solution)/shard_map/ppermute | solution.py:321
  61.6 4.1 %collective-permute-start.13 = (bf16[512,128]{1,0:T(8,128)(2,1)S(1)}, bf16[512,128]{1,0:T(8,128)(2,1)S(1)}, u32[]{:S(2)}, u32[]{:S(2)}) collective-permute-start(bf16[512,128]{1,0:T(8,128)(2,1)S(1)} %get-tuple-element.82), channel_id=1, source_target_pairs={{0,16},{1,17},{2,18},{3,19},{4,20},{5,21},{6,22},{7,23},{8,24},{9,... | collective-permute-start | bytes 393224 | tf_op jit(solution)/shard_map/ppermute | solution.py:321
  65.8 1.0 collective-permute-done.13.refs_1_
  66.8 1.2 pointwise.1
  67.9 0.4 collective-permute-start.15
  68.3 0.1 collective-permute-start.14
  68.4 1.2 collective-permute-done.14.refs_1_
  69.7 2.7 %collective-permute-start.18 = (bf16[1024,128]{1,0:T(8,128)(2,1)S(1)}, bf16[1024,128]{1,0:T(8,128)(2,1)S(1)}, u32[]{:S(2)}, u32[]{:S(2)}) collective-permute-start(bf16[1024,128]{1,0:T(8,128)(2,1)S(1)} %pair_grads.1.refs_0_), channel_id=1, source_target_pairs={{0,3},{1,0},{2,1},{3,2},{4,7},{5,4},{6,5},{7,6},{8,11},{9,8},{10,9... | collective-permute-start | bytes 786440 | tf_op jit(solution)/shard_map/ppermute | solution.py:321
  72.5 0.8 collective-permute-start.16
  73.4 4.6 %collective-permute-done.19 = f32[136,256]{1,0:T(8,128)S(1)} collective-permute-done((f32[136,256]{1,0:T(8,128)S(1)}, f32[136,256]{1,0:T(8,128)S(1)}, u32[]{:S(2)}, u32[]{:S(2)}) %collective-permute-start.19) | collective-permute-done | bytes 139296 | tf_op jit(solution)/shard_map/ppermute | solution.py:321
  78.0 0.6 collective-permute-done.18.refs_3_
  78.5 0.9 collective-permute-done.17.refs_2_
  79.5 2.5 %collective-permute-done.16.refs_1_ = bf16[1024,128]{1,0:T(8,128)(2,1)S(1)} collective-permute-done((bf16[1024,128]{1,0:T(8,128)(2,1)S(1)}, bf16[1024,128]{1,0:T(8,128)(2,1)S(1)}, u32[]{:S(2)}, u32[]{:S(2)}) %collective-permute-start.16) | collective-permute-done | bytes 262176 | tf_op jit(solution)/shard_map/ppermute | solution.py:321
  82.1 1.6 %collective-permute-start.21 = (bf16[4096,128]{1,0:T(8,128)(2,1)S(1)}, bf16[4096,128]{1,0:T(8,128)(2,1)S(1)}, u32[]{:S(2)}, u32[]{:S(2)}) collective-permute-start(bf16[4096,128]{1,0:T(8,128)(2,1)S(1)} %join.1.refs_4_), channel_id=1, source_target_pairs={{0,12},{1,13},{2,14},{3,15},{4,0},{5,1},{6,2},{7,3},{8,4},{9,5},{1... | collective-permute-start | bytes 3145736 | tf_op jit(solution)/shard_map/ppermute | solution.py:321
  83.7 5.4 %collective-permute-done.22 = f32[136,256]{1,0:T(8,128)S(1)} collective-permute-done((f32[136,256]{1,0:T(8,128)S(1)}, f32[136,256]{1,0:T(8,128)S(1)}, u32[]{:S(2)}, u32[]{:S(2)}) %collective-permute-start.22) | collective-permute-done | bytes 139296 | tf_op jit(solution)/shard_map/ppermute | solution.py:321
  89.2 6.9 %collective-permute-done.21.refs_6_.right = bf16[4096,128]{1,0:T(8,128)(2,1)S(1)} collective-permute-done((bf16[4096,128]{1,0:T(8,128)(2,1)S(1)}, bf16[4096,128]{1,0:T(8,128)(2,1)S(1)}, u32[]{:S(2)}, u32[]{:S(2)}) %collective-permute-start.21) | collective-permute-done | bytes 1048608 | tf_op jit(solution)/shard_map/ppermute | solution.py:321
  96.1 2.8 %collective-permute-done.20.refs_5_.left = bf16[4096,128]{1,0:T(8,128)(2,1)S(1)} collective-permute-done((bf16[4096,128]{1,0:T(8,128)(2,1)S(1)}, bf16[4096,128]{1,0:T(8,128)(2,1)S(1)}, u32[]{:S(2)}, u32[]{:S(2)}) %collective-permute-start.20) | collective-permute-done | bytes 1048608 | tf_op jit(solution)/shard_map/ppermute | solution.py:321
  99.0 2.7 %collective-permute-start.24 = (bf16[2048,128]{1,0:T(8,128)(2,1)S(1)}, bf16[2048,128]{1,0:T(8,128)(2,1)S(1)}, u32[]{:S(2)}, u32[]{:S(2)}) collective-permute-start(bf16[2048,128]{1,0:T(8,128)(2,1)S(1)} %get-tuple-element.101), channel_id=1, source_target_pairs={{0,12},{1,13},{2,14},{3,15},{4,0},{5,1},{6,2},{7,3},{8,4},{9,5},{1... | collective-permute-start | bytes 1572872 | tf_op jit(solution)/shard_map/ppermute | solution.py:321
  101.7 0.6 collective-permute-start.29
  102.4 0.8 collective-permute-start.28
  103.2 3.3 %backward_early.1.refs_4_ = f32[4096,128]{1,0:T(8,128)S(1)} custom-call(s32[2,128]{1,0:T(2,128)S(1)} %ids.1.refs_0_, bf16[128,128,128]{2,1,0:T(8,128)(2,1)S(1)} %get-tuple-element.67.refs_1_, s32[2,128]{1,0:T(2,128)S(1)} %collective-permute-done.2.refs_2_, bf16[128,128,128]{2,1,0:T(8,128)(2,1)S(1)} %collective-permute-done.3.refs_3_, ...), custom_call_target="tpu_custom_call" | custom-call | flops 805306368 | bytes 10485760 | tf_op jit(solution)/shard_map/backward_early/pallas_call | solution.py:58
  106.5 3.6 %collective-permute-done.23.refs_5_ = bf16[2048,128]{1,0:T(8,128)(2,1)S(1)} collective-permute-done((bf16[2048,128]{1,0:T(8,128)(2,1)S(1)}, bf16[2048,128]{1,0:T(8,128)(2,1)S(1)}, u32[]{:S(2)}, u32[]{:S(2)}) %collective-permute-start.23) | collective-permute-done | bytes 524320 | tf_op jit(solution)/shard_map/ppermute | solution.py:321
  110.1 1.8 %backward_late.1 = (bf16[1024,128]{1,0:T(8,128)(2,1)S(1)}, bf16[1024,128]{1,0:T(8,128)(2,1)S(1)}, bf16[1024,128]{1,0:T(8,128)(2,1)S(1)}, bf16[1024,128]{1,0:T(8,128)(2,1)S(1)}) custom-call(s32[2,128]{1,0:T(2,128)S(1)} %ids.1.refs_0_, bf16[128,128,128]{2,1,0:T(8,128)(2,1)S(1)} %get-tuple-element.67.refs_1_, s32[2,128]{1,0:T(2,128)S(1)} %collective-permute-done.2.refs_2_, ...), custom_call_target="tpu_custom_call" | custom-call | flops 268435456 | bytes 6291456 | tf_op jit(solution)/shard_map/backward_late/pallas_call | solution.py:58
  112.0 1.1 collective-permute-start.25
  113.1 0.1 collective-permute-start.26
  113.3 0.5 collective-permute-start.27
  113.8 2.1 %collective-permute-done.31 = f32[136,256]{1,0:T(8,128)S(1)} collective-permute-done((f32[136,256]{1,0:T(8,128)S(1)}, f32[136,256]{1,0:T(8,128)S(1)}, u32[]{:S(2)}, u32[]{:S(2)}) %collective-permute-start.31) | collective-permute-done | bytes 139296 | tf_op jit(solution)/shard_map/ppermute | solution.py:321
  115.9 1.6 %collective-permute-start.32 = (f32[136,256]{1,0:T(8,128)S(1)}, f32[136,256]{1,0:T(8,128)S(1)}, u32[]{:S(2)}, u32[]{:S(2)}) collective-permute-start(f32[136,256]{1,0:T(8,128)S(1)} %add.18), channel_id=1, source_target_pairs={{0,2},{1,3},{2,0},{3,1},{4,6},{5,7},{6,4},{7,5},{8,10},{9,11},{10,... | collective-permute-start | bytes 417800 | tf_op jit(solution)/shard_map/ppermute | solution.py:321
  117.5 3.9 %collective-permute-done.32 = f32[136,256]{1,0:T(8,128)S(1)} collective-permute-done((f32[136,256]{1,0:T(8,128)S(1)}, f32[136,256]{1,0:T(8,128)S(1)}, u32[]{:S(2)}, u32[]{:S(2)}) %collective-permute-start.32) | collective-permute-done | bytes 139296 | tf_op jit(solution)/shard_map/ppermute | solution.py:321
  121.5 3.7 %collective-permute-done.27.refs_3_ = bf16[1024,128]{1,0:T(8,128)(2,1)S(1)} collective-permute-done((bf16[1024,128]{1,0:T(8,128)(2,1)S(1)}, bf16[1024,128]{1,0:T(8,128)(2,1)S(1)}, u32[]{:S(2)}, u32[]{:S(2)}) %collective-permute-start.27) | collective-permute-done | bytes 262176 | tf_op jit(solution)/shard_map/ppermute | solution.py:321
  125.1 3.9 %collective-permute-start.34 = (f32[136,256]{1,0:T(8,128)S(1)}, f32[136,256]{1,0:T(8,128)S(1)}, u32[]{:S(2)}, u32[]{:S(2)}) collective-permute-start(f32[136,256]{1,0:T(8,128)S(1)} %add.19.mine), channel_id=1, source_target_pairs={{0,16},{1,17},{2,18},{3,19},{4,20},{5,21},{6,22},{7,23},{8,24},{9,... | collective-permute-start | bytes 417800 | tf_op jit(solution)/shard_map/ppermute | solution.py:321
  129.0 0.1 sum_x.1
  129.2 1.3 %collective-permute-done.33.peer = bf16[512,128]{1,0:T(8,128)(2,1)S(1)} collective-permute-done((bf16[512,128]{1,0:T(8,128)(2,1)S(1)}, bf16[512,128]{1,0:T(8,128)(2,1)S(1)}, u32[]{:S(2)}, u32[]{:S(2)}) %collective-permute-start.33) | collective-permute-done | bytes 131104 | tf_op jit(solution)/shard_map/ppermute | solution.py:321
  130.6 0.9 last.1
  (43 shorter events, 1.0 us)
Async XLA Ops:
  0.6 1.0 copy-start.2
  1.6 2.5 %collective-permute-start = (bf16[512,128]{1,0:T(8,128)(2,1)S(1)}, bf16[512,128]{1,0:T(8,128)(2,1)S(1)}, u32[]{:S(2)}, u32[]{:S(2)}) collective-permute-start(bf16[512,128]{1,0:T(8,128)(2,1)S(1)} %get-tuple-element.60), channel_id=1, source_target_pairs={{0,16},{1,17},{2,18},{3,19},{4,20},{5,21},{6,22},{7,23},{8,24},{9,... | collective-permute-start | bytes 393224 | tf_op jit(solution)/shard_map/ppermute | solution.py:321
  4.1 17.2 %collective-permute-start.3 = (bf16[128,128,128]{2,1,0:T(8,128)(2,1)}, bf16[128,128,128]{2,1,0:T(8,128)(2,1)S(1)}, u32[]{:S(2)}, u32[]{:S(2)}) collective-permute-start(bf16[128,128,128]{2,1,0:T(8,128)(2,1)} %bitcast.5), channel_id=1, source_target_pairs={{0,16},{1,17},{2,18},{3,19},{4,20},{5,21},{6,22},{7,23},{8,24},{9,... | collective-permute-start | bytes 12582920 | tf_op jit(solution)/shard_map/ppermute | solution.py:321
  4.5 13.8 %collective-permute-start.1 = (bf16[1024,128]{1,0:T(8,128)(2,1)S(1)}, bf16[1024,128]{1,0:T(8,128)(2,1)S(1)}, u32[]{:S(2)}, u32[]{:S(2)}) collective-permute-start(bf16[1024,128]{1,0:T(8,128)(2,1)S(1)} %pair.1.refs_4_), channel_id=1, source_target_pairs={{0,32},{1,33},{2,34},{3,35},{4,36},{5,37},{6,38},{7,39},{8,40},{9,... | collective-permute-start | bytes 786440 | tf_op jit(solution)/shard_map/ppermute | solution.py:321
  7.4 10.9 %collective-permute-start.5 = (bf16[1024,128]{1,0:T(8,128)(2,1)S(1)}, bf16[1024,128]{1,0:T(8,128)(2,1)S(1)}, u32[]{:S(2)}, u32[]{:S(2)}) collective-permute-start(bf16[1024,128]{1,0:T(8,128)(2,1)S(1)} %pair.1.refs_4_), channel_id=1, source_target_pairs={{0,96},{1,97},{2,98},{3,99},{4,100},{5,101},{6,102},{7,103},{8,104... | collective-permute-start | bytes 786440 | tf_op jit(solution)/shard_map/ppermute | solution.py:321
  7.4 14.0 %collective-permute-start.4 = (bf16[1024,128]{1,0:T(8,128)(2,1)S(1)}, bf16[1024,128]{1,0:T(8,128)(2,1)S(1)}, u32[]{:S(2)}, u32[]{:S(2)}) collective-permute-start(bf16[1024,128]{1,0:T(8,128)(2,1)S(1)} %pair.1.refs_4_), channel_id=1, source_target_pairs={{0,64},{1,65},{2,66},{3,67},{4,68},{5,69},{6,70},{7,71},{8,72},{9,... | collective-permute-start | bytes 786440 | tf_op jit(solution)/shard_map/ppermute | solution.py:321
  9.0 0.7 copy-start.5
  9.7 0.7 copy-start.6
  10.3 7.9 %collective-permute-start.2 = (s32[2,128]{1,0:T(2,128)S(1)}, s32[2,128]{1,0:T(2,128)S(1)}, u32[]{:S(2)}, u32[]{:S(2)}) collective-permute-start(s32[2,128]{1,0:T(2,128)S(1)} %ids.1.refs_0_), channel_id=1, source_target_pairs={{0,16},{1,17},{2,18},{3,19},{4,20},{5,21},{6,22},{7,23},{8,24},{9,... | collective-permute-start | bytes 3080 | tf_op jit(solution)/shard_map/ppermute | solution.py:321
  11.3 2.2 %copy-start = (bf16[1,1,128,128,128]{4,3,2,1,0:T(8,128)(2,1)S(1)}, bf16[1,1,128,128,128]{4,3,2,1,0:T(8,128)(2,1)}, u32[]{:S(2)}) copy-start(bf16[1,1,128,128,128]{4,3,2,1,0:T(8,128)(2,1)} %param.8) | copy-start | bytes 12582916
  13.5 0.9 copy-start.1
  14.5 0.9 copy-start.3
  15.4 0.7 copy-start.4
  24.5 10.6 %collective-permute-start.6 = (bf16[2048,128]{1,0:T(8,128)(2,1)S(1)}, bf16[2048,128]{1,0:T(8,128)(2,1)S(1)}, u32[]{:S(2)}, u32[]{:S(2)}) collective-permute-start(bf16[2048,128]{1,0:T(8,128)(2,1)S(1)} %get-tuple-element.73), channel_id=1, source_target_pairs={{0,4},{1,5},{2,6},{3,7},{4,8},{5,9},{6,10},{7,11},{8,12},{9,13},{1... | collective-permute-start | bytes 1572872 | tf_op jit(solution)/shard_map/ppermute | solution.py:321
  26.2 8.9 %collective-permute-start.7 = (bf16[2048,128]{1,0:T(8,128)(2,1)S(1)}, bf16[2048,128]{1,0:T(8,128)(2,1)S(1)}, u32[]{:S(2)}, u32[]{:S(2)}) collective-permute-start(bf16[2048,128]{1,0:T(8,128)(2,1)S(1)} %get-tuple-element.74), channel_id=1, source_target_pairs={{0,12},{1,13},{2,14},{3,15},{4,0},{5,1},{6,2},{7,3},{8,4},{9,5},{1... | collective-permute-start | bytes 1572872 | tf_op jit(solution)/shard_map/ppermute | solution.py:321
  35.4 15.4 %collective-permute-start.8 = (bf16[4096,128]{1,0:T(8,128)(2,1)S(1)}, bf16[4096,128]{1,0:T(8,128)(2,1)S(1)}, u32[]{:S(2)}, u32[]{:S(2)}) collective-permute-start(bf16[4096,128]{1,0:T(8,128)(2,1)S(1)} %get-tuple-element.75), channel_id=1, source_target_pairs={{0,4},{1,5},{2,6},{3,7},{4,8},{5,9},{6,10},{7,11},{8,12},{9,13},{1... | collective-permute-start | bytes 3145736 | tf_op jit(solution)/shard_map/ppermute | solution.py:321
  36.6 14.3 %collective-permute-start.9 = (bf16[4096,128]{1,0:T(8,128)(2,1)S(1)}, bf16[4096,128]{1,0:T(8,128)(2,1)S(1)}, u32[]{:S(2)}, u32[]{:S(2)}) collective-permute-start(bf16[4096,128]{1,0:T(8,128)(2,1)S(1)} %get-tuple-element.76), channel_id=1, source_target_pairs={{0,12},{1,13},{2,14},{3,15},{4,0},{5,1},{6,2},{7,3},{8,4},{9,5},{1... | collective-permute-start | bytes 3145736 | tf_op jit(solution)/shard_map/ppermute | solution.py:321
  51.2 6.5 %collective-permute-start.10 = (bf16[1024,128]{1,0:T(8,128)(2,1)S(1)}, bf16[1024,128]{1,0:T(8,128)(2,1)S(1)}, u32[]{:S(2)}, u32[]{:S(2)}) collective-permute-start(bf16[1024,128]{1,0:T(8,128)(2,1)S(1)} %get-tuple-element.78), channel_id=1, source_target_pairs={{0,1},{1,2},{2,3},{3,0},{4,5},{5,6},{6,7},{7,4},{8,9},{9,10},{10,1... | collective-permute-start | bytes 786440 | tf_op jit(solution)/shard_map/ppermute | solution.py:321
  52.2 9.3 %collective-permute-start.11 = (bf16[1024,128]{1,0:T(8,128)(2,1)S(1)}, bf16[1024,128]{1,0:T(8,128)(2,1)S(1)}, u32[]{:S(2)}, u32[]{:S(2)}) collective-permute-start(bf16[1024,128]{1,0:T(8,128)(2,1)S(1)} %get-tuple-element.79), channel_id=1, source_target_pairs={{0,2},{1,3},{2,0},{3,1},{4,6},{5,7},{6,4},{7,5},{8,10},{9,11},{10,... | collective-permute-start | bytes 786440 | tf_op jit(solution)/shard_map/ppermute | solution.py:321
  54.9 6.6 %collective-permute-start.12 = (bf16[1024,128]{1,0:T(8,128)(2,1)S(1)}, bf16[1024,128]{1,0:T(8,128)(2,1)S(1)}, u32[]{:S(2)}, u32[]{:S(2)}) collective-permute-start(bf16[1024,128]{1,0:T(8,128)(2,1)S(1)} %get-tuple-element.80), channel_id=1, source_target_pairs={{0,3},{1,0},{2,1},{3,2},{4,7},{5,4},{6,5},{7,6},{8,11},{9,8},{10,9... | collective-permute-start | bytes 786440 | tf_op jit(solution)/shard_map/ppermute | solution.py:321
  61.6 5.1 %collective-permute-start.13 = (bf16[512,128]{1,0:T(8,128)(2,1)S(1)}, bf16[512,128]{1,0:T(8,128)(2,1)S(1)}, u32[]{:S(2)}, u32[]{:S(2)}) collective-permute-start(bf16[512,128]{1,0:T(8,128)(2,1)S(1)} %get-tuple-element.82), channel_id=1, source_target_pairs={{0,16},{1,17},{2,18},{3,19},{4,20},{5,21},{6,22},{7,23},{8,24},{9,... | collective-permute-start | bytes 393224 | tf_op jit(solution)/shard_map/ppermute | solution.py:321
  67.9 1.7 %collective-permute-start.15 = (f32[136,256]{1,0:T(8,128)S(1)}, f32[136,256]{1,0:T(8,128)S(1)}, u32[]{:S(2)}, u32[]{:S(2)}) collective-permute-start(f32[136,256]{1,0:T(8,128)S(1)} %get-tuple-element.89), channel_id=1, source_target_pairs={{0,16},{1,17},{2,18},{3,19},{4,20},{5,21},{6,22},{7,23},{8,24},{9,... | collective-permute-start | bytes 417800 | tf_op jit(solution)/shard_map/ppermute | solution.py:321
  68.3 1.3 %collective-permute-start.14 = (bf16[512,128]{1,0:T(8,128)(2,1)S(1)}, bf16[512,128]{1,0:T(8,128)(2,1)S(1)}, u32[]{:S(2)}, u32[]{:S(2)}) collective-permute-start(bf16[512,128]{1,0:T(8,128)(2,1)S(1)} %get-tuple-element.88), channel_id=1, source_target_pairs={{0,16},{1,17},{2,18},{3,19},{4,20},{5,21},{6,22},{7,23},{8,24},{9,... | collective-permute-start | bytes 393224 | tf_op jit(solution)/shard_map/ppermute | solution.py:321
  69.7 8.9 %collective-permute-start.18 = (bf16[1024,128]{1,0:T(8,128)(2,1)S(1)}, bf16[1024,128]{1,0:T(8,128)(2,1)S(1)}, u32[]{:S(2)}, u32[]{:S(2)}) collective-permute-start(bf16[1024,128]{1,0:T(8,128)(2,1)S(1)} %pair_grads.1.refs_0_), channel_id=1, source_target_pairs={{0,3},{1,0},{2,1},{3,2},{4,7},{5,4},{6,5},{7,6},{8,11},{9,8},{10,9... | collective-permute-start | bytes 786440 | tf_op jit(solution)/shard_map/ppermute | solution.py:321
  72.4 7.1 %collective-permute-start.17 = (bf16[1024,128]{1,0:T(8,128)(2,1)S(1)}, bf16[1024,128]{1,0:T(8,128)(2,1)S(1)}, u32[]{:S(2)}, u32[]{:S(2)}) collective-permute-start(bf16[1024,128]{1,0:T(8,128)(2,1)S(1)} %pair_grads.1.refs_0_), channel_id=1, source_target_pairs={{0,2},{1,3},{2,0},{3,1},{4,6},{5,7},{6,4},{7,5},{8,10},{9,11},{10,... | collective-permute-start | bytes 786440 | tf_op jit(solution)/shard_map/ppermute | solution.py:321
  72.5 9.5 %collective-permute-start.16 = (bf16[1024,128]{1,0:T(8,128)(2,1)S(1)}, bf16[1024,128]{1,0:T(8,128)(2,1)S(1)}, u32[]{:S(2)}, u32[]{:S(2)}) collective-permute-start(bf16[1024,128]{1,0:T(8,128)(2,1)S(1)} %pair_grads.1.refs_0_), channel_id=1, source_target_pairs={{0,1},{1,2},{2,3},{3,0},{4,5},{5,6},{6,7},{7,4},{8,9},{9,10},{10,1... | collective-permute-start | bytes 786440 | tf_op jit(solution)/shard_map/ppermute | solution.py:321
  73.3 4.7 %collective-permute-start.19 = (f32[136,256]{1,0:T(8,128)S(1)}, f32[136,256]{1,0:T(8,128)S(1)}, u32[]{:S(2)}, u32[]{:S(2)}) collective-permute-start(f32[136,256]{1,0:T(8,128)S(1)} %add.15), channel_id=1, source_target_pairs={{0,32},{1,33},{2,34},{3,35},{4,36},{5,37},{6,38},{7,39},{8,40},{9,... | collective-permute-start | bytes 417800 | tf_op jit(solution)/shard_map/ppermute | solution.py:321
  82.1 14.0 %collective-permute-start.21 = (bf16[4096,128]{1,0:T(8,128)(2,1)S(1)}, bf16[4096,128]{1,0:T(8,128)(2,1)S(1)}, u32[]{:S(2)}, u32[]{:S(2)}) collective-permute-start(bf16[4096,128]{1,0:T(8,128)(2,1)S(1)} %join.1.refs_4_), channel_id=1, source_target_pairs={{0,12},{1,13},{2,14},{3,15},{4,0},{5,1},{6,2},{7,3},{8,4},{9,5},{1... | collective-permute-start | bytes 3145736 | tf_op jit(solution)/shard_map/ppermute | solution.py:321
  83.7 15.2 %collective-permute-start.20 = (bf16[4096,128]{1,0:T(8,128)(2,1)S(1)}, bf16[4096,128]{1,0:T(8,128)(2,1)S(1)}, u32[]{:S(2)}, u32[]{:S(2)}) collective-permute-start(bf16[4096,128]{1,0:T(8,128)(2,1)S(1)} %join.1.refs_4_), channel_id=1, source_target_pairs={{0,4},{1,5},{2,6},{3,7},{4,8},{5,9},{6,10},{7,11},{8,12},{9,13},{1... | collective-permute-start | bytes 3145736 | tf_op jit(solution)/shard_map/ppermute | solution.py:321
  83.7 5.4 %collective-permute-start.22 = (f32[136,256]{1,0:T(8,128)S(1)}, f32[136,256]{1,0:T(8,128)S(1)}, u32[]{:S(2)}, u32[]{:S(2)}) collective-permute-start(f32[136,256]{1,0:T(8,128)S(1)} %add.16), channel_id=1, source_target_pairs={{0,64},{1,65},{2,66},{3,67},{4,68},{5,69},{6,70},{7,71},{8,72},{9,... | collective-permute-start | bytes 417800 | tf_op jit(solution)/shard_map/ppermute | solution.py:321
  99.0 11.1 %collective-permute-start.23 = (bf16[2048,128]{1,0:T(8,128)(2,1)S(1)}, bf16[2048,128]{1,0:T(8,128)(2,1)S(1)}, u32[]{:S(2)}, u32[]{:S(2)}) collective-permute-start(bf16[2048,128]{1,0:T(8,128)(2,1)S(1)} %get-tuple-element.100), channel_id=1, source_target_pairs={{0,4},{1,5},{2,6},{3,7},{4,8},{5,9},{6,10},{7,11},{8,12},{9,13},{1... | collective-permute-start | bytes 1572872 | tf_op jit(solution)/shard_map/ppermute | solution.py:321
  99.0 11.0 %collective-permute-start.24 = (bf16[2048,128]{1,0:T(8,128)(2,1)S(1)}, bf16[2048,128]{1,0:T(8,128)(2,1)S(1)}, u32[]{:S(2)}, u32[]{:S(2)}) collective-permute-start(bf16[2048,128]{1,0:T(8,128)(2,1)S(1)} %get-tuple-element.101), channel_id=1, source_target_pairs={{0,12},{1,13},{2,14},{3,15},{4,0},{5,1},{6,2},{7,3},{8,4},{9,5},{1... | collective-permute-start | bytes 1572872 | tf_op jit(solution)/shard_map/ppermute | solution.py:321
  101.7 10.1 %collective-permute-start.30 = (f32[136,256]{1,0:T(8,128)S(1)}, f32[136,256]{1,0:T(8,128)S(1)}, u32[]{:S(2)}, u32[]{:S(2)}) collective-permute-start(f32[136,256]{1,0:T(8,128)S(1)} %add.17.s0), channel_id=1, source_target_pairs={{0,12},{1,13},{2,14},{3,15},{4,0},{5,1},{6,2},{7,3},{8,4},{9,5},{1... | collective-permute-start | bytes 417800 | tf_op jit(solution)/shard_map/ppermute | solution.py:321
  101.7 10.1 %collective-permute-start.29 = (f32[136,256]{1,0:T(8,128)S(1)}, f32[136,256]{1,0:T(8,128)S(1)}, u32[]{:S(2)}, u32[]{:S(2)}) collective-permute-start(f32[136,256]{1,0:T(8,128)S(1)} %add.17.s0), channel_id=1, source_target_pairs={{0,8},{1,9},{2,10},{3,11},{4,12},{5,13},{6,14},{7,15},{8,0},{9,1},... | collective-permute-start | bytes 417800 | tf_op jit(solution)/shard_map/ppermute | solution.py:321
  102.4 9.5 %collective-permute-start.28 = (f32[136,256]{1,0:T(8,128)S(1)}, f32[136,256]{1,0:T(8,128)S(1)}, u32[]{:S(2)}, u32[]{:S(2)}) collective-permute-start(f32[136,256]{1,0:T(8,128)S(1)} %add.17.s0), channel_id=1, source_target_pairs={{0,4},{1,5},{2,6},{3,7},{4,8},{5,9},{6,10},{7,11},{8,12},{9,13},{1... | collective-permute-start | bytes 417800 | tf_op jit(solution)/shard_map/ppermute | solution.py:321
  111.9 4.0 %collective-permute-start.31 = (f32[136,256]{1,0:T(8,128)S(1)}, f32[136,256]{1,0:T(8,128)S(1)}, u32[]{:S(2)}, u32[]{:S(2)}) collective-permute-start(f32[136,256]{1,0:T(8,128)S(1)} %sum_u.1), channel_id=1, source_target_pairs={{0,1},{1,0},{2,3},{3,2},{4,5},{5,4},{6,7},{7,6},{8,9},{9,8},{10,11... | collective-permute-start | bytes 417800 | tf_op jit(solution)/shard_map/ppermute | solution.py:321
  112.0 9.4 %collective-permute-start.25 = (bf16[1024,128]{1,0:T(8,128)(2,1)S(1)}, bf16[1024,128]{1,0:T(8,128)(2,1)S(1)}, u32[]{:S(2)}, u32[]{:S(2)}) collective-permute-start(bf16[1024,128]{1,0:T(8,128)(2,1)S(1)} %get-tuple-element.103), channel_id=1, source_target_pairs={{0,32},{1,33},{2,34},{3,35},{4,36},{5,37},{6,38},{7,39},{8,40},{9,... | collective-permute-start | bytes 786440 | tf_op jit(solution)/shard_map/ppermute | solution.py:321
  113.1 8.3 %collective-permute-start.26 = (bf16[1024,128]{1,0:T(8,128)(2,1)S(1)}, bf16[1024,128]{1,0:T(8,128)(2,1)S(1)}, u32[]{:S(2)}, u32[]{:S(2)}) collective-permute-start(bf16[1024,128]{1,0:T(8,128)(2,1)S(1)} %get-tuple-element.104), channel_id=1, source_target_pairs={{0,64},{1,65},{2,66},{3,67},{4,68},{5,69},{6,70},{7,71},{8,72},{9,... | collective-permute-start | bytes 786440 | tf_op jit(solution)/shard_map/ppermute | solution.py:321
  113.3 11.9 %collective-permute-start.27 = (bf16[1024,128]{1,0:T(8,128)(2,1)S(1)}, bf16[1024,128]{1,0:T(8,128)(2,1)S(1)}, u32[]{:S(2)}, u32[]{:S(2)}) collective-permute-start(bf16[1024,128]{1,0:T(8,128)(2,1)S(1)} %get-tuple-element.105), channel_id=1, source_target_pairs={{0,96},{1,97},{2,98},{3,99},{4,100},{5,101},{6,102},{7,103},{8,104... | collective-permute-start | bytes 786440 | tf_op jit(solution)/shard_map/ppermute | solution.py:321
  115.9 5.5 %collective-permute-start.32 = (f32[136,256]{1,0:T(8,128)S(1)}, f32[136,256]{1,0:T(8,128)S(1)}, u32[]{:S(2)}, u32[]{:S(2)}) collective-permute-start(f32[136,256]{1,0:T(8,128)S(1)} %add.18), channel_id=1, source_target_pairs={{0,2},{1,3},{2,0},{3,1},{4,6},{5,7},{6,4},{7,5},{8,10},{9,11},{10,... | collective-permute-start | bytes 417800 | tf_op jit(solution)/shard_map/ppermute | solution.py:321
  125.1 5.4 %collective-permute-start.34 = (f32[136,256]{1,0:T(8,128)S(1)}, f32[136,256]{1,0:T(8,128)S(1)}, u32[]{:S(2)}, u32[]{:S(2)}) collective-permute-start(f32[136,256]{1,0:T(8,128)S(1)} %add.19.mine), channel_id=1, source_target_pairs={{0,16},{1,17},{2,18},{3,19},{4,20},{5,21},{6,22},{7,23},{8,24},{9,... | collective-permute-start | bytes 417800 | tf_op jit(solution)/shard_map/ppermute | solution.py:321
  129.1 1.4 %collective-permute-start.33 = (bf16[512,128]{1,0:T(8,128)(2,1)S(1)}, bf16[512,128]{1,0:T(8,128)(2,1)S(1)}, u32[]{:S(2)}, u32[]{:S(2)}) collective-permute-start(bf16[512,128]{1,0:T(8,128)(2,1)S(1)} %get-tuple-element.111), channel_id=1, source_target_pairs={{0,16},{1,17},{2,18},{3,19},{4,20},{5,21},{6,22},{7,23},{8,24},{9,... | collective-permute-start | bytes 393224 | tf_op jit(solution)/shard_map/ppermute | solution.py:321

commit v5 on v4

--- a/solution.py
+++ b/solution.py
@@ -168,31 +168,29 @@
 def near_kernel(*refs):
     tiles = (refs[0:2], refs[2:4])
     panel = refs[4]
-    outs = dict(zip((1, 3, 0), refs[5:8]))
-    acc = refs[8]
-    u, v, y, c = coords()
-    for p, out in outs.items():
+    outs = {1: refs[5:7], 3: refs[7:9], 0: refs[9:11]}
+    acc = refs[11]
+    u, v, y, c = coords()
+    for p, halves in outs.items():
         for r in range(4):
             for t in range(2):
                 ids, values = tiles[t]
                 forward_group(ids, values, panel, acc.at[t], target_group(u, v, c, p, r))
-                start = (r * 2 + t) * ROWS
-                out[start:start + ROWS, :] = acc[t].astype(BF)
-
-
-def relay_kernel(*refs):
-    for n in range(2):
-        own, extra, out = refs[n], refs[2 + n], refs[4 + n]
-        mixed = pl.ds(n * 4 * ROWS, 4 * ROWS)
-        plain = pl.ds((1 - n) * 4 * ROWS, 4 * ROWS)
-        out[mixed, :] = (own[mixed, :].astype(F32) + extra[...].astype(F32)).astype(BF)
-        out[plain, :] = own[plain, :]
+                start = ((r % 2) * 2 + t) * ROWS
+                halves[r // 2][start:start + ROWS, :] = acc[t].astype(BF)
+
+
+def relay_kernel(own1, own3, extra1, extra3, out1, out3):
+    out1[...] = (own1[...].astype(F32) + extra1[...].astype(F32)).astype(BF)
+    out3[...] = (own3[...].astype(F32) + extra3[...].astype(F32)).astype(BF)
 
 
 def stage_kernel(*refs):
-    for n, out in enumerate(refs[3:]):
-        here = pl.ds(n * 2 * ROWS, 2 * ROWS)
-        p0, p1, p3 = (part[here, :].astype(F32) for part in refs[:3])
+    for n, out in enumerate(refs[6:]):
+        here = pl.ds((n % 2) * 2 * ROWS, 2 * ROWS)
+        p0, p1, p3 = (
+            part[here, :].astype(F32) for part in refs[3 * (n // 2):3 * (n // 2) + 3]
+        )
         out[...] = (p0 + (p1 + p3)).astype(BF)
 
 
@@ -240,9 +238,10 @@
         out[HALF:, :] = jnp.broadcast_to(bias_grad, (8, F))
 
 
-def cut_kernel(left, right, low, high):
-    low[...] = left[:4 * ROWS, :]
-    high[...] = right[4 * ROWS:, :]
+def join_kernel(*refs):
+    for n in range(4):
+        start = (n % 2) * 2 * ROWS
+        refs[4 + n // 2][start:start + 2 * ROWS, :] = refs[n][...]
 
 
 def backward_group(ids, values, acc, part, base, group):
@@ -258,16 +257,17 @@
 
 def early_kernel(*refs):
     tiles = (refs[0:2], refs[2:4])
-    parts = dict(zip((0, 1, 3), refs[4:7]))
-    acc = refs[7]
+    parts = {0: refs[4:6], 1: refs[6:8], 3: refs[8:10]}
+    acc = refs[10]
     u, v, y, c = coords()
     acc[...] = jnp.zeros_like(acc)
-    for p, part in parts.items():
+    for p, halves in parts.items():
         for r in range(4):
             for t in range(2):
                 ids, values = tiles[t]
                 group = source_group(u, v, c, p, r)
-                backward_group(ids, values, acc, part, (r * 2 + t) * ROWS, group)
+                base = ((r % 2) * 2 + t) * ROWS
+                backward_group(ids, values, acc, halves[r // 2], base, group)
 
 
 def late_kernel(*refs):
@@ -393,19 +393,21 @@
         scratch=[pltpu.VMEM((2, ROWS, HALF), F32), pltpu.SemaphoreType.DMA((8,))],
     )
     extra = [along_u(low, 1), along_u(high, 3)]
-    p1, p3, p0 = local_call(
-        near_kernel, "forward_near", tile_specs + [vmem()], [shape(8 * ROWS)] * 3,
+    half = shape(4 * ROWS)
+    near1, plain1, plain3, near3, home1, home3 = local_call(
+        near_kernel, "forward_near", tile_specs + [vmem()], [half] * 6,
         tiles + [panel], 8, flops=3 * slab // 2, moved=10 * MIB,
         scratch=[pltpu.VMEM((2, ROWS, HALF), F32)],
     )
-    p1, p3 = local_call(
-        relay_kernel, "relay_sum", [vmem()] * 4, [shape(8 * ROWS)] * 2,
-        [p1, p3] + extra, 8, flops=8 * ROWS * HALF, moved=5 * MIB,
+    plain1, plain3 = along_u(plain1, 1), along_u(plain3, 3)
+    mixed1, mixed3 = local_call(
+        relay_kernel, "relay_sum", [vmem()] * 4, [half] * 2, [near1, near3] + extra, 8,
+        flops=8 * ROWS * HALF, moved=3 * MIB,
     )
     sums = local_call(
-        stage_kernel, "stage_sum", [vmem()] * 3, [shape(2 * ROWS)] * 4,
-        [p0, along_u(p1, 1), along_u(p3, 3)], 8, flops=16 * ROWS * HALF,
-        moved=4 * MIB,
+        stage_kernel, "stage_sum", [vmem()] * 6, [shape(2 * ROWS)] * 4,
+        [home1, along_u(mixed1, 1), plain3, home3, plain1, along_u(mixed3, 3)], 8,
+        flops=16 * ROWS * HALF, moved=4 * MIB,
     )
     own, other = finish_call(exchange(sums, along_v), "aggregate")
     out_act, keep_g, give_g, keep_w, give_w = local_call(
@@ -425,19 +427,19 @@
     firsts = spread(grads, along_v)
     piece = with_y(keep_w + piece, 1)
     *firsts, piece = lax.optimization_barrier((*firsts, piece))
-    join = stack_call(firsts, "join")
-    left, right = along_u(join, 1), along_u(join, 3)
+    join1, join3 = local_call(
+        join_kernel, "join", [vmem()] * 4, [half] * 2, firsts, 8,
+    )
+    left1, right3 = along_u(join1, 1), along_u(join3, 3)
+    left3, right1 = along_u(join3, 1), along_u(join1, 3)
+    far = [along_u(left1, 1), along_u(right3, 3)]
     piece = with_y(piece, 2)
-    gate = lax.optimization_barrier((left, right, piece))
-    left, right = gate[:2]
+    left3, piece = lax.optimization_barrier((left3, piece))
     s0, s1, s2, s3 = spread(piece, along_u)
-    low, high = local_call(
-        cut_kernel, "cut", [vmem()] * 2, [shape(4 * ROWS)] * 2, [left, right], 8,
-    )
-    far = [along_u(low, 1), along_u(high, 3)]
     (start,) = local_call(
-        early_kernel, "backward_early", tile_specs + [vmem()] * 3,
-        [shape(8 * ROWS, HALF, F32)], tiles + [join, left, right], 8,
+        early_kernel, "backward_early", tile_specs + [vmem()] * 6,
+        [shape(8 * ROWS, HALF, F32)],
+        tiles + [join1, join3, left1, left3, right1, right3], 8,
         flops=3 * slab // 2, moved=10 * MIB,
     )
     outs = local_call(

time: 132 us -> 124 us (0.939)
  waiting for transfers between devices: 67.4 us -> 48.7 us
  starting transfers between devices: 40.4 us -> 51.7 us
    ppermute x35 -> x39, waiting for transfers between devices: 67.4 us -> 48.7 us  [permute(): return lax.ppermute(value, ('row', 'col'), pairs)]
    ppermute x35 -> x39, starting transfers between devices: 40.4 us -> 51.7 us  [permute(): return lax.ppermute(value, ('row', 'col'), pairs)]
    pallas_call x18 -> x17, Pallas kernels: 15.7 us -> 15.7 us  [local_call(): pl.pallas_call(kernel, out_shape=outs, in_specs=ins, out_specs=[vmem()] *...]
  transfers between devices with their start and end apart: 35 -> 39, of which waited for: 21 -> 21; matrix products, arithmetic and copies ran while one was open for 0% -> 0% of each run, Pallas kernels for 7% -> 8%
where the time goes in v5:
time: 124 us
  starting transfers between devices  51.7 us (42%)
  waiting for transfers between devices  48.7 us (39%)
  Pallas kernels  15.7 us (13%)
  local copies, waits for them, and re-layouts  6.97 us (6%)
    ppermute x39, starting transfers between devices, permute(): return lax.ppermute(value, ('row', 'col'), pairs)  51.7 us
    ppermute x39, waiting for transfers between devices, permute(): return lax.ppermute(value, ('row', 'col'), pairs)  48.7 us
    pallas_call x17, Pallas kernels, local_call(): pl.pallas_call(kernel, out_shape=outs, in_specs=ins, out_specs=[vmem()] *...  15.7 us
    unnamed x14, local copies, waits for them, and re-layouts  6.97 us
  transfers between devices with their start and end apart: 39, of which 21 were waited for; matrix products, arithmetic and copies ran while one was open for 0% of the time, Pallas kernels for 8%

profile of v5, /device:TPU:1, one launch (start us, length us, event | category | flops | bytes accessed | tf_op | source)
XLA Modules:
  0.0 124.0 jit_solution(1657590080913719281)
XLA Ops:
  0.6 0.9 copy-done.2
  1.6 1.5 %collective-permute-start = (bf16[512,128]{1,0:T(8,128)(2,1)S(1)}, bf16[512,128]{1,0:T(8,128)(2,1)S(1)}, u32[]{:S(2)}, u32[]{:S(2)}) collective-permute-start(bf16[512,128]{1,0:T(8,128)(2,1)S(1)} %get-tuple-element.63), channel_id=1, source_target_pairs={{0,16},{1,17},{2,18},{3,19},{4,20},{5,21},{6,22},{7,23},{8,24},{9,... | collective-permute-start | bytes 393224 | tf_op jit(solution)/shard_map/ppermute | solution.py:321
  3.1 1.0 collective-permute-done.refs_1_
  4.1 0.4 collective-permute-start.3
  4.5 2.9 %collective-permute-start.1 = (bf16[1024,128]{1,0:T(8,128)(2,1)S(1)}, bf16[1024,128]{1,0:T(8,128)(2,1)S(1)}, u32[]{:S(2)}, u32[]{:S(2)}) collective-permute-start(bf16[1024,128]{1,0:T(8,128)(2,1)S(1)} %pair.1.refs_4_), channel_id=1, source_target_pairs={{0,32},{1,33},{2,34},{3,35},{4,36},{5,37},{6,38},{7,39},{8,40},{9,... | collective-permute-start | bytes 786440 | tf_op jit(solution)/shard_map/ppermute | solution.py:321
  7.4 0.3 collective-permute-start.4
  7.7 0.7 collective-permute-start.5
  8.4 0.7 copy-done.5
  9.1 0.7 copy-done.6
  9.7 2.2 %collective-permute-start.2 = (s32[2,128]{1,0:T(2,128)S(1)}, s32[2,128]{1,0:T(2,128)S(1)}, u32[]{:S(2)}, u32[]{:S(2)}) collective-permute-start(s32[2,128]{1,0:T(2,128)S(1)} %ids.1.refs_0_), channel_id=1, source_target_pairs={{0,16},{1,17},{2,18},{3,19},{4,20},{5,21},{6,22},{7,23},{8,24},{9,... | collective-permute-start | bytes 3080 | tf_op jit(solution)/shard_map/ppermute | solution.py:321
  11.9 2.2 %copy-done = bf16[1,1,128,128,128]{4,3,2,1,0:T(8,128)(2,1)S(1)} copy-done((bf16[1,1,128,128,128]{4,3,2,1,0:T(8,128)(2,1)S(1)}, bf16[1,1,128,128,128]{4,3,2,1,0:T(8,128)(2,1)}, u32[]{:S(2)}) %copy-start) | copy-done | bytes 4194328
  14.1 0.9 copy-done.1
  15.1 0.9 copy-done.3
  16.0 0.7 copy-done.4
  16.7 0.5 prologue.1
  17.2 0.6 collective-permute-done.1.refs_5_
  17.8 2.4 %collective-permute-done.5.refs_7_ = bf16[1024,128]{1,0:T(8,128)(2,1)S(1)} collective-permute-done((bf16[1024,128]{1,0:T(8,128)(2,1)S(1)}, bf16[1024,128]{1,0:T(8,128)(2,1)S(1)}, u32[]{:S(2)}, u32[]{:S(2)}) %collective-permute-start.5) | collective-permute-done | bytes 262176 | tf_op jit(solution)/shard_map/ppermute | solution.py:321
  20.2 3.1 %forward_far.1 = (bf16[4096,128]{1,0:T(8,128)(2,1)S(1)}, bf16[2048,128]{1,0:T(8,128)(2,1)S(1)}, bf16[2048,128]{1,0:T(8,128)(2,1)S(1)}) custom-call(s32[2,128]{1,0:T(2,128)S(1)} %ids.1.refs_0_, bf16[128,128,128]{2,1,0:T(8,128)(2,1)S(1)} %get-tuple-element.70.refs_1_, s32[2,128]{1,0:T(2,128)S(1)} %collective-permute-done.2.refs_2_, ...), custom_call_target="tpu_custom_call" | custom-call | flops 268435456 | bytes 6291456 | tf_op jit(solution)/shard_map/forward_far/pallas_call | solution.py:58
  23.3 1.9 %collective-permute-start.6 = (bf16[2048,128]{1,0:T(8,128)(2,1)S(1)}, bf16[2048,128]{1,0:T(8,128)(2,1)S(1)}, u32[]{:S(2)}, u32[]{:S(2)}) collective-permute-start(bf16[2048,128]{1,0:T(8,128)(2,1)S(1)} %get-tuple-element.76), channel_id=1, source_target_pairs={{0,4},{1,5},{2,6},{3,7},{4,8},{5,9},{6,10},{7,11},{8,12},{9,13},{1... | collective-permute-start | bytes 1572872 | tf_op jit(solution)/shard_map/ppermute | solution.py:321
  25.2 2.2 %collective-permute-start.7 = (bf16[2048,128]{1,0:T(8,128)(2,1)S(1)}, bf16[2048,128]{1,0:T(8,128)(2,1)S(1)}, u32[]{:S(2)}, u32[]{:S(2)}) collective-permute-start(bf16[2048,128]{1,0:T(8,128)(2,1)S(1)} %get-tuple-element.77), channel_id=1, source_target_pairs={{0,12},{1,13},{2,14},{3,15},{4,0},{5,1},{6,2},{7,3},{8,4},{9,5},{1... | collective-permute-start | bytes 1572872 | tf_op jit(solution)/shard_map/ppermute | solution.py:321
  27.4 3.8 %forward_near.1 = (bf16[2048,128]{1,0:T(8,128)(2,1)S(1)}, bf16[2048,128]{1,0:T(8,128)(2,1)S(1)}, bf16[2048,128]{1,0:T(8,128)(2,1)S(1)}, bf16[2048,128]{1,0:T(8,1...) custom-call(s32[2,128]{1,0:T(2,128)S(1)} %ids.1.refs_0_, ...), custom_call_target="tpu_custom_call" | custom-call | flops 805306368 | bytes 10485760 | tf_op jit(solution)/shard_map/forward_near/pallas_call | solution.py:58
  31.2 1.4 %collective-permute-start.9 = (bf16[2048,128]{1,0:T(8,128)(2,1)S(1)}, bf16[2048,128]{1,0:T(8,128)(2,1)S(1)}, u32[]{:S(2)}, u32[]{:S(2)}) collective-permute-start(bf16[2048,128]{1,0:T(8,128)(2,1)S(1)} %get-tuple-element.79), channel_id=1, source_target_pairs={{0,12},{1,13},{2,14},{3,15},{4,0},{5,1},{6,2},{7,3},{8,4},{9,5},{1... | collective-permute-start | bytes 1572872 | tf_op jit(solution)/shard_map/ppermute | solution.py:321
  32.8 1.4 %collective-permute-done.6.extra1 = bf16[2048,128]{1,0:T(8,128)(2,1)S(1)} collective-permute-done((bf16[2048,128]{1,0:T(8,128)(2,1)S(1)}, bf16[2048,128]{1,0:T(8,128)(2,1)S(1)}, u32[]{:S(2)}, u32[]{:S(2)}) %collective-permute-start.6) | collective-permute-done | bytes 524320 | tf_op jit(solution)/shard_map/ppermute | solution.py:321
  34.4 1.1 collective-permute-start.8
  35.5 1.9 %collective-permute-start.11 = (bf16[2048,128]{1,0:T(8,128)(2,1)S(1)}, bf16[2048,128]{1,0:T(8,128)(2,1)S(1)}, u32[]{:S(2)}, u32[]{:S(2)}) collective-permute-start(bf16[2048,128]{1,0:T(8,128)(2,1)S(1)} %get-tuple-element.82), channel_id=1, source_target_pairs={{0,12},{1,13},{2,14},{3,15},{4,0},{5,1},{6,2},{7,3},{8,4},{9,5},{1... | collective-permute-start | bytes 1572872 | tf_op jit(solution)/shard_map/ppermute | solution.py:321
  37.3 2.3 %collective-permute-done.9.refs_2_ = bf16[2048,128]{1,0:T(8,128)(2,1)S(1)} collective-permute-done((bf16[2048,128]{1,0:T(8,128)(2,1)S(1)}, bf16[2048,128]{1,0:T(8,128)(2,1)S(1)}, u32[]{:S(2)}, u32[]{:S(2)}) %collective-permute-start.9) | collective-permute-done | bytes 524320 | tf_op jit(solution)/shard_map/ppermute | solution.py:321
  39.6 2.6 %collective-permute-done.10.refs_4_ = bf16[2048,128]{1,0:T(8,128)(2,1)S(1)} collective-permute-done((bf16[2048,128]{1,0:T(8,128)(2,1)S(1)}, bf16[2048,128]{1,0:T(8,128)(2,1)S(1)}, u32[]{:S(2)}, u32[]{:S(2)}) %collective-permute-start.10) | collective-permute-done | bytes 524320 | tf_op jit(solution)/shard_map/ppermute | solution.py:321
  42.2 5.6 %collective-permute-done.8.refs_1_ = bf16[2048,128]{1,0:T(8,128)(2,1)S(1)} collective-permute-done((bf16[2048,128]{1,0:T(8,128)(2,1)S(1)}, bf16[2048,128]{1,0:T(8,128)(2,1)S(1)}, u32[]{:S(2)}, u32[]{:S(2)}) %collective-permute-start.8) | collective-permute-done | bytes 524320 | tf_op jit(solution)/shard_map/ppermute | solution.py:321
  47.8 0.4 stage_sum.1
  48.2 1.0 collective-permute-start.12
  49.2 2.5 %collective-permute-start.13 = (bf16[1024,128]{1,0:T(8,128)(2,1)S(1)}, bf16[1024,128]{1,0:T(8,128)(2,1)S(1)}, u32[]{:S(2)}, u32[]{:S(2)}) collective-permute-start(bf16[1024,128]{1,0:T(8,128)(2,1)S(1)} %get-tuple-element.85), channel_id=1, source_target_pairs={{0,2},{1,3},{2,0},{3,1},{4,6},{5,7},{6,4},{7,5},{8,10},{9,11},{10,... | collective-permute-start | bytes 786440 | tf_op jit(solution)/shard_map/ppermute | solution.py:321
  51.7 1.1 collective-permute-start.14
  52.8 2.2 %collective-permute-done.12.refs_1_ = bf16[1024,128]{1,0:T(8,128)(2,1)S(1)} collective-permute-done((bf16[1024,128]{1,0:T(8,128)(2,1)S(1)}, bf16[1024,128]{1,0:T(8,128)(2,1)S(1)}, u32[]{:S(2)}, u32[]{:S(2)}) %collective-permute-start.12) | collective-permute-done | bytes 262176 | tf_op jit(solution)/shard_map/ppermute | solution.py:321
  55.0 3.2 %collective-permute-done.13.refs_2_ = bf16[1024,128]{1,0:T(8,128)(2,1)S(1)} collective-permute-done((bf16[1024,128]{1,0:T(8,128)(2,1)S(1)}, bf16[1024,128]{1,0:T(8,128)(2,1)S(1)}, u32[]{:S(2)}, u32[]{:S(2)}) %collective-permute-start.13) | collective-permute-done | bytes 262176 | tf_op jit(solution)/shard_map/ppermute | solution.py:321
  58.5 3.6 %collective-permute-start.15 = (bf16[512,128]{1,0:T(8,128)(2,1)S(1)}, bf16[512,128]{1,0:T(8,128)(2,1)S(1)}, u32[]{:S(2)}, u32[]{:S(2)}) collective-permute-start(bf16[512,128]{1,0:T(8,128)(2,1)S(1)} %get-tuple-element.88), channel_id=1, source_target_pairs={{0,16},{1,17},{2,18},{3,19},{4,20},{5,21},{6,22},{7,23},{8,24},{9,... | collective-permute-start | bytes 393224 | tf_op jit(solution)/shard_map/ppermute | solution.py:321
  62.1 1.0 collective-permute-done.15.refs_1_
  63.1 1.2 pointwise.1
  64.3 0.4 collective-permute-start.17
  64.8 1.2 collective-permute-done.16.refs_1_
  66.0 0.3 collective-permute-start.18
  66.3 1.1 collective-permute-start.19
  67.3 1.6 %collective-permute-start.20 = (bf16[1024,128]{1,0:T(8,128)(2,1)S(1)}, bf16[1024,128]{1,0:T(8,128)(2,1)S(1)}, u32[]{:S(2)}, u32[]{:S(2)}) collective-permute-start(bf16[1024,128]{1,0:T(8,128)(2,1)S(1)} %pair_grads.1.refs_0_), channel_id=1, source_target_pairs={{0,3},{1,0},{2,1},{3,2},{4,7},{5,4},{6,5},{7,6},{8,11},{9,8},{10,9... | collective-permute-start | bytes 786440 | tf_op jit(solution)/shard_map/ppermute | solution.py:321
  69.1 4.2 %collective-permute-done.21 = f32[136,256]{1,0:T(8,128)S(1)} collective-permute-done((f32[136,256]{1,0:T(8,128)S(1)}, f32[136,256]{1,0:T(8,128)S(1)}, u32[]{:S(2)}, u32[]{:S(2)}) %collective-permute-start.21) | collective-permute-done | bytes 139296 | tf_op jit(solution)/shard_map/ppermute | solution.py:321
  73.3 2.5 %collective-permute-done.18.refs_1_ = bf16[1024,128]{1,0:T(8,128)(2,1)S(1)} collective-permute-done((bf16[1024,128]{1,0:T(8,128)(2,1)S(1)}, bf16[1024,128]{1,0:T(8,128)(2,1)S(1)}, u32[]{:S(2)}, u32[]{:S(2)}) %collective-permute-start.18) | collective-permute-done | bytes 262176 | tf_op jit(solution)/shard_map/ppermute | solution.py:321
  75.8 0.6 collective-permute-done.20.refs_3_
  76.5 1.3 %collective-permute-start.22 = (bf16[2048,128]{1,0:T(8,128)(2,1)S(1)}, bf16[2048,128]{1,0:T(8,128)(2,1)S(1)}, u32[]{:S(2)}, u32[]{:S(2)}) collective-permute-start(bf16[2048,128]{1,0:T(8,128)(2,1)S(1)} %get-tuple-element.103.refs_4_), channel_id=1, source_target_pairs={{0,4},{1,5},{2,6},{3,7},{4,8},{5,9},{6,10},{7,11},{8,12},{9,13},{1... | collective-permute-start | bytes 1572872 | tf_op jit(solution)/shard_map/ppermute | solution.py:321
  77.8 1.4 %collective-permute-start.26 = (bf16[2048,128]{1,0:T(8,128)(2,1)S(1)}, bf16[2048,128]{1,0:T(8,128)(2,1)S(1)}, u32[]{:S(2)}, u32[]{:S(2)}) collective-permute-start(bf16[2048,128]{1,0:T(8,128)(2,1)S(1)} %get-tuple-element.104.refs_5_), channel_id=1, source_target_pairs={{0,12},{1,13},{2,14},{3,15},{4,0},{5,1},{6,2},{7,3},{8,4},{9,5},{1... | collective-permute-start | bytes 1572872 | tf_op jit(solution)/shard_map/ppermute | solution.py:321
  79.3 2.7 %collective-permute-start.25 = (bf16[2048,128]{1,0:T(8,128)(2,1)S(1)}, bf16[2048,128]{1,0:T(8,128)(2,1)S(1)}, u32[]{:S(2)}, u32[]{:S(2)}) collective-permute-start(bf16[2048,128]{1,0:T(8,128)(2,1)S(1)} %get-tuple-element.103.refs_4_), channel_id=1, source_target_pairs={{0,12},{1,13},{2,14},{3,15},{4,0},{5,1},{6,2},{7,3},{8,4},{9,5},{1... | collective-permute-start | bytes 1572872 | tf_op jit(solution)/shard_map/ppermute | solution.py:321
  81.9 4.2 %collective-permute-done.22.refs_6_ = bf16[2048,128]{1,0:T(8,128)(2,1)S(1)} collective-permute-done((bf16[2048,128]{1,0:T(8,128)(2,1)S(1)}, bf16[2048,128]{1,0:T(8,128)(2,1)S(1)}, u32[]{:S(2)}, u32[]{:S(2)}) %collective-permute-start.22) | collective-permute-done | bytes 524320 | tf_op jit(solution)/shard_map/ppermute | solution.py:321
  86.1 2.7 %collective-permute-start.28 = (bf16[2048,128]{1,0:T(8,128)(2,1)S(1)}, bf16[2048,128]{1,0:T(8,128)(2,1)S(1)}, u32[]{:S(2)}, u32[]{:S(2)}) collective-permute-start(bf16[2048,128]{1,0:T(8,128)(2,1)S(1)} %collective-permute-done.26.refs_9_), channel_id=1, source_target_pairs={{0,12},{1,13},{2,14},{3,15},{4,0},{5,1},{6,2},{7,3},{8,4},{9,5},{1... | collective-permute-start | bytes 1572872 | tf_op jit(solution)/shard_map/ppermute | solution.py:321
  88.8 1.0 collective-permute-start.24
  89.8 4.4 %collective-permute-done.24 = f32[136,256]{1,0:T(8,128)S(1)} collective-permute-done((f32[136,256]{1,0:T(8,128)S(1)}, f32[136,256]{1,0:T(8,128)S(1)}, u32[]{:S(2)}, u32[]{:S(2)}) %collective-permute-start.24) | collective-permute-done | bytes 139296 | tf_op jit(solution)/shard_map/ppermute | solution.py:321
  94.3 1.2 collective-permute-start.33
  95.5 1.5 %collective-permute-start.34 = (f32[136,256]{1,0:T(8,128)S(1)}, f32[136,256]{1,0:T(8,128)S(1)}, u32[]{:S(2)}, u32[]{:S(2)}) collective-permute-start(f32[136,256]{1,0:T(8,128)S(1)} %add.17.s0), channel_id=1, source_target_pairs={{0,12},{1,13},{2,14},{3,15},{4,0},{5,1},{6,2},{7,3},{8,4},{9,5},{1... | collective-permute-start | bytes 417800 | tf_op jit(solution)/shard_map/ppermute | solution.py:321
  97.0 3.3 %backward_early.1.refs_4_ = f32[4096,128]{1,0:T(8,128)S(1)} custom-call(s32[2,128]{1,0:T(2,128)S(1)} %ids.1.refs_0_, bf16[128,128,128]{2,1,0:T(8,128)(2,1)S(1)} %get-tuple-element.70.refs_1_, s32[2,128]{1,0:T(2,128)S(1)} %collective-permute-done.2.refs_2_, bf16[128,128,128]{2,1,0:T(8,128)(2,1)S(1)} %collective-permute-done.3.refs_3_, ...), custom_call_target="tpu_custom_call" | custom-call | flops 805306368 | bytes 10485760 | tf_op jit(solution)/shard_map/backward_early/pallas_call | solution.py:58
  100.3 1.8 %backward_late.1 = (bf16[1024,128]{1,0:T(8,128)(2,1)S(1)}, bf16[1024,128]{1,0:T(8,128)(2,1)S(1)}, bf16[1024,128]{1,0:T(8,128)(2,1)S(1)}, bf16[1024,128]{1,0:T(8,128)(2,1)S(1)}) custom-call(s32[2,128]{1,0:T(2,128)S(1)} %ids.1.refs_0_, bf16[128,128,128]{2,1,0:T(8,128)(2,1)S(1)} %get-tuple-element.70.refs_1_, s32[2,128]{1,0:T(2,128)S(1)} %collective-permute-done.2.refs_2_, ...), custom_call_target="tpu_custom_call" | custom-call | flops 268435456 | bytes 6291456 | tf_op jit(solution)/shard_map/backward_late/pallas_call | solution.py:58
  102.2 2.1 %collective-permute-start.29 = (bf16[1024,128]{1,0:T(8,128)(2,1)S(1)}, bf16[1024,128]{1,0:T(8,128)(2,1)S(1)}, u32[]{:S(2)}, u32[]{:S(2)}) collective-permute-start(bf16[1024,128]{1,0:T(8,128)(2,1)S(1)} %get-tuple-element.108), channel_id=1, source_target_pairs={{0,32},{1,33},{2,34},{3,35},{4,36},{5,37},{6,38},{7,39},{8,40},{9,... | collective-permute-start | bytes 786440 | tf_op jit(solution)/shard_map/ppermute | solution.py:321
  104.3 0.7 collective-permute-start.31
  105.0 2.8 %collective-permute-done.35 = f32[136,256]{1,0:T(8,128)S(1)} collective-permute-done((f32[136,256]{1,0:T(8,128)S(1)}, f32[136,256]{1,0:T(8,128)S(1)}, u32[]{:S(2)}, u32[]{:S(2)}) %collective-permute-start.35) | collective-permute-done | bytes 139296 | tf_op jit(solution)/shard_map/ppermute | solution.py:321
  107.9 0.7 collective-permute-start.36
  108.5 4.8 %collective-permute-done.36 = f32[136,256]{1,0:T(8,128)S(1)} collective-permute-done((f32[136,256]{1,0:T(8,128)S(1)}, f32[136,256]{1,0:T(8,128)S(1)}, u32[]{:S(2)}, u32[]{:S(2)}) %collective-permute-start.36) | collective-permute-done | bytes 139296 | tf_op jit(solution)/shard_map/ppermute | solution.py:321
  113.6 8.0 %collective-permute-start.38 = (f32[136,256]{1,0:T(8,128)S(1)}, f32[136,256]{1,0:T(8,128)S(1)}, u32[]{:S(2)}, u32[]{:S(2)}) collective-permute-start(f32[136,256]{1,0:T(8,128)S(1)} %add.19.mine), channel_id=1, source_target_pairs={{0,16},{1,17},{2,18},{3,19},{4,20},{5,21},{6,22},{7,23},{8,24},{9,... | collective-permute-start | bytes 417800 | tf_op jit(solution)/shard_map/ppermute | solution.py:321
  121.8 1.3 %collective-permute-done.37.peer = bf16[512,128]{1,0:T(8,128)(2,1)S(1)} collective-permute-done((bf16[512,128]{1,0:T(8,128)(2,1)S(1)}, bf16[512,128]{1,0:T(8,128)(2,1)S(1)}, u32[]{:S(2)}, u32[]{:S(2)}) %collective-permute-start.37) | collective-permute-done | bytes 131104 | tf_op jit(solution)/shard_map/ppermute | solution.py:321
  123.2 0.9 last.1
  (50 shorter events, 1.8 us)
Async XLA Ops:
  0.6 1.0 copy-start.2
  1.6 2.5 %collective-permute-start = (bf16[512,128]{1,0:T(8,128)(2,1)S(1)}, bf16[512,128]{1,0:T(8,128)(2,1)S(1)}, u32[]{:S(2)}, u32[]{:S(2)}) collective-permute-start(bf16[512,128]{1,0:T(8,128)(2,1)S(1)} %get-tuple-element.63), channel_id=1, source_target_pairs={{0,16},{1,17},{2,18},{3,19},{4,20},{5,21},{6,22},{7,23},{8,24},{9,... | collective-permute-start | bytes 393224 | tf_op jit(solution)/shard_map/ppermute | solution.py:321
  4.1 16.0 %collective-permute-start.3 = (bf16[128,128,128]{2,1,0:T(8,128)(2,1)}, bf16[128,128,128]{2,1,0:T(8,128)(2,1)S(1)}, u32[]{:S(2)}, u32[]{:S(2)}) collective-permute-start(bf16[128,128,128]{2,1,0:T(8,128)(2,1)} %bitcast.5), channel_id=1, source_target_pairs={{0,16},{1,17},{2,18},{3,19},{4,20},{5,21},{6,22},{7,23},{8,24},{9,... | collective-permute-start | bytes 12582920 | tf_op jit(solution)/shard_map/ppermute | solution.py:321
  4.5 13.3 %collective-permute-start.1 = (bf16[1024,128]{1,0:T(8,128)(2,1)S(1)}, bf16[1024,128]{1,0:T(8,128)(2,1)S(1)}, u32[]{:S(2)}, u32[]{:S(2)}) collective-permute-start(bf16[1024,128]{1,0:T(8,128)(2,1)S(1)} %pair.1.refs_4_), channel_id=1, source_target_pairs={{0,32},{1,33},{2,34},{3,35},{4,36},{5,37},{6,38},{7,39},{8,40},{9,... | collective-permute-start | bytes 786440 | tf_op jit(solution)/shard_map/ppermute | solution.py:321
  7.4 10.4 %collective-permute-start.4 = (bf16[1024,128]{1,0:T(8,128)(2,1)S(1)}, bf16[1024,128]{1,0:T(8,128)(2,1)S(1)}, u32[]{:S(2)}, u32[]{:S(2)}) collective-permute-start(bf16[1024,128]{1,0:T(8,128)(2,1)S(1)} %pair.1.refs_4_), channel_id=1, source_target_pairs={{0,64},{1,65},{2,66},{3,67},{4,68},{5,69},{6,70},{7,71},{8,72},{9,... | collective-permute-start | bytes 786440 | tf_op jit(solution)/shard_map/ppermute | solution.py:321
  7.7 12.4 %collective-permute-start.5 = (bf16[1024,128]{1,0:T(8,128)(2,1)S(1)}, bf16[1024,128]{1,0:T(8,128)(2,1)S(1)}, u32[]{:S(2)}, u32[]{:S(2)}) collective-permute-start(bf16[1024,128]{1,0:T(8,128)(2,1)S(1)} %pair.1.refs_4_), channel_id=1, source_target_pairs={{0,96},{1,97},{2,98},{3,99},{4,100},{5,101},{6,102},{7,103},{8,104... | collective-permute-start | bytes 786440 | tf_op jit(solution)/shard_map/ppermute | solution.py:321
  8.4 0.7 copy-start.5
  9.1 0.7 copy-start.6
  9.7 8.1 %collective-permute-start.2 = (s32[2,128]{1,0:T(2,128)S(1)}, s32[2,128]{1,0:T(2,128)S(1)}, u32[]{:S(2)}, u32[]{:S(2)}) collective-permute-start(s32[2,128]{1,0:T(2,128)S(1)} %ids.1.refs_0_), channel_id=1, source_target_pairs={{0,16},{1,17},{2,18},{3,19},{4,20},{5,21},{6,22},{7,23},{8,24},{9,... | collective-permute-start | bytes 3080 | tf_op jit(solution)/shard_map/ppermute | solution.py:321
  11.9 2.2 %copy-start = (bf16[1,1,128,128,128]{4,3,2,1,0:T(8,128)(2,1)S(1)}, bf16[1,1,128,128,128]{4,3,2,1,0:T(8,128)(2,1)}, u32[]{:S(2)}) copy-start(bf16[1,1,128,128,128]{4,3,2,1,0:T(8,128)(2,1)} %param.8) | copy-start | bytes 12582916
  14.1 0.9 copy-start.1
  15.1 0.9 copy-start.3
  16.0 0.7 copy-start.4
  23.3 10.8 %collective-permute-start.6 = (bf16[2048,128]{1,0:T(8,128)(2,1)S(1)}, bf16[2048,128]{1,0:T(8,128)(2,1)S(1)}, u32[]{:S(2)}, u32[]{:S(2)}) collective-permute-start(bf16[2048,128]{1,0:T(8,128)(2,1)S(1)} %get-tuple-element.76), channel_id=1, source_target_pairs={{0,4},{1,5},{2,6},{3,7},{4,8},{5,9},{6,10},{7,11},{8,12},{9,13},{1... | collective-permute-start | bytes 1572872 | tf_op jit(solution)/shard_map/ppermute | solution.py:321
  25.2 8.9 %collective-permute-start.7 = (bf16[2048,128]{1,0:T(8,128)(2,1)S(1)}, bf16[2048,128]{1,0:T(8,128)(2,1)S(1)}, u32[]{:S(2)}, u32[]{:S(2)}) collective-permute-start(bf16[2048,128]{1,0:T(8,128)(2,1)S(1)} %get-tuple-element.77), channel_id=1, source_target_pairs={{0,12},{1,13},{2,14},{3,15},{4,0},{5,1},{6,2},{7,3},{8,4},{9,5},{1... | collective-permute-start | bytes 1572872 | tf_op jit(solution)/shard_map/ppermute | solution.py:321
  31.2 8.4 %collective-permute-start.9 = (bf16[2048,128]{1,0:T(8,128)(2,1)S(1)}, bf16[2048,128]{1,0:T(8,128)(2,1)S(1)}, u32[]{:S(2)}, u32[]{:S(2)}) collective-permute-start(bf16[2048,128]{1,0:T(8,128)(2,1)S(1)} %get-tuple-element.79), channel_id=1, source_target_pairs={{0,12},{1,13},{2,14},{3,15},{4,0},{5,1},{6,2},{7,3},{8,4},{9,5},{1... | collective-permute-start | bytes 1572872 | tf_op jit(solution)/shard_map/ppermute | solution.py:321
  32.7 9.5 %collective-permute-start.10 = (bf16[2048,128]{1,0:T(8,128)(2,1)S(1)}, bf16[2048,128]{1,0:T(8,128)(2,1)S(1)}, u32[]{:S(2)}, u32[]{:S(2)}) collective-permute-start(bf16[2048,128]{1,0:T(8,128)(2,1)S(1)} %get-tuple-element.81), channel_id=1, source_target_pairs={{0,4},{1,5},{2,6},{3,7},{4,8},{5,9},{6,10},{7,11},{8,12},{9,13},{1... | collective-permute-start | bytes 1572872 | tf_op jit(solution)/shard_map/ppermute | solution.py:321
  34.4 13.4 %collective-permute-start.8 = (bf16[2048,128]{1,0:T(8,128)(2,1)S(1)}, bf16[2048,128]{1,0:T(8,128)(2,1)S(1)}, u32[]{:S(2)}, u32[]{:S(2)}) collective-permute-start(bf16[2048,128]{1,0:T(8,128)(2,1)S(1)} %get-tuple-element.78), channel_id=1, source_target_pairs={{0,4},{1,5},{2,6},{3,7},{4,8},{5,9},{6,10},{7,11},{8,12},{9,13},{1... | collective-permute-start | bytes 1572872 | tf_op jit(solution)/shard_map/ppermute | solution.py:321
  35.5 12.4 %collective-permute-start.11 = (bf16[2048,128]{1,0:T(8,128)(2,1)S(1)}, bf16[2048,128]{1,0:T(8,128)(2,1)S(1)}, u32[]{:S(2)}, u32[]{:S(2)}) collective-permute-start(bf16[2048,128]{1,0:T(8,128)(2,1)S(1)} %get-tuple-element.82), channel_id=1, source_target_pairs={{0,12},{1,13},{2,14},{3,15},{4,0},{5,1},{6,2},{7,3},{8,4},{9,5},{1... | collective-permute-start | bytes 1572872 | tf_op jit(solution)/shard_map/ppermute | solution.py:321
  48.2 6.8 %collective-permute-start.12 = (bf16[1024,128]{1,0:T(8,128)(2,1)S(1)}, bf16[1024,128]{1,0:T(8,128)(2,1)S(1)}, u32[]{:S(2)}, u32[]{:S(2)}) collective-permute-start(bf16[1024,128]{1,0:T(8,128)(2,1)S(1)} %get-tuple-element.84), channel_id=1, source_target_pairs={{0,1},{1,2},{2,3},{3,0},{4,5},{5,6},{6,7},{7,4},{8,9},{9,10},{10,1... | collective-permute-start | bytes 786440 | tf_op jit(solution)/shard_map/ppermute | solution.py:321
  49.2 9.0 %collective-permute-start.13 = (bf16[1024,128]{1,0:T(8,128)(2,1)S(1)}, bf16[1024,128]{1,0:T(8,128)(2,1)S(1)}, u32[]{:S(2)}, u32[]{:S(2)}) collective-permute-start(bf16[1024,128]{1,0:T(8,128)(2,1)S(1)} %get-tuple-element.85), channel_id=1, source_target_pairs={{0,2},{1,3},{2,0},{3,1},{4,6},{5,7},{6,4},{7,5},{8,10},{9,11},{10,... | collective-permute-start | bytes 786440 | tf_op jit(solution)/shard_map/ppermute | solution.py:321
  51.7 6.7 %collective-permute-start.14 = (bf16[1024,128]{1,0:T(8,128)(2,1)S(1)}, bf16[1024,128]{1,0:T(8,128)(2,1)S(1)}, u32[]{:S(2)}, u32[]{:S(2)}) collective-permute-start(bf16[1024,128]{1,0:T(8,128)(2,1)S(1)} %get-tuple-element.86), channel_id=1, source_target_pairs={{0,3},{1,0},{2,1},{3,2},{4,7},{5,4},{6,5},{7,6},{8,11},{9,8},{10,9... | collective-permute-start | bytes 786440 | tf_op jit(solution)/shard_map/ppermute | solution.py:321
  58.5 4.6 %collective-permute-start.15 = (bf16[512,128]{1,0:T(8,128)(2,1)S(1)}, bf16[512,128]{1,0:T(8,128)(2,1)S(1)}, u32[]{:S(2)}, u32[]{:S(2)}) collective-permute-start(bf16[512,128]{1,0:T(8,128)(2,1)S(1)} %get-tuple-element.88), channel_id=1, source_target_pairs={{0,16},{1,17},{2,18},{3,19},{4,20},{5,21},{6,22},{7,23},{8,24},{9,... | collective-permute-start | bytes 393224 | tf_op jit(solution)/shard_map/ppermute | solution.py:321
  64.3 1.7 %collective-permute-start.17 = (f32[136,256]{1,0:T(8,128)S(1)}, f32[136,256]{1,0:T(8,128)S(1)}, u32[]{:S(2)}, u32[]{:S(2)}) collective-permute-start(f32[136,256]{1,0:T(8,128)S(1)} %get-tuple-element.95), channel_id=1, source_target_pairs={{0,16},{1,17},{2,18},{3,19},{4,20},{5,21},{6,22},{7,23},{8,24},{9,... | collective-permute-start | bytes 417800 | tf_op jit(solution)/shard_map/ppermute | solution.py:321
  64.6 1.3 %collective-permute-start.16 = (bf16[512,128]{1,0:T(8,128)(2,1)S(1)}, bf16[512,128]{1,0:T(8,128)(2,1)S(1)}, u32[]{:S(2)}, u32[]{:S(2)}) collective-permute-start(bf16[512,128]{1,0:T(8,128)(2,1)S(1)} %get-tuple-element.94), channel_id=1, source_target_pairs={{0,16},{1,17},{2,18},{3,19},{4,20},{5,21},{6,22},{7,23},{8,24},{9,... | collective-permute-start | bytes 393224 | tf_op jit(solution)/shard_map/ppermute | solution.py:321
  66.0 9.8 %collective-permute-start.18 = (bf16[1024,128]{1,0:T(8,128)(2,1)S(1)}, bf16[1024,128]{1,0:T(8,128)(2,1)S(1)}, u32[]{:S(2)}, u32[]{:S(2)}) collective-permute-start(bf16[1024,128]{1,0:T(8,128)(2,1)S(1)} %pair_grads.1.refs_0_), channel_id=1, source_target_pairs={{0,1},{1,2},{2,3},{3,0},{4,5},{5,6},{6,7},{7,4},{8,9},{9,10},{10,1... | collective-permute-start | bytes 786440 | tf_op jit(solution)/shard_map/ppermute | solution.py:321
  66.3 9.5 %collective-permute-start.19 = (bf16[1024,128]{1,0:T(8,128)(2,1)S(1)}, bf16[1024,128]{1,0:T(8,128)(2,1)S(1)}, u32[]{:S(2)}, u32[]{:S(2)}) collective-permute-start(bf16[1024,128]{1,0:T(8,128)(2,1)S(1)} %pair_grads.1.refs_0_), channel_id=1, source_target_pairs={{0,2},{1,3},{2,0},{3,1},{4,6},{5,7},{6,4},{7,5},{8,10},{9,11},{10,... | collective-permute-start | bytes 786440 | tf_op jit(solution)/shard_map/ppermute | solution.py:321
  67.3 9.1 %collective-permute-start.20 = (bf16[1024,128]{1,0:T(8,128)(2,1)S(1)}, bf16[1024,128]{1,0:T(8,128)(2,1)S(1)}, u32[]{:S(2)}, u32[]{:S(2)}) collective-permute-start(bf16[1024,128]{1,0:T(8,128)(2,1)S(1)} %pair_grads.1.refs_0_), channel_id=1, source_target_pairs={{0,3},{1,0},{2,1},{3,2},{4,7},{5,4},{6,5},{7,6},{8,11},{9,8},{10,9... | collective-permute-start | bytes 786440 | tf_op jit(solution)/shard_map/ppermute | solution.py:321
  69.0 4.3 %collective-permute-start.21 = (f32[136,256]{1,0:T(8,128)S(1)}, f32[136,256]{1,0:T(8,128)S(1)}, u32[]{:S(2)}, u32[]{:S(2)}) collective-permute-start(f32[136,256]{1,0:T(8,128)S(1)} %add.15), channel_id=1, source_target_pairs={{0,32},{1,33},{2,34},{3,35},{4,36},{5,37},{6,38},{7,39},{8,40},{9,... | collective-permute-start | bytes 417800 | tf_op jit(solution)/shard_map/ppermute | solution.py:321
  76.5 9.6 %collective-permute-start.22 = (bf16[2048,128]{1,0:T(8,128)(2,1)S(1)}, bf16[2048,128]{1,0:T(8,128)(2,1)S(1)}, u32[]{:S(2)}, u32[]{:S(2)}) collective-permute-start(bf16[2048,128]{1,0:T(8,128)(2,1)S(1)} %get-tuple-element.103.refs_4_), channel_id=1, source_target_pairs={{0,4},{1,5},{2,6},{3,7},{4,8},{5,9},{6,10},{7,11},{8,12},{9,13},{1... | collective-permute-start | bytes 1572872 | tf_op jit(solution)/shard_map/ppermute | solution.py:321
  77.8 8.3 %collective-permute-start.26 = (bf16[2048,128]{1,0:T(8,128)(2,1)S(1)}, bf16[2048,128]{1,0:T(8,128)(2,1)S(1)}, u32[]{:S(2)}, u32[]{:S(2)}) collective-permute-start(bf16[2048,128]{1,0:T(8,128)(2,1)S(1)} %get-tuple-element.104.refs_5_), channel_id=1, source_target_pairs={{0,12},{1,13},{2,14},{3,15},{4,0},{5,1},{6,2},{7,3},{8,4},{9,5},{1... | collective-permute-start | bytes 1572872 | tf_op jit(solution)/shard_map/ppermute | solution.py:321
  79.2 15.0 %collective-permute-start.23 = (bf16[2048,128]{1,0:T(8,128)(2,1)S(1)}, bf16[2048,128]{1,0:T(8,128)(2,1)S(1)}, u32[]{:S(2)}, u32[]{:S(2)}) collective-permute-start(bf16[2048,128]{1,0:T(8,128)(2,1)S(1)} %get-tuple-element.104.refs_5_), channel_id=1, source_target_pairs={{0,4},{1,5},{2,6},{3,7},{4,8},{5,9},{6,10},{7,11},{8,12},{9,13},{1... | collective-permute-start | bytes 1572872 | tf_op jit(solution)/shard_map/ppermute | solution.py:321
  79.3 16.2 %collective-permute-start.25 = (bf16[2048,128]{1,0:T(8,128)(2,1)S(1)}, bf16[2048,128]{1,0:T(8,128)(2,1)S(1)}, u32[]{:S(2)}, u32[]{:S(2)}) collective-permute-start(bf16[2048,128]{1,0:T(8,128)(2,1)S(1)} %get-tuple-element.103.refs_4_), channel_id=1, source_target_pairs={{0,12},{1,13},{2,14},{3,15},{4,0},{5,1},{6,2},{7,3},{8,4},{9,5},{1... | collective-permute-start | bytes 1572872 | tf_op jit(solution)/shard_map/ppermute | solution.py:321
  86.1 14.2 %collective-permute-start.27 = (bf16[2048,128]{1,0:T(8,128)(2,1)S(1)}, bf16[2048,128]{1,0:T(8,128)(2,1)S(1)}, u32[]{:S(2)}, u32[]{:S(2)}) collective-permute-start(bf16[2048,128]{1,0:T(8,128)(2,1)S(1)} %collective-permute-done.22.refs_6_), channel_id=1, source_target_pairs={{0,4},{1,5},{2,6},{3,7},{4,8},{5,9},{6,10},{7,11},{8,12},{9,13},{1... | collective-permute-start | bytes 1572872 | tf_op jit(solution)/shard_map/ppermute | solution.py:321
  86.1 14.2 %collective-permute-start.28 = (bf16[2048,128]{1,0:T(8,128)(2,1)S(1)}, bf16[2048,128]{1,0:T(8,128)(2,1)S(1)}, u32[]{:S(2)}, u32[]{:S(2)}) collective-permute-start(bf16[2048,128]{1,0:T(8,128)(2,1)S(1)} %collective-permute-done.26.refs_9_), channel_id=1, source_target_pairs={{0,12},{1,13},{2,14},{3,15},{4,0},{5,1},{6,2},{7,3},{8,4},{9,5},{1... | collective-permute-start | bytes 1572872 | tf_op jit(solution)/shard_map/ppermute | solution.py:321
  88.8 5.4 %collective-permute-start.24 = (f32[136,256]{1,0:T(8,128)S(1)}, f32[136,256]{1,0:T(8,128)S(1)}, u32[]{:S(2)}, u32[]{:S(2)}) collective-permute-start(f32[136,256]{1,0:T(8,128)S(1)} %add.16), channel_id=1, source_target_pairs={{0,64},{1,65},{2,66},{3,67},{4,68},{5,69},{6,70},{7,71},{8,72},{9,... | collective-permute-start | bytes 417800 | tf_op jit(solution)/shard_map/ppermute | solution.py:321
  94.2 7.8 %collective-permute-start.32 = (f32[136,256]{1,0:T(8,128)S(1)}, f32[136,256]{1,0:T(8,128)S(1)}, u32[]{:S(2)}, u32[]{:S(2)}) collective-permute-start(f32[136,256]{1,0:T(8,128)S(1)} %add.17.s0), channel_id=1, source_target_pairs={{0,4},{1,5},{2,6},{3,7},{4,8},{5,9},{6,10},{7,11},{8,12},{9,13},{1... | collective-permute-start | bytes 417800 | tf_op jit(solution)/shard_map/ppermute | solution.py:321
  94.3 7.8 %collective-permute-start.33 = (f32[136,256]{1,0:T(8,128)S(1)}, f32[136,256]{1,0:T(8,128)S(1)}, u32[]{:S(2)}, u32[]{:S(2)}) collective-permute-start(f32[136,256]{1,0:T(8,128)S(1)} %add.17.s0), channel_id=1, source_target_pairs={{0,8},{1,9},{2,10},{3,11},{4,12},{5,13},{6,14},{7,15},{8,0},{9,1},... | collective-permute-start | bytes 417800 | tf_op jit(solution)/shard_map/ppermute | solution.py:321
  95.5 6.6 %collective-permute-start.34 = (f32[136,256]{1,0:T(8,128)S(1)}, f32[136,256]{1,0:T(8,128)S(1)}, u32[]{:S(2)}, u32[]{:S(2)}) collective-permute-start(f32[136,256]{1,0:T(8,128)S(1)} %add.17.s0), channel_id=1, source_target_pairs={{0,12},{1,13},{2,14},{3,15},{4,0},{5,1},{6,2},{7,3},{8,4},{9,5},{1... | collective-permute-start | bytes 417800 | tf_op jit(solution)/shard_map/ppermute | solution.py:321
  102.1 5.7 %collective-permute-start.35 = (f32[136,256]{1,0:T(8,128)S(1)}, f32[136,256]{1,0:T(8,128)S(1)}, u32[]{:S(2)}, u32[]{:S(2)}) collective-permute-start(f32[136,256]{1,0:T(8,128)S(1)} %sum_u.1), channel_id=1, source_target_pairs={{0,1},{1,0},{2,3},{3,2},{4,5},{5,4},{6,7},{7,6},{8,9},{9,8},{10,11... | collective-permute-start | bytes 417800 | tf_op jit(solution)/shard_map/ppermute | solution.py:321
  102.2 11.1 %collective-permute-start.29 = (bf16[1024,128]{1,0:T(8,128)(2,1)S(1)}, bf16[1024,128]{1,0:T(8,128)(2,1)S(1)}, u32[]{:S(2)}, u32[]{:S(2)}) collective-permute-start(bf16[1024,128]{1,0:T(8,128)(2,1)S(1)} %get-tuple-element.108), channel_id=1, source_target_pairs={{0,32},{1,33},{2,34},{3,35},{4,36},{5,37},{6,38},{7,39},{8,40},{9,... | collective-permute-start | bytes 786440 | tf_op jit(solution)/shard_map/ppermute | solution.py:321
  104.3 9.1 %collective-permute-start.30 = (bf16[1024,128]{1,0:T(8,128)(2,1)S(1)}, bf16[1024,128]{1,0:T(8,128)(2,1)S(1)}, u32[]{:S(2)}, u32[]{:S(2)}) collective-permute-start(bf16[1024,128]{1,0:T(8,128)(2,1)S(1)} %get-tuple-element.109), channel_id=1, source_target_pairs={{0,64},{1,65},{2,66},{3,67},{4,68},{5,69},{6,70},{7,71},{8,72},{9,... | collective-permute-start | bytes 786440 | tf_op jit(solution)/shard_map/ppermute | solution.py:321
  104.3 9.2 %collective-permute-start.31 = (bf16[1024,128]{1,0:T(8,128)(2,1)S(1)}, bf16[1024,128]{1,0:T(8,128)(2,1)S(1)}, u32[]{:S(2)}, u32[]{:S(2)}) collective-permute-start(bf16[1024,128]{1,0:T(8,128)(2,1)S(1)} %get-tuple-element.110), channel_id=1, source_target_pairs={{0,96},{1,97},{2,98},{3,99},{4,100},{5,101},{6,102},{7,103},{8,104... | collective-permute-start | bytes 786440 | tf_op jit(solution)/shard_map/ppermute | solution.py:321
  107.9 5.5 %collective-permute-start.36 = (f32[136,256]{1,0:T(8,128)S(1)}, f32[136,256]{1,0:T(8,128)S(1)}, u32[]{:S(2)}, u32[]{:S(2)}) collective-permute-start(f32[136,256]{1,0:T(8,128)S(1)} %add.18), channel_id=1, source_target_pairs={{0,2},{1,3},{2,0},{3,1},{4,6},{5,7},{6,4},{7,5},{8,10},{9,11},{10,... | collective-permute-start | bytes 417800 | tf_op jit(solution)/shard_map/ppermute | solution.py:321
  113.6 9.6 %collective-permute-start.38 = (f32[136,256]{1,0:T(8,128)S(1)}, f32[136,256]{1,0:T(8,128)S(1)}, u32[]{:S(2)}, u32[]{:S(2)}) collective-permute-start(f32[136,256]{1,0:T(8,128)S(1)} %add.19.mine), channel_id=1, source_target_pairs={{0,16},{1,17},{2,18},{3,19},{4,20},{5,21},{6,22},{7,23},{8,24},{9,... | collective-permute-start | bytes 417800 | tf_op jit(solution)/shard_map/ppermute | solution.py:321
  121.7 1.4 %collective-permute-start.37 = (bf16[512,128]{1,0:T(8,128)(2,1)S(1)}, bf16[512,128]{1,0:T(8,128)(2,1)S(1)}, u32[]{:S(2)}, u32[]{:S(2)}) collective-permute-start(bf16[512,128]{1,0:T(8,128)(2,1)S(1)} %get-tuple-element.117), channel_id=1, source_target_pairs={{0,16},{1,17},{2,18},{3,19},{4,20},{5,21},{6,22},{7,23},{8,24},{9,... | collective-permute-start | bytes 393224 | tf_op jit(solution)/shard_map/ppermute | solution.py:321

commit v6 on v5

--- a/solution.py
+++ b/solution.py
@@ -140,23 +140,12 @@
 def far_kernel(*refs):
     tiles = (refs[0:2], refs[2:4])
     pieces = refs[4:8]
-    panel, low, high, acc, sems = refs[8:]
-    u, v, y, c = coords()
-    copies = []
-    for n in range(8):
-        d, t = n // 2, n % 2
-        shard = ahead(y, c, -d) * 2 + (c if t == 0 else 1 - c)
-        copies.append(
-            pltpu.make_async_copy(
-                pieces[d].at[pl.ds(t * ROWS, ROWS)],
-                panel.at[rows_at(shard * ROWS, ROWS)],
-                sems.at[n],
-            )
-        )
-    for copy in copies:
-        copy.start()
-    for copy in copies:
-        copy.wait()
+    panel, low, high, acc = refs[8:]
+    u, v, y, c = coords()
+    for d in range(4):
+        for t, core in ((0, c), (1, 1 - c)):
+            shard = ahead(y, c, -d) * 2 + core
+            panel[rows_at(shard * ROWS, ROWS), :] = pieces[d][t * ROWS:(t + 1) * ROWS, :]
     for r in range(4):
         for t in range(2):
             ids, values = tiles[t]
@@ -387,10 +376,10 @@
     tile_specs = [smem(), vmem(), smem(), vmem()]
 
     panel, low, high = local_call(
-        far_kernel, "forward_far", tile_specs + [hbm()] * 4,
+        far_kernel, "forward_far", tile_specs + [vmem()] * 4,
         [shape(8 * ROWS), shape(4 * ROWS), shape(4 * ROWS)], tiles + pieces, 8,
         flops=slab // 2, moved=6 * MIB,
-        scratch=[pltpu.VMEM((2, ROWS, HALF), F32), pltpu.SemaphoreType.DMA((8,))],
+        scratch=[pltpu.VMEM((2, ROWS, HALF), F32)],
     )
     extra = [along_u(low, 1), along_u(high, 3)]
     half = shape(4 * ROWS)
@@ -432,9 +421,9 @@
     )
     left1, right3 = along_u(join1, 1), along_u(join3, 3)
     left3, right1 = along_u(join3, 1), along_u(join1, 3)
+    piece = with_y(piece, 2)
+    left1, piece = lax.optimization_barrier((left1, piece))
     far = [along_u(left1, 1), along_u(right3, 3)]
-    piece = with_y(piece, 2)
-    left3, piece = lax.optimization_barrier((left3, piece))
     s0, s1, s2, s3 = spread(piece, along_u)
     (start,) = local_call(
         early_kernel, "backward_early", tile_specs + [vmem()] * 6,

time: 124 us -> 120 us (0.968)
  starting transfers between devices: 51.7 us -> 48.7 us
  Pallas kernels: 15.7 us -> 14.4 us
    ppermute x39, starting transfers between devices: 51.7 us -> 48.7 us  [permute(): return lax.ppermute(value, ('row', 'col'), pairs)]
    pallas_call x17, Pallas kernels: 15.7 us -> 14.4 us  [local_call(): pl.pallas_call(kernel, out_shape=outs, in_specs=ins, out_specs=[vmem()] *...]
  transfers between devices with their start and end apart: 39 -> 39, of which waited for: 21 -> 23; matrix products, arithmetic and copies ran while one was open for 0% -> 0% of each run, Pallas kernels for 8% -> 8%
where the time goes in v6:
time: 120 us
  waiting for transfers between devices  48.9 us (41%)
  starting transfers between devices  48.7 us (41%)
  Pallas kernels  14.4 us (12%)
  local copies, waits for them, and re-layouts  6.97 us (6%)
    ppermute x39, waiting for transfers between devices, permute(): return lax.ppermute(value, ('row', 'col'), pairs)  48.9 us
    ppermute x39, starting transfers between devices, permute(): return lax.ppermute(value, ('row', 'col'), pairs)  48.7 us
    pallas_call x17, Pallas kernels, local_call(): pl.pallas_call(kernel, out_shape=outs, in_specs=ins, out_specs=[vmem()] *...  14.4 us
    unnamed x14, local copies, waits for them, and re-layouts  6.97 us
  transfers between devices with their start and end apart: 39, of which 23 were waited for; matrix products, arithmetic and copies ran while one was open for 0% of the time, Pallas kernels for 8%

profile of v6, /device:TPU:1, one launch (start us, length us, event | category | flops | bytes accessed | tf_op | source)
XLA Modules:
  0.0 119.8 jit_solution(5100046021412986410)
XLA Ops:
  0.6 0.9 copy-done.2
  1.6 1.5 %collective-permute-start = (bf16[512,128]{1,0:T(8,128)(2,1)S(1)}, bf16[512,128]{1,0:T(8,128)(2,1)S(1)}, u32[]{:S(2)}, u32[]{:S(2)}) collective-permute-start(bf16[512,128]{1,0:T(8,128)(2,1)S(1)} %get-tuple-element.63), channel_id=1, source_target_pairs={{0,16},{1,17},{2,18},{3,19},{4,20},{5,21},{6,22},{7,23},{8,24},{9,... | collective-permute-start | bytes 393224 | tf_op jit(solution)/shard_map/ppermute | solution.py:310
  3.1 1.0 collective-permute-done.refs_1_
  4.5 2.9 %collective-permute-start.1 = (bf16[1024,128]{1,0:T(8,128)(2,1)S(1)}, bf16[1024,128]{1,0:T(8,128)(2,1)S(1)}, u32[]{:S(2)}, u32[]{:S(2)}) collective-permute-start(bf16[1024,128]{1,0:T(8,128)(2,1)S(1)} %pair.1.refs_4_), channel_id=1, source_target_pairs={{0,32},{1,33},{2,34},{3,35},{4,36},{5,37},{6,38},{7,39},{8,40},{9,... | collective-permute-start | bytes 786440 | tf_op jit(solution)/shard_map/ppermute | solution.py:310
  7.7 0.7 collective-permute-start.5
  8.4 0.7 copy-done.5
  9.1 0.7 copy-done.6
  9.7 2.2 %collective-permute-start.2 = (s32[2,128]{1,0:T(2,128)S(1)}, s32[2,128]{1,0:T(2,128)S(1)}, u32[]{:S(2)}, u32[]{:S(2)}) collective-permute-start(s32[2,128]{1,0:T(2,128)S(1)} %ids.1.refs_0_), channel_id=1, source_target_pairs={{0,16},{1,17},{2,18},{3,19},{4,20},{5,21},{6,22},{7,23},{8,24},{9,... | collective-permute-start | bytes 3080 | tf_op jit(solution)/shard_map/ppermute | solution.py:310
  11.9 2.2 %copy-done = bf16[1,1,128,128,128]{4,3,2,1,0:T(8,128)(2,1)S(1)} copy-done((bf16[1,1,128,128,128]{4,3,2,1,0:T(8,128)(2,1)S(1)}, bf16[1,1,128,128,128]{4,3,2,1,0:T(8,128)(2,1)}, u32[]{:S(2)}) %copy-start) | copy-done | bytes 4194328
  14.1 0.9 copy-done.1
  15.1 0.9 copy-done.3
  16.0 0.7 copy-done.4
  16.7 0.5 prologue.1
  17.2 0.6 collective-permute-done.1.refs_5_
  17.8 2.4 %collective-permute-done.5.refs_7_ = bf16[1024,128]{1,0:T(8,128)(2,1)S(1)} collective-permute-done((bf16[1024,128]{1,0:T(8,128)(2,1)S(1)}, bf16[1024,128]{1,0:T(8,128)(2,1)S(1)}, u32[]{:S(2)}, u32[]{:S(2)}) %collective-permute-start.5) | collective-permute-done | bytes 262176 | tf_op jit(solution)/shard_map/ppermute | solution.py:310
  20.2 1.8 %forward_far.1 = (bf16[4096,128]{1,0:T(8,128)(2,1)S(1)}, bf16[2048,128]{1,0:T(8,128)(2,1)S(1)}, bf16[2048,128]{1,0:T(8,128)(2,1)S(1)}) custom-call(s32[2,128]{1,0:T(2,128)S(1)} %ids.1.refs_0_, bf16[128,128,128]{2,1,0:T(8,128)(2,1)S(1)} %get-tuple-element.70.refs_1_, s32[2,128]{1,0:T(2,128)S(1)} %collective-permute-done.2.refs_2_, ...), custom_call_target="tpu_custom_call" | custom-call | flops 268435456 | bytes 6291456 | tf_op jit(solution)/shard_map/forward_far/pallas_call | solution.py:58
  22.0 1.9 %collective-permute-start.6 = (bf16[2048,128]{1,0:T(8,128)(2,1)S(1)}, bf16[2048,128]{1,0:T(8,128)(2,1)S(1)}, u32[]{:S(2)}, u32[]{:S(2)}) collective-permute-start(bf16[2048,128]{1,0:T(8,128)(2,1)S(1)} %get-tuple-element.76), channel_id=1, source_target_pairs={{0,4},{1,5},{2,6},{3,7},{4,8},{5,9},{6,10},{7,11},{8,12},{9,13},{1... | collective-permute-start | bytes 1572872 | tf_op jit(solution)/shard_map/ppermute | solution.py:310
  23.9 2.2 %collective-permute-start.7 = (bf16[2048,128]{1,0:T(8,128)(2,1)S(1)}, bf16[2048,128]{1,0:T(8,128)(2,1)S(1)}, u32[]{:S(2)}, u32[]{:S(2)}) collective-permute-start(bf16[2048,128]{1,0:T(8,128)(2,1)S(1)} %get-tuple-element.77), channel_id=1, source_target_pairs={{0,12},{1,13},{2,14},{3,15},{4,0},{5,1},{6,2},{7,3},{8,4},{9,5},{1... | collective-permute-start | bytes 1572872 | tf_op jit(solution)/shard_map/ppermute | solution.py:310
  26.1 3.8 %forward_near.1 = (bf16[2048,128]{1,0:T(8,128)(2,1)S(1)}, bf16[2048,128]{1,0:T(8,128)(2,1)S(1)}, bf16[2048,128]{1,0:T(8,128)(2,1)S(1)}, bf16[2048,128]{1,0:T(8,1...) custom-call(s32[2,128]{1,0:T(2,128)S(1)} %ids.1.refs_0_, ...), custom_call_target="tpu_custom_call" | custom-call | flops 805306368 | bytes 10485760 | tf_op jit(solution)/shard_map/forward_near/pallas_call | solution.py:58
  29.9 1.4 %collective-permute-start.9 = (bf16[2048,128]{1,0:T(8,128)(2,1)S(1)}, bf16[2048,128]{1,0:T(8,128)(2,1)S(1)}, u32[]{:S(2)}, u32[]{:S(2)}) collective-permute-start(bf16[2048,128]{1,0:T(8,128)(2,1)S(1)} %get-tuple-element.79), channel_id=1, source_target_pairs={{0,12},{1,13},{2,14},{3,15},{4,0},{5,1},{6,2},{7,3},{8,4},{9,5},{1... | collective-permute-start | bytes 1572872 | tf_op jit(solution)/shard_map/ppermute | solution.py:310
  31.4 1.4 %collective-permute-done.6.extra1 = bf16[2048,128]{1,0:T(8,128)(2,1)S(1)} collective-permute-done((bf16[2048,128]{1,0:T(8,128)(2,1)S(1)}, bf16[2048,128]{1,0:T(8,128)(2,1)S(1)}, u32[]{:S(2)}, u32[]{:S(2)}) %collective-permute-start.6) | collective-permute-done | bytes 524320 | tf_op jit(solution)/shard_map/ppermute | solution.py:310
  33.1 1.1 collective-permute-start.8
  34.1 1.9 %collective-permute-start.11 = (bf16[2048,128]{1,0:T(8,128)(2,1)S(1)}, bf16[2048,128]{1,0:T(8,128)(2,1)S(1)}, u32[]{:S(2)}, u32[]{:S(2)}) collective-permute-start(bf16[2048,128]{1,0:T(8,128)(2,1)S(1)} %get-tuple-element.82), channel_id=1, source_target_pairs={{0,12},{1,13},{2,14},{3,15},{4,0},{5,1},{6,2},{7,3},{8,4},{9,5},{1... | collective-permute-start | bytes 1572872 | tf_op jit(solution)/shard_map/ppermute | solution.py:310
  36.0 2.3 %collective-permute-done.9.refs_2_ = bf16[2048,128]{1,0:T(8,128)(2,1)S(1)} collective-permute-done((bf16[2048,128]{1,0:T(8,128)(2,1)S(1)}, bf16[2048,128]{1,0:T(8,128)(2,1)S(1)}, u32[]{:S(2)}, u32[]{:S(2)}) %collective-permute-start.9) | collective-permute-done | bytes 524320 | tf_op jit(solution)/shard_map/ppermute | solution.py:310
  38.3 2.6 %collective-permute-done.10.refs_4_ = bf16[2048,128]{1,0:T(8,128)(2,1)S(1)} collective-permute-done((bf16[2048,128]{1,0:T(8,128)(2,1)S(1)}, bf16[2048,128]{1,0:T(8,128)(2,1)S(1)}, u32[]{:S(2)}, u32[]{:S(2)}) %collective-permute-start.10) | collective-permute-done | bytes 524320 | tf_op jit(solution)/shard_map/ppermute | solution.py:310
  40.9 5.6 %collective-permute-done.8.refs_1_ = bf16[2048,128]{1,0:T(8,128)(2,1)S(1)} collective-permute-done((bf16[2048,128]{1,0:T(8,128)(2,1)S(1)}, bf16[2048,128]{1,0:T(8,128)(2,1)S(1)}, u32[]{:S(2)}, u32[]{:S(2)}) %collective-permute-start.8) | collective-permute-done | bytes 524320 | tf_op jit(solution)/shard_map/ppermute | solution.py:310
  46.5 0.4 stage_sum.1
  46.9 1.0 collective-permute-start.12
  47.9 2.5 %collective-permute-start.13 = (bf16[1024,128]{1,0:T(8,128)(2,1)S(1)}, bf16[1024,128]{1,0:T(8,128)(2,1)S(1)}, u32[]{:S(2)}, u32[]{:S(2)}) collective-permute-start(bf16[1024,128]{1,0:T(8,128)(2,1)S(1)} %get-tuple-element.85), channel_id=1, source_target_pairs={{0,2},{1,3},{2,0},{3,1},{4,6},{5,7},{6,4},{7,5},{8,10},{9,11},{10,... | collective-permute-start | bytes 786440 | tf_op jit(solution)/shard_map/ppermute | solution.py:310
  50.3 1.2 collective-permute-start.14
  51.5 2.2 %collective-permute-done.12.refs_1_ = bf16[1024,128]{1,0:T(8,128)(2,1)S(1)} collective-permute-done((bf16[1024,128]{1,0:T(8,128)(2,1)S(1)}, bf16[1024,128]{1,0:T(8,128)(2,1)S(1)}, u32[]{:S(2)}, u32[]{:S(2)}) %collective-permute-start.12) | collective-permute-done | bytes 262176 | tf_op jit(solution)/shard_map/ppermute | solution.py:310
  53.7 3.2 %collective-permute-done.13.refs_2_ = bf16[1024,128]{1,0:T(8,128)(2,1)S(1)} collective-permute-done((bf16[1024,128]{1,0:T(8,128)(2,1)S(1)}, bf16[1024,128]{1,0:T(8,128)(2,1)S(1)}, u32[]{:S(2)}, u32[]{:S(2)}) %collective-permute-start.13) | collective-permute-done | bytes 262176 | tf_op jit(solution)/shard_map/ppermute | solution.py:310
  57.2 3.6 %collective-permute-start.15 = (bf16[512,128]{1,0:T(8,128)(2,1)S(1)}, bf16[512,128]{1,0:T(8,128)(2,1)S(1)}, u32[]{:S(2)}, u32[]{:S(2)}) collective-permute-start(bf16[512,128]{1,0:T(8,128)(2,1)S(1)} %get-tuple-element.88), channel_id=1, source_target_pairs={{0,16},{1,17},{2,18},{3,19},{4,20},{5,21},{6,22},{7,23},{8,24},{9,... | collective-permute-start | bytes 393224 | tf_op jit(solution)/shard_map/ppermute | solution.py:310
  60.8 1.0 collective-permute-done.15.refs_1_
  61.8 1.2 pointwise.1
  63.0 0.4 collective-permute-start.17
  63.5 1.2 %collective-permute-done.16.refs_1_ = bf16[512,128]{1,0:T(8,128)(2,1)S(1)} collective-permute-done((bf16[512,128]{1,0:T(8,128)(2,1)S(1)}, bf16[512,128]{1,0:T(8,128)(2,1)S(1)}, u32[]{:S(2)}, u32[]{:S(2)}) %collective-permute-start.16) | collective-permute-done | bytes 131104 | tf_op jit(solution)/shard_map/ppermute | solution.py:310
  65.0 1.1 collective-permute-start.19
  66.0 1.6 %collective-permute-start.20 = (bf16[1024,128]{1,0:T(8,128)(2,1)S(1)}, bf16[1024,128]{1,0:T(8,128)(2,1)S(1)}, u32[]{:S(2)}, u32[]{:S(2)}) collective-permute-start(bf16[1024,128]{1,0:T(8,128)(2,1)S(1)} %pair_grads.1.refs_0_), channel_id=1, source_target_pairs={{0,3},{1,0},{2,1},{3,2},{4,7},{5,4},{6,5},{7,6},{8,11},{9,8},{10,9... | collective-permute-start | bytes 786440 | tf_op jit(solution)/shard_map/ppermute | solution.py:310
  67.7 4.2 %collective-permute-done.21 = f32[136,256]{1,0:T(8,128)S(1)} collective-permute-done((f32[136,256]{1,0:T(8,128)S(1)}, f32[136,256]{1,0:T(8,128)S(1)}, u32[]{:S(2)}, u32[]{:S(2)}) %collective-permute-start.21) | collective-permute-done | bytes 139296 | tf_op jit(solution)/shard_map/ppermute | solution.py:310
  72.0 2.5 %collective-permute-done.18.refs_1_ = bf16[1024,128]{1,0:T(8,128)(2,1)S(1)} collective-permute-done((bf16[1024,128]{1,0:T(8,128)(2,1)S(1)}, bf16[1024,128]{1,0:T(8,128)(2,1)S(1)}, u32[]{:S(2)}, u32[]{:S(2)}) %collective-permute-start.18) | collective-permute-done | bytes 262176 | tf_op jit(solution)/shard_map/ppermute | solution.py:310
  74.5 0.6 collective-permute-done.20.refs_3_
  75.2 1.3 %collective-permute-start.22 = (bf16[2048,128]{1,0:T(8,128)(2,1)S(1)}, bf16[2048,128]{1,0:T(8,128)(2,1)S(1)}, u32[]{:S(2)}, u32[]{:S(2)}) collective-permute-start(bf16[2048,128]{1,0:T(8,128)(2,1)S(1)} %get-tuple-element.103.refs_4_), channel_id=1, source_target_pairs={{0,4},{1,5},{2,6},{3,7},{4,8},{5,9},{6,10},{7,11},{8,12},{9,13},{1... | collective-permute-start | bytes 1572872 | tf_op jit(solution)/shard_map/ppermute | solution.py:310
  76.5 1.4 %collective-permute-start.26 = (bf16[2048,128]{1,0:T(8,128)(2,1)S(1)}, bf16[2048,128]{1,0:T(8,128)(2,1)S(1)}, u32[]{:S(2)}, u32[]{:S(2)}) collective-permute-start(bf16[2048,128]{1,0:T(8,128)(2,1)S(1)} %get-tuple-element.104.refs_5_), channel_id=1, source_target_pairs={{0,12},{1,13},{2,14},{3,15},{4,0},{5,1},{6,2},{7,3},{8,4},{9,5},{1... | collective-permute-start | bytes 1572872 | tf_op jit(solution)/shard_map/ppermute | solution.py:310
  77.9 1.1 collective-permute-start.23
  79.0 2.7 %collective-permute-start.25 = (bf16[2048,128]{1,0:T(8,128)(2,1)S(1)}, bf16[2048,128]{1,0:T(8,128)(2,1)S(1)}, u32[]{:S(2)}, u32[]{:S(2)}) collective-permute-start(bf16[2048,128]{1,0:T(8,128)(2,1)S(1)} %get-tuple-element.103.refs_4_), channel_id=1, source_target_pairs={{0,12},{1,13},{2,14},{3,15},{4,0},{5,1},{6,2},{7,3},{8,4},{9,5},{1... | collective-permute-start | bytes 1572872 | tf_op jit(solution)/shard_map/ppermute | solution.py:310
  81.7 1.7 %collective-permute-done.23 = f32[136,256]{1,0:T(8,128)S(1)} collective-permute-done((f32[136,256]{1,0:T(8,128)S(1)}, f32[136,256]{1,0:T(8,128)S(1)}, u32[]{:S(2)}, u32[]{:S(2)}) %collective-permute-start.23) | collective-permute-done | bytes 139296 | tf_op jit(solution)/shard_map/ppermute | solution.py:310
  83.4 1.4 %collective-permute-done.22.refs_6_ = bf16[2048,128]{1,0:T(8,128)(2,1)S(1)} collective-permute-done((bf16[2048,128]{1,0:T(8,128)(2,1)S(1)}, bf16[2048,128]{1,0:T(8,128)(2,1)S(1)}, u32[]{:S(2)}, u32[]{:S(2)}) %collective-permute-start.22) | collective-permute-done | bytes 524320 | tf_op jit(solution)/shard_map/ppermute | solution.py:310
  84.8 2.7 %collective-permute-start.28 = (bf16[2048,128]{1,0:T(8,128)(2,1)S(1)}, bf16[2048,128]{1,0:T(8,128)(2,1)S(1)}, u32[]{:S(2)}, u32[]{:S(2)}) collective-permute-start(bf16[2048,128]{1,0:T(8,128)(2,1)S(1)} %collective-permute-done.26.refs_9_), channel_id=1, source_target_pairs={{0,12},{1,13},{2,14},{3,15},{4,0},{5,1},{6,2},{7,3},{8,4},{9,5},{1... | collective-permute-start | bytes 1572872 | tf_op jit(solution)/shard_map/ppermute | solution.py:310
  87.5 2.9 %collective-permute-done.24.refs_7_ = bf16[2048,128]{1,0:T(8,128)(2,1)S(1)} collective-permute-done((bf16[2048,128]{1,0:T(8,128)(2,1)S(1)}, bf16[2048,128]{1,0:T(8,128)(2,1)S(1)}, u32[]{:S(2)}, u32[]{:S(2)}) %collective-permute-start.24) | collective-permute-done | bytes 524320 | tf_op jit(solution)/shard_map/ppermute | solution.py:310
  90.4 1.0 collective-permute-start.33
  91.5 1.6 %collective-permute-start.34 = (f32[136,256]{1,0:T(8,128)S(1)}, f32[136,256]{1,0:T(8,128)S(1)}, u32[]{:S(2)}, u32[]{:S(2)}) collective-permute-start(f32[136,256]{1,0:T(8,128)S(1)} %add.17.s0), channel_id=1, source_target_pairs={{0,12},{1,13},{2,14},{3,15},{4,0},{5,1},{6,2},{7,3},{8,4},{9,5},{1... | collective-permute-start | bytes 417800 | tf_op jit(solution)/shard_map/ppermute | solution.py:310
  93.1 3.3 %backward_early.1.refs_4_ = f32[4096,128]{1,0:T(8,128)S(1)} custom-call(s32[2,128]{1,0:T(2,128)S(1)} %ids.1.refs_0_, bf16[128,128,128]{2,1,0:T(8,128)(2,1)S(1)} %get-tuple-element.70.refs_1_, s32[2,128]{1,0:T(2,128)S(1)} %collective-permute-done.2.refs_2_, bf16[128,128,128]{2,1,0:T(8,128)(2,1)S(1)} %collective-permute-done.3.refs_3_, ...), custom_call_target="tpu_custom_call" | custom-call | flops 805306368 | bytes 10485760 | tf_op jit(solution)/shard_map/backward_early/pallas_call | solution.py:58
  96.4 1.8 %backward_late.1 = (bf16[1024,128]{1,0:T(8,128)(2,1)S(1)}, bf16[1024,128]{1,0:T(8,128)(2,1)S(1)}, bf16[1024,128]{1,0:T(8,128)(2,1)S(1)}, bf16[1024,128]{1,0:T(8,128)(2,1)S(1)}) custom-call(s32[2,128]{1,0:T(2,128)S(1)} %ids.1.refs_0_, bf16[128,128,128]{2,1,0:T(8,128)(2,1)S(1)} %get-tuple-element.70.refs_1_, s32[2,128]{1,0:T(2,128)S(1)} %collective-permute-done.2.refs_2_, ...), custom_call_target="tpu_custom_call" | custom-call | flops 268435456 | bytes 6291456 | tf_op jit(solution)/shard_map/backward_late/pallas_call | solution.py:58
  98.2 1.0 collective-permute-done.33.s2
  99.3 2.1 %collective-permute-start.29 = (bf16[1024,128]{1,0:T(8,128)(2,1)S(1)}, bf16[1024,128]{1,0:T(8,128)(2,1)S(1)}, u32[]{:S(2)}, u32[]{:S(2)}) collective-permute-start(bf16[1024,128]{1,0:T(8,128)(2,1)S(1)} %get-tuple-element.108), channel_id=1, source_target_pairs={{0,32},{1,33},{2,34},{3,35},{4,36},{5,37},{6,38},{7,39},{8,40},{9,... | collective-permute-start | bytes 786440 | tf_op jit(solution)/shard_map/ppermute | solution.py:310
  101.5 0.7 collective-permute-start.31
  102.1 1.1 collective-permute-done.35
  103.3 1.6 %collective-permute-start.36 = (f32[136,256]{1,0:T(8,128)S(1)}, f32[136,256]{1,0:T(8,128)S(1)}, u32[]{:S(2)}, u32[]{:S(2)}) collective-permute-start(f32[136,256]{1,0:T(8,128)S(1)} %add.18), channel_id=1, source_target_pairs={{0,2},{1,3},{2,0},{3,1},{4,6},{5,7},{6,4},{7,5},{8,10},{9,11},{10,... | collective-permute-start | bytes 417800 | tf_op jit(solution)/shard_map/ppermute | solution.py:310
  104.9 3.9 %collective-permute-done.36 = f32[136,256]{1,0:T(8,128)S(1)} collective-permute-done((f32[136,256]{1,0:T(8,128)S(1)}, f32[136,256]{1,0:T(8,128)S(1)}, u32[]{:S(2)}, u32[]{:S(2)}) %collective-permute-start.36) | collective-permute-done | bytes 139296 | tf_op jit(solution)/shard_map/ppermute | solution.py:310
  108.8 4.6 %collective-permute-done.31.refs_3_ = bf16[1024,128]{1,0:T(8,128)(2,1)S(1)} collective-permute-done((bf16[1024,128]{1,0:T(8,128)(2,1)S(1)}, bf16[1024,128]{1,0:T(8,128)(2,1)S(1)}, u32[]{:S(2)}, u32[]{:S(2)}) %collective-permute-start.31) | collective-permute-done | bytes 262176 | tf_op jit(solution)/shard_map/ppermute | solution.py:310
  113.3 4.0 %collective-permute-start.38 = (f32[136,256]{1,0:T(8,128)S(1)}, f32[136,256]{1,0:T(8,128)S(1)}, u32[]{:S(2)}, u32[]{:S(2)}) collective-permute-start(f32[136,256]{1,0:T(8,128)S(1)} %add.19.mine), channel_id=1, source_target_pairs={{0,16},{1,17},{2,18},{3,19},{4,20},{5,21},{6,22},{7,23},{8,24},{9,... | collective-permute-start | bytes 417800 | tf_op jit(solution)/shard_map/ppermute | solution.py:310
  117.6 1.3 %collective-permute-done.37.peer = bf16[512,128]{1,0:T(8,128)(2,1)S(1)} collective-permute-done((bf16[512,128]{1,0:T(8,128)(2,1)S(1)}, bf16[512,128]{1,0:T(8,128)(2,1)S(1)}, u32[]{:S(2)}, u32[]{:S(2)}) %collective-permute-start.37) | collective-permute-done | bytes 131104 | tf_op jit(solution)/shard_map/ppermute | solution.py:310
  118.9 0.9 last.1
  (50 shorter events, 2.5 us)
Async XLA Ops:
  0.6 1.0 copy-start.2
  1.6 2.5 %collective-permute-start = (bf16[512,128]{1,0:T(8,128)(2,1)S(1)}, bf16[512,128]{1,0:T(8,128)(2,1)S(1)}, u32[]{:S(2)}, u32[]{:S(2)}) collective-permute-start(bf16[512,128]{1,0:T(8,128)(2,1)S(1)} %get-tuple-element.63), channel_id=1, source_target_pairs={{0,16},{1,17},{2,18},{3,19},{4,20},{5,21},{6,22},{7,23},{8,24},{9,... | collective-permute-start | bytes 393224 | tf_op jit(solution)/shard_map/ppermute | solution.py:310
  4.1 16.0 %collective-permute-start.3 = (bf16[128,128,128]{2,1,0:T(8,128)(2,1)}, bf16[128,128,128]{2,1,0:T(8,128)(2,1)S(1)}, u32[]{:S(2)}, u32[]{:S(2)}) collective-permute-start(bf16[128,128,128]{2,1,0:T(8,128)(2,1)} %bitcast.5), channel_id=1, source_target_pairs={{0,16},{1,17},{2,18},{3,19},{4,20},{5,21},{6,22},{7,23},{8,24},{9,... | collective-permute-start | bytes 12582920 | tf_op jit(solution)/shard_map/ppermute | solution.py:310
  4.5 13.3 %collective-permute-start.1 = (bf16[1024,128]{1,0:T(8,128)(2,1)S(1)}, bf16[1024,128]{1,0:T(8,128)(2,1)S(1)}, u32[]{:S(2)}, u32[]{:S(2)}) collective-permute-start(bf16[1024,128]{1,0:T(8,128)(2,1)S(1)} %pair.1.refs_4_), channel_id=1, source_target_pairs={{0,32},{1,33},{2,34},{3,35},{4,36},{5,37},{6,38},{7,39},{8,40},{9,... | collective-permute-start | bytes 786440 | tf_op jit(solution)/shard_map/ppermute | solution.py:310
  7.4 10.4 %collective-permute-start.4 = (bf16[1024,128]{1,0:T(8,128)(2,1)S(1)}, bf16[1024,128]{1,0:T(8,128)(2,1)S(1)}, u32[]{:S(2)}, u32[]{:S(2)}) collective-permute-start(bf16[1024,128]{1,0:T(8,128)(2,1)S(1)} %pair.1.refs_4_), channel_id=1, source_target_pairs={{0,64},{1,65},{2,66},{3,67},{4,68},{5,69},{6,70},{7,71},{8,72},{9,... | collective-permute-start | bytes 786440 | tf_op jit(solution)/shard_map/ppermute | solution.py:310
  7.7 12.4 %collective-permute-start.5 = (bf16[1024,128]{1,0:T(8,128)(2,1)S(1)}, bf16[1024,128]{1,0:T(8,128)(2,1)S(1)}, u32[]{:S(2)}, u32[]{:S(2)}) collective-permute-start(bf16[1024,128]{1,0:T(8,128)(2,1)S(1)} %pair.1.refs_4_), channel_id=1, source_target_pairs={{0,96},{1,97},{2,98},{3,99},{4,100},{5,101},{6,102},{7,103},{8,104... | collective-permute-start | bytes 786440 | tf_op jit(solution)/shard_map/ppermute | solution.py:310
  8.4 0.7 copy-start.5
  9.1 0.7 copy-start.6
  9.7 8.1 %collective-permute-start.2 = (s32[2,128]{1,0:T(2,128)S(1)}, s32[2,128]{1,0:T(2,128)S(1)}, u32[]{:S(2)}, u32[]{:S(2)}) collective-permute-start(s32[2,128]{1,0:T(2,128)S(1)} %ids.1.refs_0_), channel_id=1, source_target_pairs={{0,16},{1,17},{2,18},{3,19},{4,20},{5,21},{6,22},{7,23},{8,24},{9,... | collective-permute-start | bytes 3080 | tf_op jit(solution)/shard_map/ppermute | solution.py:310
  11.9 2.2 %copy-start = (bf16[1,1,128,128,128]{4,3,2,1,0:T(8,128)(2,1)S(1)}, bf16[1,1,128,128,128]{4,3,2,1,0:T(8,128)(2,1)}, u32[]{:S(2)}) copy-start(bf16[1,1,128,128,128]{4,3,2,1,0:T(8,128)(2,1)} %param.8) | copy-start | bytes 12582916
  14.1 0.9 copy-start.1
  15.1 0.9 copy-start.3
  16.0 0.7 copy-start.4
  22.0 10.8 %collective-permute-start.6 = (bf16[2048,128]{1,0:T(8,128)(2,1)S(1)}, bf16[2048,128]{1,0:T(8,128)(2,1)S(1)}, u32[]{:S(2)}, u32[]{:S(2)}) collective-permute-start(bf16[2048,128]{1,0:T(8,128)(2,1)S(1)} %get-tuple-element.76), channel_id=1, source_target_pairs={{0,4},{1,5},{2,6},{3,7},{4,8},{5,9},{6,10},{7,11},{8,12},{9,13},{1... | collective-permute-start | bytes 1572872 | tf_op jit(solution)/shard_map/ppermute | solution.py:310
  23.9 8.9 %collective-permute-start.7 = (bf16[2048,128]{1,0:T(8,128)(2,1)S(1)}, bf16[2048,128]{1,0:T(8,128)(2,1)S(1)}, u32[]{:S(2)}, u32[]{:S(2)}) collective-permute-start(bf16[2048,128]{1,0:T(8,128)(2,1)S(1)} %get-tuple-element.77), channel_id=1, source_target_pairs={{0,12},{1,13},{2,14},{3,15},{4,0},{5,1},{6,2},{7,3},{8,4},{9,5},{1... | collective-permute-start | bytes 1572872 | tf_op jit(solution)/shard_map/ppermute | solution.py:310
  29.9 8.4 %collective-permute-start.9 = (bf16[2048,128]{1,0:T(8,128)(2,1)S(1)}, bf16[2048,128]{1,0:T(8,128)(2,1)S(1)}, u32[]{:S(2)}, u32[]{:S(2)}) collective-permute-start(bf16[2048,128]{1,0:T(8,128)(2,1)S(1)} %get-tuple-element.79), channel_id=1, source_target_pairs={{0,12},{1,13},{2,14},{3,15},{4,0},{5,1},{6,2},{7,3},{8,4},{9,5},{1... | collective-permute-start | bytes 1572872 | tf_op jit(solution)/shard_map/ppermute | solution.py:310
  31.4 9.5 %collective-permute-start.10 = (bf16[2048,128]{1,0:T(8,128)(2,1)S(1)}, bf16[2048,128]{1,0:T(8,128)(2,1)S(1)}, u32[]{:S(2)}, u32[]{:S(2)}) collective-permute-start(bf16[2048,128]{1,0:T(8,128)(2,1)S(1)} %get-tuple-element.81), channel_id=1, source_target_pairs={{0,4},{1,5},{2,6},{3,7},{4,8},{5,9},{6,10},{7,11},{8,12},{9,13},{1... | collective-permute-start | bytes 1572872 | tf_op jit(solution)/shard_map/ppermute | solution.py:310
  33.1 13.5 %collective-permute-start.8 = (bf16[2048,128]{1,0:T(8,128)(2,1)S(1)}, bf16[2048,128]{1,0:T(8,128)(2,1)S(1)}, u32[]{:S(2)}, u32[]{:S(2)}) collective-permute-start(bf16[2048,128]{1,0:T(8,128)(2,1)S(1)} %get-tuple-element.78), channel_id=1, source_target_pairs={{0,4},{1,5},{2,6},{3,7},{4,8},{5,9},{6,10},{7,11},{8,12},{9,13},{1... | collective-permute-start | bytes 1572872 | tf_op jit(solution)/shard_map/ppermute | solution.py:310
  34.1 12.4 %collective-permute-start.11 = (bf16[2048,128]{1,0:T(8,128)(2,1)S(1)}, bf16[2048,128]{1,0:T(8,128)(2,1)S(1)}, u32[]{:S(2)}, u32[]{:S(2)}) collective-permute-start(bf16[2048,128]{1,0:T(8,128)(2,1)S(1)} %get-tuple-element.82), channel_id=1, source_target_pairs={{0,12},{1,13},{2,14},{3,15},{4,0},{5,1},{6,2},{7,3},{8,4},{9,5},{1... | collective-permute-start | bytes 1572872 | tf_op jit(solution)/shard_map/ppermute | solution.py:310
  46.9 6.8 %collective-permute-start.12 = (bf16[1024,128]{1,0:T(8,128)(2,1)S(1)}, bf16[1024,128]{1,0:T(8,128)(2,1)S(1)}, u32[]{:S(2)}, u32[]{:S(2)}) collective-permute-start(bf16[1024,128]{1,0:T(8,128)(2,1)S(1)} %get-tuple-element.84), channel_id=1, source_target_pairs={{0,1},{1,2},{2,3},{3,0},{4,5},{5,6},{6,7},{7,4},{8,9},{9,10},{10,1... | collective-permute-start | bytes 786440 | tf_op jit(solution)/shard_map/ppermute | solution.py:310
  47.9 9.0 %collective-permute-start.13 = (bf16[1024,128]{1,0:T(8,128)(2,1)S(1)}, bf16[1024,128]{1,0:T(8,128)(2,1)S(1)}, u32[]{:S(2)}, u32[]{:S(2)}) collective-permute-start(bf16[1024,128]{1,0:T(8,128)(2,1)S(1)} %get-tuple-element.85), channel_id=1, source_target_pairs={{0,2},{1,3},{2,0},{3,1},{4,6},{5,7},{6,4},{7,5},{8,10},{9,11},{10,... | collective-permute-start | bytes 786440 | tf_op jit(solution)/shard_map/ppermute | solution.py:310
  50.3 6.8 %collective-permute-start.14 = (bf16[1024,128]{1,0:T(8,128)(2,1)S(1)}, bf16[1024,128]{1,0:T(8,128)(2,1)S(1)}, u32[]{:S(2)}, u32[]{:S(2)}) collective-permute-start(bf16[1024,128]{1,0:T(8,128)(2,1)S(1)} %get-tuple-element.86), channel_id=1, source_target_pairs={{0,3},{1,0},{2,1},{3,2},{4,7},{5,4},{6,5},{7,6},{8,11},{9,8},{10,9... | collective-permute-start | bytes 786440 | tf_op jit(solution)/shard_map/ppermute | solution.py:310
  57.2 4.6 %collective-permute-start.15 = (bf16[512,128]{1,0:T(8,128)(2,1)S(1)}, bf16[512,128]{1,0:T(8,128)(2,1)S(1)}, u32[]{:S(2)}, u32[]{:S(2)}) collective-permute-start(bf16[512,128]{1,0:T(8,128)(2,1)S(1)} %get-tuple-element.88), channel_id=1, source_target_pairs={{0,16},{1,17},{2,18},{3,19},{4,20},{5,21},{6,22},{7,23},{8,24},{9,... | collective-permute-start | bytes 393224 | tf_op jit(solution)/shard_map/ppermute | solution.py:310
  63.0 1.7 %collective-permute-start.17 = (f32[136,256]{1,0:T(8,128)S(1)}, f32[136,256]{1,0:T(8,128)S(1)}, u32[]{:S(2)}, u32[]{:S(2)}) collective-permute-start(f32[136,256]{1,0:T(8,128)S(1)} %get-tuple-element.95), channel_id=1, source_target_pairs={{0,16},{1,17},{2,18},{3,19},{4,20},{5,21},{6,22},{7,23},{8,24},{9,... | collective-permute-start | bytes 417800 | tf_op jit(solution)/shard_map/ppermute | solution.py:310
  63.3 1.3 %collective-permute-start.16 = (bf16[512,128]{1,0:T(8,128)(2,1)S(1)}, bf16[512,128]{1,0:T(8,128)(2,1)S(1)}, u32[]{:S(2)}, u32[]{:S(2)}) collective-permute-start(bf16[512,128]{1,0:T(8,128)(2,1)S(1)} %get-tuple-element.94), channel_id=1, source_target_pairs={{0,16},{1,17},{2,18},{3,19},{4,20},{5,21},{6,22},{7,23},{8,24},{9,... | collective-permute-start | bytes 393224 | tf_op jit(solution)/shard_map/ppermute | solution.py:310
  64.7 9.8 %collective-permute-start.18 = (bf16[1024,128]{1,0:T(8,128)(2,1)S(1)}, bf16[1024,128]{1,0:T(8,128)(2,1)S(1)}, u32[]{:S(2)}, u32[]{:S(2)}) collective-permute-start(bf16[1024,128]{1,0:T(8,128)(2,1)S(1)} %pair_grads.1.refs_0_), channel_id=1, source_target_pairs={{0,1},{1,2},{2,3},{3,0},{4,5},{5,6},{6,7},{7,4},{8,9},{9,10},{10,1... | collective-permute-start | bytes 786440 | tf_op jit(solution)/shard_map/ppermute | solution.py:310
  65.0 9.5 %collective-permute-start.19 = (bf16[1024,128]{1,0:T(8,128)(2,1)S(1)}, bf16[1024,128]{1,0:T(8,128)(2,1)S(1)}, u32[]{:S(2)}, u32[]{:S(2)}) collective-permute-start(bf16[1024,128]{1,0:T(8,128)(2,1)S(1)} %pair_grads.1.refs_0_), channel_id=1, source_target_pairs={{0,2},{1,3},{2,0},{3,1},{4,6},{5,7},{6,4},{7,5},{8,10},{9,11},{10,... | collective-permute-start | bytes 786440 | tf_op jit(solution)/shard_map/ppermute | solution.py:310
  66.0 9.1 %collective-permute-start.20 = (bf16[1024,128]{1,0:T(8,128)(2,1)S(1)}, bf16[1024,128]{1,0:T(8,128)(2,1)S(1)}, u32[]{:S(2)}, u32[]{:S(2)}) collective-permute-start(bf16[1024,128]{1,0:T(8,128)(2,1)S(1)} %pair_grads.1.refs_0_), channel_id=1, source_target_pairs={{0,3},{1,0},{2,1},{3,2},{4,7},{5,4},{6,5},{7,6},{8,11},{9,8},{10,9... | collective-permute-start | bytes 786440 | tf_op jit(solution)/shard_map/ppermute | solution.py:310
  67.7 4.3 %collective-permute-start.21 = (f32[136,256]{1,0:T(8,128)S(1)}, f32[136,256]{1,0:T(8,128)S(1)}, u32[]{:S(2)}, u32[]{:S(2)}) collective-permute-start(f32[136,256]{1,0:T(8,128)S(1)} %add.15), channel_id=1, source_target_pairs={{0,32},{1,33},{2,34},{3,35},{4,36},{5,37},{6,38},{7,39},{8,40},{9,... | collective-permute-start | bytes 417800 | tf_op jit(solution)/shard_map/ppermute | solution.py:310
  75.2 9.6 %collective-permute-start.22 = (bf16[2048,128]{1,0:T(8,128)(2,1)S(1)}, bf16[2048,128]{1,0:T(8,128)(2,1)S(1)}, u32[]{:S(2)}, u32[]{:S(2)}) collective-permute-start(bf16[2048,128]{1,0:T(8,128)(2,1)S(1)} %get-tuple-element.103.refs_4_), channel_id=1, source_target_pairs={{0,4},{1,5},{2,6},{3,7},{4,8},{5,9},{6,10},{7,11},{8,12},{9,13},{1... | collective-permute-start | bytes 1572872 | tf_op jit(solution)/shard_map/ppermute | solution.py:310
  76.5 8.3 %collective-permute-start.26 = (bf16[2048,128]{1,0:T(8,128)(2,1)S(1)}, bf16[2048,128]{1,0:T(8,128)(2,1)S(1)}, u32[]{:S(2)}, u32[]{:S(2)}) collective-permute-start(bf16[2048,128]{1,0:T(8,128)(2,1)S(1)} %get-tuple-element.104.refs_5_), channel_id=1, source_target_pairs={{0,12},{1,13},{2,14},{3,15},{4,0},{5,1},{6,2},{7,3},{8,4},{9,5},{1... | collective-permute-start | bytes 1572872 | tf_op jit(solution)/shard_map/ppermute | solution.py:310
  77.9 5.4 %collective-permute-start.23 = (f32[136,256]{1,0:T(8,128)S(1)}, f32[136,256]{1,0:T(8,128)S(1)}, u32[]{:S(2)}, u32[]{:S(2)}) collective-permute-start(f32[136,256]{1,0:T(8,128)S(1)} %add.16), channel_id=1, source_target_pairs={{0,64},{1,65},{2,66},{3,67},{4,68},{5,69},{6,70},{7,71},{8,72},{9,... | collective-permute-start | bytes 417800 | tf_op jit(solution)/shard_map/ppermute | solution.py:310
  79.0 11.4 %collective-permute-start.24 = (bf16[2048,128]{1,0:T(8,128)(2,1)S(1)}, bf16[2048,128]{1,0:T(8,128)(2,1)S(1)}, u32[]{:S(2)}, u32[]{:S(2)}) collective-permute-start(bf16[2048,128]{1,0:T(8,128)(2,1)S(1)} %get-tuple-element.104.refs_5_), channel_id=1, source_target_pairs={{0,4},{1,5},{2,6},{3,7},{4,8},{5,9},{6,10},{7,11},{8,12},{9,13},{1... | collective-permute-start | bytes 1572872 | tf_op jit(solution)/shard_map/ppermute | solution.py:310
  79.0 12.5 %collective-permute-start.25 = (bf16[2048,128]{1,0:T(8,128)(2,1)S(1)}, bf16[2048,128]{1,0:T(8,128)(2,1)S(1)}, u32[]{:S(2)}, u32[]{:S(2)}) collective-permute-start(bf16[2048,128]{1,0:T(8,128)(2,1)S(1)} %get-tuple-element.103.refs_4_), channel_id=1, source_target_pairs={{0,12},{1,13},{2,14},{3,15},{4,0},{5,1},{6,2},{7,3},{8,4},{9,5},{1... | collective-permute-start | bytes 1572872 | tf_op jit(solution)/shard_map/ppermute | solution.py:310
  84.8 11.6 %collective-permute-start.27 = (bf16[2048,128]{1,0:T(8,128)(2,1)S(1)}, bf16[2048,128]{1,0:T(8,128)(2,1)S(1)}, u32[]{:S(2)}, u32[]{:S(2)}) collective-permute-start(bf16[2048,128]{1,0:T(8,128)(2,1)S(1)} %collective-permute-done.22.refs_6_), channel_id=1, source_target_pairs={{0,4},{1,5},{2,6},{3,7},{4,8},{5,9},{6,10},{7,11},{8,12},{9,13},{1... | collective-permute-start | bytes 1572872 | tf_op jit(solution)/shard_map/ppermute | solution.py:310
  84.8 11.6 %collective-permute-start.28 = (bf16[2048,128]{1,0:T(8,128)(2,1)S(1)}, bf16[2048,128]{1,0:T(8,128)(2,1)S(1)}, u32[]{:S(2)}, u32[]{:S(2)}) collective-permute-start(bf16[2048,128]{1,0:T(8,128)(2,1)S(1)} %collective-permute-done.26.refs_9_), channel_id=1, source_target_pairs={{0,12},{1,13},{2,14},{3,15},{4,0},{5,1},{6,2},{7,3},{8,4},{9,5},{1... | collective-permute-start | bytes 1572872 | tf_op jit(solution)/shard_map/ppermute | solution.py:310
  87.5 10.7 %collective-permute-start.32 = (f32[136,256]{1,0:T(8,128)S(1)}, f32[136,256]{1,0:T(8,128)S(1)}, u32[]{:S(2)}, u32[]{:S(2)}) collective-permute-start(f32[136,256]{1,0:T(8,128)S(1)} %add.17.s0), channel_id=1, source_target_pairs={{0,4},{1,5},{2,6},{3,7},{4,8},{5,9},{6,10},{7,11},{8,12},{9,13},{1... | collective-permute-start | bytes 417800 | tf_op jit(solution)/shard_map/ppermute | solution.py:310
  90.4 8.8 %collective-permute-start.33 = (f32[136,256]{1,0:T(8,128)S(1)}, f32[136,256]{1,0:T(8,128)S(1)}, u32[]{:S(2)}, u32[]{:S(2)}) collective-permute-start(f32[136,256]{1,0:T(8,128)S(1)} %add.17.s0), channel_id=1, source_target_pairs={{0,8},{1,9},{2,10},{3,11},{4,12},{5,13},{6,14},{7,15},{8,0},{9,1},... | collective-permute-start | bytes 417800 | tf_op jit(solution)/shard_map/ppermute | solution.py:310
  91.5 7.8 %collective-permute-start.34 = (f32[136,256]{1,0:T(8,128)S(1)}, f32[136,256]{1,0:T(8,128)S(1)}, u32[]{:S(2)}, u32[]{:S(2)}) collective-permute-start(f32[136,256]{1,0:T(8,128)S(1)} %add.17.s0), channel_id=1, source_target_pairs={{0,12},{1,13},{2,14},{3,15},{4,0},{5,1},{6,2},{7,3},{8,4},{9,5},{1... | collective-permute-start | bytes 417800 | tf_op jit(solution)/shard_map/ppermute | solution.py:310
  99.2 4.0 %collective-permute-start.35 = (f32[136,256]{1,0:T(8,128)S(1)}, f32[136,256]{1,0:T(8,128)S(1)}, u32[]{:S(2)}, u32[]{:S(2)}) collective-permute-start(f32[136,256]{1,0:T(8,128)S(1)} %sum_u.1), channel_id=1, source_target_pairs={{0,1},{1,0},{2,3},{3,2},{4,5},{5,4},{6,7},{7,6},{8,9},{9,8},{10,11... | collective-permute-start | bytes 417800 | tf_op jit(solution)/shard_map/ppermute | solution.py:310
  99.3 9.4 %collective-permute-start.29 = (bf16[1024,128]{1,0:T(8,128)(2,1)S(1)}, bf16[1024,128]{1,0:T(8,128)(2,1)S(1)}, u32[]{:S(2)}, u32[]{:S(2)}) collective-permute-start(bf16[1024,128]{1,0:T(8,128)(2,1)S(1)} %get-tuple-element.108), channel_id=1, source_target_pairs={{0,32},{1,33},{2,34},{3,35},{4,36},{5,37},{6,38},{7,39},{8,40},{9,... | collective-permute-start | bytes 786440 | tf_op jit(solution)/shard_map/ppermute | solution.py:310
  101.5 7.3 %collective-permute-start.30 = (bf16[1024,128]{1,0:T(8,128)(2,1)S(1)}, bf16[1024,128]{1,0:T(8,128)(2,1)S(1)}, u32[]{:S(2)}, u32[]{:S(2)}) collective-permute-start(bf16[1024,128]{1,0:T(8,128)(2,1)S(1)} %get-tuple-element.109), channel_id=1, source_target_pairs={{0,64},{1,65},{2,66},{3,67},{4,68},{5,69},{6,70},{7,71},{8,72},{9,... | collective-permute-start | bytes 786440 | tf_op jit(solution)/shard_map/ppermute | solution.py:310
  101.5 11.9 %collective-permute-start.31 = (bf16[1024,128]{1,0:T(8,128)(2,1)S(1)}, bf16[1024,128]{1,0:T(8,128)(2,1)S(1)}, u32[]{:S(2)}, u32[]{:S(2)}) collective-permute-start(bf16[1024,128]{1,0:T(8,128)(2,1)S(1)} %get-tuple-element.110), channel_id=1, source_target_pairs={{0,96},{1,97},{2,98},{3,99},{4,100},{5,101},{6,102},{7,103},{8,104... | collective-permute-start | bytes 786440 | tf_op jit(solution)/shard_map/ppermute | solution.py:310
  103.3 5.5 %collective-permute-start.36 = (f32[136,256]{1,0:T(8,128)S(1)}, f32[136,256]{1,0:T(8,128)S(1)}, u32[]{:S(2)}, u32[]{:S(2)}) collective-permute-start(f32[136,256]{1,0:T(8,128)S(1)} %add.18), channel_id=1, source_target_pairs={{0,2},{1,3},{2,0},{3,1},{4,6},{5,7},{6,4},{7,5},{8,10},{9,11},{10,... | collective-permute-start | bytes 417800 | tf_op jit(solution)/shard_map/ppermute | solution.py:310
  113.3 5.6 %collective-permute-start.38 = (f32[136,256]{1,0:T(8,128)S(1)}, f32[136,256]{1,0:T(8,128)S(1)}, u32[]{:S(2)}, u32[]{:S(2)}) collective-permute-start(f32[136,256]{1,0:T(8,128)S(1)} %add.19.mine), channel_id=1, source_target_pairs={{0,16},{1,17},{2,18},{3,19},{4,20},{5,21},{6,22},{7,23},{8,24},{9,... | collective-permute-start | bytes 417800 | tf_op jit(solution)/shard_map/ppermute | solution.py:310
  117.5 1.4 %collective-permute-start.37 = (bf16[512,128]{1,0:T(8,128)(2,1)S(1)}, bf16[512,128]{1,0:T(8,128)(2,1)S(1)}, u32[]{:S(2)}, u32[]{:S(2)}) collective-permute-start(bf16[512,128]{1,0:T(8,128)(2,1)S(1)} %get-tuple-element.117), channel_id=1, source_target_pairs={{0,16},{1,17},{2,18},{3,19},{4,20},{5,21},{6,22},{7,23},{8,24},{9,... | collective-permute-start | bytes 393224 | tf_op jit(solution)/shard_map/ppermute | solution.py:310

commit v7 on v6

--- a/solution.py
+++ b/solution.py
@@ -154,19 +154,19 @@
             (low, high)[r // 2][start:start + ROWS, :] = acc[t].astype(BF)
 
 
-def near_kernel(*refs):
+def near_kernel(parts, *refs):
     tiles = (refs[0:2], refs[2:4])
     panel = refs[4]
-    outs = {1: refs[5:7], 3: refs[7:9], 0: refs[9:11]}
-    acc = refs[11]
-    u, v, y, c = coords()
-    for p, halves in outs.items():
-        for r in range(4):
+    outs = refs[5:-1]
+    acc = refs[-1]
+    u, v, y, c = coords()
+    for (p, half), out in zip(parts, outs):
+        for r in (2 * half, 2 * half + 1):
             for t in range(2):
                 ids, values = tiles[t]
                 forward_group(ids, values, panel, acc.at[t], target_group(u, v, c, p, r))
                 start = ((r % 2) * 2 + t) * ROWS
-                halves[r // 2][start:start + ROWS, :] = acc[t].astype(BF)
+                out[start:start + ROWS, :] = acc[t].astype(BF)
 
 
 def relay_kernel(own1, own3, extra1, extra3, out1, out3):
@@ -383,10 +383,17 @@
     )
     extra = [along_u(low, 1), along_u(high, 3)]
     half = shape(4 * ROWS)
-    near1, plain1, plain3, near3, home1, home3 = local_call(
-        near_kernel, "forward_near", tile_specs + [vmem()], [half] * 6,
-        tiles + [panel], 8, flops=3 * slab // 2, moved=10 * MIB,
-        scratch=[pltpu.VMEM((2, ROWS, HALF), F32)],
+
+    def near_call(parts, name):
+        return local_call(
+            lambda *refs: near_kernel(parts, *refs), name, tile_specs + [vmem()],
+            [half] * len(parts), tiles + [panel], 8, flops=len(parts) * slab // 4,
+            moved=(1 + len(parts)) * MIB, scratch=[pltpu.VMEM((2, ROWS, HALF), F32)],
+        )
+
+    plain1, plain3 = near_call(((1, 1), (3, 0)), "forward_plain")
+    near1, near3, home1, home3 = near_call(
+        ((1, 0), (3, 1), (0, 0), (0, 1)), "forward_near"
     )
     plain1, plain3 = along_u(plain1, 1), along_u(plain3, 3)
     mixed1, mixed3 = local_call(
@@ -442,7 +449,6 @@
     )
     lasts = exchange(outs, along_y)
     piece = with_v(with_v(piece, 1), 2)
-    *lasts, piece = lax.optimization_barrier((*lasts, piece))
     own, other = finish_call(lasts, "sum_x")
     x_grad, weight_grad, bias_grad = local_call(
         last_kernel, "last", [vmem()] * 4,

time: 120 us -> 119 us (level)
  waiting for transfers between devices: 48.9 us -> 38.6 us
  starting transfers between devices: 48.7 us -> 56.7 us
    ppermute x39, waiting for transfers between devices: 48.9 us -> 38.6 us  [permute(): return lax.ppermute(value, ('row', 'col'), pairs)]
    ppermute x39, starting transfers between devices: 48.7 us -> 56.7 us  [permute(): return lax.ppermute(value, ('row', 'col'), pairs)]
    pallas_call x17 -> x18, Pallas kernels: 14.4 us -> 15.1 us  [local_call(): pl.pallas_call(kernel, out_shape=outs, in_specs=ins, out_specs=[vmem()] *...]
  transfers between devices with their start and end apart: 39 -> 39, of which waited for: 23 -> 21; matrix products, arithmetic and copies ran while one was open for 0% -> 0% of each run, Pallas kernels for 8% -> 9%
where the time goes in v7:
time: 119 us; the launch traced here: 118 us
  starting transfers between devices  56.7 us (48%)
  waiting for transfers between devices  38.6 us (32%)
  Pallas kernels  15.1 us (13%)
  local copies, waits for them, and re-layouts  6.97 us (6%)
    ppermute x39, starting transfers between devices, permute(): return lax.ppermute(value, ('row', 'col'), pairs)  56.7 us
    ppermute x39, waiting for transfers between devices, permute(): return lax.ppermute(value, ('row', 'col'), pairs)  38.6 us
    pallas_call x18, Pallas kernels, local_call(): pl.pallas_call(kernel, out_shape=outs, in_specs=ins, out_specs=[vmem()] *...  15.1 us
    unnamed x14, local copies, waits for them, and re-layouts  6.97 us
  transfers between devices with their start and end apart: 39, of which 21 were waited for; matrix products, arithmetic and copies ran while one was open for 0% of the time, Pallas kernels for 9%

profile of v7, /device:TPU:1, one launch (start us, length us, event | category | flops | bytes accessed | tf_op | source)
XLA Modules:
  0.0 118.3 jit_solution(15262753791809884882)
XLA Ops:
  0.6 0.9 copy-done.2
  1.6 1.5 %collective-permute-start = (bf16[512,128]{1,0:T(8,128)(2,1)S(1)}, bf16[512,128]{1,0:T(8,128)(2,1)S(1)}, u32[]{:S(2)}, u32[]{:S(2)}) collective-permute-start(bf16[512,128]{1,0:T(8,128)(2,1)S(1)} %get-tuple-element.58), channel_id=1, source_target_pairs={{0,16},{1,17},{2,18},{3,19},{4,20},{5,21},{6,22},{7,23},{8,24},{9,... | collective-permute-start | bytes 393224 | tf_op jit(solution)/shard_map/ppermute | solution.py:310
  3.1 1.0 collective-permute-done.refs_1_
  4.5 2.9 %collective-permute-start.1 = (bf16[1024,128]{1,0:T(8,128)(2,1)S(1)}, bf16[1024,128]{1,0:T(8,128)(2,1)S(1)}, u32[]{:S(2)}, u32[]{:S(2)}) collective-permute-start(bf16[1024,128]{1,0:T(8,128)(2,1)S(1)} %pair.1.refs_4_), channel_id=1, source_target_pairs={{0,32},{1,33},{2,34},{3,35},{4,36},{5,37},{6,38},{7,39},{8,40},{9,... | collective-permute-start | bytes 786440 | tf_op jit(solution)/shard_map/ppermute | solution.py:310
  7.7 0.7 collective-permute-start.5
  8.4 0.7 copy-done.5
  9.1 0.7 copy-done.6
  9.7 2.2 %collective-permute-start.2 = (s32[2,128]{1,0:T(2,128)S(1)}, s32[2,128]{1,0:T(2,128)S(1)}, u32[]{:S(2)}, u32[]{:S(2)}) collective-permute-start(s32[2,128]{1,0:T(2,128)S(1)} %ids.1.refs_0_), channel_id=1, source_target_pairs={{0,16},{1,17},{2,18},{3,19},{4,20},{5,21},{6,22},{7,23},{8,24},{9,... | collective-permute-start | bytes 3080 | tf_op jit(solution)/shard_map/ppermute | solution.py:310
  11.9 2.2 %copy-done = bf16[1,1,128,128,128]{4,3,2,1,0:T(8,128)(2,1)S(1)} copy-done((bf16[1,1,128,128,128]{4,3,2,1,0:T(8,128)(2,1)S(1)}, bf16[1,1,128,128,128]{4,3,2,1,0:T(8,128)(2,1)}, u32[]{:S(2)}) %copy-start) | copy-done | bytes 4194328
  14.1 0.9 copy-done.1
  15.1 0.9 copy-done.3
  16.0 0.7 copy-done.4
  16.7 0.5 prologue.1
  17.2 0.6 collective-permute-done.1.refs_5_
  17.8 2.4 %collective-permute-done.5.refs_7_ = bf16[1024,128]{1,0:T(8,128)(2,1)S(1)} collective-permute-done((bf16[1024,128]{1,0:T(8,128)(2,1)S(1)}, bf16[1024,128]{1,0:T(8,128)(2,1)S(1)}, u32[]{:S(2)}, u32[]{:S(2)}) %collective-permute-start.5) | collective-permute-done | bytes 262176 | tf_op jit(solution)/shard_map/ppermute | solution.py:310
  20.2 1.8 %forward_far.1 = (bf16[4096,128]{1,0:T(8,128)(2,1)S(1)}, bf16[2048,128]{1,0:T(8,128)(2,1)S(1)}, bf16[2048,128]{1,0:T(8,128)(2,1)S(1)}) custom-call(s32[2,128]{1,0:T(2,128)S(1)} %ids.1.refs_0_, bf16[128,128,128]{2,1,0:T(8,128)(2,1)S(1)} %get-tuple-element.65.refs_1_, s32[2,128]{1,0:T(2,128)S(1)} %collective-permute-done.2.refs_2_, ...), custom_call_target="tpu_custom_call" | custom-call | flops 268435456 | bytes 6291456 | tf_op jit(solution)/shard_map/forward_far/pallas_call | solution.py:58
  22.0 1.9 %collective-permute-start.6 = (bf16[2048,128]{1,0:T(8,128)(2,1)S(1)}, bf16[2048,128]{1,0:T(8,128)(2,1)S(1)}, u32[]{:S(2)}, u32[]{:S(2)}) collective-permute-start(bf16[2048,128]{1,0:T(8,128)(2,1)S(1)} %get-tuple-element.71), channel_id=1, source_target_pairs={{0,4},{1,5},{2,6},{3,7},{4,8},{5,9},{6,10},{7,11},{8,12},{9,13},{1... | collective-permute-start | bytes 1572872 | tf_op jit(solution)/shard_map/ppermute | solution.py:310
  23.9 2.2 %collective-permute-start.7 = (bf16[2048,128]{1,0:T(8,128)(2,1)S(1)}, bf16[2048,128]{1,0:T(8,128)(2,1)S(1)}, u32[]{:S(2)}, u32[]{:S(2)}) collective-permute-start(bf16[2048,128]{1,0:T(8,128)(2,1)S(1)} %get-tuple-element.72), channel_id=1, source_target_pairs={{0,12},{1,13},{2,14},{3,15},{4,0},{5,1},{6,2},{7,3},{8,4},{9,5},{1... | collective-permute-start | bytes 1572872 | tf_op jit(solution)/shard_map/ppermute | solution.py:310
  26.1 1.7 %forward_plain.1 = (bf16[2048,128]{1,0:T(8,128)(2,1)S(1)}, bf16[2048,128]{1,0:T(8,128)(2,1)S(1)}) custom-call(s32[2,128]{1,0:T(2,128)S(1)} %ids.1.refs_0_, bf16[128,128,128]{2,1,0:T(8,128)(2,1)S(1)} %get-tuple-element.65.refs_1_, s32[2,128]{1,0:T(2,128)S(1)} %collective-permute-done.2.refs_2_, bf16[128,128,128]{2,1,0:T(8,128)(2,1)S(1)} %collective-permute-done.3.refs_3_, ...), custom_call_target="tpu_custom_call" | custom-call | flops 268435456 | bytes 3145728 | tf_op jit(solution)/shard_map/forward_plain/pallas_call | solution.py:58
  27.8 1.5 %collective-permute-start.9 = (bf16[2048,128]{1,0:T(8,128)(2,1)S(1)}, bf16[2048,128]{1,0:T(8,128)(2,1)S(1)}, u32[]{:S(2)}, u32[]{:S(2)}) collective-permute-start(bf16[2048,128]{1,0:T(8,128)(2,1)S(1)} %get-tuple-element.74), channel_id=1, source_target_pairs={{0,12},{1,13},{2,14},{3,15},{4,0},{5,1},{6,2},{7,3},{8,4},{9,5},{1... | collective-permute-start | bytes 1572872 | tf_op jit(solution)/shard_map/ppermute | solution.py:310
  29.3 2.9 %forward_near.1 = (bf16[2048,128]{1,0:T(8,128)(2,1)S(1)}, bf16[2048,128]{1,0:T(8,128)(2,1)S(1)}, bf16[2048,128]{1,0:T(8,128)(2,1)S(1)}, bf16[2048,128]{1,0:T(8,128)(2,1)S(1)}) custom-call(s32[2,128]{1,0:T(2,128)S(1)} %ids.1.refs_0_, bf16[128,128,128]{2,1,0:T(8,128)(2,1)S(1)} %get-tuple-element.65.refs_1_, s32[2,128]{1,0:T(2,128)S(1)} %collective-permute-done.2.refs_2_, ...), custom_call_target="tpu_custom_call" | custom-call | flops 536870912 | bytes 5242880 | tf_op jit(solution)/shard_map/forward_near/pallas_call | solution.py:58
  32.2 0.6 collective-permute-done.6.extra1
  33.1 1.1 collective-permute-start.8
  34.1 1.9 %collective-permute-start.11 = (bf16[2048,128]{1,0:T(8,128)(2,1)S(1)}, bf16[2048,128]{1,0:T(8,128)(2,1)S(1)}, u32[]{:S(2)}, u32[]{:S(2)}) collective-permute-start(bf16[2048,128]{1,0:T(8,128)(2,1)S(1)} %get-tuple-element.77), channel_id=1, source_target_pairs={{0,12},{1,13},{2,14},{3,15},{4,0},{5,1},{6,2},{7,3},{8,4},{9,5},{1... | collective-permute-start | bytes 1572872 | tf_op jit(solution)/shard_map/ppermute | solution.py:310
  36.0 2.0 %collective-permute-done.9.refs_2_ = bf16[2048,128]{1,0:T(8,128)(2,1)S(1)} collective-permute-done((bf16[2048,128]{1,0:T(8,128)(2,1)S(1)}, bf16[2048,128]{1,0:T(8,128)(2,1)S(1)}, u32[]{:S(2)}, u32[]{:S(2)}) %collective-permute-start.9) | collective-permute-done | bytes 524320 | tf_op jit(solution)/shard_map/ppermute | solution.py:310
  38.0 0.8 collective-permute-done.10.refs_4_
  38.8 5.6 %collective-permute-done.8.refs_1_ = bf16[2048,128]{1,0:T(8,128)(2,1)S(1)} collective-permute-done((bf16[2048,128]{1,0:T(8,128)(2,1)S(1)}, bf16[2048,128]{1,0:T(8,128)(2,1)S(1)}, u32[]{:S(2)}, u32[]{:S(2)}) %collective-permute-start.8) | collective-permute-done | bytes 524320 | tf_op jit(solution)/shard_map/ppermute | solution.py:310
  44.4 0.4 stage_sum.1
  44.8 1.0 collective-permute-start.12
  45.8 2.8 %collective-permute-start.13 = (bf16[1024,128]{1,0:T(8,128)(2,1)S(1)}, bf16[1024,128]{1,0:T(8,128)(2,1)S(1)}, u32[]{:S(2)}, u32[]{:S(2)}) collective-permute-start(bf16[1024,128]{1,0:T(8,128)(2,1)S(1)} %get-tuple-element.80), channel_id=1, source_target_pairs={{0,2},{1,3},{2,0},{3,1},{4,6},{5,7},{6,4},{7,5},{8,10},{9,11},{10,... | collective-permute-start | bytes 786440 | tf_op jit(solution)/shard_map/ppermute | solution.py:310
  48.5 0.9 collective-permute-start.14
  49.4 2.2 %collective-permute-done.12.refs_1_ = bf16[1024,128]{1,0:T(8,128)(2,1)S(1)} collective-permute-done((bf16[1024,128]{1,0:T(8,128)(2,1)S(1)}, bf16[1024,128]{1,0:T(8,128)(2,1)S(1)}, u32[]{:S(2)}, u32[]{:S(2)}) %collective-permute-start.12) | collective-permute-done | bytes 262176 | tf_op jit(solution)/shard_map/ppermute | solution.py:310
  51.6 3.8 %collective-permute-done.13.refs_2_ = bf16[1024,128]{1,0:T(8,128)(2,1)S(1)} collective-permute-done((bf16[1024,128]{1,0:T(8,128)(2,1)S(1)}, bf16[1024,128]{1,0:T(8,128)(2,1)S(1)}, u32[]{:S(2)}, u32[]{:S(2)}) %collective-permute-start.13) | collective-permute-done | bytes 262176 | tf_op jit(solution)/shard_map/ppermute | solution.py:310
  55.5 3.2 %collective-permute-start.15 = (bf16[512,128]{1,0:T(8,128)(2,1)S(1)}, bf16[512,128]{1,0:T(8,128)(2,1)S(1)}, u32[]{:S(2)}, u32[]{:S(2)}) collective-permute-start(bf16[512,128]{1,0:T(8,128)(2,1)S(1)} %get-tuple-element.83), channel_id=1, source_target_pairs={{0,16},{1,17},{2,18},{3,19},{4,20},{5,21},{6,22},{7,23},{8,24},{9,... | collective-permute-start | bytes 393224 | tf_op jit(solution)/shard_map/ppermute | solution.py:310
  58.7 1.0 collective-permute-done.15.refs_1_
  59.7 1.2 pointwise.1
  61.4 1.2 %collective-permute-done.16.refs_1_ = bf16[512,128]{1,0:T(8,128)(2,1)S(1)} collective-permute-done((bf16[512,128]{1,0:T(8,128)(2,1)S(1)}, bf16[512,128]{1,0:T(8,128)(2,1)S(1)}, u32[]{:S(2)}, u32[]{:S(2)}) %collective-permute-start.16) | collective-permute-done | bytes 131104 | tf_op jit(solution)/shard_map/ppermute | solution.py:310
  62.6 0.8 collective-permute-start.18
  63.4 2.6 %collective-permute-start.19 = (bf16[1024,128]{1,0:T(8,128)(2,1)S(1)}, bf16[1024,128]{1,0:T(8,128)(2,1)S(1)}, u32[]{:S(2)}, u32[]{:S(2)}) collective-permute-start(bf16[1024,128]{1,0:T(8,128)(2,1)S(1)} %pair_grads.1.refs_0_), channel_id=1, source_target_pairs={{0,2},{1,3},{2,0},{3,1},{4,6},{5,7},{6,4},{7,5},{8,10},{9,11},{10,... | collective-permute-start | bytes 786440 | tf_op jit(solution)/shard_map/ppermute | solution.py:310
  66.0 0.7 collective-permute-start.20
  66.8 4.2 %collective-permute-done.21 = f32[136,256]{1,0:T(8,128)S(1)} collective-permute-done((f32[136,256]{1,0:T(8,128)S(1)}, f32[136,256]{1,0:T(8,128)S(1)}, u32[]{:S(2)}, u32[]{:S(2)}) %collective-permute-start.21) | collective-permute-done | bytes 139296 | tf_op jit(solution)/shard_map/ppermute | solution.py:310
  71.0 1.9 %collective-permute-done.19.refs_2_ = bf16[1024,128]{1,0:T(8,128)(2,1)S(1)} collective-permute-done((bf16[1024,128]{1,0:T(8,128)(2,1)S(1)}, bf16[1024,128]{1,0:T(8,128)(2,1)S(1)}, u32[]{:S(2)}, u32[]{:S(2)}) %collective-permute-start.19) | collective-permute-done | bytes 262176 | tf_op jit(solution)/shard_map/ppermute | solution.py:310
  73.1 1.3 %collective-permute-start.22 = (bf16[2048,128]{1,0:T(8,128)(2,1)S(1)}, bf16[2048,128]{1,0:T(8,128)(2,1)S(1)}, u32[]{:S(2)}, u32[]{:S(2)}) collective-permute-start(bf16[2048,128]{1,0:T(8,128)(2,1)S(1)} %get-tuple-element.98.refs_4_), channel_id=1, source_target_pairs={{0,4},{1,5},{2,6},{3,7},{4,8},{5,9},{6,10},{7,11},{8,12},{9,13},{1... | collective-permute-start | bytes 1572872 | tf_op jit(solution)/shard_map/ppermute | solution.py:310
  74.4 1.4 %collective-permute-start.26 = (bf16[2048,128]{1,0:T(8,128)(2,1)S(1)}, bf16[2048,128]{1,0:T(8,128)(2,1)S(1)}, u32[]{:S(2)}, u32[]{:S(2)}) collective-permute-start(bf16[2048,128]{1,0:T(8,128)(2,1)S(1)} %get-tuple-element.99.refs_5_), channel_id=1, source_target_pairs={{0,12},{1,13},{2,14},{3,15},{4,0},{5,1},{6,2},{7,3},{8,4},{9,5},{1... | collective-permute-start | bytes 1572872 | tf_op jit(solution)/shard_map/ppermute | solution.py:310
  75.8 1.1 collective-permute-start.23
  76.9 2.7 %collective-permute-start.25 = (bf16[2048,128]{1,0:T(8,128)(2,1)S(1)}, bf16[2048,128]{1,0:T(8,128)(2,1)S(1)}, u32[]{:S(2)}, u32[]{:S(2)}) collective-permute-start(bf16[2048,128]{1,0:T(8,128)(2,1)S(1)} %get-tuple-element.98.refs_4_), channel_id=1, source_target_pairs={{0,12},{1,13},{2,14},{3,15},{4,0},{5,1},{6,2},{7,3},{8,4},{9,5},{1... | collective-permute-start | bytes 1572872 | tf_op jit(solution)/shard_map/ppermute | solution.py:310
  79.6 1.7 %collective-permute-done.23 = f32[136,256]{1,0:T(8,128)S(1)} collective-permute-done((f32[136,256]{1,0:T(8,128)S(1)}, f32[136,256]{1,0:T(8,128)S(1)}, u32[]{:S(2)}, u32[]{:S(2)}) %collective-permute-start.23) | collective-permute-done | bytes 139296 | tf_op jit(solution)/shard_map/ppermute | solution.py:310
  81.3 1.4 %collective-permute-done.22.refs_6_ = bf16[2048,128]{1,0:T(8,128)(2,1)S(1)} collective-permute-done((bf16[2048,128]{1,0:T(8,128)(2,1)S(1)}, bf16[2048,128]{1,0:T(8,128)(2,1)S(1)}, u32[]{:S(2)}, u32[]{:S(2)}) %collective-permute-start.22) | collective-permute-done | bytes 524320 | tf_op jit(solution)/shard_map/ppermute | solution.py:310
  82.7 2.7 %collective-permute-start.28 = (bf16[2048,128]{1,0:T(8,128)(2,1)S(1)}, bf16[2048,128]{1,0:T(8,128)(2,1)S(1)}, u32[]{:S(2)}, u32[]{:S(2)}) collective-permute-start(bf16[2048,128]{1,0:T(8,128)(2,1)S(1)} %collective-permute-done.26.refs_9_), channel_id=1, source_target_pairs={{0,12},{1,13},{2,14},{3,15},{4,0},{5,1},{6,2},{7,3},{8,4},{9,5},{1... | collective-permute-start | bytes 1572872 | tf_op jit(solution)/shard_map/ppermute | solution.py:310
  85.4 2.9 %collective-permute-done.24.refs_7_ = bf16[2048,128]{1,0:T(8,128)(2,1)S(1)} collective-permute-done((bf16[2048,128]{1,0:T(8,128)(2,1)S(1)}, bf16[2048,128]{1,0:T(8,128)(2,1)S(1)}, u32[]{:S(2)}, u32[]{:S(2)}) %collective-permute-start.24) | collective-permute-done | bytes 524320 | tf_op jit(solution)/shard_map/ppermute | solution.py:310
  88.3 1.0 collective-permute-start.34
  89.3 1.6 %collective-permute-start.35 = (f32[136,256]{1,0:T(8,128)S(1)}, f32[136,256]{1,0:T(8,128)S(1)}, u32[]{:S(2)}, u32[]{:S(2)}) collective-permute-start(f32[136,256]{1,0:T(8,128)S(1)} %add.17.s0), channel_id=1, source_target_pairs={{0,12},{1,13},{2,14},{3,15},{4,0},{5,1},{6,2},{7,3},{8,4},{9,5},{1... | collective-permute-start | bytes 417800 | tf_op jit(solution)/shard_map/ppermute | solution.py:310
  91.0 3.3 %backward_early.1.refs_4_ = f32[4096,128]{1,0:T(8,128)S(1)} custom-call(s32[2,128]{1,0:T(2,128)S(1)} %ids.1.refs_0_, bf16[128,128,128]{2,1,0:T(8,128)(2,1)S(1)} %get-tuple-element.65.refs_1_, s32[2,128]{1,0:T(2,128)S(1)} %collective-permute-done.2.refs_2_, bf16[128,128,128]{2,1,0:T(8,128)(2,1)S(1)} %collective-permute-done.3.refs_3_, ...), custom_call_target="tpu_custom_call" | custom-call | flops 805306368 | bytes 10485760 | tf_op jit(solution)/shard_map/backward_early/pallas_call | solution.py:58
  94.3 1.8 %backward_late.1 = (bf16[1024,128]{1,0:T(8,128)(2,1)S(1)}, bf16[1024,128]{1,0:T(8,128)(2,1)S(1)}, bf16[1024,128]{1,0:T(8,128)(2,1)S(1)}, bf16[1024,128]{1,0:T(8,128)(2,1)S(1)}) custom-call(s32[2,128]{1,0:T(2,128)S(1)} %ids.1.refs_0_, bf16[128,128,128]{2,1,0:T(8,128)(2,1)S(1)} %get-tuple-element.65.refs_1_, s32[2,128]{1,0:T(2,128)S(1)} %collective-permute-done.2.refs_2_, ...), custom_call_target="tpu_custom_call" | custom-call | flops 268435456 | bytes 6291456 | tf_op jit(solution)/shard_map/backward_late/pallas_call | solution.py:58
  96.1 0.9 collective-permute-done.34.s2
  97.0 1.2 %collective-permute-start.36 = (f32[136,256]{1,0:T(8,128)S(1)}, f32[136,256]{1,0:T(8,128)S(1)}, u32[]{:S(2)}, u32[]{:S(2)}) collective-permute-start(f32[136,256]{1,0:T(8,128)S(1)} %sum_u.1), channel_id=1, source_target_pairs={{0,1},{1,0},{2,3},{3,2},{4,5},{5,4},{6,7},{7,6},{8,9},{9,8},{10,11... | collective-permute-start | bytes 417800 | tf_op jit(solution)/shard_map/ppermute | solution.py:310
  98.2 2.0 %collective-permute-start.29 = (bf16[1024,128]{1,0:T(8,128)(2,1)S(1)}, bf16[1024,128]{1,0:T(8,128)(2,1)S(1)}, u32[]{:S(2)}, u32[]{:S(2)}) collective-permute-start(bf16[1024,128]{1,0:T(8,128)(2,1)S(1)} %get-tuple-element.103), channel_id=1, source_target_pairs={{0,32},{1,33},{2,34},{3,35},{4,36},{5,37},{6,38},{7,39},{8,40},{9,... | collective-permute-start | bytes 786440 | tf_op jit(solution)/shard_map/ppermute | solution.py:310
  100.3 0.6 collective-permute-start.31
  101.0 2.4 %collective-permute-start.37 = (f32[136,256]{1,0:T(8,128)S(1)}, f32[136,256]{1,0:T(8,128)S(1)}, u32[]{:S(2)}, u32[]{:S(2)}) collective-permute-start(f32[136,256]{1,0:T(8,128)S(1)} %add.18), channel_id=1, source_target_pairs={{0,2},{1,3},{2,0},{3,1},{4,6},{5,7},{6,4},{7,5},{8,10},{9,11},{10,... | collective-permute-start | bytes 417800 | tf_op jit(solution)/shard_map/ppermute | solution.py:310
  103.4 3.1 %collective-permute-done.37 = f32[136,256]{1,0:T(8,128)S(1)} collective-permute-done((f32[136,256]{1,0:T(8,128)S(1)}, f32[136,256]{1,0:T(8,128)S(1)}, u32[]{:S(2)}, u32[]{:S(2)}) %collective-permute-start.37) | collective-permute-done | bytes 139296 | tf_op jit(solution)/shard_map/ppermute | solution.py:310
  106.6 5.8 %collective-permute-start.38 = (f32[136,256]{1,0:T(8,128)S(1)}, f32[136,256]{1,0:T(8,128)S(1)}, u32[]{:S(2)}, u32[]{:S(2)}) collective-permute-start(f32[136,256]{1,0:T(8,128)S(1)} %add.19.mine), channel_id=1, source_target_pairs={{0,16},{1,17},{2,18},{3,19},{4,20},{5,21},{6,22},{7,23},{8,24},{9,... | collective-permute-start | bytes 417800 | tf_op jit(solution)/shard_map/ppermute | solution.py:310
  112.5 3.9 %collective-permute-start.32 = (bf16[512,128]{1,0:T(8,128)(2,1)S(1)}, bf16[512,128]{1,0:T(8,128)(2,1)S(1)}, u32[]{:S(2)}, u32[]{:S(2)}) collective-permute-start(bf16[512,128]{1,0:T(8,128)(2,1)S(1)} %get-tuple-element.107), channel_id=1, source_target_pairs={{0,16},{1,17},{2,18},{3,19},{4,20},{5,21},{6,22},{7,23},{8,24},{9,... | collective-permute-start | bytes 393224 | tf_op jit(solution)/shard_map/ppermute | solution.py:310
  116.4 1.0 collective-permute-done.32.peer
  117.4 0.9 last.1
  (51 shorter events, 2.6 us)
Async XLA Ops:
  0.6 1.0 copy-start.2
  1.6 2.5 %collective-permute-start = (bf16[512,128]{1,0:T(8,128)(2,1)S(1)}, bf16[512,128]{1,0:T(8,128)(2,1)S(1)}, u32[]{:S(2)}, u32[]{:S(2)}) collective-permute-start(bf16[512,128]{1,0:T(8,128)(2,1)S(1)} %get-tuple-element.58), channel_id=1, source_target_pairs={{0,16},{1,17},{2,18},{3,19},{4,20},{5,21},{6,22},{7,23},{8,24},{9,... | collective-permute-start | bytes 393224 | tf_op jit(solution)/shard_map/ppermute | solution.py:310
  4.1 16.0 %collective-permute-start.3 = (bf16[128,128,128]{2,1,0:T(8,128)(2,1)}, bf16[128,128,128]{2,1,0:T(8,128)(2,1)S(1)}, u32[]{:S(2)}, u32[]{:S(2)}) collective-permute-start(bf16[128,128,128]{2,1,0:T(8,128)(2,1)} %bitcast.5), channel_id=1, source_target_pairs={{0,16},{1,17},{2,18},{3,19},{4,20},{5,21},{6,22},{7,23},{8,24},{9,... | collective-permute-start | bytes 12582920 | tf_op jit(solution)/shard_map/ppermute | solution.py:310
  4.5 13.3 %collective-permute-start.1 = (bf16[1024,128]{1,0:T(8,128)(2,1)S(1)}, bf16[1024,128]{1,0:T(8,128)(2,1)S(1)}, u32[]{:S(2)}, u32[]{:S(2)}) collective-permute-start(bf16[1024,128]{1,0:T(8,128)(2,1)S(1)} %pair.1.refs_4_), channel_id=1, source_target_pairs={{0,32},{1,33},{2,34},{3,35},{4,36},{5,37},{6,38},{7,39},{8,40},{9,... | collective-permute-start | bytes 786440 | tf_op jit(solution)/shard_map/ppermute | solution.py:310
  7.4 10.4 %collective-permute-start.4 = (bf16[1024,128]{1,0:T(8,128)(2,1)S(1)}, bf16[1024,128]{1,0:T(8,128)(2,1)S(1)}, u32[]{:S(2)}, u32[]{:S(2)}) collective-permute-start(bf16[1024,128]{1,0:T(8,128)(2,1)S(1)} %pair.1.refs_4_), channel_id=1, source_target_pairs={{0,64},{1,65},{2,66},{3,67},{4,68},{5,69},{6,70},{7,71},{8,72},{9,... | collective-permute-start | bytes 786440 | tf_op jit(solution)/shard_map/ppermute | solution.py:310
  7.7 12.4 %collective-permute-start.5 = (bf16[1024,128]{1,0:T(8,128)(2,1)S(1)}, bf16[1024,128]{1,0:T(8,128)(2,1)S(1)}, u32[]{:S(2)}, u32[]{:S(2)}) collective-permute-start(bf16[1024,128]{1,0:T(8,128)(2,1)S(1)} %pair.1.refs_4_), channel_id=1, source_target_pairs={{0,96},{1,97},{2,98},{3,99},{4,100},{5,101},{6,102},{7,103},{8,104... | collective-permute-start | bytes 786440 | tf_op jit(solution)/shard_map/ppermute | solution.py:310
  8.4 0.7 copy-start.5
  9.1 0.7 copy-start.6
  9.7 8.1 %collective-permute-start.2 = (s32[2,128]{1,0:T(2,128)S(1)}, s32[2,128]{1,0:T(2,128)S(1)}, u32[]{:S(2)}, u32[]{:S(2)}) collective-permute-start(s32[2,128]{1,0:T(2,128)S(1)} %ids.1.refs_0_), channel_id=1, source_target_pairs={{0,16},{1,17},{2,18},{3,19},{4,20},{5,21},{6,22},{7,23},{8,24},{9,... | collective-permute-start | bytes 3080 | tf_op jit(solution)/shard_map/ppermute | solution.py:310
  11.9 2.2 %copy-start = (bf16[1,1,128,128,128]{4,3,2,1,0:T(8,128)(2,1)S(1)}, bf16[1,1,128,128,128]{4,3,2,1,0:T(8,128)(2,1)}, u32[]{:S(2)}) copy-start(bf16[1,1,128,128,128]{4,3,2,1,0:T(8,128)(2,1)} %param.8) | copy-start | bytes 12582916
  14.1 0.9 copy-start.1
  15.1 0.9 copy-start.3
  16.0 0.7 copy-start.4
  22.0 10.8 %collective-permute-start.6 = (bf16[2048,128]{1,0:T(8,128)(2,1)S(1)}, bf16[2048,128]{1,0:T(8,128)(2,1)S(1)}, u32[]{:S(2)}, u32[]{:S(2)}) collective-permute-start(bf16[2048,128]{1,0:T(8,128)(2,1)S(1)} %get-tuple-element.71), channel_id=1, source_target_pairs={{0,4},{1,5},{2,6},{3,7},{4,8},{5,9},{6,10},{7,11},{8,12},{9,13},{1... | collective-permute-start | bytes 1572872 | tf_op jit(solution)/shard_map/ppermute | solution.py:310
  23.9 8.9 %collective-permute-start.7 = (bf16[2048,128]{1,0:T(8,128)(2,1)S(1)}, bf16[2048,128]{1,0:T(8,128)(2,1)S(1)}, u32[]{:S(2)}, u32[]{:S(2)}) collective-permute-start(bf16[2048,128]{1,0:T(8,128)(2,1)S(1)} %get-tuple-element.72), channel_id=1, source_target_pairs={{0,12},{1,13},{2,14},{3,15},{4,0},{5,1},{6,2},{7,3},{8,4},{9,5},{1... | collective-permute-start | bytes 1572872 | tf_op jit(solution)/shard_map/ppermute | solution.py:310
  27.8 10.2 %collective-permute-start.9 = (bf16[2048,128]{1,0:T(8,128)(2,1)S(1)}, bf16[2048,128]{1,0:T(8,128)(2,1)S(1)}, u32[]{:S(2)}, u32[]{:S(2)}) collective-permute-start(bf16[2048,128]{1,0:T(8,128)(2,1)S(1)} %get-tuple-element.74), channel_id=1, source_target_pairs={{0,12},{1,13},{2,14},{3,15},{4,0},{5,1},{6,2},{7,3},{8,4},{9,5},{1... | collective-permute-start | bytes 1572872 | tf_op jit(solution)/shard_map/ppermute | solution.py:310
  29.3 9.5 %collective-permute-start.10 = (bf16[2048,128]{1,0:T(8,128)(2,1)S(1)}, bf16[2048,128]{1,0:T(8,128)(2,1)S(1)}, u32[]{:S(2)}, u32[]{:S(2)}) collective-permute-start(bf16[2048,128]{1,0:T(8,128)(2,1)S(1)} %get-tuple-element.76), channel_id=1, source_target_pairs={{0,4},{1,5},{2,6},{3,7},{4,8},{5,9},{6,10},{7,11},{8,12},{9,13},{1... | collective-permute-start | bytes 1572872 | tf_op jit(solution)/shard_map/ppermute | solution.py:310
  33.1 11.4 %collective-permute-start.8 = (bf16[2048,128]{1,0:T(8,128)(2,1)S(1)}, bf16[2048,128]{1,0:T(8,128)(2,1)S(1)}, u32[]{:S(2)}, u32[]{:S(2)}) collective-permute-start(bf16[2048,128]{1,0:T(8,128)(2,1)S(1)} %get-tuple-element.73), channel_id=1, source_target_pairs={{0,4},{1,5},{2,6},{3,7},{4,8},{5,9},{6,10},{7,11},{8,12},{9,13},{1... | collective-permute-start | bytes 1572872 | tf_op jit(solution)/shard_map/ppermute | solution.py:310
  34.1 10.3 %collective-permute-start.11 = (bf16[2048,128]{1,0:T(8,128)(2,1)S(1)}, bf16[2048,128]{1,0:T(8,128)(2,1)S(1)}, u32[]{:S(2)}, u32[]{:S(2)}) collective-permute-start(bf16[2048,128]{1,0:T(8,128)(2,1)S(1)} %get-tuple-element.77), channel_id=1, source_target_pairs={{0,12},{1,13},{2,14},{3,15},{4,0},{5,1},{6,2},{7,3},{8,4},{9,5},{1... | collective-permute-start | bytes 1572872 | tf_op jit(solution)/shard_map/ppermute | solution.py:310
  44.8 6.8 %collective-permute-start.12 = (bf16[1024,128]{1,0:T(8,128)(2,1)S(1)}, bf16[1024,128]{1,0:T(8,128)(2,1)S(1)}, u32[]{:S(2)}, u32[]{:S(2)}) collective-permute-start(bf16[1024,128]{1,0:T(8,128)(2,1)S(1)} %get-tuple-element.79), channel_id=1, source_target_pairs={{0,1},{1,2},{2,3},{3,0},{4,5},{5,6},{6,7},{7,4},{8,9},{9,10},{10,1... | collective-permute-start | bytes 786440 | tf_op jit(solution)/shard_map/ppermute | solution.py:310
  45.8 9.6 %collective-permute-start.13 = (bf16[1024,128]{1,0:T(8,128)(2,1)S(1)}, bf16[1024,128]{1,0:T(8,128)(2,1)S(1)}, u32[]{:S(2)}, u32[]{:S(2)}) collective-permute-start(bf16[1024,128]{1,0:T(8,128)(2,1)S(1)} %get-tuple-element.80), channel_id=1, source_target_pairs={{0,2},{1,3},{2,0},{3,1},{4,6},{5,7},{6,4},{7,5},{8,10},{9,11},{10,... | collective-permute-start | bytes 786440 | tf_op jit(solution)/shard_map/ppermute | solution.py:310
  48.5 6.9 %collective-permute-start.14 = (bf16[1024,128]{1,0:T(8,128)(2,1)S(1)}, bf16[1024,128]{1,0:T(8,128)(2,1)S(1)}, u32[]{:S(2)}, u32[]{:S(2)}) collective-permute-start(bf16[1024,128]{1,0:T(8,128)(2,1)S(1)} %get-tuple-element.81), channel_id=1, source_target_pairs={{0,3},{1,0},{2,1},{3,2},{4,7},{5,4},{6,5},{7,6},{8,11},{9,8},{10,9... | collective-permute-start | bytes 786440 | tf_op jit(solution)/shard_map/ppermute | solution.py:310
  55.5 4.2 %collective-permute-start.15 = (bf16[512,128]{1,0:T(8,128)(2,1)S(1)}, bf16[512,128]{1,0:T(8,128)(2,1)S(1)}, u32[]{:S(2)}, u32[]{:S(2)}) collective-permute-start(bf16[512,128]{1,0:T(8,128)(2,1)S(1)} %get-tuple-element.83), channel_id=1, source_target_pairs={{0,16},{1,17},{2,18},{3,19},{4,20},{5,21},{6,22},{7,23},{8,24},{9,... | collective-permute-start | bytes 393224 | tf_op jit(solution)/shard_map/ppermute | solution.py:310
  60.9 1.7 %collective-permute-start.17 = (f32[136,256]{1,0:T(8,128)S(1)}, f32[136,256]{1,0:T(8,128)S(1)}, u32[]{:S(2)}, u32[]{:S(2)}) collective-permute-start(f32[136,256]{1,0:T(8,128)S(1)} %get-tuple-element.90), channel_id=1, source_target_pairs={{0,16},{1,17},{2,18},{3,19},{4,20},{5,21},{6,22},{7,23},{8,24},{9,... | collective-permute-start | bytes 417800 | tf_op jit(solution)/shard_map/ppermute | solution.py:310
  61.2 1.3 %collective-permute-start.16 = (bf16[512,128]{1,0:T(8,128)(2,1)S(1)}, bf16[512,128]{1,0:T(8,128)(2,1)S(1)}, u32[]{:S(2)}, u32[]{:S(2)}) collective-permute-start(bf16[512,128]{1,0:T(8,128)(2,1)S(1)} %get-tuple-element.89), channel_id=1, source_target_pairs={{0,16},{1,17},{2,18},{3,19},{4,20},{5,21},{6,22},{7,23},{8,24},{9,... | collective-permute-start | bytes 393224 | tf_op jit(solution)/shard_map/ppermute | solution.py:310
  62.6 8.4 %collective-permute-start.18 = (bf16[1024,128]{1,0:T(8,128)(2,1)S(1)}, bf16[1024,128]{1,0:T(8,128)(2,1)S(1)}, u32[]{:S(2)}, u32[]{:S(2)}) collective-permute-start(bf16[1024,128]{1,0:T(8,128)(2,1)S(1)} %pair_grads.1.refs_0_), channel_id=1, source_target_pairs={{0,1},{1,2},{2,3},{3,0},{4,5},{5,6},{6,7},{7,4},{8,9},{9,10},{10,1... | collective-permute-start | bytes 786440 | tf_op jit(solution)/shard_map/ppermute | solution.py:310
  63.4 9.5 %collective-permute-start.19 = (bf16[1024,128]{1,0:T(8,128)(2,1)S(1)}, bf16[1024,128]{1,0:T(8,128)(2,1)S(1)}, u32[]{:S(2)}, u32[]{:S(2)}) collective-permute-start(bf16[1024,128]{1,0:T(8,128)(2,1)S(1)} %pair_grads.1.refs_0_), channel_id=1, source_target_pairs={{0,2},{1,3},{2,0},{3,1},{4,6},{5,7},{6,4},{7,5},{8,10},{9,11},{10,... | collective-permute-start | bytes 786440 | tf_op jit(solution)/shard_map/ppermute | solution.py:310
  66.0 7.0 %collective-permute-start.20 = (bf16[1024,128]{1,0:T(8,128)(2,1)S(1)}, bf16[1024,128]{1,0:T(8,128)(2,1)S(1)}, u32[]{:S(2)}, u32[]{:S(2)}) collective-permute-start(bf16[1024,128]{1,0:T(8,128)(2,1)S(1)} %pair_grads.1.refs_0_), channel_id=1, source_target_pairs={{0,3},{1,0},{2,1},{3,2},{4,7},{5,4},{6,5},{7,6},{8,11},{9,8},{10,9... | collective-permute-start | bytes 786440 | tf_op jit(solution)/shard_map/ppermute | solution.py:310
  66.7 4.3 %collective-permute-start.21 = (f32[136,256]{1,0:T(8,128)S(1)}, f32[136,256]{1,0:T(8,128)S(1)}, u32[]{:S(2)}, u32[]{:S(2)}) collective-permute-start(f32[136,256]{1,0:T(8,128)S(1)} %add.15), channel_id=1, source_target_pairs={{0,32},{1,33},{2,34},{3,35},{4,36},{5,37},{6,38},{7,39},{8,40},{9,... | collective-permute-start | bytes 417800 | tf_op jit(solution)/shard_map/ppermute | solution.py:310
  73.1 9.6 %collective-permute-start.22 = (bf16[2048,128]{1,0:T(8,128)(2,1)S(1)}, bf16[2048,128]{1,0:T(8,128)(2,1)S(1)}, u32[]{:S(2)}, u32[]{:S(2)}) collective-permute-start(bf16[2048,128]{1,0:T(8,128)(2,1)S(1)} %get-tuple-element.98.refs_4_), channel_id=1, source_target_pairs={{0,4},{1,5},{2,6},{3,7},{4,8},{5,9},{6,10},{7,11},{8,12},{9,13},{1... | collective-permute-start | bytes 1572872 | tf_op jit(solution)/shard_map/ppermute | solution.py:310
  74.4 8.3 %collective-permute-start.26 = (bf16[2048,128]{1,0:T(8,128)(2,1)S(1)}, bf16[2048,128]{1,0:T(8,128)(2,1)S(1)}, u32[]{:S(2)}, u32[]{:S(2)}) collective-permute-start(bf16[2048,128]{1,0:T(8,128)(2,1)S(1)} %get-tuple-element.99.refs_5_), channel_id=1, source_target_pairs={{0,12},{1,13},{2,14},{3,15},{4,0},{5,1},{6,2},{7,3},{8,4},{9,5},{1... | collective-permute-start | bytes 1572872 | tf_op jit(solution)/shard_map/ppermute | solution.py:310
  75.8 5.4 %collective-permute-start.23 = (f32[136,256]{1,0:T(8,128)S(1)}, f32[136,256]{1,0:T(8,128)S(1)}, u32[]{:S(2)}, u32[]{:S(2)}) collective-permute-start(f32[136,256]{1,0:T(8,128)S(1)} %add.16), channel_id=1, source_target_pairs={{0,64},{1,65},{2,66},{3,67},{4,68},{5,69},{6,70},{7,71},{8,72},{9,... | collective-permute-start | bytes 417800 | tf_op jit(solution)/shard_map/ppermute | solution.py:310
  76.9 11.4 %collective-permute-start.24 = (bf16[2048,128]{1,0:T(8,128)(2,1)S(1)}, bf16[2048,128]{1,0:T(8,128)(2,1)S(1)}, u32[]{:S(2)}, u32[]{:S(2)}) collective-permute-start(bf16[2048,128]{1,0:T(8,128)(2,1)S(1)} %get-tuple-element.99.refs_5_), channel_id=1, source_target_pairs={{0,4},{1,5},{2,6},{3,7},{4,8},{5,9},{6,10},{7,11},{8,12},{9,13},{1... | collective-permute-start | bytes 1572872 | tf_op jit(solution)/shard_map/ppermute | solution.py:310
  76.9 12.4 %collective-permute-start.25 = (bf16[2048,128]{1,0:T(8,128)(2,1)S(1)}, bf16[2048,128]{1,0:T(8,128)(2,1)S(1)}, u32[]{:S(2)}, u32[]{:S(2)}) collective-permute-start(bf16[2048,128]{1,0:T(8,128)(2,1)S(1)} %get-tuple-element.98.refs_4_), channel_id=1, source_target_pairs={{0,12},{1,13},{2,14},{3,15},{4,0},{5,1},{6,2},{7,3},{8,4},{9,5},{1... | collective-permute-start | bytes 1572872 | tf_op jit(solution)/shard_map/ppermute | solution.py:310
  82.7 11.6 %collective-permute-start.27 = (bf16[2048,128]{1,0:T(8,128)(2,1)S(1)}, bf16[2048,128]{1,0:T(8,128)(2,1)S(1)}, u32[]{:S(2)}, u32[]{:S(2)}) collective-permute-start(bf16[2048,128]{1,0:T(8,128)(2,1)S(1)} %collective-permute-done.22.refs_6_), channel_id=1, source_target_pairs={{0,4},{1,5},{2,6},{3,7},{4,8},{5,9},{6,10},{7,11},{8,12},{9,13},{1... | collective-permute-start | bytes 1572872 | tf_op jit(solution)/shard_map/ppermute | solution.py:310
  82.7 11.6 %collective-permute-start.28 = (bf16[2048,128]{1,0:T(8,128)(2,1)S(1)}, bf16[2048,128]{1,0:T(8,128)(2,1)S(1)}, u32[]{:S(2)}, u32[]{:S(2)}) collective-permute-start(bf16[2048,128]{1,0:T(8,128)(2,1)S(1)} %collective-permute-done.26.refs_9_), channel_id=1, source_target_pairs={{0,12},{1,13},{2,14},{3,15},{4,0},{5,1},{6,2},{7,3},{8,4},{9,5},{1... | collective-permute-start | bytes 1572872 | tf_op jit(solution)/shard_map/ppermute | solution.py:310
  85.4 10.7 %collective-permute-start.33 = (f32[136,256]{1,0:T(8,128)S(1)}, f32[136,256]{1,0:T(8,128)S(1)}, u32[]{:S(2)}, u32[]{:S(2)}) collective-permute-start(f32[136,256]{1,0:T(8,128)S(1)} %add.17.s0), channel_id=1, source_target_pairs={{0,4},{1,5},{2,6},{3,7},{4,8},{5,9},{6,10},{7,11},{8,12},{9,13},{1... | collective-permute-start | bytes 417800 | tf_op jit(solution)/shard_map/ppermute | solution.py:310
  88.3 8.7 %collective-permute-start.34 = (f32[136,256]{1,0:T(8,128)S(1)}, f32[136,256]{1,0:T(8,128)S(1)}, u32[]{:S(2)}, u32[]{:S(2)}) collective-permute-start(f32[136,256]{1,0:T(8,128)S(1)} %add.17.s0), channel_id=1, source_target_pairs={{0,8},{1,9},{2,10},{3,11},{4,12},{5,13},{6,14},{7,15},{8,0},{9,1},... | collective-permute-start | bytes 417800 | tf_op jit(solution)/shard_map/ppermute | solution.py:310
  89.3 7.7 %collective-permute-start.35 = (f32[136,256]{1,0:T(8,128)S(1)}, f32[136,256]{1,0:T(8,128)S(1)}, u32[]{:S(2)}, u32[]{:S(2)}) collective-permute-start(f32[136,256]{1,0:T(8,128)S(1)} %add.17.s0), channel_id=1, source_target_pairs={{0,12},{1,13},{2,14},{3,15},{4,0},{5,1},{6,2},{7,3},{8,4},{9,5},{1... | collective-permute-start | bytes 417800 | tf_op jit(solution)/shard_map/ppermute | solution.py:310
  97.0 4.0 %collective-permute-start.36 = (f32[136,256]{1,0:T(8,128)S(1)}, f32[136,256]{1,0:T(8,128)S(1)}, u32[]{:S(2)}, u32[]{:S(2)}) collective-permute-start(f32[136,256]{1,0:T(8,128)S(1)} %sum_u.1), channel_id=1, source_target_pairs={{0,1},{1,0},{2,3},{3,2},{4,5},{5,4},{6,7},{7,6},{8,9},{9,8},{10,11... | collective-permute-start | bytes 417800 | tf_op jit(solution)/shard_map/ppermute | solution.py:310
  98.2 14.1 %collective-permute-start.29 = (bf16[1024,128]{1,0:T(8,128)(2,1)S(1)}, bf16[1024,128]{1,0:T(8,128)(2,1)S(1)}, u32[]{:S(2)}, u32[]{:S(2)}) collective-permute-start(bf16[1024,128]{1,0:T(8,128)(2,1)S(1)} %get-tuple-element.103), channel_id=1, source_target_pairs={{0,32},{1,33},{2,34},{3,35},{4,36},{5,37},{6,38},{7,39},{8,40},{9,... | collective-permute-start | bytes 786440 | tf_op jit(solution)/shard_map/ppermute | solution.py:310
  100.3 12.1 %collective-permute-start.30 = (bf16[1024,128]{1,0:T(8,128)(2,1)S(1)}, bf16[1024,128]{1,0:T(8,128)(2,1)S(1)}, u32[]{:S(2)}, u32[]{:S(2)}) collective-permute-start(bf16[1024,128]{1,0:T(8,128)(2,1)S(1)} %get-tuple-element.104), channel_id=1, source_target_pairs={{0,64},{1,65},{2,66},{3,67},{4,68},{5,69},{6,70},{7,71},{8,72},{9,... | collective-permute-start | bytes 786440 | tf_op jit(solution)/shard_map/ppermute | solution.py:310
  100.3 12.1 %collective-permute-start.31 = (bf16[1024,128]{1,0:T(8,128)(2,1)S(1)}, bf16[1024,128]{1,0:T(8,128)(2,1)S(1)}, u32[]{:S(2)}, u32[]{:S(2)}) collective-permute-start(bf16[1024,128]{1,0:T(8,128)(2,1)S(1)} %get-tuple-element.105), channel_id=1, source_target_pairs={{0,96},{1,97},{2,98},{3,99},{4,100},{5,101},{6,102},{7,103},{8,104... | collective-permute-start | bytes 786440 | tf_op jit(solution)/shard_map/ppermute | solution.py:310
  101.0 5.5 %collective-permute-start.37 = (f32[136,256]{1,0:T(8,128)S(1)}, f32[136,256]{1,0:T(8,128)S(1)}, u32[]{:S(2)}, u32[]{:S(2)}) collective-permute-start(f32[136,256]{1,0:T(8,128)S(1)} %add.18), channel_id=1, source_target_pairs={{0,2},{1,3},{2,0},{3,1},{4,6},{5,7},{6,4},{7,5},{8,10},{9,11},{10,... | collective-permute-start | bytes 417800 | tf_op jit(solution)/shard_map/ppermute | solution.py:310
  106.6 10.8 %collective-permute-start.38 = (f32[136,256]{1,0:T(8,128)S(1)}, f32[136,256]{1,0:T(8,128)S(1)}, u32[]{:S(2)}, u32[]{:S(2)}) collective-permute-start(f32[136,256]{1,0:T(8,128)S(1)} %add.19.mine), channel_id=1, source_target_pairs={{0,16},{1,17},{2,18},{3,19},{4,20},{5,21},{6,22},{7,23},{8,24},{9,... | collective-permute-start | bytes 417800 | tf_op jit(solution)/shard_map/ppermute | solution.py:310
  112.5 4.9 %collective-permute-start.32 = (bf16[512,128]{1,0:T(8,128)(2,1)S(1)}, bf16[512,128]{1,0:T(8,128)(2,1)S(1)}, u32[]{:S(2)}, u32[]{:S(2)}) collective-permute-start(bf16[512,128]{1,0:T(8,128)(2,1)S(1)} %get-tuple-element.107), channel_id=1, source_target_pairs={{0,16},{1,17},{2,18},{3,19},{4,20},{5,21},{6,22},{7,23},{8,24},{9,... | collective-permute-start | bytes 393224 | tf_op jit(solution)/shard_map/ppermute | solution.py:310

commit v8 on v7

--- a/solution.py
+++ b/solution.py
@@ -200,9 +200,9 @@
     )
 
 
-def point_kernel(scale, *refs):
+def point_kernel(*refs):
     own, peer, weight, bias, cotangent = refs[:5]
-    out_act, keep_g, give_g, keep_w, give_w, whole, grads, full = refs[5:]
+    out_act, keep_g, give_g, whole, grad_out, grads = refs[5:]
     u, v, y, c = coords()
     whole[:, lanes_of(c)] = own[...]
     whole[:, lanes_of(1 - c)] = peer[...]
@@ -218,10 +218,15 @@
     ).astype(BF)
     keep_g[...] = grads[:, lanes_of(c)]
     give_g[...] = grads[:, lanes_of(1 - c)]
+    grad_out[...] = grad_pre
+
+
+def gradient_kernel(scale, whole, grad_pre, keep_w, give_w, full):
+    u, v, y, c = coords()
     full[...] = lax.dot_general(
-        aggregated, grad_pre, (((0,), (0,)), ((), ())), preferred_element_type=F32
+        whole[...], grad_pre[...], (((0,), (0,)), ((), ())), preferred_element_type=F32
     ) * scale
-    bias_grad = jnp.sum(grad_pre.astype(F32), axis=0, keepdims=True) * scale
+    bias_grad = jnp.sum(grad_pre[...].astype(F32), axis=0, keepdims=True) * scale
     for out, core in ((keep_w, c), (give_w, 1 - c)):
         out[:HALF, :] = full[rows_at(core * HALF, HALF), :]
         out[HALF:, :] = jnp.broadcast_to(bias_grad, (8, F))
@@ -406,19 +411,19 @@
         flops=16 * ROWS * HALF, moved=4 * MIB,
     )
     own, other = finish_call(exchange(sums, along_v), "aggregate")
-    out_act, keep_g, give_g, keep_w, give_w = local_call(
-        lambda *refs: point_kernel(scale, *refs), "pointwise", [vmem()] * 5,
-        [shape(ROWS, F), shape(ROWS), shape(ROWS)] + [shape(HALF + 8, F, F32)] * 2,
-        [own, to_peer(other), weight, bias, cotangent], 8, flops=6 * ROWS * F * F,
-        moved=2 * MIB,
-        scratch=[
-            pltpu.VMEM((ROWS, F), BF), pltpu.VMEM((ROWS, F), BF), pltpu.VMEM((F, F), F32),
-        ],
-    )
-
+    out_act, keep_g, give_g, whole, grad_pre = local_call(
+        point_kernel, "pointwise", [vmem()] * 5,
+        [shape(ROWS, F), shape(ROWS), shape(ROWS), shape(ROWS, F), shape(ROWS, F)],
+        [own, to_peer(other), weight, bias, cotangent], 8, flops=4 * ROWS * F * F,
+        moved=2 * MIB, scratch=[pltpu.VMEM((ROWS, F), BF)],
+    )
     got_g = to_peer(give_g)
+    keep_w, give_w = local_call(
+        lambda *refs: gradient_kernel(scale, *refs), "gradients", [vmem()] * 2,
+        [shape(HALF + 8, F, F32)] * 2, [whole, grad_pre], 8, flops=2 * ROWS * F * F,
+        scratch=[pltpu.VMEM((F, F), F32)],
+    )
     piece = to_peer(give_w)
-    got_g, piece = lax.optimization_barrier((got_g, piece))
     grads = stack_call([keep_g, got_g], "pair_grads")
     firsts = spread(grads, along_v)
     piece = with_y(keep_w + piece, 1)

time: 119 us -> 118 us (level)
    pallas_call x18 -> x19, Pallas kernels: 15.1 us -> 15.4 us  [local_call(): pl.pallas_call(kernel, out_shape=outs, in_specs=ins, out_specs=[vmem()] *...]
where the time goes in v8:
time: 118 us
  starting transfers between devices  56.8 us (48%)
  waiting for transfers between devices  37.6 us (32%)
  Pallas kernels  15.4 us (13%)
  local copies, waits for them, and re-layouts  6.97 us (6%)
    ppermute x39, starting transfers between devices, permute(): return lax.ppermute(value, ('row', 'col'), pairs)  56.8 us
    ppermute x39, waiting for transfers between devices, permute(): return lax.ppermute(value, ('row', 'col'), pairs)  37.6 us
    pallas_call x19, Pallas kernels, local_call(): pl.pallas_call(kernel, out_shape=outs, in_specs=ins, out_specs=[vmem()] *...  15.4 us
    unnamed x14, local copies, waits for them, and re-layouts  6.97 us
  transfers between devices with their start and end apart: 39, of which 21 were waited for; matrix products, arithmetic and copies ran while one was open for 0% of the time, Pallas kernels for 9%

profile of v8, /device:TPU:1, one launch (start us, length us, event | category | flops | bytes accessed | tf_op | source)
XLA Modules:
  0.0 117.7 jit_solution(4051879395453979823)
XLA Ops:
  0.6 0.9 copy-done.2
  1.6 1.5 %collective-permute-start = (bf16[512,128]{1,0:T(8,128)(2,1)S(1)}, bf16[512,128]{1,0:T(8,128)(2,1)S(1)}, u32[]{:S(2)}, u32[]{:S(2)}) collective-permute-start(bf16[512,128]{1,0:T(8,128)(2,1)S(1)} %get-tuple-element.58), channel_id=1, source_target_pairs={{0,16},{1,17},{2,18},{3,19},{4,20},{5,21},{6,22},{7,23},{8,24},{9,... | collective-permute-start | bytes 393224 | tf_op jit(solution)/shard_map/ppermute | solution.py:315
  3.1 1.0 collective-permute-done.refs_1_
  4.5 2.9 %collective-permute-start.1 = (bf16[1024,128]{1,0:T(8,128)(2,1)S(1)}, bf16[1024,128]{1,0:T(8,128)(2,1)S(1)}, u32[]{:S(2)}, u32[]{:S(2)}) collective-permute-start(bf16[1024,128]{1,0:T(8,128)(2,1)S(1)} %pair.1.refs_4_), channel_id=1, source_target_pairs={{0,32},{1,33},{2,34},{3,35},{4,36},{5,37},{6,38},{7,39},{8,40},{9,... | collective-permute-start | bytes 786440 | tf_op jit(solution)/shard_map/ppermute | solution.py:315
  7.7 0.7 collective-permute-start.5
  8.4 0.7 copy-done.5
  9.1 0.7 copy-done.6
  9.7 2.2 %collective-permute-start.2 = (s32[2,128]{1,0:T(2,128)S(1)}, s32[2,128]{1,0:T(2,128)S(1)}, u32[]{:S(2)}, u32[]{:S(2)}) collective-permute-start(s32[2,128]{1,0:T(2,128)S(1)} %ids.1.refs_0_), channel_id=1, source_target_pairs={{0,16},{1,17},{2,18},{3,19},{4,20},{5,21},{6,22},{7,23},{8,24},{9,... | collective-permute-start | bytes 3080 | tf_op jit(solution)/shard_map/ppermute | solution.py:315
  11.9 2.2 %copy-done = bf16[1,1,128,128,128]{4,3,2,1,0:T(8,128)(2,1)S(1)} copy-done((bf16[1,1,128,128,128]{4,3,2,1,0:T(8,128)(2,1)S(1)}, bf16[1,1,128,128,128]{4,3,2,1,0:T(8,128)(2,1)}, u32[]{:S(2)}) %copy-start) | copy-done | bytes 4194328
  14.1 0.9 copy-done.1
  15.1 0.9 copy-done.3
  16.0 0.7 copy-done.4
  16.7 0.5 prologue.1
  17.2 0.6 collective-permute-done.1.refs_5_
  17.8 2.4 %collective-permute-done.5.refs_7_ = bf16[1024,128]{1,0:T(8,128)(2,1)S(1)} collective-permute-done((bf16[1024,128]{1,0:T(8,128)(2,1)S(1)}, bf16[1024,128]{1,0:T(8,128)(2,1)S(1)}, u32[]{:S(2)}, u32[]{:S(2)}) %collective-permute-start.5) | collective-permute-done | bytes 262176 | tf_op jit(solution)/shard_map/ppermute | solution.py:315
  20.2 1.8 %forward_far.1 = (bf16[4096,128]{1,0:T(8,128)(2,1)S(1)}, bf16[2048,128]{1,0:T(8,128)(2,1)S(1)}, bf16[2048,128]{1,0:T(8,128)(2,1)S(1)}) custom-call(s32[2,128]{1,0:T(2,128)S(1)} %ids.1.refs_0_, bf16[128,128,128]{2,1,0:T(8,128)(2,1)S(1)} %get-tuple-element.65.refs_1_, s32[2,128]{1,0:T(2,128)S(1)} %collective-permute-done.2.refs_2_, ...), custom_call_target="tpu_custom_call" | custom-call | flops 268435456 | bytes 6291456 | tf_op jit(solution)/shard_map/forward_far/pallas_call | solution.py:58
  22.0 1.9 %collective-permute-start.6 = (bf16[2048,128]{1,0:T(8,128)(2,1)S(1)}, bf16[2048,128]{1,0:T(8,128)(2,1)S(1)}, u32[]{:S(2)}, u32[]{:S(2)}) collective-permute-start(bf16[2048,128]{1,0:T(8,128)(2,1)S(1)} %get-tuple-element.71), channel_id=1, source_target_pairs={{0,4},{1,5},{2,6},{3,7},{4,8},{5,9},{6,10},{7,11},{8,12},{9,13},{1... | collective-permute-start | bytes 1572872 | tf_op jit(solution)/shard_map/ppermute | solution.py:315
  23.9 2.2 %collective-permute-start.7 = (bf16[2048,128]{1,0:T(8,128)(2,1)S(1)}, bf16[2048,128]{1,0:T(8,128)(2,1)S(1)}, u32[]{:S(2)}, u32[]{:S(2)}) collective-permute-start(bf16[2048,128]{1,0:T(8,128)(2,1)S(1)} %get-tuple-element.72), channel_id=1, source_target_pairs={{0,12},{1,13},{2,14},{3,15},{4,0},{5,1},{6,2},{7,3},{8,4},{9,5},{1... | collective-permute-start | bytes 1572872 | tf_op jit(solution)/shard_map/ppermute | solution.py:315
  26.1 1.7 %forward_plain.1 = (bf16[2048,128]{1,0:T(8,128)(2,1)S(1)}, bf16[2048,128]{1,0:T(8,128)(2,1)S(1)}) custom-call(s32[2,128]{1,0:T(2,128)S(1)} %ids.1.refs_0_, bf16[128,128,128]{2,1,0:T(8,128)(2,1)S(1)} %get-tuple-element.65.refs_1_, s32[2,128]{1,0:T(2,128)S(1)} %collective-permute-done.2.refs_2_, bf16[128,128,128]{2,1,0:T(8,128)(2,1)S(1)} %collective-permute-done.3.refs_3_, ...), custom_call_target="tpu_custom_call" | custom-call | flops 268435456 | bytes 3145728 | tf_op jit(solution)/shard_map/forward_plain/pallas_call | solution.py:58
  27.8 1.4 %collective-permute-start.9 = (bf16[2048,128]{1,0:T(8,128)(2,1)S(1)}, bf16[2048,128]{1,0:T(8,128)(2,1)S(1)}, u32[]{:S(2)}, u32[]{:S(2)}) collective-permute-start(bf16[2048,128]{1,0:T(8,128)(2,1)S(1)} %get-tuple-element.74), channel_id=1, source_target_pairs={{0,12},{1,13},{2,14},{3,15},{4,0},{5,1},{6,2},{7,3},{8,4},{9,5},{1... | collective-permute-start | bytes 1572872 | tf_op jit(solution)/shard_map/ppermute | solution.py:315
  29.3 2.9 %forward_near.1 = (bf16[2048,128]{1,0:T(8,128)(2,1)S(1)}, bf16[2048,128]{1,0:T(8,128)(2,1)S(1)}, bf16[2048,128]{1,0:T(8,128)(2,1)S(1)}, bf16[2048,128]{1,0:T(8,128)(2,1)S(1)}) custom-call(s32[2,128]{1,0:T(2,128)S(1)} %ids.1.refs_0_, bf16[128,128,128]{2,1,0:T(8,128)(2,1)S(1)} %get-tuple-element.65.refs_1_, s32[2,128]{1,0:T(2,128)S(1)} %collective-permute-done.2.refs_2_, ...), custom_call_target="tpu_custom_call" | custom-call | flops 536870912 | bytes 5242880 | tf_op jit(solution)/shard_map/forward_near/pallas_call | solution.py:58
  32.2 0.6 collective-permute-done.6.extra1
  33.1 1.1 collective-permute-start.8
  34.1 1.9 %collective-permute-start.11 = (bf16[2048,128]{1,0:T(8,128)(2,1)S(1)}, bf16[2048,128]{1,0:T(8,128)(2,1)S(1)}, u32[]{:S(2)}, u32[]{:S(2)}) collective-permute-start(bf16[2048,128]{1,0:T(8,128)(2,1)S(1)} %get-tuple-element.77), channel_id=1, source_target_pairs={{0,12},{1,13},{2,14},{3,15},{4,0},{5,1},{6,2},{7,3},{8,4},{9,5},{1... | collective-permute-start | bytes 1572872 | tf_op jit(solution)/shard_map/ppermute | solution.py:315
  36.0 2.0 %collective-permute-done.9.refs_2_ = bf16[2048,128]{1,0:T(8,128)(2,1)S(1)} collective-permute-done((bf16[2048,128]{1,0:T(8,128)(2,1)S(1)}, bf16[2048,128]{1,0:T(8,128)(2,1)S(1)}, u32[]{:S(2)}, u32[]{:S(2)}) %collective-permute-start.9) | collective-permute-done | bytes 524320 | tf_op jit(solution)/shard_map/ppermute | solution.py:315
  38.0 0.8 collective-permute-done.10.refs_4_
  38.8 5.6 %collective-permute-done.8.refs_1_ = bf16[2048,128]{1,0:T(8,128)(2,1)S(1)} collective-permute-done((bf16[2048,128]{1,0:T(8,128)(2,1)S(1)}, bf16[2048,128]{1,0:T(8,128)(2,1)S(1)}, u32[]{:S(2)}, u32[]{:S(2)}) %collective-permute-start.8) | collective-permute-done | bytes 524320 | tf_op jit(solution)/shard_map/ppermute | solution.py:315
  44.4 0.4 stage_sum.1
  44.8 1.0 collective-permute-start.12
  45.8 2.7 %collective-permute-start.13 = (bf16[1024,128]{1,0:T(8,128)(2,1)S(1)}, bf16[1024,128]{1,0:T(8,128)(2,1)S(1)}, u32[]{:S(2)}, u32[]{:S(2)}) collective-permute-start(bf16[1024,128]{1,0:T(8,128)(2,1)S(1)} %get-tuple-element.80), channel_id=1, source_target_pairs={{0,2},{1,3},{2,0},{3,1},{4,6},{5,7},{6,4},{7,5},{8,10},{9,11},{10,... | collective-permute-start | bytes 786440 | tf_op jit(solution)/shard_map/ppermute | solution.py:315
  48.5 0.9 collective-permute-start.14
  49.4 2.2 %collective-permute-done.12.refs_1_ = bf16[1024,128]{1,0:T(8,128)(2,1)S(1)} collective-permute-done((bf16[1024,128]{1,0:T(8,128)(2,1)S(1)}, bf16[1024,128]{1,0:T(8,128)(2,1)S(1)}, u32[]{:S(2)}, u32[]{:S(2)}) %collective-permute-start.12) | collective-permute-done | bytes 262176 | tf_op jit(solution)/shard_map/ppermute | solution.py:315
  51.6 3.8 %collective-permute-done.13.refs_2_ = bf16[1024,128]{1,0:T(8,128)(2,1)S(1)} collective-permute-done((bf16[1024,128]{1,0:T(8,128)(2,1)S(1)}, bf16[1024,128]{1,0:T(8,128)(2,1)S(1)}, u32[]{:S(2)}, u32[]{:S(2)}) %collective-permute-start.13) | collective-permute-done | bytes 262176 | tf_op jit(solution)/shard_map/ppermute | solution.py:315
  55.5 3.2 %collective-permute-start.15 = (bf16[512,128]{1,0:T(8,128)(2,1)S(1)}, bf16[512,128]{1,0:T(8,128)(2,1)S(1)}, u32[]{:S(2)}, u32[]{:S(2)}) collective-permute-start(bf16[512,128]{1,0:T(8,128)(2,1)S(1)} %get-tuple-element.83), channel_id=1, source_target_pairs={{0,16},{1,17},{2,18},{3,19},{4,20},{5,21},{6,22},{7,23},{8,24},{9,... | collective-permute-start | bytes 393224 | tf_op jit(solution)/shard_map/ppermute | solution.py:315
  58.7 1.0 collective-permute-done.15.refs_1_
  59.7 1.1 pointwise.1
  61.5 0.4 collective-permute-start.20
  62.2 0.6 collective-permute-start.17
  62.8 2.7 %collective-permute-start.18 = (bf16[1024,128]{1,0:T(8,128)(2,1)S(1)}, bf16[1024,128]{1,0:T(8,128)(2,1)S(1)}, u32[]{:S(2)}, u32[]{:S(2)}) collective-permute-start(bf16[1024,128]{1,0:T(8,128)(2,1)S(1)} %pair_grads.1.refs_0_), channel_id=1, source_target_pairs={{0,2},{1,3},{2,0},{3,1},{4,6},{5,7},{6,4},{7,5},{8,10},{9,11},{10,... | collective-permute-start | bytes 786440 | tf_op jit(solution)/shard_map/ppermute | solution.py:315
  65.5 0.7 collective-permute-start.19
  66.2 4.2 %collective-permute-done.21 = f32[136,256]{1,0:T(8,128)S(1)} collective-permute-done((f32[136,256]{1,0:T(8,128)S(1)}, f32[136,256]{1,0:T(8,128)S(1)}, u32[]{:S(2)}, u32[]{:S(2)}) %collective-permute-start.21) | collective-permute-done | bytes 139296 | tf_op jit(solution)/shard_map/ppermute | solution.py:315
  70.4 1.9 %collective-permute-done.18.refs_2_ = bf16[1024,128]{1,0:T(8,128)(2,1)S(1)} collective-permute-done((bf16[1024,128]{1,0:T(8,128)(2,1)S(1)}, bf16[1024,128]{1,0:T(8,128)(2,1)S(1)}, u32[]{:S(2)}, u32[]{:S(2)}) %collective-permute-start.18) | collective-permute-done | bytes 262176 | tf_op jit(solution)/shard_map/ppermute | solution.py:315
  72.5 1.3 %collective-permute-start.22 = (bf16[2048,128]{1,0:T(8,128)(2,1)S(1)}, bf16[2048,128]{1,0:T(8,128)(2,1)S(1)}, u32[]{:S(2)}, u32[]{:S(2)}) collective-permute-start(bf16[2048,128]{1,0:T(8,128)(2,1)S(1)} %get-tuple-element.98.refs_4_), channel_id=1, source_target_pairs={{0,4},{1,5},{2,6},{3,7},{4,8},{5,9},{6,10},{7,11},{8,12},{9,13},{1... | collective-permute-start | bytes 1572872 | tf_op jit(solution)/shard_map/ppermute | solution.py:315
  73.8 1.4 %collective-permute-start.26 = (bf16[2048,128]{1,0:T(8,128)(2,1)S(1)}, bf16[2048,128]{1,0:T(8,128)(2,1)S(1)}, u32[]{:S(2)}, u32[]{:S(2)}) collective-permute-start(bf16[2048,128]{1,0:T(8,128)(2,1)S(1)} %get-tuple-element.99.refs_5_), channel_id=1, source_target_pairs={{0,12},{1,13},{2,14},{3,15},{4,0},{5,1},{6,2},{7,3},{8,4},{9,5},{1... | collective-permute-start | bytes 1572872 | tf_op jit(solution)/shard_map/ppermute | solution.py:315
  75.2 1.1 collective-permute-start.23
  76.3 2.7 %collective-permute-start.25 = (bf16[2048,128]{1,0:T(8,128)(2,1)S(1)}, bf16[2048,128]{1,0:T(8,128)(2,1)S(1)}, u32[]{:S(2)}, u32[]{:S(2)}) collective-permute-start(bf16[2048,128]{1,0:T(8,128)(2,1)S(1)} %get-tuple-element.98.refs_4_), channel_id=1, source_target_pairs={{0,12},{1,13},{2,14},{3,15},{4,0},{5,1},{6,2},{7,3},{8,4},{9,5},{1... | collective-permute-start | bytes 1572872 | tf_op jit(solution)/shard_map/ppermute | solution.py:315
  79.0 1.7 %collective-permute-done.23 = f32[136,256]{1,0:T(8,128)S(1)} collective-permute-done((f32[136,256]{1,0:T(8,128)S(1)}, f32[136,256]{1,0:T(8,128)S(1)}, u32[]{:S(2)}, u32[]{:S(2)}) %collective-permute-start.23) | collective-permute-done | bytes 139296 | tf_op jit(solution)/shard_map/ppermute | solution.py:315
  80.7 1.4 %collective-permute-done.22.refs_6_ = bf16[2048,128]{1,0:T(8,128)(2,1)S(1)} collective-permute-done((bf16[2048,128]{1,0:T(8,128)(2,1)S(1)}, bf16[2048,128]{1,0:T(8,128)(2,1)S(1)}, u32[]{:S(2)}, u32[]{:S(2)}) %collective-permute-start.22) | collective-permute-done | bytes 524320 | tf_op jit(solution)/shard_map/ppermute | solution.py:315
  82.1 2.7 %collective-permute-start.28 = (bf16[2048,128]{1,0:T(8,128)(2,1)S(1)}, bf16[2048,128]{1,0:T(8,128)(2,1)S(1)}, u32[]{:S(2)}, u32[]{:S(2)}) collective-permute-start(bf16[2048,128]{1,0:T(8,128)(2,1)S(1)} %collective-permute-done.26.refs_9_), channel_id=1, source_target_pairs={{0,12},{1,13},{2,14},{3,15},{4,0},{5,1},{6,2},{7,3},{8,4},{9,5},{1... | collective-permute-start | bytes 1572872 | tf_op jit(solution)/shard_map/ppermute | solution.py:315
  84.8 2.9 %collective-permute-done.24.refs_7_ = bf16[2048,128]{1,0:T(8,128)(2,1)S(1)} collective-permute-done((bf16[2048,128]{1,0:T(8,128)(2,1)S(1)}, bf16[2048,128]{1,0:T(8,128)(2,1)S(1)}, u32[]{:S(2)}, u32[]{:S(2)}) %collective-permute-start.24) | collective-permute-done | bytes 524320 | tf_op jit(solution)/shard_map/ppermute | solution.py:315
  87.7 1.0 collective-permute-start.34
  88.8 1.6 %collective-permute-start.35 = (f32[136,256]{1,0:T(8,128)S(1)}, f32[136,256]{1,0:T(8,128)S(1)}, u32[]{:S(2)}, u32[]{:S(2)}) collective-permute-start(f32[136,256]{1,0:T(8,128)S(1)} %add.17.s0), channel_id=1, source_target_pairs={{0,12},{1,13},{2,14},{3,15},{4,0},{5,1},{6,2},{7,3},{8,4},{9,5},{1... | collective-permute-start | bytes 417800 | tf_op jit(solution)/shard_map/ppermute | solution.py:315
  90.4 3.3 %backward_early.1.refs_4_ = f32[4096,128]{1,0:T(8,128)S(1)} custom-call(s32[2,128]{1,0:T(2,128)S(1)} %ids.1.refs_0_, bf16[128,128,128]{2,1,0:T(8,128)(2,1)S(1)} %get-tuple-element.65.refs_1_, s32[2,128]{1,0:T(2,128)S(1)} %collective-permute-done.2.refs_2_, bf16[128,128,128]{2,1,0:T(8,128)(2,1)S(1)} %collective-permute-done.3.refs_3_, ...), custom_call_target="tpu_custom_call" | custom-call | flops 805306368 | bytes 10485760 | tf_op jit(solution)/shard_map/backward_early/pallas_call | solution.py:58
  93.7 1.8 %backward_late.1 = (bf16[1024,128]{1,0:T(8,128)(2,1)S(1)}, bf16[1024,128]{1,0:T(8,128)(2,1)S(1)}, bf16[1024,128]{1,0:T(8,128)(2,1)S(1)}, bf16[1024,128]{1,0:T(8,128)(2,1)S(1)}) custom-call(s32[2,128]{1,0:T(2,128)S(1)} %ids.1.refs_0_, bf16[128,128,128]{2,1,0:T(8,128)(2,1)S(1)} %get-tuple-element.65.refs_1_, s32[2,128]{1,0:T(2,128)S(1)} %collective-permute-done.2.refs_2_, ...), custom_call_target="tpu_custom_call" | custom-call | flops 268435456 | bytes 6291456 | tf_op jit(solution)/shard_map/backward_late/pallas_call | solution.py:58
  95.5 0.9 collective-permute-done.34.s2
  96.5 1.2 %collective-permute-start.36 = (f32[136,256]{1,0:T(8,128)S(1)}, f32[136,256]{1,0:T(8,128)S(1)}, u32[]{:S(2)}, u32[]{:S(2)}) collective-permute-start(f32[136,256]{1,0:T(8,128)S(1)} %sum_u.1), channel_id=1, source_target_pairs={{0,1},{1,0},{2,3},{3,2},{4,5},{5,4},{6,7},{7,6},{8,9},{9,8},{10,11... | collective-permute-start | bytes 417800 | tf_op jit(solution)/shard_map/ppermute | solution.py:315
  97.7 2.0 %collective-permute-start.29 = (bf16[1024,128]{1,0:T(8,128)(2,1)S(1)}, bf16[1024,128]{1,0:T(8,128)(2,1)S(1)}, u32[]{:S(2)}, u32[]{:S(2)}) collective-permute-start(bf16[1024,128]{1,0:T(8,128)(2,1)S(1)} %get-tuple-element.103), channel_id=1, source_target_pairs={{0,32},{1,33},{2,34},{3,35},{4,36},{5,37},{6,38},{7,39},{8,40},{9,... | collective-permute-start | bytes 786440 | tf_op jit(solution)/shard_map/ppermute | solution.py:315
  99.7 0.6 collective-permute-start.31
  100.5 2.4 %collective-permute-start.37 = (f32[136,256]{1,0:T(8,128)S(1)}, f32[136,256]{1,0:T(8,128)S(1)}, u32[]{:S(2)}, u32[]{:S(2)}) collective-permute-start(f32[136,256]{1,0:T(8,128)S(1)} %add.18), channel_id=1, source_target_pairs={{0,2},{1,3},{2,0},{3,1},{4,6},{5,7},{6,4},{7,5},{8,10},{9,11},{10,... | collective-permute-start | bytes 417800 | tf_op jit(solution)/shard_map/ppermute | solution.py:315
  102.8 3.1 %collective-permute-done.37 = f32[136,256]{1,0:T(8,128)S(1)} collective-permute-done((f32[136,256]{1,0:T(8,128)S(1)}, f32[136,256]{1,0:T(8,128)S(1)}, u32[]{:S(2)}, u32[]{:S(2)}) %collective-permute-start.37) | collective-permute-done | bytes 139296 | tf_op jit(solution)/shard_map/ppermute | solution.py:315
  106.0 5.9 %collective-permute-start.38 = (f32[136,256]{1,0:T(8,128)S(1)}, f32[136,256]{1,0:T(8,128)S(1)}, u32[]{:S(2)}, u32[]{:S(2)}) collective-permute-start(f32[136,256]{1,0:T(8,128)S(1)} %add.19.mine), channel_id=1, source_target_pairs={{0,16},{1,17},{2,18},{3,19},{4,20},{5,21},{6,22},{7,23},{8,24},{9,... | collective-permute-start | bytes 417800 | tf_op jit(solution)/shard_map/ppermute | solution.py:315
  112.1 3.7 %collective-permute-start.32 = (bf16[512,128]{1,0:T(8,128)(2,1)S(1)}, bf16[512,128]{1,0:T(8,128)(2,1)S(1)}, u32[]{:S(2)}, u32[]{:S(2)}) collective-permute-start(bf16[512,128]{1,0:T(8,128)(2,1)S(1)} %get-tuple-element.107), channel_id=1, source_target_pairs={{0,16},{1,17},{2,18},{3,19},{4,20},{5,21},{6,22},{7,23},{8,24},{9,... | collective-permute-start | bytes 393224 | tf_op jit(solution)/shard_map/ppermute | solution.py:315
  115.8 1.0 collective-permute-done.32.peer
  116.8 0.9 last.1
  (52 shorter events, 3.0 us)
Async XLA Ops:
  0.6 1.0 copy-start.2
  1.6 2.5 %collective-permute-start = (bf16[512,128]{1,0:T(8,128)(2,1)S(1)}, bf16[512,128]{1,0:T(8,128)(2,1)S(1)}, u32[]{:S(2)}, u32[]{:S(2)}) collective-permute-start(bf16[512,128]{1,0:T(8,128)(2,1)S(1)} %get-tuple-element.58), channel_id=1, source_target_pairs={{0,16},{1,17},{2,18},{3,19},{4,20},{5,21},{6,22},{7,23},{8,24},{9,... | collective-permute-start | bytes 393224 | tf_op jit(solution)/shard_map/ppermute | solution.py:315
  4.1 16.0 %collective-permute-start.3 = (bf16[128,128,128]{2,1,0:T(8,128)(2,1)}, bf16[128,128,128]{2,1,0:T(8,128)(2,1)S(1)}, u32[]{:S(2)}, u32[]{:S(2)}) collective-permute-start(bf16[128,128,128]{2,1,0:T(8,128)(2,1)} %bitcast.5), channel_id=1, source_target_pairs={{0,16},{1,17},{2,18},{3,19},{4,20},{5,21},{6,22},{7,23},{8,24},{9,... | collective-permute-start | bytes 12582920 | tf_op jit(solution)/shard_map/ppermute | solution.py:315
  4.5 13.3 %collective-permute-start.1 = (bf16[1024,128]{1,0:T(8,128)(2,1)S(1)}, bf16[1024,128]{1,0:T(8,128)(2,1)S(1)}, u32[]{:S(2)}, u32[]{:S(2)}) collective-permute-start(bf16[1024,128]{1,0:T(8,128)(2,1)S(1)} %pair.1.refs_4_), channel_id=1, source_target_pairs={{0,32},{1,33},{2,34},{3,35},{4,36},{5,37},{6,38},{7,39},{8,40},{9,... | collective-permute-start | bytes 786440 | tf_op jit(solution)/shard_map/ppermute | solution.py:315
  7.4 10.4 %collective-permute-start.4 = (bf16[1024,128]{1,0:T(8,128)(2,1)S(1)}, bf16[1024,128]{1,0:T(8,128)(2,1)S(1)}, u32[]{:S(2)}, u32[]{:S(2)}) collective-permute-start(bf16[1024,128]{1,0:T(8,128)(2,1)S(1)} %pair.1.refs_4_), channel_id=1, source_target_pairs={{0,64},{1,65},{2,66},{3,67},{4,68},{5,69},{6,70},{7,71},{8,72},{9,... | collective-permute-start | bytes 786440 | tf_op jit(solution)/shard_map/ppermute | solution.py:315
  7.7 12.4 %collective-permute-start.5 = (bf16[1024,128]{1,0:T(8,128)(2,1)S(1)}, bf16[1024,128]{1,0:T(8,128)(2,1)S(1)}, u32[]{:S(2)}, u32[]{:S(2)}) collective-permute-start(bf16[1024,128]{1,0:T(8,128)(2,1)S(1)} %pair.1.refs_4_), channel_id=1, source_target_pairs={{0,96},{1,97},{2,98},{3,99},{4,100},{5,101},{6,102},{7,103},{8,104... | collective-permute-start | bytes 786440 | tf_op jit(solution)/shard_map/ppermute | solution.py:315
  8.4 0.7 copy-start.5
  9.1 0.7 copy-start.6
  9.7 8.1 %collective-permute-start.2 = (s32[2,128]{1,0:T(2,128)S(1)}, s32[2,128]{1,0:T(2,128)S(1)}, u32[]{:S(2)}, u32[]{:S(2)}) collective-permute-start(s32[2,128]{1,0:T(2,128)S(1)} %ids.1.refs_0_), channel_id=1, source_target_pairs={{0,16},{1,17},{2,18},{3,19},{4,20},{5,21},{6,22},{7,23},{8,24},{9,... | collective-permute-start | bytes 3080 | tf_op jit(solution)/shard_map/ppermute | solution.py:315
  11.9 2.2 %copy-start = (bf16[1,1,128,128,128]{4,3,2,1,0:T(8,128)(2,1)S(1)}, bf16[1,1,128,128,128]{4,3,2,1,0:T(8,128)(2,1)}, u32[]{:S(2)}) copy-start(bf16[1,1,128,128,128]{4,3,2,1,0:T(8,128)(2,1)} %param.8) | copy-start | bytes 12582916
  14.1 0.9 copy-start.1
  15.1 0.9 copy-start.3
  16.0 0.7 copy-start.4
  22.0 10.8 %collective-permute-start.6 = (bf16[2048,128]{1,0:T(8,128)(2,1)S(1)}, bf16[2048,128]{1,0:T(8,128)(2,1)S(1)}, u32[]{:S(2)}, u32[]{:S(2)}) collective-permute-start(bf16[2048,128]{1,0:T(8,128)(2,1)S(1)} %get-tuple-element.71), channel_id=1, source_target_pairs={{0,4},{1,5},{2,6},{3,7},{4,8},{5,9},{6,10},{7,11},{8,12},{9,13},{1... | collective-permute-start | bytes 1572872 | tf_op jit(solution)/shard_map/ppermute | solution.py:315
  23.9 8.9 %collective-permute-start.7 = (bf16[2048,128]{1,0:T(8,128)(2,1)S(1)}, bf16[2048,128]{1,0:T(8,128)(2,1)S(1)}, u32[]{:S(2)}, u32[]{:S(2)}) collective-permute-start(bf16[2048,128]{1,0:T(8,128)(2,1)S(1)} %get-tuple-element.72), channel_id=1, source_target_pairs={{0,12},{1,13},{2,14},{3,15},{4,0},{5,1},{6,2},{7,3},{8,4},{9,5},{1... | collective-permute-start | bytes 1572872 | tf_op jit(solution)/shard_map/ppermute | solution.py:315
  27.8 10.2 %collective-permute-start.9 = (bf16[2048,128]{1,0:T(8,128)(2,1)S(1)}, bf16[2048,128]{1,0:T(8,128)(2,1)S(1)}, u32[]{:S(2)}, u32[]{:S(2)}) collective-permute-start(bf16[2048,128]{1,0:T(8,128)(2,1)S(1)} %get-tuple-element.74), channel_id=1, source_target_pairs={{0,12},{1,13},{2,14},{3,15},{4,0},{5,1},{6,2},{7,3},{8,4},{9,5},{1... | collective-permute-start | bytes 1572872 | tf_op jit(solution)/shard_map/ppermute | solution.py:315
  29.3 9.5 %collective-permute-start.10 = (bf16[2048,128]{1,0:T(8,128)(2,1)S(1)}, bf16[2048,128]{1,0:T(8,128)(2,1)S(1)}, u32[]{:S(2)}, u32[]{:S(2)}) collective-permute-start(bf16[2048,128]{1,0:T(8,128)(2,1)S(1)} %get-tuple-element.76), channel_id=1, source_target_pairs={{0,4},{1,5},{2,6},{3,7},{4,8},{5,9},{6,10},{7,11},{8,12},{9,13},{1... | collective-permute-start | bytes 1572872 | tf_op jit(solution)/shard_map/ppermute | solution.py:315
  33.1 11.4 %collective-permute-start.8 = (bf16[2048,128]{1,0:T(8,128)(2,1)S(1)}, bf16[2048,128]{1,0:T(8,128)(2,1)S(1)}, u32[]{:S(2)}, u32[]{:S(2)}) collective-permute-start(bf16[2048,128]{1,0:T(8,128)(2,1)S(1)} %get-tuple-element.73), channel_id=1, source_target_pairs={{0,4},{1,5},{2,6},{3,7},{4,8},{5,9},{6,10},{7,11},{8,12},{9,13},{1... | collective-permute-start | bytes 1572872 | tf_op jit(solution)/shard_map/ppermute | solution.py:315
  34.1 10.3 %collective-permute-start.11 = (bf16[2048,128]{1,0:T(8,128)(2,1)S(1)}, bf16[2048,128]{1,0:T(8,128)(2,1)S(1)}, u32[]{:S(2)}, u32[]{:S(2)}) collective-permute-start(bf16[2048,128]{1,0:T(8,128)(2,1)S(1)} %get-tuple-element.77), channel_id=1, source_target_pairs={{0,12},{1,13},{2,14},{3,15},{4,0},{5,1},{6,2},{7,3},{8,4},{9,5},{1... | collective-permute-start | bytes 1572872 | tf_op jit(solution)/shard_map/ppermute | solution.py:315
  44.8 6.8 %collective-permute-start.12 = (bf16[1024,128]{1,0:T(8,128)(2,1)S(1)}, bf16[1024,128]{1,0:T(8,128)(2,1)S(1)}, u32[]{:S(2)}, u32[]{:S(2)}) collective-permute-start(bf16[1024,128]{1,0:T(8,128)(2,1)S(1)} %get-tuple-element.79), channel_id=1, source_target_pairs={{0,1},{1,2},{2,3},{3,0},{4,5},{5,6},{6,7},{7,4},{8,9},{9,10},{10,1... | collective-permute-start | bytes 786440 | tf_op jit(solution)/shard_map/ppermute | solution.py:315
  45.8 9.6 %collective-permute-start.13 = (bf16[1024,128]{1,0:T(8,128)(2,1)S(1)}, bf16[1024,128]{1,0:T(8,128)(2,1)S(1)}, u32[]{:S(2)}, u32[]{:S(2)}) collective-permute-start(bf16[1024,128]{1,0:T(8,128)(2,1)S(1)} %get-tuple-element.80), channel_id=1, source_target_pairs={{0,2},{1,3},{2,0},{3,1},{4,6},{5,7},{6,4},{7,5},{8,10},{9,11},{10,... | collective-permute-start | bytes 786440 | tf_op jit(solution)/shard_map/ppermute | solution.py:315
  48.5 6.9 %collective-permute-start.14 = (bf16[1024,128]{1,0:T(8,128)(2,1)S(1)}, bf16[1024,128]{1,0:T(8,128)(2,1)S(1)}, u32[]{:S(2)}, u32[]{:S(2)}) collective-permute-start(bf16[1024,128]{1,0:T(8,128)(2,1)S(1)} %get-tuple-element.81), channel_id=1, source_target_pairs={{0,3},{1,0},{2,1},{3,2},{4,7},{5,4},{6,5},{7,6},{8,11},{9,8},{10,9... | collective-permute-start | bytes 786440 | tf_op jit(solution)/shard_map/ppermute | solution.py:315
  55.5 4.2 %collective-permute-start.15 = (bf16[512,128]{1,0:T(8,128)(2,1)S(1)}, bf16[512,128]{1,0:T(8,128)(2,1)S(1)}, u32[]{:S(2)}, u32[]{:S(2)}) collective-permute-start(bf16[512,128]{1,0:T(8,128)(2,1)S(1)} %get-tuple-element.83), channel_id=1, source_target_pairs={{0,16},{1,17},{2,18},{3,19},{4,20},{5,21},{6,22},{7,23},{8,24},{9,... | collective-permute-start | bytes 393224 | tf_op jit(solution)/shard_map/ppermute | solution.py:315
  60.8 1.3 %collective-permute-start.16 = (bf16[512,128]{1,0:T(8,128)(2,1)S(1)}, bf16[512,128]{1,0:T(8,128)(2,1)S(1)}, u32[]{:S(2)}, u32[]{:S(2)}) collective-permute-start(bf16[512,128]{1,0:T(8,128)(2,1)S(1)} %get-tuple-element.89), channel_id=1, source_target_pairs={{0,16},{1,17},{2,18},{3,19},{4,20},{5,21},{6,22},{7,23},{8,24},{9,... | collective-permute-start | bytes 393224 | tf_op jit(solution)/shard_map/ppermute | solution.py:315
  61.5 4.6 %collective-permute-start.20 = (f32[136,256]{1,0:T(8,128)S(1)}, f32[136,256]{1,0:T(8,128)S(1)}, u32[]{:S(2)}, u32[]{:S(2)}) collective-permute-start(f32[136,256]{1,0:T(8,128)S(1)} %get-tuple-element.93), channel_id=1, source_target_pairs={{0,16},{1,17},{2,18},{3,19},{4,20},{5,21},{6,22},{7,23},{8,24},{9,... | collective-permute-start | bytes 417800 | tf_op jit(solution)/shard_map/ppermute | solution.py:315
  62.2 8.2 %collective-permute-start.17 = (bf16[1024,128]{1,0:T(8,128)(2,1)S(1)}, bf16[1024,128]{1,0:T(8,128)(2,1)S(1)}, u32[]{:S(2)}, u32[]{:S(2)}) collective-permute-start(bf16[1024,128]{1,0:T(8,128)(2,1)S(1)} %pair_grads.1.refs_0_), channel_id=1, source_target_pairs={{0,1},{1,2},{2,3},{3,0},{4,5},{5,6},{6,7},{7,4},{8,9},{9,10},{10,1... | collective-permute-start | bytes 786440 | tf_op jit(solution)/shard_map/ppermute | solution.py:315
  62.8 9.5 %collective-permute-start.18 = (bf16[1024,128]{1,0:T(8,128)(2,1)S(1)}, bf16[1024,128]{1,0:T(8,128)(2,1)S(1)}, u32[]{:S(2)}, u32[]{:S(2)}) collective-permute-start(bf16[1024,128]{1,0:T(8,128)(2,1)S(1)} %pair_grads.1.refs_0_), channel_id=1, source_target_pairs={{0,2},{1,3},{2,0},{3,1},{4,6},{5,7},{6,4},{7,5},{8,10},{9,11},{10,... | collective-permute-start | bytes 786440 | tf_op jit(solution)/shard_map/ppermute | solution.py:315
  65.5 7.0 %collective-permute-start.19 = (bf16[1024,128]{1,0:T(8,128)(2,1)S(1)}, bf16[1024,128]{1,0:T(8,128)(2,1)S(1)}, u32[]{:S(2)}, u32[]{:S(2)}) collective-permute-start(bf16[1024,128]{1,0:T(8,128)(2,1)S(1)} %pair_grads.1.refs_0_), channel_id=1, source_target_pairs={{0,3},{1,0},{2,1},{3,2},{4,7},{5,4},{6,5},{7,6},{8,11},{9,8},{10,9... | collective-permute-start | bytes 786440 | tf_op jit(solution)/shard_map/ppermute | solution.py:315
  66.1 4.3 %collective-permute-start.21 = (f32[136,256]{1,0:T(8,128)S(1)}, f32[136,256]{1,0:T(8,128)S(1)}, u32[]{:S(2)}, u32[]{:S(2)}) collective-permute-start(f32[136,256]{1,0:T(8,128)S(1)} %add.15), channel_id=1, source_target_pairs={{0,32},{1,33},{2,34},{3,35},{4,36},{5,37},{6,38},{7,39},{8,40},{9,... | collective-permute-start | bytes 417800 | tf_op jit(solution)/shard_map/ppermute | solution.py:315
  72.5 9.6 %collective-permute-start.22 = (bf16[2048,128]{1,0:T(8,128)(2,1)S(1)}, bf16[2048,128]{1,0:T(8,128)(2,1)S(1)}, u32[]{:S(2)}, u32[]{:S(2)}) collective-permute-start(bf16[2048,128]{1,0:T(8,128)(2,1)S(1)} %get-tuple-element.98.refs_4_), channel_id=1, source_target_pairs={{0,4},{1,5},{2,6},{3,7},{4,8},{5,9},{6,10},{7,11},{8,12},{9,13},{1... | collective-permute-start | bytes 1572872 | tf_op jit(solution)/shard_map/ppermute | solution.py:315
  73.8 8.3 %collective-permute-start.26 = (bf16[2048,128]{1,0:T(8,128)(2,1)S(1)}, bf16[2048,128]{1,0:T(8,128)(2,1)S(1)}, u32[]{:S(2)}, u32[]{:S(2)}) collective-permute-start(bf16[2048,128]{1,0:T(8,128)(2,1)S(1)} %get-tuple-element.99.refs_5_), channel_id=1, source_target_pairs={{0,12},{1,13},{2,14},{3,15},{4,0},{5,1},{6,2},{7,3},{8,4},{9,5},{1... | collective-permute-start | bytes 1572872 | tf_op jit(solution)/shard_map/ppermute | solution.py:315
  75.2 5.4 %collective-permute-start.23 = (f32[136,256]{1,0:T(8,128)S(1)}, f32[136,256]{1,0:T(8,128)S(1)}, u32[]{:S(2)}, u32[]{:S(2)}) collective-permute-start(f32[136,256]{1,0:T(8,128)S(1)} %add.16), channel_id=1, source_target_pairs={{0,64},{1,65},{2,66},{3,67},{4,68},{5,69},{6,70},{7,71},{8,72},{9,... | collective-permute-start | bytes 417800 | tf_op jit(solution)/shard_map/ppermute | solution.py:315
  76.3 11.4 %collective-permute-start.24 = (bf16[2048,128]{1,0:T(8,128)(2,1)S(1)}, bf16[2048,128]{1,0:T(8,128)(2,1)S(1)}, u32[]{:S(2)}, u32[]{:S(2)}) collective-permute-start(bf16[2048,128]{1,0:T(8,128)(2,1)S(1)} %get-tuple-element.99.refs_5_), channel_id=1, source_target_pairs={{0,4},{1,5},{2,6},{3,7},{4,8},{5,9},{6,10},{7,11},{8,12},{9,13},{1... | collective-permute-start | bytes 1572872 | tf_op jit(solution)/shard_map/ppermute | solution.py:315
  76.3 12.4 %collective-permute-start.25 = (bf16[2048,128]{1,0:T(8,128)(2,1)S(1)}, bf16[2048,128]{1,0:T(8,128)(2,1)S(1)}, u32[]{:S(2)}, u32[]{:S(2)}) collective-permute-start(bf16[2048,128]{1,0:T(8,128)(2,1)S(1)} %get-tuple-element.98.refs_4_), channel_id=1, source_target_pairs={{0,12},{1,13},{2,14},{3,15},{4,0},{5,1},{6,2},{7,3},{8,4},{9,5},{1... | collective-permute-start | bytes 1572872 | tf_op jit(solution)/shard_map/ppermute | solution.py:315
  82.1 11.6 %collective-permute-start.27 = (bf16[2048,128]{1,0:T(8,128)(2,1)S(1)}, bf16[2048,128]{1,0:T(8,128)(2,1)S(1)}, u32[]{:S(2)}, u32[]{:S(2)}) collective-permute-start(bf16[2048,128]{1,0:T(8,128)(2,1)S(1)} %collective-permute-done.22.refs_6_), channel_id=1, source_target_pairs={{0,4},{1,5},{2,6},{3,7},{4,8},{5,9},{6,10},{7,11},{8,12},{9,13},{1... | collective-permute-start | bytes 1572872 | tf_op jit(solution)/shard_map/ppermute | solution.py:315
  82.1 11.6 %collective-permute-start.28 = (bf16[2048,128]{1,0:T(8,128)(2,1)S(1)}, bf16[2048,128]{1,0:T(8,128)(2,1)S(1)}, u32[]{:S(2)}, u32[]{:S(2)}) collective-permute-start(bf16[2048,128]{1,0:T(8,128)(2,1)S(1)} %collective-permute-done.26.refs_9_), channel_id=1, source_target_pairs={{0,12},{1,13},{2,14},{3,15},{4,0},{5,1},{6,2},{7,3},{8,4},{9,5},{1... | collective-permute-start | bytes 1572872 | tf_op jit(solution)/shard_map/ppermute | solution.py:315
  84.8 10.7 %collective-permute-start.33 = (f32[136,256]{1,0:T(8,128)S(1)}, f32[136,256]{1,0:T(8,128)S(1)}, u32[]{:S(2)}, u32[]{:S(2)}) collective-permute-start(f32[136,256]{1,0:T(8,128)S(1)} %add.17.s0), channel_id=1, source_target_pairs={{0,4},{1,5},{2,6},{3,7},{4,8},{5,9},{6,10},{7,11},{8,12},{9,13},{1... | collective-permute-start | bytes 417800 | tf_op jit(solution)/shard_map/ppermute | solution.py:315
  87.7 8.7 %collective-permute-start.34 = (f32[136,256]{1,0:T(8,128)S(1)}, f32[136,256]{1,0:T(8,128)S(1)}, u32[]{:S(2)}, u32[]{:S(2)}) collective-permute-start(f32[136,256]{1,0:T(8,128)S(1)} %add.17.s0), channel_id=1, source_target_pairs={{0,8},{1,9},{2,10},{3,11},{4,12},{5,13},{6,14},{7,15},{8,0},{9,1},... | collective-permute-start | bytes 417800 | tf_op jit(solution)/shard_map/ppermute | solution.py:315
  88.8 7.6 %collective-permute-start.35 = (f32[136,256]{1,0:T(8,128)S(1)}, f32[136,256]{1,0:T(8,128)S(1)}, u32[]{:S(2)}, u32[]{:S(2)}) collective-permute-start(f32[136,256]{1,0:T(8,128)S(1)} %add.17.s0), channel_id=1, source_target_pairs={{0,12},{1,13},{2,14},{3,15},{4,0},{5,1},{6,2},{7,3},{8,4},{9,5},{1... | collective-permute-start | bytes 417800 | tf_op jit(solution)/shard_map/ppermute | solution.py:315
  96.5 4.0 %collective-permute-start.36 = (f32[136,256]{1,0:T(8,128)S(1)}, f32[136,256]{1,0:T(8,128)S(1)}, u32[]{:S(2)}, u32[]{:S(2)}) collective-permute-start(f32[136,256]{1,0:T(8,128)S(1)} %sum_u.1), channel_id=1, source_target_pairs={{0,1},{1,0},{2,3},{3,2},{4,5},{5,4},{6,7},{7,6},{8,9},{9,8},{10,11... | collective-permute-start | bytes 417800 | tf_op jit(solution)/shard_map/ppermute | solution.py:315
  97.7 14.3 %collective-permute-start.29 = (bf16[1024,128]{1,0:T(8,128)(2,1)S(1)}, bf16[1024,128]{1,0:T(8,128)(2,1)S(1)}, u32[]{:S(2)}, u32[]{:S(2)}) collective-permute-start(bf16[1024,128]{1,0:T(8,128)(2,1)S(1)} %get-tuple-element.103), channel_id=1, source_target_pairs={{0,32},{1,33},{2,34},{3,35},{4,36},{5,37},{6,38},{7,39},{8,40},{9,... | collective-permute-start | bytes 786440 | tf_op jit(solution)/shard_map/ppermute | solution.py:315
  99.7 12.2 %collective-permute-start.30 = (bf16[1024,128]{1,0:T(8,128)(2,1)S(1)}, bf16[1024,128]{1,0:T(8,128)(2,1)S(1)}, u32[]{:S(2)}, u32[]{:S(2)}) collective-permute-start(bf16[1024,128]{1,0:T(8,128)(2,1)S(1)} %get-tuple-element.104), channel_id=1, source_target_pairs={{0,64},{1,65},{2,66},{3,67},{4,68},{5,69},{6,70},{7,71},{8,72},{9,... | collective-permute-start | bytes 786440 | tf_op jit(solution)/shard_map/ppermute | solution.py:315
  99.7 12.2 %collective-permute-start.31 = (bf16[1024,128]{1,0:T(8,128)(2,1)S(1)}, bf16[1024,128]{1,0:T(8,128)(2,1)S(1)}, u32[]{:S(2)}, u32[]{:S(2)}) collective-permute-start(bf16[1024,128]{1,0:T(8,128)(2,1)S(1)} %get-tuple-element.105), channel_id=1, source_target_pairs={{0,96},{1,97},{2,98},{3,99},{4,100},{5,101},{6,102},{7,103},{8,104... | collective-permute-start | bytes 786440 | tf_op jit(solution)/shard_map/ppermute | solution.py:315
  100.5 5.5 %collective-permute-start.37 = (f32[136,256]{1,0:T(8,128)S(1)}, f32[136,256]{1,0:T(8,128)S(1)}, u32[]{:S(2)}, u32[]{:S(2)}) collective-permute-start(f32[136,256]{1,0:T(8,128)S(1)} %add.18), channel_id=1, source_target_pairs={{0,2},{1,3},{2,0},{3,1},{4,6},{5,7},{6,4},{7,5},{8,10},{9,11},{10,... | collective-permute-start | bytes 417800 | tf_op jit(solution)/shard_map/ppermute | solution.py:315
  106.0 10.8 %collective-permute-start.38 = (f32[136,256]{1,0:T(8,128)S(1)}, f32[136,256]{1,0:T(8,128)S(1)}, u32[]{:S(2)}, u32[]{:S(2)}) collective-permute-start(f32[136,256]{1,0:T(8,128)S(1)} %add.19.mine), channel_id=1, source_target_pairs={{0,16},{1,17},{2,18},{3,19},{4,20},{5,21},{6,22},{7,23},{8,24},{9,... | collective-permute-start | bytes 417800 | tf_op jit(solution)/shard_map/ppermute | solution.py:315
  112.1 4.7 %collective-permute-start.32 = (bf16[512,128]{1,0:T(8,128)(2,1)S(1)}, bf16[512,128]{1,0:T(8,128)(2,1)S(1)}, u32[]{:S(2)}, u32[]{:S(2)}) collective-permute-start(bf16[512,128]{1,0:T(8,128)(2,1)S(1)} %get-tuple-element.107), channel_id=1, source_target_pairs={{0,16},{1,17},{2,18},{3,19},{4,20},{5,21},{6,22},{7,23},{8,24},{9,... | collective-permute-start | bytes 393224 | tf_op jit(solution)/shard_map/ppermute | solution.py:315
